TPU v7x, 256 devices: a whole 4x4x8 slice. The times are simulated.
256 devices in a mesh: ctx: 32 (over x_hi, z, core), tp: 8 (over y, x_lo).
Axes of the slice: x: 4 (x_hi: 2, x_lo: 2; x = x_hi * 2 + x_lo), y: 4, z: 8, core: 2. Of those that a mesh axis runs over, the one named last changes fastest.
Arguments:
- queries: bfloat16 [4096, 4096], P('ctx', 'tp'), may hold values from -6 to 6
- keys: bfloat16 [4096, 8192], P('ctx', 'tp'), may hold values from -6 to 6
- values: bfloat16 [4096, 8192], P('ctx', 'tp'), may hold values from -6 to 6
- beta_logit: float32 [32, 8192], P('tp', 'ctx'), may hold values from -8 to 8
- out_weight: bfloat16 [4096, 4096], P('ctx', 'tp'), may hold values from -0.1875 to 0.1875
- out_grad: bfloat16 [4096, 4096], P('ctx', 'tp'), may hold values from -6 to 6
Outputs:
- mixed: bfloat16 [4096, 4096], P('ctx', 'tp')
- query_grad: bfloat16 [4096, 4096], P('ctx', 'tp')
- key_grad: bfloat16 [4096, 8192], P('ctx', 'tp')
- value_grad: bfloat16 [4096, 8192], P('ctx', 'tp')
- logit_grad: float32 [32, 8192], P('tp', 'ctx')
- weight_grad: float32 [4096, 4096], P('ctx', 'tp')
All inputs are finite; a program needn't handle non-finite values.
Results may differ from a plain program's by a relative error of at most 0.023.
Values may be sent and summed in bfloat16 or wider, within the bound.
No kernel may reach another device: no remote copies, remote signals or barrier semaphores. Data moves between devices by JAX's collectives and lax.ppermute only.
A program may use at most 128 MiB of HBM per device.

v0:
```python
import math

import jax
import jax.numpy as jnp
from jax import lax
from jax.sharding import PartitionSpec as P


def shifted(block, axis, distance):
    devices = range(lax.axis_size(axis))
    route = [(i - distance, i) for i in devices if i - distance in devices]
    return lax.ppermute(block, axis, route)


def normalize(matrix):
    return matrix * lax.rsqrt(jnp.sum(matrix * matrix, axis=-1, keepdims=True) + 1e-06)


def mix_blocks(memory, query_heads, key_heads, value_heads, strength):
    head_count, length, width = query_heads.shape
    blocks = length // 64
    query_blk = query_heads.reshape(head_count, blocks, 64, width).transpose(1, 0, 2, 3)
    key_blk = key_heads.reshape(head_count, blocks, 128, width).transpose(1, 0, 2, 3)
    value_blk = value_heads.reshape(head_count, blocks, 128, value_heads.shape[2]).transpose(
        1, 0, 2, 3
    )
    gate_blk = strength.reshape(head_count, blocks, 128).transpose(1, 0, 2)
    row_ids = lax.broadcasted_iota(jnp.int32, (128, 128), 0)
    col_ids = lax.broadcasted_iota(jnp.int32, (128, 128), 1)
    below_diag = col_ids < row_ids
    token_ids = lax.broadcasted_iota(jnp.int32, (64, 128), 0)
    refl_ids = lax.broadcasted_iota(jnp.int32, (64, 128), 1)
    visible = refl_ids <= 2 * token_ids + 1
    identity_map = jnp.eye(128, dtype=jnp.float32)
    highest = lax.Precision.HIGHEST

    def advance(current, pieces):
        query_x, key_x, value_x, gate_x = pieces
        key_gram = jnp.einsum("hid,hjd->hij", key_x, key_x, precision=highest)
        system = identity_map + jnp.where(below_diag, gate_x[:, :, None] * key_gram, 0.0)
        right_side = gate_x[:, :, None] * (
            value_x - jnp.einsum("hid,hde->hie", key_x, current, precision=highest)
        )
        updates = lax.linalg.triangular_solve(
            system, right_side, left_side=True, lower=True, unit_diagonal=True
        )
        scores = jnp.where(
            visible, jnp.einsum("htd,hid->hti", query_x, key_x, precision=highest), 0.0
        )
        result = jnp.einsum("htd,hde->hte", query_x, current, precision=highest)
        result = result + jnp.einsum("hti,hie->hte", scores, updates, precision=highest)
        current = current + jnp.einsum("hid,hie->hde", key_x, updates, precision=highest)
        return (current, result)

    memory, block_out = lax.scan(advance, memory, (query_blk, key_blk, value_blk, gate_blk))
    block_out = block_out.transpose(1, 0, 2, 3).reshape(head_count, length, block_out.shape[3])
    return (block_out, memory)


def head_layout(query_f, key_f, value_f, logits):
    head_count = logits.shape[0]
    length = query_f.shape[0]
    width = query_f.shape[1] // head_count
    query_heads = normalize(query_f.reshape(length, head_count, width)).transpose(1, 0, 2)
    key_heads = (
        normalize(key_f.reshape(length, head_count, 2, width))
        .transpose(1, 0, 2, 3)
        .reshape(head_count, 2 * length, width)
    )
    value_heads = (
        value_f.reshape(length, head_count, 2, width)
        .transpose(1, 0, 2, 3)
        .reshape(head_count, 2 * length, width)
    )
    strength = 2.0 * jax.nn.sigmoid(logits)
    return (query_heads, key_heads, value_heads, strength)


def group_map(memory, query_f, key_f, value_f, logits):
    head_count = logits.shape[0]
    length = query_f.shape[0]
    width = query_f.shape[1] // head_count
    query_heads, key_heads, value_heads, strength = head_layout(query_f, key_f, value_f, logits)
    block_out, memory = mix_blocks(memory, query_heads, key_heads, value_heads, strength)
    return (block_out.transpose(1, 0, 2).reshape(length, head_count * width), memory)


def matmul_heads(left, right):
    return jnp.einsum("hij,hjk->hik", left, right, precision=lax.Precision.HIGHEST)


def local(queries, keys, values, beta_logit, out_weight, out_grad):
    head_count = beta_logit.shape[0]
    length = queries.shape[0]
    width = queries.shape[1] // head_count
    query_f = queries.astype(jnp.float32)
    key_f = keys.astype(jnp.float32)
    value_f = values.astype(jnp.float32)
    identity_map = jnp.broadcast_to(jnp.eye(width, dtype=jnp.float32), (head_count, width, width))
    zero_state = jnp.zeros((head_count, width, width), jnp.float32)
    query_heads, key_heads, value_heads, strength = head_layout(query_f, key_f, value_f, beta_logit)
    widened_values = jnp.concatenate([jnp.zeros_like(value_heads), value_heads], axis=2)
    widened_start = jnp.concatenate([identity_map, zero_state], axis=2)
    _, widened_end = mix_blocks(widened_start, query_heads, key_heads, widened_values, strength)
    transition = widened_end[:, :, :width]
    offset = widened_end[:, :, width:]

    def hand_on(turn_index, memory):
        return shifted(
            (matmul_heads(transition, memory) + offset).astype(jnp.bfloat16), "ctx", 1
        ).astype(jnp.float32)

    state_in = lax.fori_loop(0, lax.axis_size("ctx") - 1, hand_on, zero_state)
    (heads_f, _), pull = jax.vjp(group_map, state_in, query_f, key_f, value_f, beta_logit)
    heads_out = heads_f.astype(jnp.bfloat16)
    weight_full = lax.all_gather(out_weight, "ctx", axis=0, tiled=True)
    mixed_cols = lax.psum_scatter(
        lax.dot_general(
            weight_full, heads_out, (((1,), (1,)), ((), ())), preferred_element_type=jnp.float32
        ).astype(jnp.bfloat16),
        "tp",
        scatter_dimension=0,
        tiled=True,
    ).astype(jnp.float32)
    mixed = mixed_cols.T.astype(jnp.bfloat16)
    grad_full = lax.all_gather(out_grad, "tp", axis=1, tiled=True)
    head_grad = jnp.dot(grad_full, weight_full, preferred_element_type=jnp.float32)

    def state_only(start_memory):
        return group_map(start_memory, query_f, key_f, value_f, beta_logit)[0]

    _, state_pull = jax.vjp(state_only, state_in)
    own_cotangent = state_pull(head_grad)[0]
    transposed = transition.transpose(0, 2, 1)

    def hand_back(turn_index, memory):
        return shifted(
            (matmul_heads(transposed, memory) + own_cotangent).astype(jnp.bfloat16), "ctx", -1
        ).astype(jnp.float32)

    state_grad = lax.fori_loop(0, lax.axis_size("ctx") - 1, hand_back, zero_state)
    _, query_grad, key_grad, value_grad, logit_grad = pull((head_grad, state_grad))
    scale_factor = 1.0 / math.sqrt(length * lax.axis_size("ctx"))
    product = lax.dot_general(
        grad_full, heads_out, (((0,), (0,)), ((), ())), preferred_element_type=jnp.float32
    )
    weight_grad = lax.psum_scatter(
        (product * scale_factor).astype(jnp.bfloat16), "ctx", scatter_dimension=0, tiled=True
    ).astype(jnp.float32)
    return (
        mixed,
        query_grad.astype(jnp.bfloat16),
        key_grad.astype(jnp.bfloat16),
        value_grad.astype(jnp.bfloat16),
        logit_grad,
        weight_grad,
    )


def solution(mesh):
    placed = (
        P("ctx", "tp"),
        P("ctx", "tp"),
        P("ctx", "tp"),
        P("tp", "ctx"),
        P("ctx", "tp"),
        P("ctx", "tp"),
    )
    return jax.shard_map(
        local,
        mesh=mesh,
        in_specs=placed,
        out_specs=(
            P("ctx", "tp"),
            P("ctx", "tp"),
            P("ctx", "tp"),
            P("ctx", "tp"),
            P("tp", "ctx"),
            P("ctx", "tp"),
        ),
        check_vma=False,
    )
```

profile of v0, /device:TPU:6, one launch (start us, length us, event | category | flops | bytes accessed | tf_op | source)
XLA Modules:
  0.0 1099.7 jit_solution(5836034309626853711)
XLA Ops:
  14.3 85.6 %while.118 = (s32[]{:T(128)}, f32[4,128,256]{2,1,0:T(8,128)S(1)}, f32[2,4,128,128]{3,2,1,0:T(8,128)S(1)}, f32[2,4,128]{2,1,0:T(4,128)}, f32[2,4,128,256]{3,2,0,1:T(8,128)S(1)}, /*index=5*/s32[]{:T(128)}) while((s32[]{:T(128)}, f32[4,128,256]{2,1,0:T(8,128)S(1)}, f32[2,4,128,128]{3,2,1,0:T(8,128)S(1)}, f32[2,4,128]{2,1,0:T(4,128)}, ...), condition=%wide.region_2.3_spmd.clone, body=%wide.region_1.2_spmd.clone.sunk | while | flops 705462400 | bytes 5843033 | solution.py:55
  16.4 39.3 %custom-call.26 = f32[4,1,128,128]{2,3,1,0:T(8,128)S(1)} custom-call(f32[4,1,128,128]{3,2,1,0:T(8,128)S(1)} %fusion.325), custom_call_target="InvertDiagBlocksLowerTriangular" | custom-call | tf_op jit(solution)/shard_map/while/body/eval_jaxpr/triangular_solve | solution.py:44
  59.2 39.3 %custom-call.26 = f32[4,1,128,128]{2,3,1,0:T(8,128)S(1)} custom-call(f32[4,1,128,128]{3,2,1,0:T(8,128)S(1)} %fusion.325), custom_call_target="InvertDiagBlocksLowerTriangular" | custom-call | tf_op jit(solution)/shard_map/while/body/eval_jaxpr/triangular_solve | solution.py:44
  103.3 324.4 %while.122 = (s32[]{:T(128)}, f32[4,128,128]{2,1,0:T(8,128)S(1)}, f32[4,128,128]{2,1,0:T(8,128)S(1)}, f32[4,128,128]{2,1,0:T(8,128)S(1)}, s32[]{:T(128)}, /*index=5*/s32[]{:T(128)}) while((s32[]{:T(128)}, f32[4,128,128]{2,1,0:T(8,128)S(1)}, f32[4,128,128]{2,1,0:T(8,128)S(1)}, f32[4,128,128]{2,1,0:T(8,128)S(1)}, s32[]{:T(128)}, ...), condition=%wide.region_4.5_spmd.clone, body=%wide.region_3.4_spmd.clone.sunk | while | flops 100925440 | bytes 1835127 | solution.py:113
  105.6 10.2 collective-permute-done
  118.1 8.3 collective-permute-done
  128.8 9.3 collective-permute-done
  140.4 8.0 collective-permute-done
  150.8 8.0 collective-permute-done
  161.1 8.0 collective-permute-done
  171.4 8.0 collective-permute-done
  181.8 8.0 collective-permute-done
  192.1 8.0 collective-permute-done
  202.5 8.0 collective-permute-done
  212.8 8.0 collective-permute-done
  223.2 8.0 collective-permute-done
  233.5 8.0 collective-permute-done
  264.5 8.0 collective-permute-done
  316.2 8.0 collective-permute-done
  347.2 8.0 collective-permute-done
  378.3 8.0 collective-permute-done
  431.6 100.7 %while.119 = (s32[]{:T(128)}, f32[4,128,128]{2,1,0:T(8,128)S(1)}, bf16[2,4,64,128]{3,2,0,1:T(8,128)(2,1)}, f32[2,4,128,128]{3,2,1,0:T(8,128)}, f32[2,4,128,1]{2,...) while((s32[]{:T(128)}, f32[4,128,128]{2,1,0:T(8,128)S(1)}, ...), condition=%wide.region_7.8_spmd.clone, body=%wide.region_6.7_spmd.clone.sunk | while | flops 554516608 | bytes 7768797 | solution.py:55
  435.5 39.9 %custom-call.27 = f32[4,1,128,128]{2,3,1,0:T(8,128)} custom-call(f32[4,1,128,128]{3,2,1,0:T(8,128)S(1)} %add_bitcast_fusion.2), custom_call_target="InvertDiagBlocksLowerTriangular" | custom-call | tf_op jit(solution)/shard_map/jvp()/while/body/eval_jaxpr/triangular_solve | solution.py:44
  485.8 39.9 %custom-call.27 = f32[4,1,128,128]{2,3,1,0:T(8,128)} custom-call(f32[4,1,128,128]{3,2,1,0:T(8,128)S(1)} %add_bitcast_fusion.2), custom_call_target="InvertDiagBlocksLowerTriangular" | custom-call | tf_op jit(solution)/shard_map/jvp()/while/body/eval_jaxpr/triangular_solve | solution.py:44
  547.4 9.3 while.120
  563.0 87.5 %while.123 = (s32[]{:T(128)}, f32[4,128,128]{2,1,0:T(8,128)S(1)}, f32[2,4,64,128]{3,2,1,0:T(8,128)S(1)}, f32[2,4,64,128]{3,2,1,0:T(8,128)S(1)}, f32[2,4,128,128]...) while((s32[]{:T(128)}, f32[4,128,128]{2,1,0:T(8,128)S(1)}, ...), condition=%wide.region_12.14_spmd.clone, body=%wide.region_11.13_spmd.clone.sunk | while | flops 403292288 | bytes 4892307 | solution.py:55
  565.7 39.3 %custom-call.29 = f32[4,1,128,128]{2,3,1,0:T(8,128)S(1)} custom-call(f32[4,1,128,128]{3,2,1,0:T(8,128)S(1)} %fusion.395), custom_call_target="InvertDiagBlocksLowerTriangular" | custom-call | tf_op jit(solution)/shard_map/transpose(jvp())/while/body/eval_jaxpr/triangular_solve/custom-call.2 | solution.py:44
  609.5 39.3 %custom-call.29 = f32[4,1,128,128]{2,3,1,0:T(8,128)S(1)} custom-call(f32[4,1,128,128]{3,2,1,0:T(8,128)S(1)} %fusion.395), custom_call_target="InvertDiagBlocksLowerTriangular" | custom-call | tf_op jit(solution)/shard_map/transpose(jvp())/while/body/eval_jaxpr/triangular_solve/custom-call.2 | solution.py:44
  650.6 315.6 %while.124 = (s32[]{:T(128)}, f32[4,128,128]{2,1,0:T(8,128)S(1)}, f32[4,128,128]{2,1,0:T(8,128)S(1)}, f32[4,128,128]{2,1,0:T(8,128)S(1)}, s32[]{:T(128)}, /*index=5*/s32[]{:T(128)}) while((s32[]{:T(128)}, f32[4,128,128]{2,1,0:T(8,128)S(1)}, f32[4,128,128]{2,1,0:T(8,128)S(1)}, f32[4,128,128]{2,1,0:T(8,128)S(1)}, s32[]{:T(128)}, ...), condition=%wide.region_14.16_spmd.clone, body=%wide.region_13.15_spmd.clone.sunk | while | flops 100925440 | bytes 1835127 | solution.py:141
  968.3 113.2 %while.121 = (s32[]{:T(128)}, f32[4,128,128]{2,1,0:T(8,128)S(1)}, f32[2,4,64,128]{3,2,0,1:T(8,128)}, f32[2,4,128,128]{3,2,0,1:T(8,128)}, bf16[2,4,128,128]{3,2,0...) while((s32[]{:T(128)}, f32[4,128,128]{2,1,0:T(8,128)S(1)}, ...), condition=%wide.region_18.20_spmd.clone, body=%wide.region_15.19_spmd.clone.sunk | while | flops 1209646720 | bytes 20684108 | solution.py:55
  973.8 39.3 %custom-call.28 = f32[4,1,128,128]{2,3,1,0:T(8,128)S(1)} custom-call(f32[4,1,128,128]{3,2,1,0:T(8,128)S(1)} %fusion.372), custom_call_target="InvertDiagBlocksLowerTriangular" | custom-call | tf_op jit(solution)/shard_map/transpose(jvp())/while/body/eval_jaxpr/triangular_solve/custom-call.2 | solution.py:44
  1030.4 39.3 %custom-call.28 = f32[4,1,128,128]{2,3,1,0:T(8,128)S(1)} custom-call(f32[4,1,128,128]{3,2,1,0:T(8,128)S(1)} %fusion.372), custom_call_target="InvertDiagBlocksLowerTriangular" | custom-call | tf_op jit(solution)/shard_map/transpose(jvp())/while/body/eval_jaxpr/triangular_solve/custom-call.2 | solution.py:44
  (497 shorter events, 627.4 us)
Async XLA Ops:
  7.2 526.3 %all-gather.5.cloned.1.call-start = ((), (), s32[]{:S(2)}) async-start(), calls=%async_computation.4 | async-start | bytes 1179648 | tf_op jit(solution)/shard_map/all_gather | solution.py:126
  7.9 548.8 %all-gather.3.cloned.1.call-start = ((), (), s32[]{:S(2)}) async-start(), calls=%async_computation.2 | async-start | bytes 4325376 | tf_op jit(solution)/shard_map/all_gather | solution.py:116
  8.7 1082.1 %reduce-scatter.7.cloned.1.call-start = ((), (), s32[]{:S(2)}) async-start(), calls=%async_computation.5 | async-start | bytes 4325376
  103.7 12.1 %collective-permute-start = (bf16[4,128,128]{2,1,0:T(8,128)(2,1)S(1)}, bf16[4,128,128]{2,1,0:T(8,128)(2,1)S(1)}, u32[]{:S(2)}, u32[]{:S(2)}) collective-permute-start(bf16[4,128,128]{2,1,0:T(8,128)(2,1)S(1)} %fusion.383), channel_id=1, source_target_pairs={{0,8},{8,16},{16,24},{24,32},{32,40},{40,48},{48,56},{56,64},{64,7... | collective-permute-start | bytes 393224 | tf_op jit(solution)/shard_map/while/body/eval_jaxpr/ppermute | solution.py:12
  116.2 10.3 collective-permute-start
  126.9 11.2 %collective-permute-start = (bf16[4,128,128]{2,1,0:T(8,128)(2,1)S(1)}, bf16[4,128,128]{2,1,0:T(8,128)(2,1)S(1)}, u32[]{:S(2)}, u32[]{:S(2)}) collective-permute-start(bf16[4,128,128]{2,1,0:T(8,128)(2,1)S(1)} %fusion.383), channel_id=1, source_target_pairs={{0,8},{8,16},{16,24},{24,32},{32,40},{40,48},{48,56},{56,64},{64,7... | collective-permute-start | bytes 393224 | tf_op jit(solution)/shard_map/while/body/eval_jaxpr/ppermute | solution.py:12
  544.5 548.7 %reduce-scatter.5.cloned.1.call-start = ((), (), s32[]{:S(2)}) async-start(), calls=%async_computation.3 | async-start | bytes 1179648 | tf_op jit(solution)/shard_map/reduce_scatter | solution.py:117
  656.0 9.9 collective-permute-start.1
  666.3 9.9 collective-permute-start.1
  676.7 9.9 collective-permute-start.1
  687.0 10.0 collective-permute-start.1
  697.5 10.0 collective-permute-start.1
  707.9 10.0 collective-permute-start.1
  718.4 9.9 collective-permute-start.1
  728.7 9.9 collective-permute-start.1
  739.0 9.9 collective-permute-start.1
  749.4 9.9 collective-permute-start.1
  759.7 9.9 collective-permute-start.1
  770.1 9.9 collective-permute-start.1
  780.4 9.9 collective-permute-start.1
  790.7 9.9 collective-permute-start.1
  801.1 9.9 collective-permute-start.1
  811.4 9.9 collective-permute-start.1
  832.1 9.9 collective-permute-start.1
  842.4 9.9 collective-permute-start.1
  863.1 9.9 collective-permute-start.1
  873.5 9.9 collective-permute-start.1
  894.2 9.9 collective-permute-start.1
  914.8 9.9 collective-permute-start.1
  925.2 9.9 collective-permute-start.1
  945.9 9.9 collective-permute-start.1
  956.2 9.9 collective-permute-start.1
  (65 other events, 1300.5 us)
Sparse Core Ops, SparseCore 0:
  9.8 44.0 all-gather.4
  56.6 87.5 all-gather.2
  544.6 122.8 reduce-scatter.6
  670.6 40.2 reduce-scatter.4
where the time goes:
time: 1100 us
  other arithmetic  332 us (30%)
  waiting for transfers between devices  330 us (30%)
  starting transfers between devices  284 us (26%)
  matrix products  91.8 us (8%)
  local copies, waits for them, and re-layouts  44.8 us (4%)
  between operations  14.2 us (1%)
    ppermute x62, waiting for transfers between devices, shifted(): return lax.ppermute(block, axis, route)  329 us
    another operation x30, other arithmetic, advance(): lax.linalg.triangular_solve(system, right_side, left_side=True, lower=Tru...  321 us
    ppermute x62, starting transfers between devices, shifted(): return lax.ppermute(block, axis, route)  284 us
    dot_general x62, matrix products, matmul_heads(): jnp.einsum('hij,hjk->hik', left, right, precision=lax.Precision.HIGHEST)  24.3 us
  transfers between devices with their start and end apart: 66, of which 62 were waited for; matrix products, arithmetic and copies ran while one was open for 42% of the time, Pallas kernels for 0%

commit v1 on v0

v1 whole, which is shorter than its diff:
```python
import functools
import math

import jax
import jax.numpy as jnp
from jax import lax
from jax.experimental import pallas as pl
from jax.experimental.pallas import tpu as pltpu
from jax.sharding import PartitionSpec as P

F32 = jnp.float32
BF16 = jnp.bfloat16
WIDTH = 128
PAIRS = 2 * WIDTH


def send(block, distance):
    devices = range(lax.axis_size("ctx"))
    route = [(i - distance, i) for i in devices if i - distance in devices]
    return lax.ppermute(block, "ctx", route)


def exchange(block, bit):
    route = [(i, i ^ bit) for i in range(lax.axis_size("ctx"))]
    return lax.ppermute(block, "ctx", route)


def split(x):
    high = x.astype(BF16)
    return high, (x - high.astype(F32)).astype(BF16)


def dot(a, b, ca=1, cb=0, passes=3):
    dims = (((ca,), (cb,)), ((), ()))
    mul = functools.partial(lax.dot_general, dimension_numbers=dims, preferred_element_type=F32)
    a_high, a_low = split(a)
    b_high, b_low = split(b)
    if passes == 1:
        return mul(a_high, b_high)
    return mul(a_high, b_high) + (mul(a_low, b_high) + mul(a_high, b_low))


def inverse_norm(x):
    return lax.rsqrt(jnp.sum(x * x, axis=-1, keepdims=True) + 1e-06)


def order_of(shape, dim):
    p = lax.broadcasted_iota(jnp.int32, shape, dim)
    return 2 * (p & (WIDTH - 1)) + (p >> 7)


def column_of(row):
    shape = (PAIRS, PAIRS)
    time = lax.broadcasted_iota(jnp.int32, shape, 1)
    return jnp.sum(jnp.where(time == order_of(shape, 0), row, 0.0), axis=1, keepdims=True)


def row_of(column):
    shape = (PAIRS, PAIRS)
    time = lax.broadcasted_iota(jnp.int32, shape, 1)
    return jnp.sum(jnp.where(time == order_of(shape, 0), column, 0.0), axis=0, keepdims=True)


def visible_mask():
    shape = (WIDTH, PAIRS)
    token = lax.broadcasted_iota(jnp.int32, shape, 0)
    return (lax.broadcasted_iota(jnp.int32, shape, 1) & (WIDTH - 1)) <= token


def stacked(ref):
    return jnp.concatenate([ref[:, :WIDTH], ref[:, WIDTH:]], axis=0).astype(F32)


def prepare_kernel(place, q_ref, k_ref, v_ref, logit_ref, ab_ref, m_ref, wy_ref, qt_ref, local_ref):
    head = pl.program_id(0)
    query = q_ref[...].astype(F32)
    query = query * inverse_norm(query)
    key = stacked(k_ref)
    key = key * inverse_norm(key)
    value = stacked(v_ref)
    strength = 2.0 / (1.0 + jnp.exp(-column_of(logit_ref[pl.ds(head, 1), :])))
    shape = (PAIRS, PAIRS)
    row, col = order_of(shape, 0), order_of(shape, 1)
    coupling = jnp.where(col < row, strength * dot(key, key, 1, 1), 0.0)
    identity = jnp.where(row == col, 1.0, 0.0).astype(F32)
    inverse = identity - jnp.where((row >> 1) == (col >> 1), coupling, 0.0)
    for level in range(1, 8):
        join = ((row >> (level + 1)) == (col >> (level + 1))) & ((row >> level) != (col >> level))
        edge = jnp.where(join, coupling, 0.0)
        inverse = inverse - dot(dot(inverse, edge), inverse)
    scores = jnp.where(visible_mask(), dot(query, key, 1, 1), 0.0)
    scaled = strength * jnp.concatenate([key, value], axis=1)
    wy_ref[0] = dot(inverse, scaled)
    reads = jnp.concatenate([dot(scores, inverse), dot(key, inverse, 0, 0)], axis=0)
    m_ref[0] = reads
    product = dot(reads, scaled)
    qt_ref[0] = query - product[:WIDTH, :WIDTH]
    local_ref[0] = product[:WIDTH, WIDTH:]
    eye = jnp.where(
        lax.broadcasted_iota(jnp.int32, (WIDTH, WIDTH), 0)
        == lax.broadcasted_iota(jnp.int32, (WIDTH, WIDTH), 1),
        1.0,
        0.0,
    )
    ab_ref[0, :, :WIDTH] = (eye - product[WIDTH:, :WIDTH]).astype(BF16)
    ab_ref[0, :, WIDTH:] = product[WIDTH:, WIDTH:].astype(BF16)


def slot(head, place):
    return (head + 2 * place[0]) % 4


def by_head(*block):
    return pl.BlockSpec((1,) + block, lambda h, place: (h,) + (0,) * len(block))


def by_slot(*block):
    return pl.BlockSpec((1,) + block, lambda h, place: (slot(h, place),) + (0,) * len(block))


def by_columns(width):
    return pl.BlockSpec((WIDTH, width), lambda h, place: (0, h))


def whole(*shape):
    return pl.BlockSpec(shape, lambda i, place: (0,) * len(shape))


def call(kernel, steps, in_specs, out_specs, out_shape, flops, moved, scratch=()):
    return pl.pallas_call(
        kernel,
        grid_spec=pltpu.PrefetchScalarGridSpec(
            num_scalar_prefetch=1,
            grid=(steps,),
            in_specs=in_specs,
            out_specs=out_specs,
            scratch_shapes=list(scratch),
        ),
        out_shape=out_shape,
        compiler_params=pltpu.CompilerParams(vmem_limit_bytes=40 << 20),
        cost_estimate=pl.CostEstimate(flops=flops, bytes_accessed=moved, transcendentals=0),
    )


def arr(dtype, *shape):
    return jax.ShapeDtypeStruct(shape, dtype)


def prepare(place, queries, keys, values, logits):
    return call(
        prepare_kernel,
        4,
        [by_columns(WIDTH), by_columns(PAIRS), by_columns(PAIRS), whole(4, PAIRS)],
        [
            by_slot(WIDTH, PAIRS),
            by_head(PAIRS, PAIRS),
            by_head(PAIRS, PAIRS),
            by_head(WIDTH, WIDTH),
            by_head(WIDTH, WIDTH),
        ],
        [
            arr(BF16, 4, WIDTH, PAIRS),
            arr(F32, 4, PAIRS, PAIRS),
            arr(F32, 4, PAIRS, PAIRS),
            arr(F32, 4, WIDTH, WIDTH),
            arr(F32, 4, WIDTH, WIDTH),
        ],
        4 * 60 * 2 * PAIRS**3,
        4 << 20,
    )(place, queries, keys, values, logits)


def feature_block(grad_ref, place, z, row, core):
    owner = (row ^ place[1]) * 4 + z // 2
    column = pl.multiple_of((z % 2) * 256 + (core ^ place[0]) * 128, 128)
    return owner, pl.ds(column, 128)


def outputs_kernel(place, qt_ref, local_ref, state_ref, grad_ref, heads_ref, mine_ref, other_ref, held):
    z = pl.program_id(0)

    @pl.when(z == 0)
    def _():
        for head in range(4):
            state = state_ref[slot(head, place)].astype(F32)
            result = dot(qt_ref[head], state) + local_ref[head]
            held[:, head * WIDTH : (head + 1) * WIDTH] = result.astype(BF16)
        heads_ref[...] = held[...]

    for row in range(2):
        for core, out_ref in ((0, mine_ref), (1, other_ref)):
            owner, columns = feature_block(grad_ref, place, z, row, core)
            block = grad_ref[owner, :, columns]
            product = lax.dot_general(
                block, held[...], (((0,), (0,)), ((), ())), preferred_element_type=F32
            )
            out_ref[0, row] = (product * (1.0 / 64.0)).astype(BF16)


def outputs(place, qt, local, state, grad_full):
    heads = arr(BF16, WIDTH, 512)
    part = arr(BF16, 8, 2, WIDTH, 512)
    tile = pl.BlockSpec((1, 2, WIDTH, 512), lambda z, place: (z, 0, 0, 0))
    return call(
        outputs_kernel,
        8,
        [whole(4, WIDTH, WIDTH), whole(4, WIDTH, WIDTH), whole(4, WIDTH, WIDTH), whole(8, WIDTH, 512)],
        [whole(WIDTH, 512), tile, tile],
        [heads, part, part],
        2 * 128 * 512 * 4096,
        6 << 20,
        [pltpu.VMEM((WIDTH, 512), BF16)],
    )(place, qt, local, state, grad_full)


def mixed_kernel(place, heads_ref, mine_ref, other_ref, out_ref):
    z = pl.program_id(0)
    for row in range(2):
        for core, w_ref in ((0, mine_ref), (1, other_ref)):
            owner, columns = feature_block(out_ref, place, z, row, core)
            product = lax.dot_general(
                heads_ref[...], w_ref[0, row], (((1,), (1,)), ((), ())), preferred_element_type=F32
            )
            out_ref[owner, :, columns] = product.astype(BF16)


def mixed_parts(place, heads, mine, other):
    tile = pl.BlockSpec((1, 2, WIDTH, 512), lambda z, place: (z, 0, 0, 0))
    return call(
        mixed_kernel,
        8,
        [whole(WIDTH, 512), tile, tile],
        whole(8, WIDTH, 512),
        arr(BF16, 8, WIDTH, 512),
        2 * 128 * 512 * 4096,
        6 << 20,
    )(place, heads, mine, other)


def head_grad_kernel(place, grad_ref, mine_ref, other_ref, qt_ref, out_ref, own_ref):
    z = pl.program_id(0)
    total = jnp.zeros((WIDTH, 512), F32)
    for row in range(2):
        for core, w_ref in ((0, mine_ref), (1, other_ref)):
            owner, columns = feature_block(grad_ref, place, z, row, core)
            total += jnp.dot(
                grad_ref[owner, :, columns], w_ref[0, row], preferred_element_type=F32
            )

    @pl.when(z == 0)
    def _():
        out_ref[...] = total

    @pl.when(z > 0)
    def _():
        out_ref[...] += total

    @pl.when(z == 7)
    def _():
        for head in range(4):
            grad = out_ref[:, head * WIDTH : (head + 1) * WIDTH]
            own_ref[slot(head, place)] = dot(qt_ref[head], grad, 0, 0).astype(BF16)


def head_gradient(place, grad_full, mine, other, qt):
    tile = pl.BlockSpec((1, 2, WIDTH, 512), lambda z, place: (z, 0, 0, 0))
    return call(
        head_grad_kernel,
        8,
        [whole(8, WIDTH, 512), tile, tile, whole(4, WIDTH, WIDTH)],
        [whole(WIDTH, 512), whole(4, WIDTH, WIDTH)],
        [arr(F32, WIDTH, 512), arr(BF16, 4, WIDTH, WIDTH)],
        2 * 128 * 512 * 4096,
        6 << 20,
    )(place, grad_full, mine, other, qt)


def pull_kernel(
    place, q_ref, k_ref, logit_ref, m_ref, wy_ref, state_ref, end_ref, grad_ref,
    dq_ref, dk_ref, dv_ref, dlogit_ref,
):
    head = pl.program_id(0)
    query = q_ref[...].astype(F32)
    query_scale = inverse_norm(query)
    query = query * query_scale
    key = stacked(k_ref)
    key_scale = inverse_norm(key)
    key = key * key_scale
    logit = column_of(logit_ref[pl.ds(head, 1), :])
    strength = 2.0 / (1.0 + jnp.exp(-logit))
    state = state_ref[0].astype(F32)
    end = end_ref[0].astype(F32)
    grad = grad_ref[...]
    shape = (PAIRS, PAIRS)
    before = order_of(shape, 1) < order_of(shape, 0)
    updates = wy_ref[0, :, WIDTH:] - dot(wy_ref[0, :, :WIDTH], state)
    pulled = dot(m_ref[0], jnp.concatenate([grad, end], axis=0), 0, 0)
    value_grad = strength * pulled
    dv_ref[:, :WIDTH] = value_grad[:WIDTH].astype(BF16)
    dv_ref[:, WIDTH:] = value_grad[WIDTH:].astype(BF16)
    slope = jnp.sum(pulled * updates, axis=1, keepdims=True) / (1.0 + jnp.exp(logit))
    dlogit_ref[pl.ds(head, 1), :] = row_of(slope)
    cross = dot(jnp.concatenate([grad, value_grad], axis=0), updates, 1, 1)
    pairs = jnp.concatenate(
        [
            jnp.where(visible_mask(), cross[:WIDTH], 0.0),
            jnp.where(before, -cross[WIDTH:], 0.0),
        ],
        axis=0,
    )
    forward = dot(pairs, key)
    backward = dot(pairs, jnp.concatenate([query, key], axis=0), 0, 0)
    by_state = dot(jnp.concatenate([grad, -value_grad], axis=0), state, 1, 1)
    query_grad = forward[:WIDTH] + by_state[:WIDTH]
    key_grad = forward[WIDTH:] + backward + dot(updates, end, 1, 1) + by_state[WIDTH:]
    query_grad = query_scale * (
        query_grad - query * jnp.sum(query * query_grad, axis=1, keepdims=True)
    )
    key_grad = key_scale * (key_grad - key * jnp.sum(key * key_grad, axis=1, keepdims=True))
    dq_ref[...] = query_grad.astype(BF16)
    dk_ref[:, :WIDTH] = key_grad[:WIDTH].astype(BF16)
    dk_ref[:, WIDTH:] = key_grad[WIDTH:].astype(BF16)


def pull(place, queries, keys, logits, reads, wy, state, end, head_grad):
    return call(
        pull_kernel,
        4,
        [
            by_columns(WIDTH),
            by_columns(PAIRS),
            whole(4, PAIRS),
            by_head(PAIRS, PAIRS),
            by_head(PAIRS, PAIRS),
            by_slot(WIDTH, WIDTH),
            by_slot(WIDTH, WIDTH),
            by_columns(WIDTH),
        ],
        [by_columns(WIDTH), by_columns(PAIRS), by_columns(PAIRS), whole(4, PAIRS)],
        [
            arr(BF16, WIDTH, 512),
            arr(BF16, WIDTH, 1024),
            arr(BF16, WIDTH, 1024),
            arr(F32, 4, PAIRS),
        ],
        4 * 14 * 2 * PAIRS**3,
        5 << 20,
    )(place, queries, keys, logits, reads, wy, state, end, head_grad)


def mul(a, b):
    return jnp.einsum("hij,hjk->hik", a, b, preferred_element_type=F32)


def mul_t(a, b):
    return jnp.einsum("hji,hjk->hik", a, b, preferred_element_type=F32)


def halves(x):
    return x[:, :, :WIDTH], x[:, :, WIDTH:]


def forward_states(ab, core):
    mine, theirs = ab[:2], exchange(ab[2:], 1)
    even = jnp.where(core == 0, mine, theirs)
    odd = jnp.where(core == 0, theirs, mine)
    even_a, even_b = halves(even)
    odd_a, odd_b = halves(odd)
    joined = mul(odd_a, even)
    chip = jnp.concatenate(
        [joined[:, :, :WIDTH], joined[:, :, WIDTH:] + odd_b.astype(F32)], axis=2
    ).astype(BF16)
    one, two = send(chip, 2), send(chip, 4)
    window, state = halves(one)
    windows = [window]
    state = state.astype(F32)
    step = mul(window, two)
    state = state + step[:, :, WIDTH:]
    window = step[:, :, :WIDTH].astype(BF16)
    for distance in (4, 8):
        windows.append(window)
        came = send(jnp.concatenate([window, state.astype(BF16)], axis=2), distance)
        step = mul(window, came)
        state = state + step[:, :, WIDTH:]
        window = step[:, :, :WIDTH].astype(BF16)
    windows.append(window)
    state = state + mul(window, send(state.astype(BF16), 16))
    first = state.astype(BF16)
    second = (mul(even_a, first) + even_b.astype(F32)).astype(BF16)
    kept = jnp.where(core == 0, first, second)
    given = jnp.where(core == 0, second, first)
    return jnp.concatenate([kept, exchange(given, 1)], axis=0), (even_a, odd_a, windows)


def backward_states(own, core, saved):
    even_a, odd_a, windows = saved
    mine, theirs = own[:2], exchange(own[2:], 1)
    even = jnp.where(core == 0, mine, theirs)
    odd = jnp.where(core == 0, theirs, mine)
    total = even.astype(F32) + mul_t(even_a, odd)
    for window, distance in zip(windows, (2, 4, 8)):
        passed = mul_t(window, total.astype(BF16)).astype(BF16)
        total = total + send(passed, -distance).astype(F32)
    rounded = total.astype(BF16)
    far = mul_t(windows[3], rounded).astype(BF16)
    second = send(rounded, -2).astype(F32) + send(far, -18).astype(F32)
    second = second.astype(BF16)
    first = (odd.astype(F32) + mul_t(odd_a, second)).astype(BF16)
    kept = jnp.where(core == 0, first, second)
    given = jnp.where(core == 0, second, first)
    return jnp.concatenate([kept, exchange(given, 1)], axis=0)


def local(queries, keys, values, beta_logit, out_weight, out_grad):
    index = lax.axis_index("ctx")
    core = index & 1
    place = jnp.stack([core, index >> 4]).astype(jnp.int32)
    rings = [[(half * 8 + z) * 2 + c for z in range(8)] for half in range(2) for c in range(2)]
    weight_pair = jnp.stack([out_weight, exchange(out_weight, 16)])
    weight_mine = lax.all_gather(weight_pair, "ctx", axis=0, axis_index_groups=rings)
    weight_other = exchange(weight_mine, 1)
    grad_full = lax.all_to_all(
        jnp.broadcast_to(out_grad[None], (8, WIDTH, 512)), "tp", 0, 0, tiled=True
    )
    ab, reads, wy, qt, local_out = prepare(place, queries, keys, values, beta_logit)
    state, saved = forward_states(ab, core)
    heads, part_mine, part_other = outputs(place, qt, local_out, state, grad_full)
    part = part_mine.astype(F32) + exchange(part_other, 1).astype(F32)
    ring_sum = lax.psum_scatter(
        part.astype(BF16).reshape(8, PAIRS, 512),
        "ctx",
        scatter_dimension=0,
        axis_index_groups=rings,
    )
    weight_grad = ring_sum[:WIDTH].astype(F32) + exchange(ring_sum[WIDTH:], 16).astype(F32)
    mixed = lax.all_to_all(
        mixed_parts(place, heads, weight_mine, weight_other), "tp", 0, 0, tiled=True
    )
    mixed = jnp.sum(mixed.astype(F32), axis=0).astype(BF16)
    head_grad, own = head_gradient(place, grad_full, weight_mine, weight_other, qt)
    end = backward_states(own, core, saved)
    query_grad, key_grad, value_grad, logit_grad = pull(
        place, queries, keys, beta_logit, reads, wy, state, end, head_grad
    )
    return mixed, query_grad, key_grad, value_grad, logit_grad, weight_grad


def solution(mesh):
    placed = P("ctx", "tp")
    return jax.shard_map(
        local,
        mesh=mesh,
        in_specs=(placed, placed, placed, P("tp", "ctx"), placed, placed),
        out_specs=(placed, placed, placed, placed, P("tp", "ctx"), placed),
        check_vma=False,
    )
```

time: 1100 us -> 192 us (0.17)
  the two profiles are of different devices: /device:TPU:6 before, /device:TPU:1 now
where the time goes in v1:
time: 192 us; the launch traced here: 188 us
  starting transfers between devices  70.5 us (37%)
  Pallas kernels  45.4 us (24%)
  waiting for transfers between devices  33.1 us (17%)
  between operations  14.7 us (8%)
  local copies, waits for them, and re-layouts  10.7 us (6%)
  other arithmetic  9.86 us (5%)
  matrix products  3.83 us (2%)
    ppermute x10, starting transfers between devices, send(): return lax.ppermute(block, 'ctx', route)  44 us
    ppermute x10, waiting for transfers between devices, send(): return lax.ppermute(block, 'ctx', route)  25.3 us
    pallas_call x1, Pallas kernels, prepare(): call(prepare_kernel, 4, [by_columns(WIDTH), by_columns(PAIRS), by_columns...  19.7 us
    ppermute x8, starting transfers between devices, exchange(): return lax.ppermute(block, 'ctx', route)  16.1 us
    unnamed x70, local copies, waits for them, and re-layouts  8.64 us
    ppermute x8, waiting for transfers between devices, exchange(): return lax.ppermute(block, 'ctx', route)  7.74 us
    pallas_call x1, Pallas kernels, pull(): call(pull_kernel, 4, [by_columns(WIDTH), by_columns(PAIRS), whole(4, PAIR...  7.03 us
    pallas_call x1, Pallas kernels, mixed_parts(): call(mixed_kernel, 8, [whole(WIDTH, 512), tile, tile], whole(8, WIDTH, 51...  6.95 us
  transfers between devices with their start and end apart: 22, of which 10 were waited for; matrix products, arithmetic and copies ran while one was open for 7% of the time, Pallas kernels for 14%

profile of v1, /device:TPU:1, one launch (start us, length us, event | category | flops | bytes accessed | tf_op | source)
XLA Modules:
  0.0 188.0 jit_solution(14611065865363408854)
XLA Ops:
  10.8 19.7 %shard_map.109 = (bf16[4,128,256]{2,1,0:T(8,128)(2,1)S(1)}, f32[4,256,256]{2,1,0:T(8,128)S(1)}, f32[4,256,256]{2,1,0:T(8,128)S(1)}, f32[4,128,128]{2,1,0:T(8,128)S(1)}, f32[4,128,128]{2,1,0:T(8,128)S(1)}) custom-call(s32[2]{0:T(128)S(1)} %pad_add_fusion.place, bf16[128,512]{1,0:T(8,128)(2,1)S(1)} %copy-done.10, bf16[128,1024]{1,0:T(8,128)(2,1)S(1)} %copy-done.6, ...), custom_call_target="tpu_custom_call" | custom-call | flops 8053063680 | bytes 4194304 | tf_op jit(solution)/shard_map/pallas_call | solution.py:150
  32.2 3.3 %collective-permute-start = (bf16[2,128,256]{2,1,0:T(8,128)(2,1)S(1)}, bf16[2,128,256]{2,1,0:T(8,128)(2,1)S(1)}, u32[]{:S(2)}, u32[]{:S(2)}) collective-permute-start(bf16[2,128,256]{2,1,0:T(8,128)(2,1)S(1)} %slice.68), channel_id=1, source_target_pairs={{0,8},{8,0},{16,24},{24,16},{32,40},{40,32},{48,56},{56,48},{64,72... | collective-permute-start | bytes 393224 | tf_op jit(solution)/shard_map/ppermute | solution.py:25
  36.8 3.2 %collective-permute-start.2 = (bf16[2,128,256]{2,1,0:T(8,128)(2,1)S(1)}, bf16[2,128,256]{2,1,0:T(8,128)(2,1)S(1)}, u32[]{:S(2)}, u32[]{:S(2)}) collective-permute-start(bf16[2,128,256]{2,1,0:T(8,128)(2,1)S(1)} %pad_maximum_fusion.1), channel_id=1, source_target_pairs={{0,32},{8,40},{16,48},{24,56},{32,64},{40,72},{48,80},{56,88},{64,... | collective-permute-start | bytes 393224 | tf_op jit(solution)/shard_map/ppermute | solution.py:20
  40.0 3.5 %collective-permute-start.1 = (bf16[2,128,256]{2,1,0:T(8,128)(2,1)S(1)}, bf16[2,128,256]{2,1,0:T(8,128)(2,1)S(1)}, u32[]{:S(2)}, u32[]{:S(2)}) collective-permute-start(bf16[2,128,256]{2,1,0:T(8,128)(2,1)S(1)} %pad_maximum_fusion.1), channel_id=1, source_target_pairs={{0,16},{8,24},{16,32},{24,40},{32,48},{40,56},{48,64},{56,72},{64,... | collective-permute-start | bytes 393224 | tf_op jit(solution)/shard_map/ppermute | solution.py:20
  43.6 2.8 %collective-permute-start.7 = (bf16[128,512]{1,0:T(8,128)(2,1)S(1)}, bf16[128,512]{1,0:T(8,128)(2,1)S(1)}, u32[]{:S(2)}, u32[]{:S(2)}) collective-permute-start(bf16[128,512]{1,0:T(8,128)(2,1)S(1)} %copy-done.34), channel_id=1, source_target_pairs={{0,128},{8,136},{16,144},{24,152},{32,160},{40,168},{48,176},{56,1... | collective-permute-start | bytes 393224 | tf_op jit(solution)/shard_map/ppermute | solution.py:25
  46.7 7.8 %collective-permute-start.3 = (bf16[2,128,256]{2,1,0:T(8,128)(2,1)S(1)}, bf16[2,128,256]{2,1,0:T(8,128)(2,1)S(1)}, u32[]{:S(2)}, u32[]{:S(2)}) collective-permute-start(bf16[2,128,256]{2,1,0:T(8,128)(2,1)S(1)} %pad_maximum_fusion.2), channel_id=1, source_target_pairs={{0,32},{8,40},{16,48},{24,56},{32,64},{40,72},{48,80},{56,88},{64,... | collective-permute-start | bytes 393224 | tf_op jit(solution)/shard_map/ppermute | solution.py:20
  56.7 12.9 %collective-permute-start.4 = (bf16[2,128,256]{2,1,0:T(8,128)(2,1)S(1)}, bf16[2,128,256]{2,1,0:T(8,128)(2,1)S(1)}, u32[]{:S(2)}, u32[]{:S(2)}) collective-permute-start(bf16[2,128,256]{2,1,0:T(8,128)(2,1)S(1)} %pad_maximum_fusion.3), channel_id=1, source_target_pairs={{0,64},{8,72},{16,80},{24,88},{32,96},{40,104},{48,112},{56,120},{... | collective-permute-start | bytes 393224 | tf_op jit(solution)/shard_map/ppermute | solution.py:20
  70.8 5.8 %all-to-all-start = ((bf16[8,128,512]{2,1,0:T(8,128)(2,1)}), bf16[8,128,512]{2,1,0:T(8,128)(2,1)S(1)}, u32[]{:S(2)}, u32[]{:S(2)}) async-start(bf16[8,128,512]{2,1,0:T(8,128)(2,1)} %broadcast_in_dim.2), calls=%async_computation | async-start | bytes 2097152 | tf_op jit(solution)/shard_map/all_to_all | solution.py:422
  76.9 10.1 %collective-permute-start.5 = (bf16[2,128,128]{2,1,0:T(8,128)(2,1)S(1)}, bf16[2,128,128]{2,1,0:T(8,128)(2,1)S(1)}, u32[]{:S(2)}, u32[]{:S(2)}) collective-permute-start(bf16[2,128,128]{2,1,0:T(8,128)(2,1)S(1)} %fusion.21), channel_id=1, source_target_pairs={{0,128},{8,136},{16,144},{24,152},{32,160},{40,168},{48,176},{56,1... | collective-permute-start | bytes 196616 | tf_op jit(solution)/shard_map/ppermute | solution.py:20
  87.0 4.0 %collective-permute-done.5 = bf16[2,128,128]{2,1,0:T(8,128)(2,1)S(1)} collective-permute-done((bf16[2,128,128]{2,1,0:T(8,128)(2,1)S(1)}, bf16[2,128,128]{2,1,0:T(8,128)(2,1)S(1)}, u32[]{:S(2)}, u32[]{:S(2)}) %collective-permute-start.5) | collective-permute-done | bytes 65568 | tf_op jit(solution)/shard_map/ppermute | solution.py:20
  91.3 1.6 collective-permute-start.6
  96.3 5.4 %shard_map.110 = (bf16[128,512]{1,0:T(8,128)(2,1)S(1)}, bf16[8,2,128,512]{3,2,1,0:T(8,128)(2,1)S(1)}, bf16[8,2,128,512]{3,2,1,0:T(8,128)(2,1)}) custom-call(s32[2]{0:T(128)S(1)} %pad_add_fusion.place, f32[4,128,128]{2,1,0:T(8,128)S(1)} %get-tuple-element.20.qt_ref, f32[4,128,128]{2,1,0:T(8,128)S(1)} %copy-done.15, bf16[4,128,128]{2,1,0:T(8,128)(2,1)S(1)} %copy-done.3, ...), custom_call_target="tpu_custom_call" | custom-call | flops 536870912 | bytes 6291456 | tf_op jit(solution)/shard_map/pallas_call | solution.py:204
  101.7 1.6 collective-permute-start.16
  103.3 4.0 %collective-permute-done.16 = bf16[8,2,128,512]{3,2,1,0:T(8,128)(2,1)} collective-permute-done((bf16[8,2,128,512]{3,2,1,0:T(8,128)(2,1)}, bf16[8,2,128,512]{3,2,1,0:T(8,128)(2,1)}, u32[]{:S(2)}, u32[]{:S(2)}) %collective-permute-start.16) | collective-permute-done | bytes 2097184 | tf_op jit(solution)/shard_map/ppermute | solution.py:25
  107.4 3.6 %add_convert_fusion = bf16[8,2,128,512]{3,2,1,0:T(8,128)(2,1)} fusion(bf16[8,2,128,512]{3,2,1,0:T(8,128)(2,1)} %collective-permute-done.16, bf16[8,2,128,512]{3,2,1,0:T(8,128)(2,1)S(1)} %get-tuple-element.32), kind=kLoop, calls=%fused_computation | loop fusion | flops 4194304 | bytes 6291456 | tf_op jit(solution)/shard_map/convert_element_type | solution.py:430
  111.0 1.5 copy-done
  112.5 6.3 %shard_map.112 = (f32[128,512]{1,0:T(8,128)S(1)}, bf16[4,128,128]{2,1,0:T(8,128)(2,1)S(1)}) custom-call(s32[2]{0:T(128)S(1)} %pad_add_fusion.place, bf16[8,128,512]{2,1,0:T(8,128)(2,1)S(1)} %all-to-all-done.grad_ref, bf16[8,2,128,512]{3,2,1,0:T(8,128)(2,1)S(1)} %bitcast.21, bf16[8,2,128,512]{3,2,1,0:T(8,128)(2,1)} %collective-permute-done.8.other_ref, ...), custom_call_target="tpu_custom_call" | custom-call | flops 536870912 | bytes 6291456 | tf_op jit(solution)/shard_map/pallas_call | solution.py:267
  120.7 1.3 collective-permute-start.10
  122.0 5.4 %collective-permute-done.10 = bf16[2,128,128]{2,1,0:T(8,128)(2,1)S(1)} collective-permute-done((bf16[2,128,128]{2,1,0:T(8,128)(2,1)S(1)}, bf16[2,128,128]{2,1,0:T(8,128)(2,1)S(1)}, u32[]{:S(2)}, u32[]{:S(2)}) %collective-permute-start.10) | collective-permute-done | bytes 65568 | tf_op jit(solution)/shard_map/ppermute | solution.py:20
  127.6 1.3 collective-permute-start.11
  128.9 7.1 %collective-permute-done.11 = bf16[2,128,128]{2,1,0:T(8,128)(2,1)S(1)} collective-permute-done((bf16[2,128,128]{2,1,0:T(8,128)(2,1)S(1)}, bf16[2,128,128]{2,1,0:T(8,128)(2,1)S(1)}, u32[]{:S(2)}, u32[]{:S(2)}) %collective-permute-start.11) | collective-permute-done | bytes 65568 | tf_op jit(solution)/shard_map/ppermute | solution.py:20
  136.9 1.3 collective-permute-start.12
  138.2 6.9 %shard_map.111 = bf16[8,128,512]{2,1,0:T(8,128)(2,1)} custom-call(s32[2]{0:T(128)S(1)} %pad_add_fusion.place, bf16[128,512]{1,0:T(8,128)(2,1)S(1)} %copy-done.2, bf16[8,2,128,512]{3,2,1,0:T(8,128)(2,1)S(1)} %bitcast.22, bf16[8,2,128,512]{3,2,1,0:T(8,128)(2,1)} %collective-permute-done.8.other_ref), custom_call_target="tpu_custom_call" | custom-call | flops 536870912 | bytes 6291456 | tf_op jit(solution)/shard_map/pallas_call | solution.py:229
  145.2 4.5 %all-to-all-start.1 = ((bf16[8,128,512]{2,1,0:T(8,128)(2,1)}), bf16[8,128,512]{2,1,0:T(8,128)(2,1)}, u32[]{:S(2)}, u32[]{:S(2)}) async-start(bf16[8,128,512]{2,1,0:T(8,128)(2,1)} %shard_map.111), calls=%async_computation.1 | async-start | bytes 2097152 | tf_op jit(solution)/shard_map/all_to_all | solution.py:436
  151.8 1.3 collective-permute-start.14
  153.1 1.3 collective-permute-start.13
  154.4 7.6 %collective-permute-done.14 = bf16[2,128,128]{2,1,0:T(8,128)(2,1)S(1)} collective-permute-done((bf16[2,128,128]{2,1,0:T(8,128)(2,1)S(1)}, bf16[2,128,128]{2,1,0:T(8,128)(2,1)S(1)}, u32[]{:S(2)}, u32[]{:S(2)}) %collective-permute-start.14) | collective-permute-done | bytes 65568 | tf_op jit(solution)/shard_map/ppermute | solution.py:20
  162.2 3.1 %collective-permute-start.15 = (bf16[2,128,128]{2,1,0:T(8,128)(2,1)S(1)}, bf16[2,128,128]{2,1,0:T(8,128)(2,1)S(1)}, u32[]{:S(2)}, u32[]{:S(2)}) collective-permute-start(bf16[2,128,128]{2,1,0:T(8,128)(2,1)S(1)} %get-tuple-element.39), channel_id=1, source_target_pairs={{0,8},{8,0},{16,24},{24,16},{32,40},{40,32},{48,56},{56,48},{64,72... | collective-permute-start | bytes 196616 | tf_op jit(solution)/shard_map/ppermute | solution.py:25
  167.2 3.2 %collective-permute-start.17 = (bf16[128,512]{1,0:T(8,128)(2,1)S(1)}, bf16[128,512]{1,0:T(8,128)(2,1)}, u32[]{:S(2)}, u32[]{:S(2)}) collective-permute-start(bf16[128,512]{1,0:T(8,128)(2,1)S(1)} %slice_bitcast_fusion), channel_id=1, source_target_pairs={{0,128},{8,136},{16,144},{24,152},{32,160},{40,168},{48,176},{56,1... | collective-permute-start | bytes 393224 | tf_op jit(solution)/shard_map/ppermute | solution.py:25
  170.4 7.0 %shard_map.113 = (bf16[128,512]{1,0:T(8,128)(2,1)}, bf16[128,1024]{1,0:T(8,128)(2,1)}, bf16[128,1024]{1,0:T(8,128)(2,1)}, f32[4,256]{1,0:T(4,128)}) custom-call(s32[2]{0:T(128)S(1)} %pad_add_fusion.place, bf16[128,512]{1,0:T(8,128)(2,1)S(1)} %copy-done.11, bf16[128,1024]{1,0:T(8,128)(2,1)S(1)} %copy-done.7, f32[4,256]{1,0:T(4,128)S(1)} %copy-done.13, ...), custom_call_target="tpu_custom_call" | custom-call | flops 1879048192 | bytes 5242880 | tf_op jit(solution)/shard_map/pallas_call | solution.py:326
  177.5 2.1 %reduce_sum.12 = bf16[128,512]{1,0:T(8,128)(2,1)} reduce(bf16[8,128,512]{2,1,0:T(8,128)(2,1)} %all-to-all-done.1, bf16[]{:T(256)} %constant.14.clone.1), dimensions={0}, to_apply=%region_0.1 | reduce | flops 458752 | bytes 1179650 | tf_op jit(solution)/shard_map/reduce_sum | solution.py:439
  179.5 1.6 convert_add_fusion
  (125 shorter events, 21.2 us)
Async XLA Ops:
  7.2 96.1 %all-gather.3.cloned.1.call-start = ((), (), s32[]{:S(2)}) async-start(), calls=%async_computation.4 | async-start | bytes 2359296 | tf_op jit(solution)/shard_map/all_gather | solution.py:420
  10.8 32.8 %copy-start.34 = (bf16[128,512]{1,0:T(8,128)(2,1)S(1)}, bf16[128,512]{1,0:T(8,128)(2,1)}, u32[]{:S(2)}) copy-start(bf16[128,512]{1,0:T(8,128)(2,1)} %param.10) | copy-start | bytes 393220
  32.2 4.3 %collective-permute-start = (bf16[2,128,256]{2,1,0:T(8,128)(2,1)S(1)}, bf16[2,128,256]{2,1,0:T(8,128)(2,1)S(1)}, u32[]{:S(2)}, u32[]{:S(2)}) collective-permute-start(bf16[2,128,256]{2,1,0:T(8,128)(2,1)S(1)} %slice.68), channel_id=1, source_target_pairs={{0,8},{8,0},{16,24},{24,16},{32,40},{40,32},{48,56},{56,48},{64,72... | collective-permute-start | bytes 393224 | tf_op jit(solution)/shard_map/ppermute | solution.py:25
  36.6 54.5 %copy-start.25 = (bf16[2,128,256]{2,1,0:T(8,128)(2,1)}, bf16[2,128,256]{2,1,0:T(8,128)(2,1)S(1)}, u32[]{:S(2)}) copy-start(bf16[2,128,256]{2,1,0:T(8,128)(2,1)S(1)} %get-tuple-element.37) | copy-start | bytes 393220
  36.8 32.9 %copy-start.33 = (bf16[128,512]{1,0:T(8,128)(2,1)S(1)}, bf16[128,512]{1,0:T(8,128)(2,1)}, u32[]{:S(2)}) copy-start(bf16[128,512]{1,0:T(8,128)(2,1)} %param.11) | copy-start | bytes 393220
  36.8 9.6 %collective-permute-start.2 = (bf16[2,128,256]{2,1,0:T(8,128)(2,1)S(1)}, bf16[2,128,256]{2,1,0:T(8,128)(2,1)S(1)}, u32[]{:S(2)}, u32[]{:S(2)}) collective-permute-start(bf16[2,128,256]{2,1,0:T(8,128)(2,1)S(1)} %pad_maximum_fusion.1), channel_id=1, source_target_pairs={{0,32},{8,40},{16,48},{24,56},{32,64},{40,72},{48,80},{56,88},{64,... | collective-permute-start | bytes 393224 | tf_op jit(solution)/shard_map/ppermute | solution.py:20
  40.0 6.4 %collective-permute-start.1 = (bf16[2,128,256]{2,1,0:T(8,128)(2,1)S(1)}, bf16[2,128,256]{2,1,0:T(8,128)(2,1)S(1)}, u32[]{:S(2)}, u32[]{:S(2)}) collective-permute-start(bf16[2,128,256]{2,1,0:T(8,128)(2,1)S(1)} %pad_maximum_fusion.1), channel_id=1, source_target_pairs={{0,16},{8,24},{16,32},{24,40},{32,48},{40,56},{48,64},{56,72},{64,... | collective-permute-start | bytes 393224 | tf_op jit(solution)/shard_map/ppermute | solution.py:20
  43.6 10.9 %collective-permute-start.7 = (bf16[128,512]{1,0:T(8,128)(2,1)S(1)}, bf16[128,512]{1,0:T(8,128)(2,1)S(1)}, u32[]{:S(2)}, u32[]{:S(2)}) collective-permute-start(bf16[128,512]{1,0:T(8,128)(2,1)S(1)} %copy-done.34), channel_id=1, source_target_pairs={{0,128},{8,136},{16,144},{24,152},{32,160},{40,168},{48,176},{56,1... | collective-permute-start | bytes 393224 | tf_op jit(solution)/shard_map/ppermute | solution.py:25
  46.7 9.7 %collective-permute-start.3 = (bf16[2,128,256]{2,1,0:T(8,128)(2,1)S(1)}, bf16[2,128,256]{2,1,0:T(8,128)(2,1)S(1)}, u32[]{:S(2)}, u32[]{:S(2)}) collective-permute-start(bf16[2,128,256]{2,1,0:T(8,128)(2,1)S(1)} %pad_maximum_fusion.2), channel_id=1, source_target_pairs={{0,32},{8,40},{16,48},{24,56},{32,64},{40,72},{48,80},{56,88},{64,... | collective-permute-start | bytes 393224 | tf_op jit(solution)/shard_map/ppermute | solution.py:20
  56.7 20.0 %collective-permute-start.4 = (bf16[2,128,256]{2,1,0:T(8,128)(2,1)S(1)}, bf16[2,128,256]{2,1,0:T(8,128)(2,1)S(1)}, u32[]{:S(2)}, u32[]{:S(2)}) collective-permute-start(bf16[2,128,256]{2,1,0:T(8,128)(2,1)S(1)} %pad_maximum_fusion.3), channel_id=1, source_target_pairs={{0,64},{8,72},{16,80},{24,88},{32,96},{40,104},{48,112},{56,120},{... | collective-permute-start | bytes 393224 | tf_op jit(solution)/shard_map/ppermute | solution.py:20
  70.8 23.7 %all-to-all-start = ((bf16[8,128,512]{2,1,0:T(8,128)(2,1)}), bf16[8,128,512]{2,1,0:T(8,128)(2,1)S(1)}, u32[]{:S(2)}, u32[]{:S(2)}) async-start(bf16[8,128,512]{2,1,0:T(8,128)(2,1)} %broadcast_in_dim.2), calls=%async_computation | async-start | bytes 2097152 | tf_op jit(solution)/shard_map/all_to_all | solution.py:422
  76.6 89.7 %reduce-scatter.2.cloned.1.call-start = ((), (), s32[]{:S(2)}) async-start(), calls=%async_computation.3 | async-start | bytes 2359296 | tf_op jit(solution)/shard_map/reduce_scatter | solution.py:429
  76.9 14.1 %collective-permute-start.5 = (bf16[2,128,128]{2,1,0:T(8,128)(2,1)S(1)}, bf16[2,128,128]{2,1,0:T(8,128)(2,1)S(1)}, u32[]{:S(2)}, u32[]{:S(2)}) collective-permute-start(bf16[2,128,128]{2,1,0:T(8,128)(2,1)S(1)} %fusion.21), channel_id=1, source_target_pairs={{0,128},{8,136},{16,144},{24,152},{32,160},{40,168},{48,176},{56,1... | collective-permute-start | bytes 196616 | tf_op jit(solution)/shard_map/ppermute | solution.py:20
  91.3 2.5 %collective-permute-start.6 = (bf16[2,128,128]{2,1,0:T(8,128)(2,1)S(1)}, bf16[2,128,128]{2,1,0:T(8,128)(2,1)S(1)}, u32[]{:S(2)}, u32[]{:S(2)}) collective-permute-start(bf16[2,128,128]{2,1,0:T(8,128)(2,1)S(1)} %get-tuple-element.41), channel_id=1, source_target_pairs={{0,8},{8,0},{16,24},{24,16},{32,40},{40,32},{48,56},{56,48},{64,72... | collective-permute-start | bytes 196616 | tf_op jit(solution)/shard_map/ppermute | solution.py:25
  101.7 5.7 %collective-permute-start.16 = (bf16[8,2,128,512]{3,2,1,0:T(8,128)(2,1)}, bf16[8,2,128,512]{3,2,1,0:T(8,128)(2,1)}, u32[]{:S(2)}, u32[]{:S(2)}) collective-permute-start(bf16[8,2,128,512]{3,2,1,0:T(8,128)(2,1)} %get-tuple-element.33), channel_id=1, source_target_pairs={{0,8},{8,0},{16,24},{24,16},{32,40},{40,32},{48,56},{56,48},{64,72... | collective-permute-start | bytes 6291464 | tf_op jit(solution)/shard_map/ppermute | solution.py:25
  103.2 7.8 %collective-permute-start.8 = (bf16[8,2,128,512]{3,2,1,0:T(8,128)(2,1)}, bf16[8,2,128,512]{3,2,1,0:T(8,128)(2,1)}, u32[]{:S(2)}, u32[]{:S(2)}) collective-permute-start(bf16[8,2,128,512]{3,2,1,0:T(8,128)(2,1)} %bitcast.20), channel_id=1, source_target_pairs={{0,8},{8,0},{16,24},{24,16},{32,40},{40,32},{48,56},{56,48},{64,72... | collective-permute-start | bytes 6291464 | tf_op jit(solution)/shard_map/ppermute | solution.py:25
  118.9 1.4 collective-permute-start.9
  120.7 6.7 %collective-permute-start.10 = (bf16[2,128,128]{2,1,0:T(8,128)(2,1)S(1)}, bf16[2,128,128]{2,1,0:T(8,128)(2,1)S(1)}, u32[]{:S(2)}, u32[]{:S(2)}) collective-permute-start(bf16[2,128,128]{2,1,0:T(8,128)(2,1)S(1)} %convolution_convert_fusion.3), channel_id=1, source_target_pairs={{16,0},{24,8},{32,16},{40,24},{48,32},{56,40},{64,48},{72,56},{80,... | collective-permute-start | bytes 196616 | tf_op jit(solution)/shard_map/ppermute | solution.py:20
  127.6 8.4 %collective-permute-start.11 = (bf16[2,128,128]{2,1,0:T(8,128)(2,1)S(1)}, bf16[2,128,128]{2,1,0:T(8,128)(2,1)S(1)}, u32[]{:S(2)}, u32[]{:S(2)}) collective-permute-start(bf16[2,128,128]{2,1,0:T(8,128)(2,1)S(1)} %convolution_convert_fusion.2), channel_id=1, source_target_pairs={{32,0},{40,8},{48,16},{56,24},{64,32},{72,40},{80,48},{88,56},{96,... | collective-permute-start | bytes 196616 | tf_op jit(solution)/shard_map/ppermute | solution.py:20
  136.9 12.8 %collective-permute-start.12 = (bf16[2,128,128]{2,1,0:T(8,128)(2,1)}, bf16[2,128,128]{2,1,0:T(8,128)(2,1)}, u32[]{:S(2)}, u32[]{:S(2)}) collective-permute-start(bf16[2,128,128]{2,1,0:T(8,128)(2,1)} %convolution_convert_fusion.1), channel_id=1, source_target_pairs={{64,0},{72,8},{80,16},{88,24},{96,32},{104,40},{112,48},{120,56},{... | collective-permute-start | bytes 196616 | tf_op jit(solution)/shard_map/ppermute | solution.py:20
  145.2 25.2 %copy-start.4 = (bf16[4,128,128]{2,1,0:T(8,128)(2,1)S(1)}, bf16[4,128,128]{2,1,0:T(8,128)(2,1)}, u32[]{:S(2)}) copy-start(bf16[4,128,128]{2,1,0:T(8,128)(2,1)} %pad_maximum_fusion.4.state_ref) | copy-start | bytes 393220
  145.2 25.2 %copy-start.7 = (bf16[128,1024]{1,0:T(8,128)(2,1)S(1)}, bf16[128,1024]{1,0:T(8,128)(2,1)}, u32[]{:S(2)}) copy-start(bf16[128,1024]{1,0:T(8,128)(2,1)} %k_ref.3) | copy-start | bytes 786436
  145.2 25.2 %copy-start.9 = (f32[128,512]{1,0:T(8,128)S(1)}, f32[128,512]{1,0:T(8,128)}, u32[]{:S(2)}) copy-start(f32[128,512]{1,0:T(8,128)} %copy-done.8) | copy-start | bytes 786436
  145.2 25.2 %copy-start.11 = (bf16[128,512]{1,0:T(8,128)(2,1)S(1)}, bf16[128,512]{1,0:T(8,128)(2,1)}, u32[]{:S(2)}) copy-start(bf16[128,512]{1,0:T(8,128)(2,1)} %q_ref.3) | copy-start | bytes 393220
  145.2 25.2 %copy-start.13 = (f32[4,256]{1,0:T(4,128)S(1)}, f32[4,256]{1,0:T(4,128)}, u32[]{:S(2)}) copy-start(f32[4,256]{1,0:T(4,128)} %logit_ref.3) | copy-start | bytes 12292
  145.2 25.2 %copy-start.17 = (f32[4,256,256]{2,1,0:T(8,128)S(1)}, f32[4,256,256]{2,1,0:T(8,128)}, u32[]{:S(2)}) copy-start(f32[4,256,256]{2,1,0:T(8,128)} %copy-done.16) | copy-start | bytes 3145732
  145.2 25.2 %copy-start.19 = (f32[4,256,256]{2,1,0:T(8,128)S(1)}, f32[4,256,256]{2,1,0:T(8,128)}, u32[]{:S(2)}) copy-start(f32[4,256,256]{2,1,0:T(8,128)} %copy-done.18) | copy-start | bytes 3145732
  145.2 32.3 %all-to-all-start.1 = ((bf16[8,128,512]{2,1,0:T(8,128)(2,1)}), bf16[8,128,512]{2,1,0:T(8,128)(2,1)}, u32[]{:S(2)}, u32[]{:S(2)}) async-start(bf16[8,128,512]{2,1,0:T(8,128)(2,1)} %shard_map.111), calls=%async_computation.1 | async-start | bytes 2097152 | tf_op jit(solution)/shard_map/all_to_all | solution.py:436
  151.8 10.2 %collective-permute-start.14 = (bf16[2,128,128]{2,1,0:T(8,128)(2,1)S(1)}, bf16[2,128,128]{2,1,0:T(8,128)(2,1)S(1)}, u32[]{:S(2)}, u32[]{:S(2)}) collective-permute-start(bf16[2,128,128]{2,1,0:T(8,128)(2,1)S(1)} %convolution_convert_fusion), channel_id=1, source_target_pairs={{144,0},{152,8},{160,16},{168,24},{176,32},{184,40},{192,48},{200,... | collective-permute-start | bytes 196616 | tf_op jit(solution)/shard_map/ppermute | solution.py:20
  153.1 8.9 %collective-permute-start.13 = (bf16[2,128,128]{2,1,0:T(8,128)(2,1)S(1)}, bf16[2,128,128]{2,1,0:T(8,128)(2,1)S(1)}, u32[]{:S(2)}, u32[]{:S(2)}) collective-permute-start(bf16[2,128,128]{2,1,0:T(8,128)(2,1)S(1)} %add_convert_fusion.3), channel_id=1, source_target_pairs={{16,0},{24,8},{32,16},{40,24},{48,32},{56,40},{64,48},{72,56},{80,... | collective-permute-start | bytes 196616 | tf_op jit(solution)/shard_map/ppermute | solution.py:20
  162.2 4.0 %collective-permute-start.15 = (bf16[2,128,128]{2,1,0:T(8,128)(2,1)S(1)}, bf16[2,128,128]{2,1,0:T(8,128)(2,1)S(1)}, u32[]{:S(2)}, u32[]{:S(2)}) collective-permute-start(bf16[2,128,128]{2,1,0:T(8,128)(2,1)S(1)} %get-tuple-element.39), channel_id=1, source_target_pairs={{0,8},{8,0},{16,24},{24,16},{32,40},{40,32},{48,56},{56,48},{64,72... | collective-permute-start | bytes 196616 | tf_op jit(solution)/shard_map/ppermute | solution.py:25
  167.2 12.3 %collective-permute-start.17 = (bf16[128,512]{1,0:T(8,128)(2,1)S(1)}, bf16[128,512]{1,0:T(8,128)(2,1)}, u32[]{:S(2)}, u32[]{:S(2)}) collective-permute-start(bf16[128,512]{1,0:T(8,128)(2,1)S(1)} %slice_bitcast_fusion), channel_id=1, source_target_pairs={{0,128},{8,136},{16,144},{24,152},{32,160},{40,168},{48,176},{56,1... | collective-permute-start | bytes 393224 | tf_op jit(solution)/shard_map/ppermute | solution.py:25
  (25 other events, 282.4 us)
Sparse Core Ops, SparseCore 0:
  55.4 42.9 all-gather.2
  111.1 40.6 reduce-scatter.1

commit v2 on v1

v2 whole, which is shorter than its diff:
```python
import functools
import math

import jax
import jax.numpy as jnp
from jax import lax
from jax.experimental import pallas as pl
from jax.experimental.pallas import tpu as pltpu
from jax.sharding import PartitionSpec as P

F32 = jnp.float32
BF16 = jnp.bfloat16
WIDTH = 128
VMEM = 56 << 20
PAIRS = 2 * WIDTH


def send(block, distance):
    devices = range(lax.axis_size("ctx"))
    route = [(i - distance, i) for i in devices if i - distance in devices]
    return lax.ppermute(block, "ctx", route)


def exchange(block, bit):
    route = [(i, i ^ bit) for i in range(lax.axis_size("ctx"))]
    return lax.ppermute(block, "ctx", route)


def split(x):
    high = x.astype(BF16)
    return high, (x - high.astype(F32)).astype(BF16)


def dot(a, b, ca=1, cb=0, passes=3):
    dims = (((ca,), (cb,)), ((), ()))
    mul = functools.partial(lax.dot_general, dimension_numbers=dims, preferred_element_type=F32)
    a_high, a_low = split(a)
    b_high, b_low = split(b)
    if passes == 1:
        return mul(a_high, b_high)
    return mul(a_high, b_high) + (mul(a_low, b_high) + mul(a_high, b_low))


def inverse_norm(x):
    return lax.rsqrt(jnp.sum(x * x, axis=-1, keepdims=True) + 1e-06)


def order_of(shape, dim):
    p = lax.broadcasted_iota(jnp.int32, shape, dim)
    return 2 * (p & (WIDTH - 1)) + (p >> 7)


def column_of(row):
    shape = (PAIRS, PAIRS)
    time = lax.broadcasted_iota(jnp.int32, shape, 1)
    return jnp.sum(jnp.where(time == order_of(shape, 0), row, 0.0), axis=1, keepdims=True)


def row_of(column):
    shape = (PAIRS, PAIRS)
    time = lax.broadcasted_iota(jnp.int32, shape, 1)
    return jnp.sum(jnp.where(time == order_of(shape, 0), column, 0.0), axis=0, keepdims=True)


def visible_mask():
    shape = (WIDTH, PAIRS)
    token = lax.broadcasted_iota(jnp.int32, shape, 0)
    return (lax.broadcasted_iota(jnp.int32, shape, 1) & (WIDTH - 1)) <= token


def stacked(ref, i):
    start = i * PAIRS
    parts = [ref[:, start : start + WIDTH], ref[:, start + WIDTH : start + PAIRS]]
    return jnp.concatenate(parts, axis=0).astype(F32)


def prepare_kernel(*refs):
    q_ref, k_ref, v_ref, logit_ref = refs[1:5]
    ab_ref, m_ref, wy_ref, qt_ref, local_ref = refs[-5:]
    two = range(2)
    shape = (PAIRS, PAIRS)
    row, col = order_of(shape, 0), order_of(shape, 1)
    identity = jnp.where(row == col, 1.0, 0.0).astype(F32)
    query = [q_ref[:, i * WIDTH : (i + 1) * WIDTH].astype(F32) for i in two]
    query = [x * inverse_norm(x) for x in query]
    key = [stacked(k_ref, i) for i in two]
    key = [x * inverse_norm(x) for x in key]
    strength = [2.0 / (1.0 + jnp.exp(-column_of(logit_ref[0, i : i + 1, :]))) for i in two]
    coupling = [jnp.where(col < row, strength[i] * dot(key[i], key[i], 1, 1), 0.0) for i in two]
    inverse = [identity - jnp.where((row >> 1) == (col >> 1), coupling[i], 0.0) for i in two]
    for level in range(1, 8):
        join = ((row >> (level + 1)) == (col >> (level + 1))) & ((row >> level) != (col >> level))
        edge = [jnp.where(join, coupling[i], 0.0) for i in two]
        step = [dot(inverse[i], edge[i], passes=1) for i in two]
        inverse = [inverse[i] - dot(step[i], inverse[i], passes=1) for i in two]
    rest = [identity - inverse[i] - dot(coupling[i], inverse[i]) for i in two]
    inverse = [inverse[i] + dot(inverse[i], rest[i], passes=1) for i in two]
    scores = [jnp.where(visible_mask(), dot(query[i], key[i], 1, 1), 0.0) for i in two]
    scaled = [strength[i] * jnp.concatenate([key[i], stacked(v_ref, i)], axis=1) for i in two]
    reads = [
        jnp.concatenate([dot(scores[i], inverse[i]), dot(key[i], inverse[i], 0, 0)], axis=0)
        for i in two
    ]
    product = [dot(reads[i], scaled[i]) for i in two]
    eye = identity[:WIDTH, :WIDTH]
    for i in two:
        ab_ref[i, :, :WIDTH] = (eye - product[i][WIDTH:, :WIDTH]).astype(BF16)
        ab_ref[i, :, WIDTH:] = product[i][WIDTH:, WIDTH:].astype(BF16)
        qt_ref[i] = query[i] - product[i][:WIDTH, :WIDTH]
        local_ref[i] = product[i][:WIDTH, WIDTH:]
        m_ref[i] = reads[i]
        wy_ref[i] = dot(inverse[i], scaled[i])


def slot(head, place):
    return (head + 2 * place[0]) % 4


def by_pair(*block):
    return pl.BlockSpec((2,) + block, lambda i, place: (i,) + (0,) * len(block))


def by_slot(*block):
    return pl.BlockSpec((2,) + block, lambda i, place: (i ^ place[0],) + (0,) * len(block))


def by_columns(width):
    return pl.BlockSpec((WIDTH, 2 * width), lambda i, place: (0, i))


def whole(*shape):
    return pl.BlockSpec(shape, lambda i, place: (0,) * len(shape))


def call(kernel, steps, in_specs, out_specs, out_shape, flops, moved, scratch=()):
    return pl.pallas_call(
        kernel,
        grid_spec=pltpu.PrefetchScalarGridSpec(
            num_scalar_prefetch=1,
            grid=(steps,),
            in_specs=in_specs,
            out_specs=out_specs,
            scratch_shapes=list(scratch),
        ),
        out_shape=out_shape,
        compiler_params=pltpu.CompilerParams(vmem_limit_bytes=VMEM),
        cost_estimate=pl.CostEstimate(flops=flops, bytes_accessed=moved, transcendentals=0),
    )


def arr(dtype, *shape):
    return jax.ShapeDtypeStruct(shape, dtype)


def prepare(place, queries, keys, values, logits, mine, filled=()):
    def pair(place):
        return place[0] if mine else 1 - place[0]

    def columns(width):
        return pl.BlockSpec((WIDTH, 2 * width), lambda i, place: (0, pair(place)))

    def heads(*block):
        return pl.BlockSpec((2,) + block, lambda i, place: (pair(place),) + (0,) * len(block))

    def stored(n):
        return arr(F32, 4, n, n)

    return pl.pallas_call(
        prepare_kernel,
        grid_spec=pltpu.PrefetchScalarGridSpec(
            num_scalar_prefetch=1,
            grid=(1,),
            in_specs=[
                columns(WIDTH),
                columns(PAIRS),
                columns(PAIRS),
                pl.BlockSpec((1, 2, PAIRS), lambda i, place: (pair(place), 0, 0)),
            ]
            + [pl.BlockSpec(memory_space=pl.ANY)] * len(filled),
            out_specs=[
                pl.BlockSpec((2, WIDTH, PAIRS), lambda i, place: (0, 0, 0)),
                heads(PAIRS, PAIRS),
                heads(PAIRS, PAIRS),
                heads(WIDTH, WIDTH),
                heads(WIDTH, WIDTH),
            ],
        ),
        out_shape=[
            arr(BF16, 2, WIDTH, PAIRS),
            stored(PAIRS),
            stored(PAIRS),
            stored(WIDTH),
            stored(WIDTH),
        ],
        input_output_aliases={5 + i: 1 + i for i in range(len(filled))},
        compiler_params=pltpu.CompilerParams(vmem_limit_bytes=VMEM),
        cost_estimate=pl.CostEstimate(
            flops=(1 if mine else 100) << 20, bytes_accessed=1 << (16 if mine else 24), transcendentals=0
        ),
    )(place, queries, keys, values, logits.reshape(2, 2, PAIRS), *filled)


def feature_block(grad_ref, place, z, row, core):
    owner = (row ^ place[1]) * 4 + z // 2
    column = pl.multiple_of((z % 2) * 256 + (core ^ place[0]) * 128, 128)
    return owner, pl.ds(column, 128)


def grad_block(grad_ref, place, z, row, core):
    owner, columns = feature_block(grad_ref, place, z, row, core)
    return grad_ref[owner, :, columns]


def weight_rows(mine_ref, other_ref):
    return jnp.concatenate([mine_ref[0, 0], mine_ref[0, 1], other_ref[0, 0], other_ref[0, 1]], axis=0)


def outputs_kernel(place, qt_ref, local_ref, state_ref, grad_ref, heads_ref, mine_ref, other_ref, held):
    z = pl.program_id(0)

    @pl.when(z == 0)
    def _():
        for head in range(4):
            state = state_ref[slot(head, place)].astype(F32)
            result = dot(qt_ref[head], state) + local_ref[head]
            held[:, head * WIDTH : (head + 1) * WIDTH] = result.astype(BF16)
        heads_ref[...] = held[...]

    blocks = jnp.concatenate(
        [grad_block(grad_ref, place, z, row, core) for core in range(2) for row in range(2)], axis=1
    )
    product = lax.dot_general(
        blocks, held[...], (((0,), (0,)), ((), ())), preferred_element_type=F32
    )
    product = (product * (1.0 / 64.0)).astype(BF16)
    for row in range(2):
        mine_ref[0, row] = product[row * WIDTH : (row + 1) * WIDTH]
        other_ref[0, row] = product[(2 + row) * WIDTH : (3 + row) * WIDTH]


def outputs(place, qt, local, state, grad_full):
    heads = arr(BF16, WIDTH, 512)
    part = arr(BF16, 8, 2, WIDTH, 512)
    tile = pl.BlockSpec((1, 2, WIDTH, 512), lambda z, place: (z, 0, 0, 0))
    return call(
        outputs_kernel,
        8,
        [whole(4, WIDTH, WIDTH), whole(4, WIDTH, WIDTH), whole(4, WIDTH, WIDTH), whole(8, WIDTH, 512)],
        [whole(WIDTH, 512), tile, tile],
        [heads, part, part],
        2 * 128 * 512 * 4096,
        6 << 20,
        [pltpu.VMEM((WIDTH, 512), BF16)],
    )(place, qt, local, state, grad_full)


def mixed_kernel(place, heads_ref, mine_ref, other_ref, out_ref):
    z = pl.program_id(0)
    product = lax.dot_general(
        heads_ref[...],
        weight_rows(mine_ref, other_ref),
        (((1,), (1,)), ((), ())),
        preferred_element_type=F32,
    ).astype(BF16)
    for core in range(2):
        for row in range(2):
            owner, columns = feature_block(out_ref, place, z, row, core)
            start = (2 * core + row) * WIDTH
            out_ref[owner, :, columns] = product[:, start : start + WIDTH]


def mixed_parts(place, heads, mine, other):
    tile = pl.BlockSpec((1, 2, WIDTH, 512), lambda z, place: (z, 0, 0, 0))
    return call(
        mixed_kernel,
        8,
        [whole(WIDTH, 512), tile, tile],
        whole(8, WIDTH, 512),
        arr(BF16, 8, WIDTH, 512),
        2 * 128 * 512 * 4096,
        6 << 20,
    )(place, heads, mine, other)


def head_grad_kernel(place, grad_ref, mine_ref, other_ref, qt_ref, out_ref, own_ref):
    z = pl.program_id(0)
    blocks = jnp.concatenate(
        [grad_block(grad_ref, place, z, row, core) for core in range(2) for row in range(2)], axis=1
    )
    total = jnp.dot(blocks, weight_rows(mine_ref, other_ref), preferred_element_type=F32)

    @pl.when(z == 0)
    def _():
        out_ref[...] = total

    @pl.when(z > 0)
    def _():
        out_ref[...] += total

    @pl.when(z == 7)
    def _():
        for head in range(4):
            grad = out_ref[:, head * WIDTH : (head + 1) * WIDTH]
            own_ref[slot(head, place)] = dot(qt_ref[head], grad, 0, 0).astype(BF16)


def head_gradient(place, grad_full, mine, other, qt):
    tile = pl.BlockSpec((1, 2, WIDTH, 512), lambda z, place: (z, 0, 0, 0))
    return call(
        head_grad_kernel,
        8,
        [whole(8, WIDTH, 512), tile, tile, whole(4, WIDTH, WIDTH)],
        [whole(WIDTH, 512), whole(4, WIDTH, WIDTH)],
        [arr(F32, WIDTH, 512), arr(BF16, 4, WIDTH, WIDTH)],
        2 * 128 * 512 * 4096,
        6 << 20,
    )(place, grad_full, mine, other, qt)


def pull_kernel(
    place, q_ref, k_ref, logit_ref, m_ref, wy_ref, state_ref, end_ref, grad_ref,
    dq_ref, dk_ref, dv_ref, dlogit_ref,
):
    two = range(2)
    shape = (PAIRS, PAIRS)
    before = order_of(shape, 1) < order_of(shape, 0)
    query = [q_ref[:, i * WIDTH : (i + 1) * WIDTH].astype(F32) for i in two]
    query_scale = [inverse_norm(x) for x in query]
    query = [query[i] * query_scale[i] for i in two]
    key = [stacked(k_ref, i) for i in two]
    key_scale = [inverse_norm(x) for x in key]
    key = [key[i] * key_scale[i] for i in two]
    logit = [column_of(logit_ref[0, i : i + 1, :]) for i in two]
    state = [state_ref[i].astype(F32) for i in two]
    end = [end_ref[i].astype(F32) for i in two]
    grad = [grad_ref[:, i * WIDTH : (i + 1) * WIDTH] for i in two]
    updates = [wy_ref[i, :, WIDTH:] - dot(wy_ref[i, :, :WIDTH], state[i]) for i in two]
    pulled = [dot(m_ref[i], jnp.concatenate([grad[i], end[i]], axis=0), 0, 0) for i in two]
    value_grad = [2.0 / (1.0 + jnp.exp(-logit[i])) * pulled[i] for i in two]
    cross = [
        dot(jnp.concatenate([grad[i], value_grad[i]], axis=0), updates[i], 1, 1) for i in two
    ]
    pairs = [
        jnp.concatenate(
            [
                jnp.where(visible_mask(), cross[i][:WIDTH], 0.0),
                jnp.where(before, -cross[i][WIDTH:], 0.0),
            ],
            axis=0,
        )
        for i in two
    ]
    forward = [dot(pairs[i], key[i]) for i in two]
    backward = [dot(pairs[i], jnp.concatenate([query[i], key[i]], axis=0), 0, 0) for i in two]
    by_state = [
        dot(jnp.concatenate([grad[i], -value_grad[i]], axis=0), state[i], 1, 1) for i in two
    ]
    by_end = [dot(updates[i], end[i], 1, 1) for i in two]
    for i in two:
        start = i * PAIRS
        dv_ref[:, start : start + WIDTH] = value_grad[i][:WIDTH].astype(BF16)
        dv_ref[:, start + WIDTH : start + PAIRS] = value_grad[i][WIDTH:].astype(BF16)
        slope = jnp.sum(pulled[i] * updates[i], axis=1, keepdims=True) / (1.0 + jnp.exp(logit[i]))
        dlogit_ref[0, i : i + 1, :] = row_of(slope)
        query_grad = forward[i][:WIDTH] + by_state[i][:WIDTH]
        query_grad = query_scale[i] * (
            query_grad - query[i] * jnp.sum(query[i] * query_grad, axis=1, keepdims=True)
        )
        dq_ref[:, i * WIDTH : (i + 1) * WIDTH] = query_grad.astype(BF16)
        key_grad = forward[i][WIDTH:] + backward[i] + by_end[i] + by_state[i][WIDTH:]
        key_grad = key_scale[i] * (
            key_grad - key[i] * jnp.sum(key[i] * key_grad, axis=1, keepdims=True)
        )
        dk_ref[:, start : start + WIDTH] = key_grad[:WIDTH].astype(BF16)
        dk_ref[:, start + WIDTH : start + PAIRS] = key_grad[WIDTH:].astype(BF16)


def pull(place, queries, keys, logits, reads, wy, state, end, head_grad):
    logit_spec = pl.BlockSpec((1, 2, PAIRS), lambda i, place: (i, 0, 0))
    *grads, logit_grad = call(
        pull_kernel,
        2,
        [
            by_columns(WIDTH),
            by_columns(PAIRS),
            logit_spec,
            by_pair(PAIRS, PAIRS),
            by_pair(PAIRS, PAIRS),
            by_slot(WIDTH, WIDTH),
            by_slot(WIDTH, WIDTH),
            by_columns(WIDTH),
        ],
        [by_columns(WIDTH), by_columns(PAIRS), by_columns(PAIRS), logit_spec],
        [
            arr(BF16, WIDTH, 512),
            arr(BF16, WIDTH, 1024),
            arr(BF16, WIDTH, 1024),
            arr(F32, 2, 2, PAIRS),
        ],
        4 * 14 * 2 * PAIRS**3,
        5 << 20,
    )(place, queries, keys, logits.reshape(2, 2, PAIRS), reads, wy, state, end, head_grad)
    return (*grads, logit_grad.reshape(4, PAIRS))


def mul(a, b):
    return jnp.einsum("hij,hjk->hik", a, b, preferred_element_type=F32)


def mul_t(a, b):
    return jnp.einsum("hji,hjk->hik", a, b, preferred_element_type=F32)


def halves(x):
    return x[:, :, :WIDTH], x[:, :, WIDTH:]


def forward_states(mine, theirs, core, gate):
    theirs = exchange(theirs, 1)
    even = jnp.where(core == 0, mine, theirs)
    odd = jnp.where(core == 0, theirs, mine)
    even_a, even_b = halves(even)
    odd_a, odd_b = halves(odd)
    joined = mul(odd_a, even)
    chip = jnp.concatenate(
        [joined[:, :, :WIDTH], joined[:, :, WIDTH:] + odd_b.astype(F32)], axis=2
    ).astype(BF16)
    one, two = send(chip, 2), send(chip, 4)
    window1, state = halves(one)
    step = mul(window1, two)
    state = state.astype(F32) + step[:, :, WIDTH:]
    window2 = step[:, :, :WIDTH].astype(BF16)
    step = mul(window2, send(jnp.concatenate([window2, state.astype(BF16)], axis=2), 4))
    state = state + step[:, :, WIDTH:]
    window4 = step[:, :, :WIDTH].astype(BF16)
    rounded = state.astype(BF16)
    both = jnp.concatenate([window4, rounded], axis=2)
    near_a, near_b = halves(send(both, 8))
    mid_a, mid_b = halves(send(both, 16))
    far_b = send(rounded, 24)
    inner = (mid_b.astype(F32) + mul(mid_a, far_b)).astype(BF16)
    inner = (near_b.astype(F32) + mul(near_a, inner)).astype(BF16)
    first = (state + mul(window4, inner)).astype(BF16)
    window8 = mul(window4, near_a).astype(BF16)
    window12 = mul(window8, mid_a).astype(BF16)
    second = (mul(even_a, first) + even_b.astype(F32)).astype(BF16)
    kept = jnp.where(core == 0, first, second)
    given = jnp.where(core == 0, second, first)
    gate, given = lax.optimization_barrier((gate, given))
    state_in = jnp.concatenate([kept, exchange(given, 1)], axis=0)
    return gate, state_in, (even_a, odd_a, window1, window2, window4, window8, window12)


def backward_states(own, core, saved):
    even_a, odd_a, window1, window2, window4, window8, window12 = saved
    mine, theirs = own[:2], exchange(own[2:], 1)
    even = jnp.where(core == 0, mine, theirs)
    odd = jnp.where(core == 0, theirs, mine)
    total = even.astype(F32) + mul_t(even_a, odd)
    for window, distance in ((window1, 2), (window2, 4)):
        passed = mul_t(window, total.astype(BF16)).astype(BF16)
        total = total + send(passed, -distance).astype(F32)
    rounded = total.astype(BF16)
    second = send(rounded, -2).astype(F32)
    for window, distance in ((window4, 10), (window8, 18), (window12, 26)):
        second += send(mul_t(window, rounded).astype(BF16), -distance).astype(F32)
    second = second.astype(BF16)
    first = (odd.astype(F32) + mul_t(odd_a, second)).astype(BF16)
    kept = jnp.where(core == 0, first, second)
    given = jnp.where(core == 0, second, first)
    return jnp.concatenate([kept, exchange(given, 1)], axis=0)


def local(queries, keys, values, beta_logit, out_weight, out_grad):
    index = lax.axis_index("ctx")
    core = index & 1
    place = jnp.stack([core, index >> 4]).astype(jnp.int32)
    rings = [[(half * 8 + z) * 2 + c for z in range(8)] for half in range(2) for c in range(2)]
    operands = (queries, keys, values, beta_logit)
    theirs, *filled = prepare(place, *operands, False)
    weight_pair = jnp.stack([out_weight, exchange(out_weight, 16)])
    weight_pair, *operands = lax.optimization_barrier((weight_pair, *operands))
    mine, reads, wy, qt, local_out = prepare(place, *operands, True, filled)
    weight_mine = lax.all_gather(weight_pair, "ctx", axis=0, axis_index_groups=rings)
    grad_full = lax.all_to_all(
        jnp.broadcast_to(out_grad[None], (8, WIDTH, 512)), "tp", 0, 0, tiled=True
    )
    weight_mine, state, saved = forward_states(mine, theirs, core, weight_mine)
    weight_other = exchange(weight_mine, 1)
    heads, part_mine, part_other = outputs(place, qt, local_out, state, grad_full)
    part = part_mine.astype(F32) + exchange(part_other, 1).astype(F32)
    ring_sum = lax.psum_scatter(
        part.astype(BF16).reshape(8, PAIRS, 512),
        "ctx",
        scatter_dimension=0,
        axis_index_groups=rings,
    )
    weight_grad = ring_sum[:WIDTH].astype(F32) + exchange(ring_sum[WIDTH:], 16).astype(F32)
    mixed = lax.all_to_all(
        mixed_parts(place, heads, weight_mine, weight_other), "tp", 0, 0, tiled=True
    )
    mixed = jnp.sum(mixed.astype(F32), axis=0).astype(BF16)
    head_grad, own = head_gradient(place, grad_full, weight_mine, weight_other, qt)
    end = backward_states(own, core, saved)
    query_grad, key_grad, value_grad, logit_grad = pull(
        place, queries, keys, beta_logit, reads, wy, state, end, head_grad
    )
    return mixed, query_grad, key_grad, value_grad, logit_grad, weight_grad


def solution(mesh):
    placed = P("ctx", "tp")
    return jax.shard_map(
        local,
        mesh=mesh,
        in_specs=(placed, placed, placed, P("tp", "ctx"), placed, placed),
        out_specs=(placed, placed, placed, placed, P("tp", "ctx"), placed),
        check_vma=False,
    )
```

time: 192 us -> 193 us (level)
  waiting for transfers between devices: 33.1 us -> 51 us
  starting transfers between devices: 70.5 us -> 60 us
  Pallas kernels: 45.4 us -> 41.7 us
  local copies, waits for them, and re-layouts: 10.7 us -> 7.73 us
    ppermute x10 -> x12, waiting for transfers between devices: 25.3 us -> 35.1 us  [send(): return lax.ppermute(block, 'ctx', route)]
    ppermute x10 -> x12, starting transfers between devices: 44 us -> 35.2 us  [send(): return lax.ppermute(block, 'ctx', route)]
    unnamed x70 -> x30, local copies, waits for them, and re-layouts: 8.64 us -> 1.02 us
    pallas_call x2 -> x3, Pallas kernels: 26.8 us -> 19.2 us  [the longest x2 12.5 us: prepare(): pl.pallas_call(prepare_kernel, grid_spec=pltpu.PrefetchScalarGridSpec(num...]
    all_to_all x1, waiting for transfers between devices: 0.01 us -> 6.46 us  [local(): lax.all_to_all(jnp.broadcast_to(out_grad[None], (8, WIDTH, 512)), 'tp', 0...]
    reshape x0 -> x3, local copies, waits for them, and re-layouts: none -> 3.86 us  [the longest x2 2.57 us: prepare(): logits.reshape(2, 2, PAIRS)]
  transfers between devices with their start and end apart: 22 -> 24, of which waited for: 10 -> 13; matrix products, arithmetic and copies ran while one was open for 7% -> 11% of each run, Pallas kernels for 14% -> 18%
where the time goes in v2:
time: 193 us; the launch traced here: 191 us
  starting transfers between devices  60 us (31%)
  waiting for transfers between devices  51 us (26%)
  Pallas kernels  41.7 us (22%)
  between operations  14.5 us (8%)
  other arithmetic  11.5 us (6%)
  local copies, waits for them, and re-layouts  7.73 us (4%)
  matrix products  4.37 us (2%)
    ppermute x12, starting transfers between devices, send(): return lax.ppermute(block, 'ctx', route)  35.2 us
    ppermute x12, waiting for transfers between devices, send(): return lax.ppermute(block, 'ctx', route)  35.1 us
    ppermute x8, starting transfers between devices, exchange(): return lax.ppermute(block, 'ctx', route)  16.6 us
    pallas_call x2, Pallas kernels, prepare(): pl.pallas_call(prepare_kernel, grid_spec=pltpu.PrefetchScalarGridSpec(num...  12.5 us
    ppermute x8, waiting for transfers between devices, exchange(): return lax.ppermute(block, 'ctx', route)  9.45 us
    pallas_call x1, Pallas kernels, head_gradient(): call(head_grad_kernel, 8, [whole(8, WIDTH, 512), tile, tile, whole(4, WID...  7.87 us
    pallas_call x1, Pallas kernels, mixed_parts(): call(mixed_kernel, 8, [whole(WIDTH, 512), tile, tile], whole(8, WIDTH, 51...  7.58 us
    pallas_call x1, Pallas kernels, outputs(): call(outputs_kernel, 8, [whole(4, WIDTH, WIDTH), whole(4, WIDTH, WIDTH),...  6.99 us
  transfers between devices with their start and end apart: 24, of which 13 were waited for; matrix products, arithmetic and copies ran while one was open for 11% of the time, Pallas kernels for 18%

profile of v2, /device:TPU:1, one launch (start us, length us, event | category | flops | bytes accessed | tf_op | source)
XLA Modules:
  0.0 190.8 jit_solution(14456775437472661189)
XLA Ops:
  7.2 3.7 %collective-permute-start = (bf16[128,512]{1,0:T(8,128)(2,1)}, bf16[128,512]{1,0:T(8,128)(2,1)S(1)}, u32[]{:S(2)}, u32[]{:S(2)}) collective-permute-start(bf16[128,512]{1,0:T(8,128)(2,1)} %param.10), channel_id=1, source_target_pairs={{0,128},{8,136},{16,144},{24,152},{32,160},{40,168},{48,176},{56,1... | collective-permute-start | bytes 393224 | tf_op jit(solution)/shard_map/ppermute | solution.py:26
  10.9 2.6 %collective-permute-done = bf16[128,512]{1,0:T(8,128)(2,1)S(1)} collective-permute-done((bf16[128,512]{1,0:T(8,128)(2,1)}, bf16[128,512]{1,0:T(8,128)(2,1)S(1)}, u32[]{:S(2)}, u32[]{:S(2)}) %collective-permute-start) | collective-permute-done | bytes 131104 | tf_op jit(solution)/shard_map/ppermute | solution.py:26
  13.4 1.6 pad_maximum_fusion
  17.0 6.2 %shard_map.109 = (bf16[2,128,256]{2,1,0:T(8,128)(2,1)}, f32[4,256,256]{2,1,0:T(8,128)}, f32[4,256,256]{2,1,0:T(8,128)}, f32[4,128,128]{2,1,0:T(8,128)}, f32[4,128,128]{2,1,0:T(8,128)}) custom-call(s32[2]{0:T(128)} %pad_add_fusion.refs_0_.place, bf16[128,512]{1,0:T(8,128)(2,1)} %q_ref.1, bf16[128,1024]{1,0:T(8,128)(2,1)} %k_ref.1, bf16[128,1024]{1,0:T(8,128)(2,1)} %refs_3_.2, ...), custom_call_target="tpu_custom_call" | custom-call | flops 104857600 | bytes 16777216 | tf_op jit(solution)/shard_map/pallas_call | solution.py:168
  23.2 3.8 %collective-permute-start.1 = (bf16[2,128,256]{2,1,0:T(8,128)(2,1)}, bf16[2,128,256]{2,1,0:T(8,128)(2,1)S(1)}, u32[]{:S(2)}, u32[]{:S(2)}) collective-permute-start(bf16[2,128,256]{2,1,0:T(8,128)(2,1)} %get-tuple-element.42), channel_id=1, source_target_pairs={{0,8},{8,0},{16,24},{24,16},{32,40},{40,32},{48,56},{56,48},{64,72... | collective-permute-start | bytes 393224 | tf_op jit(solution)/shard_map/ppermute | solution.py:26
  28.3 6.2 %shard_map.110 = (bf16[2,128,256]{2,1,0:T(8,128)(2,1)}, f32[4,256,256]{2,1,0:T(8,128)}, f32[4,256,256]{2,1,0:T(8,128)}, f32[4,128,128]{2,1,0:T(8,128)}, f32[4,128,128]{2,1,0:T(8,128)}) custom-call(s32[2]{0:T(128)} %pad_add_fusion.refs_0_.place, bf16[128,512]{1,0:T(8,128)(2,1)} %q_ref.1, ...), custom_call_target="tpu_custom_call", output_to_operand_aliasing={{1}: (5, {}), {2}: (6, {}), {3}: (7, {}), {4}: (8, {})} | custom-call | flops 1048576 | bytes 65536 | tf_op jit(solution)/shard_map/pallas_call | solution.py:168
  35.7 3.4 %collective-permute-start.3 = (bf16[2,128,256]{2,1,0:T(8,128)(2,1)S(1)}, bf16[2,128,256]{2,1,0:T(8,128)(2,1)S(1)}, u32[]{:S(2)}, u32[]{:S(2)}) collective-permute-start(bf16[2,128,256]{2,1,0:T(8,128)(2,1)S(1)} %pad_maximum_fusion.1), channel_id=1, source_target_pairs={{0,32},{8,40},{16,48},{24,56},{32,64},{40,72},{48,80},{56,88},{64,... | collective-permute-start | bytes 393224 | tf_op jit(solution)/shard_map/ppermute | solution.py:21
  39.2 3.6 %collective-permute-start.2 = (bf16[2,128,256]{2,1,0:T(8,128)(2,1)S(1)}, bf16[2,128,256]{2,1,0:T(8,128)(2,1)S(1)}, u32[]{:S(2)}, u32[]{:S(2)}) collective-permute-start(bf16[2,128,256]{2,1,0:T(8,128)(2,1)S(1)} %pad_maximum_fusion.1), channel_id=1, source_target_pairs={{0,16},{8,24},{16,32},{24,40},{32,48},{40,56},{48,64},{56,72},{64,... | collective-permute-start | bytes 393224 | tf_op jit(solution)/shard_map/ppermute | solution.py:21
  42.8 1.7 collective-permute-done.3
  44.5 8.5 %collective-permute-done.2 = bf16[2,128,256]{2,1,0:T(8,128)(2,1)S(1)} collective-permute-done((bf16[2,128,256]{2,1,0:T(8,128)(2,1)S(1)}, bf16[2,128,256]{2,1,0:T(8,128)(2,1)S(1)}, u32[]{:S(2)}, u32[]{:S(2)}) %collective-permute-start.2) | collective-permute-done | bytes 131104 | tf_op jit(solution)/shard_map/ppermute | solution.py:21
  53.2 6.0 %collective-permute-start.4 = (bf16[2,128,256]{2,1,0:T(8,128)(2,1)S(1)}, bf16[2,128,256]{2,1,0:T(8,128)(2,1)S(1)}, u32[]{:S(2)}, u32[]{:S(2)}) collective-permute-start(bf16[2,128,256]{2,1,0:T(8,128)(2,1)S(1)} %pad_maximum_fusion.2), channel_id=1, source_target_pairs={{0,32},{8,40},{16,48},{24,56},{32,64},{40,72},{48,80},{56,88},{64,... | collective-permute-start | bytes 393224 | tf_op jit(solution)/shard_map/ppermute | solution.py:21
  59.2 7.3 %collective-permute-done.4 = bf16[2,128,256]{2,1,0:T(8,128)(2,1)S(1)} collective-permute-done((bf16[2,128,256]{2,1,0:T(8,128)(2,1)S(1)}, bf16[2,128,256]{2,1,0:T(8,128)(2,1)S(1)}, u32[]{:S(2)}, u32[]{:S(2)}) %collective-permute-start.4) | collective-permute-done | bytes 131104 | tf_op jit(solution)/shard_map/ppermute | solution.py:21
  66.8 9.2 %collective-permute-start.6 = (bf16[2,128,256]{2,1,0:T(8,128)(2,1)S(1)}, bf16[2,128,256]{2,1,0:T(8,128)(2,1)S(1)}, u32[]{:S(2)}, u32[]{:S(2)}) collective-permute-start(bf16[2,128,256]{2,1,0:T(8,128)(2,1)S(1)} %pad_maximum_fusion.3), channel_id=1, source_target_pairs={{0,128},{8,136},{16,144},{24,152},{32,160},{40,168},{48,176},{56,1... | collective-permute-start | bytes 393224 | tf_op jit(solution)/shard_map/ppermute | solution.py:21
  75.9 3.7 %collective-permute-start.7 = (bf16[2,128,128]{2,1,0:T(8,128)(2,1)S(1)}, bf16[2,128,128]{2,1,0:T(8,128)(2,1)S(1)}, u32[]{:S(2)}, u32[]{:S(2)}) collective-permute-start(bf16[2,128,128]{2,1,0:T(8,128)(2,1)S(1)} %fusion.30), channel_id=1, source_target_pairs={{0,192},{8,200},{16,208},{24,216},{32,224},{40,232},{48,240},{56,2... | collective-permute-start | bytes 196616 | tf_op jit(solution)/shard_map/ppermute | solution.py:21
  80.7 4.5 %all-to-all-start = ((bf16[8,128,512]{2,1,0:T(8,128)(2,1)}), bf16[8,128,512]{2,1,0:T(8,128)(2,1)S(1)}, u32[]{:S(2)}, u32[]{:S(2)}) async-start(bf16[8,128,512]{2,1,0:T(8,128)(2,1)} %broadcast_in_dim.2), calls=%async_computation | async-start | bytes 2097152 | tf_op jit(solution)/shard_map/all_to_all | solution.py:485
  85.2 1.6 collective-permute-start.5
  87.0 4.3 %collective-permute-done.5 = bf16[2,128,256]{2,1,0:T(8,128)(2,1)S(1)} collective-permute-done((bf16[2,128,256]{2,1,0:T(8,128)(2,1)S(1)}, bf16[2,128,256]{2,1,0:T(8,128)(2,1)S(1)}, u32[]{:S(2)}, u32[]{:S(2)}) %collective-permute-start.5) | collective-permute-done | bytes 131104 | tf_op jit(solution)/shard_map/ppermute | solution.py:21
  94.2 1.5 pad_maximum_fusion.4.state_ref
  95.7 6.5 %all-to-all-done.grad_ref = bf16[8,128,512]{2,1,0:T(8,128)(2,1)S(1)} async-done(((bf16[8,128,512]{2,1,0:T(8,128)(2,1)}), bf16[8,128,512]{2,1,0:T(8,128)(2,1)S(1)}, u32[]{:S(2)}, u32[]{:S(2)}) %all-to-all-start) | async-done | bytes 1048608 | tf_op jit(solution)/shard_map/all_to_all | solution.py:485
  103.2 7.0 %shard_map.111 = (bf16[128,512]{1,0:T(8,128)(2,1)}, bf16[8,2,128,512]{3,2,1,0:T(8,128)(2,1)}, bf16[8,2,128,512]{3,2,1,0:T(8,128)(2,1)}) custom-call(s32[2]{0:T(128)} %pad_add_fusion.refs_0_.place, f32[4,128,128]{2,1,0:T(8,128)} %get-tuple-element.40.qt_ref, f32[4,128,128]{2,1,0:T(8,128)} %get-tuple-element.41.local_ref, ...), custom_call_target="tpu_custom_call" | custom-call | flops 536870912 | bytes 6291456 | tf_op jit(solution)/shard_map/pallas_call | solution.py:245
  110.2 2.4 %collective-permute-start.18 = (bf16[8,2,128,512]{3,2,1,0:T(8,128)(2,1)}, bf16[8,2,128,512]{3,2,1,0:T(8,128)(2,1)S(1)}, u32[]{:S(2)}, u32[]{:S(2)}) collective-permute-start(bf16[8,2,128,512]{3,2,1,0:T(8,128)(2,1)} %get-tuple-element.57), channel_id=1, source_target_pairs={{0,8},{8,0},{16,24},{24,16},{32,40},{40,32},{48,56},{56,48},{64,72... | collective-permute-start | bytes 6291464 | tf_op jit(solution)/shard_map/ppermute | solution.py:26
  112.9 4.0 %collective-permute-done.18 = bf16[8,2,128,512]{3,2,1,0:T(8,128)(2,1)S(1)} collective-permute-done((bf16[8,2,128,512]{3,2,1,0:T(8,128)(2,1)}, bf16[8,2,128,512]{3,2,1,0:T(8,128)(2,1)S(1)}, u32[]{:S(2)}, u32[]{:S(2)}) %collective-permute-start.18) | collective-permute-done | bytes 2097184 | tf_op jit(solution)/shard_map/ppermute | solution.py:26
  116.8 3.6 %add_convert_fusion = bf16[8,2,128,512]{3,2,1,0:T(8,128)(2,1)} fusion(bf16[8,2,128,512]{3,2,1,0:T(8,128)(2,1)S(1)} %collective-permute-done.18, bf16[8,2,128,512]{3,2,1,0:T(8,128)(2,1)} %get-tuple-element.56), kind=kLoop, calls=%fused_computation | loop fusion | flops 4194304 | bytes 6291456 | tf_op jit(solution)/shard_map/convert_element_type | solution.py:493
  120.5 7.9 %shard_map.113 = (f32[128,512]{1,0:T(8,128)}, bf16[4,128,128]{2,1,0:T(8,128)(2,1)}) custom-call(s32[2]{0:T(128)} %pad_add_fusion.refs_0_.place, bf16[8,128,512]{2,1,0:T(8,128)(2,1)} %copy-done.1, bf16[8,2,128,512]{3,2,1,0:T(8,128)(2,1)} %bitcast.24, bf16[8,2,128,512]{3,2,1,0:T(8,128)(2,1)} %collective-permute-done.9.other_ref, ...), custom_call_target="tpu_custom_call" | custom-call | flops 536870912 | bytes 6291456 | tf_op jit(solution)/shard_map/pallas_call | solution.py:309
  133.9 5.1 %collective-permute-done.11 = bf16[2,128,128]{2,1,0:T(8,128)(2,1)S(1)} collective-permute-done((bf16[2,128,128]{2,1,0:T(8,128)(2,1)S(1)}, bf16[2,128,128]{2,1,0:T(8,128)(2,1)S(1)}, u32[]{:S(2)}, u32[]{:S(2)}) %collective-permute-start.11) | collective-permute-done | bytes 65568 | tf_op jit(solution)/shard_map/ppermute | solution.py:21
  140.6 7.6 %shard_map.112 = bf16[8,128,512]{2,1,0:T(8,128)(2,1)} custom-call(s32[2]{0:T(128)} %pad_add_fusion.refs_0_.place, bf16[128,512]{1,0:T(8,128)(2,1)} %get-tuple-element.46.heads_ref, bf16[8,2,128,512]{3,2,1,0:T(8,128)(2,1)} %bitcast.25, bf16[8,2,128,512]{3,2,1,0:T(8,128)(2,1)} %collective-permute-done.9.other_ref), custom_call_target="tpu_custom_call" | custom-call | flops 536870912 | bytes 6291456 | tf_op jit(solution)/shard_map/pallas_call | solution.py:274
  148.2 3.7 %all-to-all-start.1 = ((bf16[8,128,512]{2,1,0:T(8,128)(2,1)}), bf16[8,128,512]{2,1,0:T(8,128)(2,1)S(1)}, u32[]{:S(2)}, u32[]{:S(2)}) async-start(bf16[8,128,512]{2,1,0:T(8,128)(2,1)} %shard_map.112), calls=%async_computation.1 | async-start | bytes 2097152 | tf_op jit(solution)/shard_map/all_to_all | solution.py:499
  154.1 1.3 collective-permute-start.16
  158.0 3.6 %collective-permute-done.15 = bf16[2,128,128]{2,1,0:T(8,128)(2,1)S(1)} collective-permute-done((bf16[2,128,128]{2,1,0:T(8,128)(2,1)S(1)}, bf16[2,128,128]{2,1,0:T(8,128)(2,1)S(1)}, u32[]{:S(2)}, u32[]{:S(2)}) %collective-permute-start.15) | collective-permute-done | bytes 65568 | tf_op jit(solution)/shard_map/ppermute | solution.py:21
  161.5 4.7 %collective-permute-done.16 = bf16[2,128,128]{2,1,0:T(8,128)(2,1)S(1)} collective-permute-done((bf16[2,128,128]{2,1,0:T(8,128)(2,1)S(1)}, bf16[2,128,128]{2,1,0:T(8,128)(2,1)S(1)}, u32[]{:S(2)}, u32[]{:S(2)}) %collective-permute-start.16) | collective-permute-done | bytes 65568 | tf_op jit(solution)/shard_map/ppermute | solution.py:21
  166.4 4.4 %collective-permute-start.17 = (bf16[2,128,128]{2,1,0:T(8,128)(2,1)S(1)}, bf16[2,128,128]{2,1,0:T(8,128)(2,1)S(1)}, u32[]{:S(2)}, u32[]{:S(2)}) collective-permute-start(bf16[2,128,128]{2,1,0:T(8,128)(2,1)S(1)} %get-tuple-element.61), channel_id=1, source_target_pairs={{0,8},{8,0},{16,24},{24,16},{32,40},{40,32},{48,56},{56,48},{64,72... | collective-permute-start | bytes 196616 | tf_op jit(solution)/shard_map/ppermute | solution.py:26
  174.3 6.8 %shard_map.114 = (bf16[128,512]{1,0:T(8,128)(2,1)}, bf16[128,1024]{1,0:T(8,128)(2,1)}, bf16[128,1024]{1,0:T(8,128)(2,1)}, f32[2,2,256]{2,1,0:T(2,128)}) custom-call(s32[2]{0:T(128)} %pad_add_fusion.refs_0_.place, bf16[128,512]{1,0:T(8,128)(2,1)} %q_ref.1, bf16[128,1024]{1,0:T(8,128)(2,1)} %k_ref.1, f32[2,2,256]{2,1,0:T(2,128)} %reshape.31.refs_4_.logit_ref, ...), custom_call_target="tpu_custom_call" | custom-call | flops 1879048192 | bytes 5242880 | tf_op jit(solution)/shard_map/pallas_call | solution.py:380
  (93 shorter events, 28.7 us)
Async XLA Ops:
  7.2 85.2 %all-gather.3.cloned.1.call-start = ((), (), s32[]{:S(2)}) async-start(), calls=%async_computation.4 | async-start | bytes 2359296 | tf_op jit(solution)/shard_map/all_gather | solution.py:484
  7.2 6.2 %collective-permute-start = (bf16[128,512]{1,0:T(8,128)(2,1)}, bf16[128,512]{1,0:T(8,128)(2,1)S(1)}, u32[]{:S(2)}, u32[]{:S(2)}) collective-permute-start(bf16[128,512]{1,0:T(8,128)(2,1)} %param.10), channel_id=1, source_target_pairs={{0,128},{8,136},{16,144},{24,152},{32,160},{40,168},{48,176},{56,1... | collective-permute-start | bytes 393224 | tf_op jit(solution)/shard_map/ppermute | solution.py:26
  23.2 11.3 %collective-permute-start.1 = (bf16[2,128,256]{2,1,0:T(8,128)(2,1)}, bf16[2,128,256]{2,1,0:T(8,128)(2,1)S(1)}, u32[]{:S(2)}, u32[]{:S(2)}) collective-permute-start(bf16[2,128,256]{2,1,0:T(8,128)(2,1)} %get-tuple-element.42), channel_id=1, source_target_pairs={{0,8},{8,0},{16,24},{24,16},{32,40},{40,32},{48,56},{56,48},{64,72... | collective-permute-start | bytes 393224 | tf_op jit(solution)/shard_map/ppermute | solution.py:26
  34.5 45.1 %copy-start.12 = (bf16[128,512]{1,0:T(8,128)(2,1)S(1)}, bf16[128,512]{1,0:T(8,128)(2,1)}, u32[]{:S(2)}) copy-start(bf16[128,512]{1,0:T(8,128)(2,1)} %param.11) | copy-start | bytes 393220
  35.5 23.8 %copy-start.6 = (bf16[2,128,256]{2,1,0:T(8,128)(2,1)}, bf16[2,128,256]{2,1,0:T(8,128)(2,1)S(1)}, u32[]{:S(2)}) copy-start(bf16[2,128,256]{2,1,0:T(8,128)(2,1)S(1)} %get-tuple-element.58) | copy-start | bytes 393220
  35.7 8.8 %collective-permute-start.3 = (bf16[2,128,256]{2,1,0:T(8,128)(2,1)S(1)}, bf16[2,128,256]{2,1,0:T(8,128)(2,1)S(1)}, u32[]{:S(2)}, u32[]{:S(2)}) collective-permute-start(bf16[2,128,256]{2,1,0:T(8,128)(2,1)S(1)} %pad_maximum_fusion.1), channel_id=1, source_target_pairs={{0,32},{8,40},{16,48},{24,56},{32,64},{40,72},{48,80},{56,88},{64,... | collective-permute-start | bytes 393224 | tf_op jit(solution)/shard_map/ppermute | solution.py:21
  39.2 13.8 %collective-permute-start.2 = (bf16[2,128,256]{2,1,0:T(8,128)(2,1)S(1)}, bf16[2,128,256]{2,1,0:T(8,128)(2,1)S(1)}, u32[]{:S(2)}, u32[]{:S(2)}) collective-permute-start(bf16[2,128,256]{2,1,0:T(8,128)(2,1)S(1)} %pad_maximum_fusion.1), channel_id=1, source_target_pairs={{0,16},{8,24},{16,32},{24,40},{32,48},{40,56},{48,64},{56,72},{64,... | collective-permute-start | bytes 393224 | tf_op jit(solution)/shard_map/ppermute | solution.py:21
  53.0 38.2 %copy-start.4 = (bf16[2,128,256]{2,1,0:T(8,128)(2,1)}, bf16[2,128,256]{2,1,0:T(8,128)(2,1)S(1)}, u32[]{:S(2)}) copy-start(bf16[2,128,256]{2,1,0:T(8,128)(2,1)S(1)} %collective-permute-done.2) | copy-start | bytes 393220
  53.2 13.3 %collective-permute-start.4 = (bf16[2,128,256]{2,1,0:T(8,128)(2,1)S(1)}, bf16[2,128,256]{2,1,0:T(8,128)(2,1)S(1)}, u32[]{:S(2)}, u32[]{:S(2)}) collective-permute-start(bf16[2,128,256]{2,1,0:T(8,128)(2,1)S(1)} %pad_maximum_fusion.2), channel_id=1, source_target_pairs={{0,32},{8,40},{16,48},{24,56},{32,64},{40,72},{48,80},{56,88},{64,... | collective-permute-start | bytes 393224 | tf_op jit(solution)/shard_map/ppermute | solution.py:21
  66.7 24.5 %copy-start.2 = (f32[2,128,256]{2,1,0:T(8,128)}, f32[2,128,256]{2,1,0:T(8,128)S(1)}, u32[]{:S(2)}) copy-start(f32[2,128,256]{2,1,0:T(8,128)S(1)} %fusion.31) | copy-start | bytes 786436
  66.8 20.0 %collective-permute-start.6 = (bf16[2,128,256]{2,1,0:T(8,128)(2,1)S(1)}, bf16[2,128,256]{2,1,0:T(8,128)(2,1)S(1)}, u32[]{:S(2)}, u32[]{:S(2)}) collective-permute-start(bf16[2,128,256]{2,1,0:T(8,128)(2,1)S(1)} %pad_maximum_fusion.3), channel_id=1, source_target_pairs={{0,128},{8,136},{16,144},{24,152},{32,160},{40,168},{48,176},{56,1... | collective-permute-start | bytes 393224 | tf_op jit(solution)/shard_map/ppermute | solution.py:21
  75.9 10.9 %collective-permute-start.7 = (bf16[2,128,128]{2,1,0:T(8,128)(2,1)S(1)}, bf16[2,128,128]{2,1,0:T(8,128)(2,1)S(1)}, u32[]{:S(2)}, u32[]{:S(2)}) collective-permute-start(bf16[2,128,128]{2,1,0:T(8,128)(2,1)S(1)} %fusion.30), channel_id=1, source_target_pairs={{0,192},{8,200},{16,208},{24,216},{32,224},{40,232},{48,240},{56,2... | collective-permute-start | bytes 196616 | tf_op jit(solution)/shard_map/ppermute | solution.py:21
  80.7 21.5 %all-to-all-start = ((bf16[8,128,512]{2,1,0:T(8,128)(2,1)}), bf16[8,128,512]{2,1,0:T(8,128)(2,1)S(1)}, u32[]{:S(2)}, u32[]{:S(2)}) async-start(bf16[8,128,512]{2,1,0:T(8,128)(2,1)} %broadcast_in_dim.2), calls=%async_computation | async-start | bytes 2097152 | tf_op jit(solution)/shard_map/all_to_all | solution.py:485
  85.2 87.3 %reduce-scatter.2.cloned.1.call-start = ((), (), s32[]{:S(2)}) async-start(), calls=%async_computation.3 | async-start | bytes 2359296 | tf_op jit(solution)/shard_map/reduce_scatter | solution.py:492
  85.2 6.0 %collective-permute-start.5 = (bf16[2,128,256]{2,1,0:T(8,128)(2,1)S(1)}, bf16[2,128,256]{2,1,0:T(8,128)(2,1)S(1)}, u32[]{:S(2)}, u32[]{:S(2)}) collective-permute-start(bf16[2,128,256]{2,1,0:T(8,128)(2,1)S(1)} %pad_maximum_fusion.3), channel_id=1, source_target_pairs={{0,64},{8,72},{16,80},{24,88},{32,96},{40,104},{48,112},{56,120},{... | collective-permute-start | bytes 393224 | tf_op jit(solution)/shard_map/ppermute | solution.py:21
  92.4 20.2 %copy-start = (bf16[16,128,512]{2,1,0:T(8,128)(2,1)S(1)}, bf16[16,128,512]{2,1,0:T(8,128)(2,1)}, u32[]{:S(2)}) copy-start(bf16[16,128,512]{2,1,0:T(8,128)(2,1)} %all-gather.3.cloned.1.call-done) | copy-start | bytes 6291460
  92.4 1.9 collective-permute-start.8
  110.2 6.7 %collective-permute-start.18 = (bf16[8,2,128,512]{3,2,1,0:T(8,128)(2,1)}, bf16[8,2,128,512]{3,2,1,0:T(8,128)(2,1)S(1)}, u32[]{:S(2)}, u32[]{:S(2)}) collective-permute-start(bf16[8,2,128,512]{3,2,1,0:T(8,128)(2,1)} %get-tuple-element.57), channel_id=1, source_target_pairs={{0,8},{8,0},{16,24},{24,16},{32,40},{40,32},{48,56},{56,48},{64,72... | collective-permute-start | bytes 6291464 | tf_op jit(solution)/shard_map/ppermute | solution.py:26
  112.6 7.9 %collective-permute-start.9 = (bf16[8,2,128,512]{3,2,1,0:T(8,128)(2,1)S(1)}, bf16[8,2,128,512]{3,2,1,0:T(8,128)(2,1)}, u32[]{:S(2)}, u32[]{:S(2)}) collective-permute-start(bf16[8,2,128,512]{3,2,1,0:T(8,128)(2,1)S(1)} %bitcast.26), channel_id=1, source_target_pairs={{0,8},{8,0},{16,24},{24,16},{32,40},{40,32},{48,56},{56,48},{64,72... | collective-permute-start | bytes 6291464 | tf_op jit(solution)/shard_map/ppermute | solution.py:26
  120.4 20.0 %copy-start.3 = (f32[2,128,256]{2,1,0:T(8,128)S(1)}, f32[2,128,256]{2,1,0:T(8,128)}, u32[]{:S(2)}) copy-start(f32[2,128,256]{2,1,0:T(8,128)} %copy-done.2) | copy-start | bytes 786436
  120.4 20.0 %copy-start.14 = (bf16[2,128,256]{2,1,0:T(8,128)(2,1)S(1)}, bf16[2,128,256]{2,1,0:T(8,128)(2,1)}, u32[]{:S(2)}) copy-start(bf16[2,128,256]{2,1,0:T(8,128)(2,1)} %copy-done.13) | copy-start | bytes 393220
  129.2 1.3 collective-permute-start.10
  132.6 6.4 %collective-permute-start.11 = (bf16[2,128,128]{2,1,0:T(8,128)(2,1)S(1)}, bf16[2,128,128]{2,1,0:T(8,128)(2,1)S(1)}, u32[]{:S(2)}, u32[]{:S(2)}) collective-permute-start(bf16[2,128,128]{2,1,0:T(8,128)(2,1)S(1)} %convolution_convert_fusion.6), channel_id=1, source_target_pairs={{16,0},{24,8},{32,16},{40,24},{48,32},{56,40},{64,48},{72,56},{80,... | collective-permute-start | bytes 196616 | tf_op jit(solution)/shard_map/ppermute | solution.py:21
  139.2 12.8 %collective-permute-start.12 = (bf16[2,128,128]{2,1,0:T(8,128)(2,1)S(1)}, bf16[2,128,128]{2,1,0:T(8,128)(2,1)S(1)}, u32[]{:S(2)}, u32[]{:S(2)}) collective-permute-start(bf16[2,128,128]{2,1,0:T(8,128)(2,1)S(1)} %convolution_convert_fusion.5), channel_id=1, source_target_pairs={{32,0},{40,8},{48,16},{56,24},{64,32},{72,40},{80,48},{88,56},{96,... | collective-permute-start | bytes 196616 | tf_op jit(solution)/shard_map/ppermute | solution.py:21
  148.2 18.0 %copy-start.8 = (bf16[4,128,128]{2,1,0:T(8,128)(2,1)S(1)}, bf16[4,128,128]{2,1,0:T(8,128)(2,1)}, u32[]{:S(2)}) copy-start(bf16[4,128,128]{2,1,0:T(8,128)(2,1)} %get-tuple-element.50) | copy-start | bytes 393220
  148.2 34.1 %all-to-all-start.1 = ((bf16[8,128,512]{2,1,0:T(8,128)(2,1)}), bf16[8,128,512]{2,1,0:T(8,128)(2,1)S(1)}, u32[]{:S(2)}, u32[]{:S(2)}) async-start(bf16[8,128,512]{2,1,0:T(8,128)(2,1)} %shard_map.112), calls=%async_computation.1 | async-start | bytes 2097152 | tf_op jit(solution)/shard_map/all_to_all | solution.py:499
  152.2 9.3 %collective-permute-start.15 = (bf16[2,128,128]{2,1,0:T(8,128)(2,1)S(1)}, bf16[2,128,128]{2,1,0:T(8,128)(2,1)S(1)}, u32[]{:S(2)}, u32[]{:S(2)}) collective-permute-start(bf16[2,128,128]{2,1,0:T(8,128)(2,1)S(1)} %convolution_convert_fusion.2), channel_id=1, source_target_pairs={{144,0},{152,8},{160,16},{168,24},{176,32},{184,40},{192,48},{200,... | collective-permute-start | bytes 196616 | tf_op jit(solution)/shard_map/ppermute | solution.py:21
  154.1 12.1 %collective-permute-start.16 = (bf16[2,128,128]{2,1,0:T(8,128)(2,1)S(1)}, bf16[2,128,128]{2,1,0:T(8,128)(2,1)S(1)}, u32[]{:S(2)}, u32[]{:S(2)}) collective-permute-start(bf16[2,128,128]{2,1,0:T(8,128)(2,1)S(1)} %convolution_convert_fusion), channel_id=1, source_target_pairs={{208,0},{216,8},{224,16},{232,24},{240,32},{248,40},{209,1},{217,9... | collective-permute-start | bytes 196616 | tf_op jit(solution)/shard_map/ppermute | solution.py:21
  155.4 10.8 %collective-permute-start.14 = (bf16[2,128,128]{2,1,0:T(8,128)(2,1)S(1)}, bf16[2,128,128]{2,1,0:T(8,128)(2,1)S(1)}, u32[]{:S(2)}, u32[]{:S(2)}) collective-permute-start(bf16[2,128,128]{2,1,0:T(8,128)(2,1)S(1)} %convolution_convert_fusion.4), channel_id=1, source_target_pairs={{80,0},{88,8},{96,16},{104,24},{112,32},{120,40},{128,48},{136,56}... | collective-permute-start | bytes 196616 | tf_op jit(solution)/shard_map/ppermute | solution.py:21
  156.7 9.5 %collective-permute-start.13 = (bf16[2,128,128]{2,1,0:T(8,128)(2,1)S(1)}, bf16[2,128,128]{2,1,0:T(8,128)(2,1)S(1)}, u32[]{:S(2)}, u32[]{:S(2)}) collective-permute-start(bf16[2,128,128]{2,1,0:T(8,128)(2,1)S(1)} %add_convert_fusion.3), channel_id=1, source_target_pairs={{16,0},{24,8},{32,16},{40,24},{48,32},{56,40},{64,48},{72,56},{80,... | collective-permute-start | bytes 196616 | tf_op jit(solution)/shard_map/ppermute | solution.py:21
  166.4 5.3 %collective-permute-start.17 = (bf16[2,128,128]{2,1,0:T(8,128)(2,1)S(1)}, bf16[2,128,128]{2,1,0:T(8,128)(2,1)S(1)}, u32[]{:S(2)}, u32[]{:S(2)}) collective-permute-start(bf16[2,128,128]{2,1,0:T(8,128)(2,1)S(1)} %get-tuple-element.61), channel_id=1, source_target_pairs={{0,8},{8,0},{16,24},{24,16},{32,40},{40,32},{48,56},{56,48},{64,72... | collective-permute-start | bytes 196616 | tf_op jit(solution)/shard_map/ppermute | solution.py:26
  173.4 9.8 %collective-permute-start.19 = (bf16[128,512]{1,0:T(8,128)(2,1)S(1)}, bf16[128,512]{1,0:T(8,128)(2,1)S(1)}, u32[]{:S(2)}, u32[]{:S(2)}) collective-permute-start(bf16[128,512]{1,0:T(8,128)(2,1)S(1)} %slice_bitcast_fusion), channel_id=1, source_target_pairs={{0,128},{8,136},{16,144},{24,152},{32,160},{40,168},{48,176},{56,1... | collective-permute-start | bytes 393224 | tf_op jit(solution)/shard_map/ppermute | solution.py:26
  (7 other events, 51.9 us)
Sparse Core Ops, SparseCore 0:
  15.2 52.3 all-gather.2
  120.5 33.1 reduce-scatter.1

commit v3 on v2

--- a/solution.py
+++ b/solution.py
@@ -34,10 +34,13 @@
 def dot(a, b, ca=1, cb=0, passes=3):
     dims = (((ca,), (cb,)), ((), ()))
     mul = functools.partial(lax.dot_general, dimension_numbers=dims, preferred_element_type=F32)
+    if passes == 1:
+        return mul(a.astype(BF16), b.astype(BF16))
+    if b.dtype == BF16:
+        a_high, a_low = split(a)
+        return mul(a_high, b) + mul(a_low, b)
     a_high, a_low = split(a)
     b_high, b_low = split(b)
-    if passes == 1:
-        return mul(a_high, b_high)
     return mul(a_high, b_high) + (mul(a_low, b_high) + mul(a_high, b_low))
 
 
@@ -74,8 +77,9 @@
     return jnp.concatenate(parts, axis=0).astype(F32)
 
 
-def prepare_kernel(*refs):
-    q_ref, k_ref, v_ref, logit_ref = refs[1:5]
+def prepare_kernel(mine, *refs):
+    place, q_ref, k_ref, v_ref, logit_ref = refs[:5]
+    first = 2 * (place[0] if mine else 1 - place[0])
     ab_ref, m_ref, wy_ref, qt_ref, local_ref = refs[-5:]
     two = range(2)
     shape = (PAIRS, PAIRS)
@@ -85,7 +89,7 @@
     query = [x * inverse_norm(x) for x in query]
     key = [stacked(k_ref, i) for i in two]
     key = [x * inverse_norm(x) for x in key]
-    strength = [2.0 / (1.0 + jnp.exp(-column_of(logit_ref[0, i : i + 1, :]))) for i in two]
+    strength = [2.0 / (1.0 + jnp.exp(-column_of(logit_ref[pl.ds(first + i, 1), :]))) for i in two]
     coupling = [jnp.where(col < row, strength[i] * dot(key[i], key[i], 1, 1), 0.0) for i in two]
     inverse = [identity - jnp.where((row >> 1) == (col >> 1), coupling[i], 0.0) for i in two]
     for level in range(1, 8):
@@ -166,7 +170,7 @@
         return arr(F32, 4, n, n)
 
     return pl.pallas_call(
-        prepare_kernel,
+        functools.partial(prepare_kernel, mine),
         grid_spec=pltpu.PrefetchScalarGridSpec(
             num_scalar_prefetch=1,
             grid=(1,),
@@ -174,7 +178,7 @@
                 columns(WIDTH),
                 columns(PAIRS),
                 columns(PAIRS),
-                pl.BlockSpec((1, 2, PAIRS), lambda i, place: (pair(place), 0, 0)),
+                whole(4, PAIRS),
             ]
             + [pl.BlockSpec(memory_space=pl.ANY)] * len(filled),
             out_specs=[
@@ -197,57 +201,54 @@
         cost_estimate=pl.CostEstimate(
             flops=(1 if mine else 100) << 20, bytes_accessed=1 << (16 if mine else 24), transcendentals=0
         ),
-    )(place, queries, keys, values, logits.reshape(2, 2, PAIRS), *filled)
-
-
-def feature_block(grad_ref, place, z, row, core):
-    owner = (row ^ place[1]) * 4 + z // 2
-    column = pl.multiple_of((z % 2) * 256 + (core ^ place[0]) * 128, 128)
-    return owner, pl.ds(column, 128)
-
-
-def grad_block(grad_ref, place, z, row, core):
-    owner, columns = feature_block(grad_ref, place, z, row, core)
-    return grad_ref[owner, :, columns]
+    )(place, queries, keys, values, logits, *filled)
+
+
+STEPS = 4
+BLOCKS = [(z, core, row) for z in range(2) for core in range(2) for row in range(2)]
+
+
+def grad_block(place, step, z, core, row):
+    column = pl.multiple_of(z * 256 + (core ^ place[0]) * 128, 128)
+    return (row ^ place[1]) * 4 + step, slice(None), pl.ds(column, 128)
 
 
 def weight_rows(mine_ref, other_ref):
-    return jnp.concatenate([mine_ref[0, 0], mine_ref[0, 1], other_ref[0, 0], other_ref[0, 1]], axis=0)
-
-
-def outputs_kernel(place, qt_ref, local_ref, state_ref, grad_ref, heads_ref, mine_ref, other_ref, held):
-    z = pl.program_id(0)
-
-    @pl.when(z == 0)
+    return jnp.concatenate([(mine_ref, other_ref)[core][z, row] for z, core, row in BLOCKS], axis=0)
+
+
+def weight_tile():
+    return pl.BlockSpec((2, 2, WIDTH, 512), lambda step, place: (step, 0, 0, 0))
+
+
+def outputs_kernel(place, qt_ref, local_ref, state_ref, grad_ref, heads_ref, out_ref, held):
+    step = pl.program_id(0)
+
+    @pl.when(step == 0)
     def _():
         for head in range(4):
-            state = state_ref[slot(head, place)].astype(F32)
-            result = dot(qt_ref[head], state) + local_ref[head]
+            result = dot(qt_ref[head], state_ref[slot(head, place)]) + local_ref[head]
             held[:, head * WIDTH : (head + 1) * WIDTH] = result.astype(BF16)
         heads_ref[...] = held[...]
 
-    blocks = jnp.concatenate(
-        [grad_block(grad_ref, place, z, row, core) for core in range(2) for row in range(2)], axis=1
-    )
-    product = lax.dot_general(
-        blocks, held[...], (((0,), (0,)), ((), ())), preferred_element_type=F32
-    )
-    product = (product * (1.0 / 64.0)).astype(BF16)
-    for row in range(2):
-        mine_ref[0, row] = product[row * WIDTH : (row + 1) * WIDTH]
-        other_ref[0, row] = product[(2 + row) * WIDTH : (3 + row) * WIDTH]
+    for z in range(2):
+        rows = [grad_ref[grad_block(place, step, *block)] for block in BLOCKS[4 * z : 4 * z + 4]]
+        product = lax.dot_general(
+            jnp.concatenate(rows, axis=1),
+            held[...],
+            (((0,), (0,)), ((), ())),
+            preferred_element_type=F32,
+        )
+        out_ref[z] = (product * (1.0 / 64.0)).astype(BF16)
 
 
 def outputs(place, qt, local, state, grad_full):
-    heads = arr(BF16, WIDTH, 512)
-    part = arr(BF16, 8, 2, WIDTH, 512)
-    tile = pl.BlockSpec((1, 2, WIDTH, 512), lambda z, place: (z, 0, 0, 0))
     return call(
         outputs_kernel,
-        8,
+        STEPS,
         [whole(4, WIDTH, WIDTH), whole(4, WIDTH, WIDTH), whole(4, WIDTH, WIDTH), whole(8, WIDTH, 512)],
-        [whole(WIDTH, 512), tile, tile],
-        [heads, part, part],
+        [whole(WIDTH, 512), pl.BlockSpec((2, 512, 512), lambda step, place: (step, 0, 0))],
+        [arr(BF16, WIDTH, 512), arr(BF16, 8, 512, 512)],
         2 * 128 * 512 * 4096,
         6 << 20,
         [pltpu.VMEM((WIDTH, 512), BF16)],
@@ -255,26 +256,22 @@
 
 
 def mixed_kernel(place, heads_ref, mine_ref, other_ref, out_ref):
-    z = pl.program_id(0)
+    step = pl.program_id(0)
     product = lax.dot_general(
         heads_ref[...],
         weight_rows(mine_ref, other_ref),
         (((1,), (1,)), ((), ())),
         preferred_element_type=F32,
     ).astype(BF16)
-    for core in range(2):
-        for row in range(2):
-            owner, columns = feature_block(out_ref, place, z, row, core)
-            start = (2 * core + row) * WIDTH
-            out_ref[owner, :, columns] = product[:, start : start + WIDTH]
+    for i, block in enumerate(BLOCKS):
+        out_ref[grad_block(place, step, *block)] = product[:, i * WIDTH : (i + 1) * WIDTH]
 
 
 def mixed_parts(place, heads, mine, other):
-    tile = pl.BlockSpec((1, 2, WIDTH, 512), lambda z, place: (z, 0, 0, 0))
     return call(
         mixed_kernel,
-        8,
-        [whole(WIDTH, 512), tile, tile],
+        STEPS,
+        [whole(WIDTH, 512), weight_tile(), weight_tile()],
         whole(8, WIDTH, 512),
         arr(BF16, 8, WIDTH, 512),
         2 * 128 * 512 * 4096,
@@ -283,21 +280,23 @@
 
 
 def head_grad_kernel(place, grad_ref, mine_ref, other_ref, qt_ref, out_ref, own_ref):
-    z = pl.program_id(0)
-    blocks = jnp.concatenate(
-        [grad_block(grad_ref, place, z, row, core) for core in range(2) for row in range(2)], axis=1
-    )
-    total = jnp.dot(blocks, weight_rows(mine_ref, other_ref), preferred_element_type=F32)
-
-    @pl.when(z == 0)
+    step = pl.program_id(0)
+    blocks = [grad_ref[grad_block(place, step, *block)] for block in BLOCKS]
+    total = jnp.dot(
+        jnp.concatenate(blocks, axis=1),
+        weight_rows(mine_ref, other_ref),
+        preferred_element_type=F32,
+    )
+
+    @pl.when(step == 0)
     def _():
         out_ref[...] = total
 
-    @pl.when(z > 0)
+    @pl.when(step > 0)
     def _():
         out_ref[...] += total
 
-    @pl.when(z == 7)
+    @pl.when(step == STEPS - 1)
     def _():
         for head in range(4):
             grad = out_ref[:, head * WIDTH : (head + 1) * WIDTH]
@@ -305,11 +304,10 @@
 
 
 def head_gradient(place, grad_full, mine, other, qt):
-    tile = pl.BlockSpec((1, 2, WIDTH, 512), lambda z, place: (z, 0, 0, 0))
     return call(
         head_grad_kernel,
-        8,
-        [whole(8, WIDTH, 512), tile, tile, whole(4, WIDTH, WIDTH)],
+        STEPS,
+        [whole(8, WIDTH, 512), weight_tile(), weight_tile(), whole(4, WIDTH, WIDTH)],
         [whole(WIDTH, 512), whole(4, WIDTH, WIDTH)],
         [arr(F32, WIDTH, 512), arr(BF16, 4, WIDTH, WIDTH)],
         2 * 128 * 512 * 4096,
@@ -330,12 +328,13 @@
     key = [stacked(k_ref, i) for i in two]
     key_scale = [inverse_norm(x) for x in key]
     key = [key[i] * key_scale[i] for i in two]
-    logit = [column_of(logit_ref[0, i : i + 1, :]) for i in two]
-    state = [state_ref[i].astype(F32) for i in two]
-    end = [end_ref[i].astype(F32) for i in two]
+    first = 2 * pl.program_id(0)
+    logit = [column_of(logit_ref[pl.ds(first + i, 1), :]) for i in two]
+    state = [state_ref[i] for i in two]
+    end = [end_ref[i] for i in two]
     grad = [grad_ref[:, i * WIDTH : (i + 1) * WIDTH] for i in two]
     updates = [wy_ref[i, :, WIDTH:] - dot(wy_ref[i, :, :WIDTH], state[i]) for i in two]
-    pulled = [dot(m_ref[i], jnp.concatenate([grad[i], end[i]], axis=0), 0, 0) for i in two]
+    pulled = [dot(m_ref[i], jnp.concatenate([grad[i], end[i].astype(F32)], axis=0), 0, 0) for i in two]
     value_grad = [2.0 / (1.0 + jnp.exp(-logit[i])) * pulled[i] for i in two]
     cross = [
         dot(jnp.concatenate([grad[i], value_grad[i]], axis=0), updates[i], 1, 1) for i in two
@@ -353,15 +352,16 @@
     forward = [dot(pairs[i], key[i]) for i in two]
     backward = [dot(pairs[i], jnp.concatenate([query[i], key[i]], axis=0), 0, 0) for i in two]
     by_state = [
-        dot(jnp.concatenate([grad[i], -value_grad[i]], axis=0), state[i], 1, 1) for i in two
+        dot(jnp.concatenate([grad[i], -value_grad[i]], axis=0), state[i], 1, 1, passes=1)
+        for i in two
     ]
-    by_end = [dot(updates[i], end[i], 1, 1) for i in two]
+    by_end = [dot(updates[i], end[i], 1, 1, passes=1) for i in two]
     for i in two:
         start = i * PAIRS
         dv_ref[:, start : start + WIDTH] = value_grad[i][:WIDTH].astype(BF16)
         dv_ref[:, start + WIDTH : start + PAIRS] = value_grad[i][WIDTH:].astype(BF16)
         slope = jnp.sum(pulled[i] * updates[i], axis=1, keepdims=True) / (1.0 + jnp.exp(logit[i]))
-        dlogit_ref[0, i : i + 1, :] = row_of(slope)
+        dlogit_ref[pl.ds(first + i, 1), :] = row_of(slope)
         query_grad = forward[i][:WIDTH] + by_state[i][:WIDTH]
         query_grad = query_scale[i] * (
             query_grad - query[i] * jnp.sum(query[i] * query_grad, axis=1, keepdims=True)
@@ -376,31 +376,29 @@
 
 
 def pull(place, queries, keys, logits, reads, wy, state, end, head_grad):
-    logit_spec = pl.BlockSpec((1, 2, PAIRS), lambda i, place: (i, 0, 0))
-    *grads, logit_grad = call(
+    return call(
         pull_kernel,
         2,
         [
             by_columns(WIDTH),
             by_columns(PAIRS),
-            logit_spec,
+            whole(4, PAIRS),
             by_pair(PAIRS, PAIRS),
             by_pair(PAIRS, PAIRS),
             by_slot(WIDTH, WIDTH),
             by_slot(WIDTH, WIDTH),
             by_columns(WIDTH),
         ],
-        [by_columns(WIDTH), by_columns(PAIRS), by_columns(PAIRS), logit_spec],
+        [by_columns(WIDTH), by_columns(PAIRS), by_columns(PAIRS), whole(4, PAIRS)],
         [
             arr(BF16, WIDTH, 512),
             arr(BF16, WIDTH, 1024),
             arr(BF16, WIDTH, 1024),
-            arr(F32, 2, 2, PAIRS),
+            arr(F32, 4, PAIRS),
         ],
         4 * 14 * 2 * PAIRS**3,
         5 << 20,
-    )(place, queries, keys, logits.reshape(2, 2, PAIRS), reads, wy, state, end, head_grad)
-    return (*grads, logit_grad.reshape(4, PAIRS))
+    )(place, queries, keys, logits, reads, wy, state, end, head_grad)
 
 
 def mul(a, b):
@@ -415,7 +413,7 @@
     return x[:, :, :WIDTH], x[:, :, WIDTH:]
 
 
-def forward_states(mine, theirs, core, gate):
+def forward_states(mine, theirs, core, grad_full, gate):
     theirs = exchange(theirs, 1)
     even = jnp.where(core == 0, mine, theirs)
     odd = jnp.where(core == 0, theirs, mine)
@@ -435,6 +433,7 @@
     window4 = step[:, :, :WIDTH].astype(BF16)
     rounded = state.astype(BF16)
     both = jnp.concatenate([window4, rounded], axis=2)
+    grad_full, both = lax.optimization_barrier((grad_full, both))
     near_a, near_b = halves(send(both, 8))
     mid_a, mid_b = halves(send(both, 16))
     far_b = send(rounded, 24)
@@ -448,7 +447,7 @@
     given = jnp.where(core == 0, second, first)
     gate, given = lax.optimization_barrier((gate, given))
     state_in = jnp.concatenate([kept, exchange(given, 1)], axis=0)
-    return gate, state_in, (even_a, odd_a, window1, window2, window4, window8, window12)
+    return grad_full, gate, state_in, (even_a, odd_a, window1, window2, window4, window8, window12)
 
 
 def backward_states(own, core, saved):
@@ -477,25 +476,27 @@
     place = jnp.stack([core, index >> 4]).astype(jnp.int32)
     rings = [[(half * 8 + z) * 2 + c for z in range(8)] for half in range(2) for c in range(2)]
     operands = (queries, keys, values, beta_logit)
+    across = exchange(out_weight, 16)
     theirs, *filled = prepare(place, *operands, False)
-    weight_pair = jnp.stack([out_weight, exchange(out_weight, 16)])
+    across, theirs = lax.optimization_barrier((across, theirs))
+    weight_pair = jnp.stack([out_weight, across])
     weight_pair, *operands = lax.optimization_barrier((weight_pair, *operands))
     mine, reads, wy, qt, local_out = prepare(place, *operands, True, filled)
     weight_mine = lax.all_gather(weight_pair, "ctx", axis=0, axis_index_groups=rings)
     grad_full = lax.all_to_all(
         jnp.broadcast_to(out_grad[None], (8, WIDTH, 512)), "tp", 0, 0, tiled=True
     )
-    weight_mine, state, saved = forward_states(mine, theirs, core, weight_mine)
+    grad_full, weight_mine, state, saved = forward_states(
+        mine, theirs, core, grad_full, weight_mine
+    )
     weight_other = exchange(weight_mine, 1)
-    heads, part_mine, part_other = outputs(place, qt, local_out, state, grad_full)
-    part = part_mine.astype(F32) + exchange(part_other, 1).astype(F32)
+    heads, part = outputs(place, qt, local_out, state, grad_full)
     ring_sum = lax.psum_scatter(
-        part.astype(BF16).reshape(8, PAIRS, 512),
-        "ctx",
-        scatter_dimension=0,
-        axis_index_groups=rings,
-    )
-    weight_grad = ring_sum[:WIDTH].astype(F32) + exchange(ring_sum[WIDTH:], 16).astype(F32)
+        part, "ctx", scatter_dimension=0, axis_index_groups=rings
+    ).reshape(2, 2, WIDTH, 512)
+    weight_grad = ring_sum[0, 0].astype(F32) + exchange(ring_sum[1, 0], 1).astype(F32)
+    weight_grad += exchange(ring_sum[0, 1], 16).astype(F32)
+    weight_grad += exchange(ring_sum[1, 1], 17).astype(F32)
     mixed = lax.all_to_all(
         mixed_parts(place, heads, weight_mine, weight_other), "tp", 0, 0, tiled=True
     )

time: 193 us -> 176 us (0.912)
  waiting for transfers between devices: 51 us -> 41.6 us
  Pallas kernels: 41.7 us -> 35.9 us
  starting transfers between devices: 60 us -> 64.9 us
  other arithmetic: 11.5 us -> 8.02 us
    all_to_all x1, waiting for transfers between devices: 6.46 us -> 0.01 us  [local(): lax.all_to_all(jnp.broadcast_to(out_grad[None], (8, WIDTH, 512)), 'tp', 0...]
    pallas_call x6, Pallas kernels: 41.7 us -> 35.9 us  [the longest x2 12.6 us: prepare(): pl.pallas_call(functools.partial(prepare_kernel, mine), grid_spec=pltpu.P...]
    reshape x3 -> x0, local copies, waits for them, and re-layouts: 3.86 us -> none  [the longest x2 2.57 us: prepare(): logits.reshape(2, 2, PAIRS)]
    convert_element_type x1 -> x0, other arithmetic: 3.58 us -> none  [local(): part.astype(BF16).reshape(8, PAIRS, 512)]
    ppermute x8 -> x9, waiting for transfers between devices: 9.45 us -> 6.54 us  [exchange(): return lax.ppermute(block, 'ctx', route)]
    unnamed x30, local copies, waits for them, and re-layouts: 1.02 us -> 3.4 us
    ppermute x8 -> x9, starting transfers between devices: 16.6 us -> 19 us  [exchange(): return lax.ppermute(block, 'ctx', route)]
  transfers between devices with their start and end apart: 24 -> 25, of which waited for: 13 -> 11; matrix products, arithmetic and copies ran while one was open for 11% -> 6% of each run, Pallas kernels for 18% -> 17%
where the time goes in v3:
time: 176 us; the launch traced here: 175 us
  starting transfers between devices  64.9 us (37%)
  waiting for transfers between devices  41.6 us (24%)
  Pallas kernels  35.9 us (20%)
  between operations  14.5 us (8%)
  other arithmetic  8.02 us (5%)
  local copies, waits for them, and re-layouts  6.4 us (4%)
  matrix products  3.7 us (2%)
    ppermute x12, starting transfers between devices, send(): return lax.ppermute(block, 'ctx', route)  36.7 us
    ppermute x12, waiting for transfers between devices, send(): return lax.ppermute(block, 'ctx', route)  35 us
    ppermute x9, starting transfers between devices, exchange(): return lax.ppermute(block, 'ctx', route)  19 us
    pallas_call x2, Pallas kernels, prepare(): pl.pallas_call(functools.partial(prepare_kernel, mine), grid_spec=pltpu.P...  12.6 us
    ppermute x9, waiting for transfers between devices, exchange(): return lax.ppermute(block, 'ctx', route)  6.54 us
    pallas_call x1, Pallas kernels, pull(): call(pull_kernel, 2, [by_columns(WIDTH), by_columns(PAIRS), whole(4, PAIR...  6.19 us
    pallas_call x1, Pallas kernels, outputs(): call(outputs_kernel, STEPS, [whole(4, WIDTH, WIDTH), whole(4, WIDTH, WIDT...  5.76 us
    pallas_call x1, Pallas kernels, mixed_parts(): call(mixed_kernel, STEPS, [whole(WIDTH, 512), weight_tile(), weight_tile(...  5.68 us
  transfers between devices with their start and end apart: 25, of which 11 were waited for; matrix products, arithmetic and copies ran while one was open for 6% of the time, Pallas kernels for 17%

profile of v3, /device:TPU:1, one launch (start us, length us, event | category | flops | bytes accessed | tf_op | source)
XLA Modules:
  0.0 175.0 jit_solution(2102848418221218952)
XLA Ops:
  7.2 3.7 %collective-permute-start = (bf16[128,512]{1,0:T(8,128)(2,1)}, bf16[128,512]{1,0:T(8,128)(2,1)S(1)}, u32[]{:S(2)}, u32[]{:S(2)}) collective-permute-start(bf16[128,512]{1,0:T(8,128)(2,1)} %param.10), channel_id=1, source_target_pairs={{0,128},{8,136},{16,144},{24,152},{32,160},{40,168},{48,176},{56,1... | collective-permute-start | bytes 393224 | tf_op jit(solution)/shard_map/ppermute | solution.py:26
  11.5 6.3 %shard_map.109 = (bf16[2,128,256]{2,1,0:T(8,128)(2,1)}, f32[4,256,256]{2,1,0:T(8,128)}, f32[4,256,256]{2,1,0:T(8,128)}, f32[4,128,128]{2,1,0:T(8,128)}, f32[4,128,128]{2,1,0:T(8,128)}) custom-call(s32[2]{0:T(128)} %pad_add_fusion.refs_0_.place, bf16[128,512]{1,0:T(8,128)(2,1)} %q_ref.1, bf16[128,1024]{1,0:T(8,128)(2,1)} %k_ref.1, bf16[128,1024]{1,0:T(8,128)(2,1)} %refs_3_.2, ...), custom_call_target="tpu_custom_call" | custom-call | flops 104857600 | bytes 16777216 | tf_op jit(solution)/shard_map/pallas_call | solution.py:172
  17.8 1.6 pad_maximum_fusion
  20.5 6.4 %shard_map.110 = (bf16[2,128,256]{2,1,0:T(8,128)(2,1)}, f32[4,256,256]{2,1,0:T(8,128)}, f32[4,256,256]{2,1,0:T(8,128)}, f32[4,128,128]{2,1,0:T(8,128)}, f32[4,128,128]{2,1,0:T(8,128)}) custom-call(s32[2]{0:T(128)} %pad_add_fusion.refs_0_.place, bf16[128,512]{1,0:T(8,128)(2,1)} %q_ref.1, ...), custom_call_target="tpu_custom_call", output_to_operand_aliasing={{1}: (5, {}), {2}: (6, {}), {3}: (7, {}), {4}: (8, {})} | custom-call | flops 1048576 | bytes 65536 | tf_op jit(solution)/shard_map/pallas_call | solution.py:172
  28.4 4.9 %collective-permute-start.3 = (bf16[2,128,256]{2,1,0:T(8,128)(2,1)S(1)}, bf16[2,128,256]{2,1,0:T(8,128)(2,1)S(1)}, u32[]{:S(2)}, u32[]{:S(2)}) collective-permute-start(bf16[2,128,256]{2,1,0:T(8,128)(2,1)S(1)} %pad_maximum_fusion.1), channel_id=1, source_target_pairs={{0,32},{8,40},{16,48},{24,56},{32,64},{40,72},{48,80},{56,88},{64,... | collective-permute-start | bytes 393224 | tf_op jit(solution)/shard_map/ppermute | solution.py:21
  33.3 3.6 %collective-permute-start.2 = (bf16[2,128,256]{2,1,0:T(8,128)(2,1)S(1)}, bf16[2,128,256]{2,1,0:T(8,128)(2,1)S(1)}, u32[]{:S(2)}, u32[]{:S(2)}) collective-permute-start(bf16[2,128,256]{2,1,0:T(8,128)(2,1)S(1)} %pad_maximum_fusion.1), channel_id=1, source_target_pairs={{0,16},{8,24},{16,32},{24,40},{32,48},{40,56},{48,64},{56,72},{64,... | collective-permute-start | bytes 393224 | tf_op jit(solution)/shard_map/ppermute | solution.py:21
  38.0 4.2 %all-to-all-start = ((bf16[8,128,512]{2,1,0:T(8,128)(2,1)}), bf16[8,128,512]{2,1,0:T(8,128)(2,1)S(1)}, u32[]{:S(2)}, u32[]{:S(2)}) async-start(bf16[8,128,512]{2,1,0:T(8,128)(2,1)} %broadcast_in_dim.2), calls=%async_computation | async-start | bytes 2097152 | tf_op jit(solution)/shard_map/all_to_all | solution.py:486
  42.3 3.3 %collective-permute-done.2 = bf16[2,128,256]{2,1,0:T(8,128)(2,1)S(1)} collective-permute-done((bf16[2,128,256]{2,1,0:T(8,128)(2,1)S(1)}, bf16[2,128,256]{2,1,0:T(8,128)(2,1)S(1)}, u32[]{:S(2)}, u32[]{:S(2)}) %collective-permute-start.2) | collective-permute-done | bytes 131104 | tf_op jit(solution)/shard_map/ppermute | solution.py:21
  45.8 7.9 %collective-permute-start.4 = (bf16[2,128,256]{2,1,0:T(8,128)(2,1)S(1)}, bf16[2,128,256]{2,1,0:T(8,128)(2,1)S(1)}, u32[]{:S(2)}, u32[]{:S(2)}) collective-permute-start(bf16[2,128,256]{2,1,0:T(8,128)(2,1)S(1)} %pad_maximum_fusion.2), channel_id=1, source_target_pairs={{0,32},{8,40},{16,48},{24,56},{32,64},{40,72},{48,80},{56,88},{64,... | collective-permute-start | bytes 393224 | tf_op jit(solution)/shard_map/ppermute | solution.py:21
  53.8 8.6 %collective-permute-done.4 = bf16[2,128,256]{2,1,0:T(8,128)(2,1)S(1)} collective-permute-done((bf16[2,128,256]{2,1,0:T(8,128)(2,1)S(1)}, bf16[2,128,256]{2,1,0:T(8,128)(2,1)S(1)}, u32[]{:S(2)}, u32[]{:S(2)}) %collective-permute-start.4) | collective-permute-done | bytes 131104 | tf_op jit(solution)/shard_map/ppermute | solution.py:21
  62.7 9.3 %collective-permute-start.6 = (bf16[2,128,256]{2,1,0:T(8,128)(2,1)S(1)}, bf16[2,128,256]{2,1,0:T(8,128)(2,1)S(1)}, u32[]{:S(2)}, u32[]{:S(2)}) collective-permute-start(bf16[2,128,256]{2,1,0:T(8,128)(2,1)S(1)} %pad_maximum_fusion.3), channel_id=1, source_target_pairs={{0,128},{8,136},{16,144},{24,152},{32,160},{40,168},{48,176},{56,1... | collective-permute-start | bytes 393224 | tf_op jit(solution)/shard_map/ppermute | solution.py:21
  72.1 1.7 collective-permute-start.7
  73.8 1.6 collective-permute-start.5
  75.3 2.0 %collective-permute-done.7 = bf16[2,128,128]{2,1,0:T(8,128)(2,1)S(1)} collective-permute-done((bf16[2,128,128]{2,1,0:T(8,128)(2,1)S(1)}, bf16[2,128,128]{2,1,0:T(8,128)(2,1)S(1)}, u32[]{:S(2)}, u32[]{:S(2)}) %collective-permute-start.7) | collective-permute-done | bytes 65568 | tf_op jit(solution)/shard_map/ppermute | solution.py:21
  77.5 2.7 %collective-permute-done.5 = bf16[2,128,256]{2,1,0:T(8,128)(2,1)S(1)} collective-permute-done((bf16[2,128,256]{2,1,0:T(8,128)(2,1)S(1)}, bf16[2,128,256]{2,1,0:T(8,128)(2,1)S(1)}, u32[]{:S(2)}, u32[]{:S(2)}) %collective-permute-start.5) | collective-permute-done | bytes 131104 | tf_op jit(solution)/shard_map/ppermute | solution.py:21
  82.8 5.8 %shard_map.111 = (bf16[128,512]{1,0:T(8,128)(2,1)}, bf16[8,512,512]{2,1,0:T(8,128)(2,1)}) custom-call(s32[2]{0:T(128)} %pad_add_fusion.refs_0_.place, f32[4,128,128]{2,1,0:T(8,128)} %get-tuple-element.45.qt_ref, f32[4,128,128]{2,1,0:T(8,128)} %get-tuple-element.46.local_ref, bf16[4,128,128]{2,1,0:T(8,128)(2,1)} %pad_maximum_fusion.4.state_ref, ...), custom_call_target="tpu_custom_call" | custom-call | flops 536870912 | bytes 6291456 | tf_op jit(solution)/shard_map/pallas_call | solution.py:246
  88.7 1.6 copy-done
  90.6 3.8 %collective-permute-done.9.other_ref = bf16[8,2,128,512]{3,2,1,0:T(8,128)(2,1)S(1)} collective-permute-done((bf16[8,2,128,512]{3,2,1,0:T(8,128)(2,1)S(1)}, bf16[8,2,128,512]{3,2,1,0:T(8,128)(2,1)S(1)}, u32[]{:S(2)}, u32[]{:S(2)}) %collective-permute-start.9) | collective-permute-done | bytes 2097184 | tf_op jit(solution)/shard_map/ppermute | solution.py:26
  94.4 1.4 copy-done.1
  95.8 5.6 %shard_map.113 = (f32[128,512]{1,0:T(8,128)}, bf16[4,128,128]{2,1,0:T(8,128)(2,1)}) custom-call(s32[2]{0:T(128)} %pad_add_fusion.refs_0_.place, bf16[8,128,512]{2,1,0:T(8,128)(2,1)} %copy-done.2, bf16[8,2,128,512]{3,2,1,0:T(8,128)(2,1)} %bitcast.27, bf16[8,2,128,512]{3,2,1,0:T(8,128)(2,1)} %copy-done.1, f32[4,128,128]{2,1,0:T(8,128)} %get-tuple-element.45.qt_ref), custom_call_target="tpu_custom_call" | custom-call | flops 536870912 | bytes 6291456 | tf_op jit(solution)/shard_map/pallas_call | solution.py:307
  105.6 1.3 collective-permute-start.11
  106.9 6.2 %collective-permute-done.11 = bf16[2,128,128]{2,1,0:T(8,128)(2,1)S(1)} collective-permute-done((bf16[2,128,128]{2,1,0:T(8,128)(2,1)S(1)}, bf16[2,128,128]{2,1,0:T(8,128)(2,1)S(1)}, u32[]{:S(2)}, u32[]{:S(2)}) %collective-permute-start.11) | collective-permute-done | bytes 65568 | tf_op jit(solution)/shard_map/ppermute | solution.py:21
  113.3 1.3 collective-permute-start.12
  114.8 5.7 %shard_map.112 = bf16[8,128,512]{2,1,0:T(8,128)(2,1)} custom-call(s32[2]{0:T(128)} %pad_add_fusion.refs_0_.place, bf16[128,512]{1,0:T(8,128)(2,1)} %get-tuple-element.53.heads_ref, bf16[8,2,128,512]{3,2,1,0:T(8,128)(2,1)} %bitcast.28, bf16[8,2,128,512]{3,2,1,0:T(8,128)(2,1)} %copy-done.1), custom_call_target="tpu_custom_call" | custom-call | flops 536870912 | bytes 6291456 | tf_op jit(solution)/shard_map/pallas_call | solution.py:271
  120.5 4.9 %all-to-all-start.1 = ((bf16[8,128,512]{2,1,0:T(8,128)(2,1)}), bf16[8,128,512]{2,1,0:T(8,128)(2,1)S(1)}, u32[]{:S(2)}, u32[]{:S(2)}) async-start(bf16[8,128,512]{2,1,0:T(8,128)(2,1)} %shard_map.112), calls=%async_computation.1 | async-start | bytes 2097152 | tf_op jit(solution)/shard_map/all_to_all | solution.py:500
  125.6 1.3 collective-permute-start.15
  127.4 1.3 collective-permute-start.16
  131.3 11.7 %collective-permute-done.15 = bf16[2,128,128]{2,1,0:T(8,128)(2,1)S(1)} collective-permute-done((bf16[2,128,128]{2,1,0:T(8,128)(2,1)S(1)}, bf16[2,128,128]{2,1,0:T(8,128)(2,1)S(1)}, u32[]{:S(2)}, u32[]{:S(2)}) %collective-permute-start.15) | collective-permute-done | bytes 65568 | tf_op jit(solution)/shard_map/ppermute | solution.py:21
  143.8 5.6 %collective-permute-start.17 = (bf16[2,128,128]{2,1,0:T(8,128)(2,1)S(1)}, bf16[2,128,128]{2,1,0:T(8,128)(2,1)S(1)}, u32[]{:S(2)}, u32[]{:S(2)}) collective-permute-start(bf16[2,128,128]{2,1,0:T(8,128)(2,1)S(1)} %get-tuple-element.70), channel_id=1, source_target_pairs={{0,8},{8,0},{16,24},{24,16},{32,40},{40,32},{48,56},{56,48},{64,72... | collective-permute-start | bytes 196616 | tf_op jit(solution)/shard_map/ppermute | solution.py:26
  152.4 7.0 %collective-permute-start.20 = (bf16[128,512]{1,0:T(8,128)(2,1)S(1)}, bf16[128,512]{1,0:T(8,128)(2,1)S(1)}, u32[]{:S(2)}, u32[]{:S(2)}) collective-permute-start(bf16[128,512]{1,0:T(8,128)(2,1)S(1)} %get-tuple-element.65), channel_id=1, source_target_pairs={{0,136},{8,128},{16,152},{24,144},{32,168},{40,160},{48,184},{56,1... | collective-permute-start | bytes 393224 | tf_op jit(solution)/shard_map/ppermute | solution.py:26
  159.4 6.2 %shard_map.114 = (bf16[128,512]{1,0:T(8,128)(2,1)}, bf16[128,1024]{1,0:T(8,128)(2,1)}, bf16[128,1024]{1,0:T(8,128)(2,1)}, f32[4,256]{1,0:T(4,128)}) custom-call(s32[2]{0:T(128)} %pad_add_fusion.refs_0_.place, bf16[128,512]{1,0:T(8,128)(2,1)} %q_ref.1, bf16[128,1024]{1,0:T(8,128)(2,1)} %k_ref.1, f32[4,256]{1,0:T(4,128)} %logit_ref.1, ...), custom_call_target="tpu_custom_call" | custom-call | flops 1879048192 | bytes 5242880 | tf_op jit(solution)/shard_map/pallas_call | solution.py:379
  166.5 1.7 fusion.3
  (91 shorter events, 20.6 us)
Async XLA Ops:
  7.2 73.5 %all-gather.3.cloned.1.call-start = ((), (), s32[]{:S(2)}) async-start(), calls=%async_computation.4 | async-start | bytes 2359296 | tf_op jit(solution)/shard_map/all_gather | solution.py:485
  7.2 10.6 %collective-permute-start = (bf16[128,512]{1,0:T(8,128)(2,1)}, bf16[128,512]{1,0:T(8,128)(2,1)S(1)}, u32[]{:S(2)}, u32[]{:S(2)}) collective-permute-start(bf16[128,512]{1,0:T(8,128)(2,1)} %param.10), channel_id=1, source_target_pairs={{0,128},{8,136},{16,144},{24,152},{32,160},{40,168},{48,176},{56,1... | collective-permute-start | bytes 393224 | tf_op jit(solution)/shard_map/ppermute | solution.py:26
  19.4 7.4 %collective-permute-start.1 = (bf16[2,128,256]{2,1,0:T(8,128)(2,1)}, bf16[2,128,256]{2,1,0:T(8,128)(2,1)S(1)}, u32[]{:S(2)}, u32[]{:S(2)}) collective-permute-start(bf16[2,128,256]{2,1,0:T(8,128)(2,1)} %get-tuple-element.47), channel_id=1, source_target_pairs={{0,8},{8,0},{16,24},{24,16},{32,40},{40,32},{48,56},{56,48},{64,72... | collective-permute-start | bytes 393224 | tf_op jit(solution)/shard_map/ppermute | solution.py:26
  28.4 13.8 %collective-permute-start.3 = (bf16[2,128,256]{2,1,0:T(8,128)(2,1)S(1)}, bf16[2,128,256]{2,1,0:T(8,128)(2,1)S(1)}, u32[]{:S(2)}, u32[]{:S(2)}) collective-permute-start(bf16[2,128,256]{2,1,0:T(8,128)(2,1)S(1)} %pad_maximum_fusion.1), channel_id=1, source_target_pairs={{0,32},{8,40},{16,48},{24,56},{32,64},{40,72},{48,80},{56,88},{64,... | collective-permute-start | bytes 393224 | tf_op jit(solution)/shard_map/ppermute | solution.py:21
  33.3 12.2 %collective-permute-start.2 = (bf16[2,128,256]{2,1,0:T(8,128)(2,1)S(1)}, bf16[2,128,256]{2,1,0:T(8,128)(2,1)S(1)}, u32[]{:S(2)}, u32[]{:S(2)}) collective-permute-start(bf16[2,128,256]{2,1,0:T(8,128)(2,1)S(1)} %pad_maximum_fusion.1), channel_id=1, source_target_pairs={{0,16},{8,24},{16,32},{24,40},{32,48},{40,56},{48,64},{56,72},{64,... | collective-permute-start | bytes 393224 | tf_op jit(solution)/shard_map/ppermute | solution.py:21
  38.0 24.7 %all-to-all-start = ((bf16[8,128,512]{2,1,0:T(8,128)(2,1)}), bf16[8,128,512]{2,1,0:T(8,128)(2,1)S(1)}, u32[]{:S(2)}, u32[]{:S(2)}) async-start(bf16[8,128,512]{2,1,0:T(8,128)(2,1)} %broadcast_in_dim.2), calls=%async_computation | async-start | bytes 2097152 | tf_op jit(solution)/shard_map/all_to_all | solution.py:486
  42.2 108.7 %reduce-scatter.2.cloned.1.call-start = ((), (), s32[]{:S(2)}) async-start(), calls=%async_computation.3 | async-start | bytes 4718592 | tf_op jit(solution)/shard_map/reduce_scatter | solution.py:494
  45.6 43.0 %copy-start.5 = (bf16[2,128,256]{2,1,0:T(8,128)(2,1)}, bf16[2,128,256]{2,1,0:T(8,128)(2,1)S(1)}, u32[]{:S(2)}) copy-start(bf16[2,128,256]{2,1,0:T(8,128)(2,1)S(1)} %collective-permute-done.2) | copy-start | bytes 393220
  45.8 16.6 %collective-permute-start.4 = (bf16[2,128,256]{2,1,0:T(8,128)(2,1)S(1)}, bf16[2,128,256]{2,1,0:T(8,128)(2,1)S(1)}, u32[]{:S(2)}, u32[]{:S(2)}) collective-permute-start(bf16[2,128,256]{2,1,0:T(8,128)(2,1)S(1)} %pad_maximum_fusion.2), channel_id=1, source_target_pairs={{0,32},{8,40},{16,48},{24,56},{32,64},{40,72},{48,80},{56,88},{64,... | collective-permute-start | bytes 393224 | tf_op jit(solution)/shard_map/ppermute | solution.py:21
  62.6 26.0 %copy-start.3 = (f32[2,128,256]{2,1,0:T(8,128)}, f32[2,128,256]{2,1,0:T(8,128)S(1)}, u32[]{:S(2)}) copy-start(f32[2,128,256]{2,1,0:T(8,128)S(1)} %fusion.33) | copy-start | bytes 786436
  62.7 20.2 %copy-start.2 = (bf16[8,128,512]{2,1,0:T(8,128)(2,1)}, bf16[8,128,512]{2,1,0:T(8,128)(2,1)S(1)}, u32[]{:S(2)}) copy-start(bf16[8,128,512]{2,1,0:T(8,128)(2,1)S(1)} %all-to-all-done.grad_ref) | copy-start | bytes 3145732
  62.7 14.6 %collective-permute-start.6 = (bf16[2,128,256]{2,1,0:T(8,128)(2,1)S(1)}, bf16[2,128,256]{2,1,0:T(8,128)(2,1)S(1)}, u32[]{:S(2)}, u32[]{:S(2)}) collective-permute-start(bf16[2,128,256]{2,1,0:T(8,128)(2,1)S(1)} %pad_maximum_fusion.3), channel_id=1, source_target_pairs={{0,128},{8,136},{16,144},{24,152},{32,160},{40,168},{48,176},{56,1... | collective-permute-start | bytes 393224 | tf_op jit(solution)/shard_map/ppermute | solution.py:21
  72.1 5.3 %collective-permute-start.7 = (bf16[2,128,128]{2,1,0:T(8,128)(2,1)S(1)}, bf16[2,128,128]{2,1,0:T(8,128)(2,1)S(1)}, u32[]{:S(2)}, u32[]{:S(2)}) collective-permute-start(bf16[2,128,128]{2,1,0:T(8,128)(2,1)S(1)} %fusion.32), channel_id=1, source_target_pairs={{0,192},{8,200},{16,208},{24,216},{32,224},{40,232},{48,240},{56,2... | collective-permute-start | bytes 196616 | tf_op jit(solution)/shard_map/ppermute | solution.py:21
  73.8 6.4 %collective-permute-start.5 = (bf16[2,128,256]{2,1,0:T(8,128)(2,1)S(1)}, bf16[2,128,256]{2,1,0:T(8,128)(2,1)S(1)}, u32[]{:S(2)}, u32[]{:S(2)}) collective-permute-start(bf16[2,128,256]{2,1,0:T(8,128)(2,1)S(1)} %pad_maximum_fusion.3), channel_id=1, source_target_pairs={{0,64},{8,72},{16,80},{24,88},{32,96},{40,104},{48,112},{56,120},{... | collective-permute-start | bytes 393224 | tf_op jit(solution)/shard_map/ppermute | solution.py:21
  80.7 1.5 collective-permute-start.8
  90.2 24.4 %copy-start.4 = (f32[2,128,256]{2,1,0:T(8,128)S(1)}, f32[2,128,256]{2,1,0:T(8,128)}, u32[]{:S(2)}) copy-start(f32[2,128,256]{2,1,0:T(8,128)} %copy-done.3) | copy-start | bytes 786436
  90.2 24.4 %copy-start.14 = (bf16[2,128,256]{2,1,0:T(8,128)(2,1)S(1)}, bf16[2,128,256]{2,1,0:T(8,128)(2,1)}, u32[]{:S(2)}) copy-start(bf16[2,128,256]{2,1,0:T(8,128)(2,1)} %copy-done.13) | copy-start | bytes 393220
  90.2 4.2 %collective-permute-start.9 = (bf16[8,2,128,512]{3,2,1,0:T(8,128)(2,1)S(1)}, bf16[8,2,128,512]{3,2,1,0:T(8,128)(2,1)S(1)}, u32[]{:S(2)}, u32[]{:S(2)}) collective-permute-start(bf16[8,2,128,512]{3,2,1,0:T(8,128)(2,1)S(1)} %bitcast.29), channel_id=1, source_target_pairs={{0,8},{8,0},{16,24},{24,16},{32,40},{40,32},{48,56},{56,48},{64,72... | collective-permute-start | bytes 6291464 | tf_op jit(solution)/shard_map/ppermute | solution.py:26
  102.2 1.3 collective-permute-start.10
  105.6 7.5 %collective-permute-start.11 = (bf16[2,128,128]{2,1,0:T(8,128)(2,1)S(1)}, bf16[2,128,128]{2,1,0:T(8,128)(2,1)S(1)}, u32[]{:S(2)}, u32[]{:S(2)}) collective-permute-start(bf16[2,128,128]{2,1,0:T(8,128)(2,1)S(1)} %convolution_convert_fusion.6), channel_id=1, source_target_pairs={{16,0},{24,8},{32,16},{40,24},{48,32},{56,40},{64,48},{72,56},{80,... | collective-permute-start | bytes 196616 | tf_op jit(solution)/shard_map/ppermute | solution.py:21
  113.3 12.0 %collective-permute-start.12 = (bf16[2,128,128]{2,1,0:T(8,128)(2,1)S(1)}, bf16[2,128,128]{2,1,0:T(8,128)(2,1)S(1)}, u32[]{:S(2)}, u32[]{:S(2)}) collective-permute-start(bf16[2,128,128]{2,1,0:T(8,128)(2,1)S(1)} %convolution_convert_fusion.5), channel_id=1, source_target_pairs={{32,0},{40,8},{48,16},{56,24},{64,32},{72,40},{80,48},{88,56},{96,... | collective-permute-start | bytes 196616 | tf_op jit(solution)/shard_map/ppermute | solution.py:21
  120.5 23.1 %copy-start.8 = (bf16[2,128,256]{2,1,0:T(8,128)(2,1)S(1)}, bf16[2,128,256]{2,1,0:T(8,128)(2,1)}, u32[]{:S(2)}) copy-start(bf16[2,128,256]{2,1,0:T(8,128)(2,1)} %copy-done.7) | copy-start | bytes 393220
  120.5 23.1 %copy-start.9 = (bf16[4,128,128]{2,1,0:T(8,128)(2,1)S(1)}, bf16[4,128,128]{2,1,0:T(8,128)(2,1)}, u32[]{:S(2)}) copy-start(bf16[4,128,128]{2,1,0:T(8,128)(2,1)} %get-tuple-element.57) | copy-start | bytes 393220
  120.5 45.2 %all-to-all-start.1 = ((bf16[8,128,512]{2,1,0:T(8,128)(2,1)}), bf16[8,128,512]{2,1,0:T(8,128)(2,1)S(1)}, u32[]{:S(2)}, u32[]{:S(2)}) async-start(bf16[8,128,512]{2,1,0:T(8,128)(2,1)} %shard_map.112), calls=%async_computation.1 | async-start | bytes 2097152 | tf_op jit(solution)/shard_map/all_to_all | solution.py:500
  125.6 17.5 %collective-permute-start.15 = (bf16[2,128,128]{2,1,0:T(8,128)(2,1)S(1)}, bf16[2,128,128]{2,1,0:T(8,128)(2,1)S(1)}, u32[]{:S(2)}, u32[]{:S(2)}) collective-permute-start(bf16[2,128,128]{2,1,0:T(8,128)(2,1)S(1)} %convolution_convert_fusion.2), channel_id=1, source_target_pairs={{144,0},{152,8},{160,16},{168,24},{176,32},{184,40},{192,48},{200,... | collective-permute-start | bytes 196616 | tf_op jit(solution)/shard_map/ppermute | solution.py:21
  127.4 16.1 %collective-permute-start.16 = (bf16[2,128,128]{2,1,0:T(8,128)(2,1)S(1)}, bf16[2,128,128]{2,1,0:T(8,128)(2,1)S(1)}, u32[]{:S(2)}, u32[]{:S(2)}) collective-permute-start(bf16[2,128,128]{2,1,0:T(8,128)(2,1)S(1)} %convolution_convert_fusion), channel_id=1, source_target_pairs={{208,0},{216,8},{224,16},{232,24},{240,32},{248,40},{209,1},{217,9... | collective-permute-start | bytes 196616 | tf_op jit(solution)/shard_map/ppermute | solution.py:21
  128.7 14.8 %collective-permute-start.14 = (bf16[2,128,128]{2,1,0:T(8,128)(2,1)S(1)}, bf16[2,128,128]{2,1,0:T(8,128)(2,1)S(1)}, u32[]{:S(2)}, u32[]{:S(2)}) collective-permute-start(bf16[2,128,128]{2,1,0:T(8,128)(2,1)S(1)} %convolution_convert_fusion.4), channel_id=1, source_target_pairs={{80,0},{88,8},{96,16},{104,24},{112,32},{120,40},{128,48},{136,56}... | collective-permute-start | bytes 196616 | tf_op jit(solution)/shard_map/ppermute | solution.py:21
  130.0 13.5 %collective-permute-start.13 = (bf16[2,128,128]{2,1,0:T(8,128)(2,1)S(1)}, bf16[2,128,128]{2,1,0:T(8,128)(2,1)S(1)}, u32[]{:S(2)}, u32[]{:S(2)}) collective-permute-start(bf16[2,128,128]{2,1,0:T(8,128)(2,1)S(1)} %add_convert_fusion.2), channel_id=1, source_target_pairs={{16,0},{24,8},{32,16},{40,24},{48,32},{56,40},{64,48},{72,56},{80,... | collective-permute-start | bytes 196616 | tf_op jit(solution)/shard_map/ppermute | solution.py:21
  143.8 6.5 %collective-permute-start.17 = (bf16[2,128,128]{2,1,0:T(8,128)(2,1)S(1)}, bf16[2,128,128]{2,1,0:T(8,128)(2,1)S(1)}, u32[]{:S(2)}, u32[]{:S(2)}) collective-permute-start(bf16[2,128,128]{2,1,0:T(8,128)(2,1)S(1)} %get-tuple-element.70), channel_id=1, source_target_pairs={{0,8},{8,0},{16,24},{24,16},{32,40},{40,32},{48,56},{56,48},{64,72... | collective-permute-start | bytes 196616 | tf_op jit(solution)/shard_map/ppermute | solution.py:26
  152.0 14.5 %collective-permute-start.18 = (bf16[128,512]{1,0:T(8,128)(2,1)S(1)}, bf16[128,512]{1,0:T(8,128)(2,1)S(1)}, u32[]{:S(2)}, u32[]{:S(2)}) collective-permute-start(bf16[128,512]{1,0:T(8,128)(2,1)S(1)} %get-tuple-element.64), channel_id=1, source_target_pairs={{0,8},{8,0},{16,24},{24,16},{32,40},{40,32},{48,56},{56,48},{64,72... | collective-permute-start | bytes 393224 | tf_op jit(solution)/shard_map/ppermute | solution.py:26
  152.4 14.0 %collective-permute-start.20 = (bf16[128,512]{1,0:T(8,128)(2,1)S(1)}, bf16[128,512]{1,0:T(8,128)(2,1)S(1)}, u32[]{:S(2)}, u32[]{:S(2)}) collective-permute-start(bf16[128,512]{1,0:T(8,128)(2,1)S(1)} %get-tuple-element.65), channel_id=1, source_target_pairs={{0,136},{8,128},{16,152},{24,144},{32,168},{40,160},{48,184},{56,1... | collective-permute-start | bytes 393224 | tf_op jit(solution)/shard_map/ppermute | solution.py:26
  159.4 7.1 %collective-permute-start.19 = (bf16[128,512]{1,0:T(8,128)(2,1)S(1)}, bf16[128,512]{1,0:T(8,128)(2,1)S(1)}, u32[]{:S(2)}, u32[]{:S(2)}) collective-permute-start(bf16[128,512]{1,0:T(8,128)(2,1)S(1)} %get-tuple-element.66), channel_id=1, source_target_pairs={{0,128},{8,136},{16,144},{24,152},{32,160},{40,168},{48,176},{56,1... | collective-permute-start | bytes 393224 | tf_op jit(solution)/shard_map/ppermute | solution.py:26
  (8 other events, 61.6 us)
Sparse Core Ops, SparseCore 0:
  19.5 51.3 all-gather.2
  88.8 59.9 reduce-scatter.1

commit v4 on v3

--- a/solution.py
+++ b/solution.py
@@ -11,7 +11,7 @@
 F32 = jnp.float32
 BF16 = jnp.bfloat16
 WIDTH = 128
-VMEM = 56 << 20
+VMEM = 62 << 20
 PAIRS = 2 * WIDTH
 
 
@@ -205,114 +205,155 @@
 
 
 STEPS = 4
-BLOCKS = [(z, core, row) for z in range(2) for core in range(2) for row in range(2)]
-
-
-def grad_block(place, step, z, core, row):
-    column = pl.multiple_of(z * 256 + (core ^ place[0]) * 128, 128)
-    return (row ^ place[1]) * 4 + step, slice(None), pl.ds(column, 128)
-
-
-def weight_rows(mine_ref, other_ref):
-    return jnp.concatenate([(mine_ref, other_ref)[core][z, row] for z, core, row in BLOCKS], axis=0)
+BLOCKS = [(z, row) for z in range(2) for row in range(2)]
+
+
+def grad_rows(place, step, own_ref, other_ref):
+    def block(ref, z, row):
+        column = pl.multiple_of(z * 256 + place[0] * 128, 128)
+        return ref[(row ^ place[1]) * 4 + step, :, pl.ds(column, 128)]
+
+    rows = [
+        jnp.concatenate([block(ref, *place_of) for place_of in BLOCKS], axis=1)
+        for ref in (own_ref, other_ref)
+    ]
+    return jnp.concatenate(rows, axis=0)
+
+
+def weight_rows(ref):
+    return jnp.concatenate([ref[z, row] for z, row in BLOCKS], axis=0)
 
 
 def weight_tile():
     return pl.BlockSpec((2, 2, WIDTH, 512), lambda step, place: (step, 0, 0, 0))
 
 
-def outputs_kernel(place, qt_ref, local_ref, state_ref, grad_ref, heads_ref, out_ref, held):
-    step = pl.program_id(0)
-
-    @pl.when(step == 0)
-    def _():
-        for head in range(4):
-            result = dot(qt_ref[head], state_ref[slot(head, place)]) + local_ref[head]
-            held[:, head * WIDTH : (head + 1) * WIDTH] = result.astype(BF16)
-        heads_ref[...] = held[...]
-
+def heads_kernel(place, qt_ref, local_ref, state_ref, heads_ref):
+    for head in range(4):
+        result = dot(qt_ref[head], state_ref[slot(head, place)]) + local_ref[head]
+        heads_ref[:, head * WIDTH : (head + 1) * WIDTH] = result.astype(BF16)
+
+
+def head_outputs(place, qt, local, state):
+    square = whole(4, WIDTH, WIDTH)
+    return call(
+        heads_kernel,
+        1,
+        [square, square, square],
+        whole(WIDTH, 512),
+        arr(BF16, WIDTH, 512),
+        2 * 4 * 128**3,
+        1 << 20,
+    )(place, qt, local, state)
+
+
+def weight_terms_kernel(place, own_ref, other_ref, heads_ref, heads_other_ref, out_ref):
+    product = lax.dot_general(
+        grad_rows(place, pl.program_id(0), own_ref, other_ref),
+        jnp.concatenate([heads_ref[...], heads_other_ref[...]], axis=0),
+        (((0,), (0,)), ((), ())),
+        preferred_element_type=F32,
+    )
+    product = (product * (1.0 / 64.0)).astype(BF16)
     for z in range(2):
-        rows = [grad_ref[grad_block(place, step, *block)] for block in BLOCKS[4 * z : 4 * z + 4]]
-        product = lax.dot_general(
-            jnp.concatenate(rows, axis=1),
-            held[...],
-            (((0,), (0,)), ((), ())),
-            preferred_element_type=F32,
-        )
-        out_ref[z] = (product * (1.0 / 64.0)).astype(BF16)
-
-
-def outputs(place, qt, local, state, grad_full):
+        out_ref[z] = product[z * 256 : z * 256 + 256]
+
+
+def weight_terms(place, grad_full, grad_other, heads, heads_other):
     return call(
-        outputs_kernel,
+        weight_terms_kernel,
         STEPS,
-        [whole(4, WIDTH, WIDTH), whole(4, WIDTH, WIDTH), whole(4, WIDTH, WIDTH), whole(8, WIDTH, 512)],
-        [whole(WIDTH, 512), pl.BlockSpec((2, 512, 512), lambda step, place: (step, 0, 0))],
-        [arr(BF16, WIDTH, 512), arr(BF16, 8, 512, 512)],
+        [whole(8, WIDTH, 512), whole(8, WIDTH, 512), whole(WIDTH, 512), whole(WIDTH, 512)],
+        pl.BlockSpec((2, 256, 512), lambda step, place: (step, 0, 0)),
+        arr(BF16, 8, 256, 512),
         2 * 128 * 512 * 4096,
-        6 << 20,
-        [pltpu.VMEM((WIDTH, 512), BF16)],
-    )(place, qt, local, state, grad_full)
-
-
-def mixed_kernel(place, heads_ref, mine_ref, other_ref, out_ref):
+        5 << 20,
+    )(place, grad_full, grad_other, heads, heads_other)
+
+
+def mixed_kernel(place, heads_ref, heads_other_ref, weight_ref, out_ref):
     step = pl.program_id(0)
     product = lax.dot_general(
-        heads_ref[...],
-        weight_rows(mine_ref, other_ref),
+        jnp.concatenate([heads_ref[...], heads_other_ref[...]], axis=0),
+        weight_rows(weight_ref),
         (((1,), (1,)), ((), ())),
         preferred_element_type=F32,
     ).astype(BF16)
-    for i, block in enumerate(BLOCKS):
-        out_ref[grad_block(place, step, *block)] = product[:, i * WIDTH : (i + 1) * WIDTH]
-
-
-def mixed_parts(place, heads, mine, other):
+    for i, (z, row) in enumerate(BLOCKS):
+        owner = (row ^ place[1]) * 4 + step
+        out_ref[owner, :, z * 128 : z * 128 + 128] = product[:, i * WIDTH : (i + 1) * WIDTH]
+
+
+def mixed_parts(place, heads, heads_other, weight):
     return call(
         mixed_kernel,
         STEPS,
-        [whole(WIDTH, 512), weight_tile(), weight_tile()],
-        whole(8, WIDTH, 512),
-        arr(BF16, 8, WIDTH, 512),
+        [whole(WIDTH, 512), whole(WIDTH, 512), weight_tile()],
+        whole(8, 256, 256),
+        arr(BF16, 8, 256, 256),
         2 * 128 * 512 * 4096,
-        6 << 20,
-    )(place, heads, mine, other)
-
-
-def head_grad_kernel(place, grad_ref, mine_ref, other_ref, qt_ref, out_ref, own_ref):
+        3 << 20,
+    )(place, heads, heads_other, weight)
+
+
+def head_grad_kernel(place, own_ref, other_ref, weight_ref, kept_ref, given_ref):
     step = pl.program_id(0)
-    blocks = [grad_ref[grad_block(place, step, *block)] for block in BLOCKS]
     total = jnp.dot(
-        jnp.concatenate(blocks, axis=1),
-        weight_rows(mine_ref, other_ref),
+        grad_rows(place, step, own_ref, other_ref),
+        weight_rows(weight_ref),
         preferred_element_type=F32,
     )
 
     @pl.when(step == 0)
     def _():
-        out_ref[...] = total
+        kept_ref[...] = total[:WIDTH]
+        given_ref[...] = total[WIDTH:]
 
     @pl.when(step > 0)
     def _():
-        out_ref[...] += total
-
-    @pl.when(step == STEPS - 1)
-    def _():
-        for head in range(4):
-            grad = out_ref[:, head * WIDTH : (head + 1) * WIDTH]
-            own_ref[slot(head, place)] = dot(qt_ref[head], grad, 0, 0).astype(BF16)
-
-
-def head_gradient(place, grad_full, mine, other, qt):
+        kept_ref[...] += total[:WIDTH]
+        given_ref[...] += total[WIDTH:]
+
+
+def head_gradient(place, grad_full, grad_other, weight):
+    part = arr(F32, WIDTH, 512)
     return call(
         head_grad_kernel,
         STEPS,
-        [whole(8, WIDTH, 512), weight_tile(), weight_tile(), whole(4, WIDTH, WIDTH)],
-        [whole(WIDTH, 512), whole(4, WIDTH, WIDTH)],
-        [arr(F32, WIDTH, 512), arr(BF16, 4, WIDTH, WIDTH)],
+        [whole(8, WIDTH, 512), whole(8, WIDTH, 512), weight_tile()],
+        [whole(WIDTH, 512), whole(WIDTH, 512)],
+        [part, part],
         2 * 128 * 512 * 4096,
-        6 << 20,
-    )(place, grad_full, mine, other, qt)
+        5 << 20,
+    )(place, grad_full, grad_other, weight)
+
+
+def own_kernel(place, kept_ref, came_ref, qt_ref, grad_ref, mine_ref, theirs_ref):
+    grad_ref[...] = kept_ref[...] + came_ref[...]
+    for head in range(4):
+        grad = grad_ref[:, head * WIDTH : (head + 1) * WIDTH]
+        own = dot(qt_ref[head], grad, 0, 0).astype(BF16)
+
+        @pl.when(place[0] == head // 2)
+        def _():
+            mine_ref[head % 2] = own
+
+        @pl.when(place[0] != head // 2)
+        def _():
+            theirs_ref[head % 2] = own
+
+
+def own_cotangent(place, kept, came, qt):
+    pair = arr(BF16, 2, WIDTH, WIDTH)
+    return call(
+        own_kernel,
+        1,
+        [whole(WIDTH, 512), whole(WIDTH, 512), whole(4, WIDTH, WIDTH)],
+        [whole(WIDTH, 512), whole(2, WIDTH, WIDTH), whole(2, WIDTH, WIDTH)],
+        [arr(F32, WIDTH, 512), pair, pair],
+        2 * 4 * 128**3,
+        1 << 20,
+    )(place, kept, came, qt)
 
 
 def pull_kernel(
@@ -450,14 +491,16 @@
     return grad_full, gate, state_in, (even_a, odd_a, window1, window2, window4, window8, window12)
 
 
-def backward_states(own, core, saved):
+def backward_states(mine, theirs, core, saved, gate):
     even_a, odd_a, window1, window2, window4, window8, window12 = saved
-    mine, theirs = own[:2], exchange(own[2:], 1)
+    theirs = exchange(theirs, 1)
     even = jnp.where(core == 0, mine, theirs)
     odd = jnp.where(core == 0, theirs, mine)
     total = even.astype(F32) + mul_t(even_a, odd)
     for window, distance in ((window1, 2), (window2, 4)):
         passed = mul_t(window, total.astype(BF16)).astype(BF16)
+        if distance == 4:
+            gate, passed = lax.optimization_barrier((gate, passed))
         total = total + send(passed, -distance).astype(F32)
     rounded = total.astype(BF16)
     second = send(rounded, -2).astype(F32)
@@ -467,7 +510,7 @@
     first = (odd.astype(F32) + mul_t(odd_a, second)).astype(BF16)
     kept = jnp.where(core == 0, first, second)
     given = jnp.where(core == 0, second, first)
-    return jnp.concatenate([kept, exchange(given, 1)], axis=0)
+    return gate, jnp.concatenate([kept, exchange(given, 1)], axis=0)
 
 
 def local(queries, keys, values, beta_logit, out_weight, out_grad):
@@ -489,20 +532,25 @@
     grad_full, weight_mine, state, saved = forward_states(
         mine, theirs, core, grad_full, weight_mine
     )
-    weight_other = exchange(weight_mine, 1)
-    heads, part = outputs(place, qt, local_out, state, grad_full)
+    grad_other = exchange(grad_full, 1)
+    heads = head_outputs(place, qt, local_out, state)
+    heads_other = exchange(heads, 1)
+    terms = weight_terms(place, grad_full, grad_other, heads, heads_other)
     ring_sum = lax.psum_scatter(
-        part, "ctx", scatter_dimension=0, axis_index_groups=rings
-    ).reshape(2, 2, WIDTH, 512)
-    weight_grad = ring_sum[0, 0].astype(F32) + exchange(ring_sum[1, 0], 1).astype(F32)
-    weight_grad += exchange(ring_sum[0, 1], 16).astype(F32)
-    weight_grad += exchange(ring_sum[1, 1], 17).astype(F32)
-    mixed = lax.all_to_all(
-        mixed_parts(place, heads, weight_mine, weight_other), "tp", 0, 0, tiled=True
-    )
-    mixed = jnp.sum(mixed.astype(F32), axis=0).astype(BF16)
-    head_grad, own = head_gradient(place, grad_full, weight_mine, weight_other, qt)
-    end = backward_states(own, core, saved)
+        terms, "ctx", scatter_dimension=0, axis_index_groups=rings
+    ).reshape(2, WIDTH, 512)
+    weight_grad = ring_sum[0].astype(F32) + exchange(ring_sum[1], 16).astype(F32)
+    kept, given = head_gradient(place, grad_full, grad_other, weight_mine)
+    head_grad, own, own_theirs = own_cotangent(place, kept, exchange(given, 1), qt)
+    parts = mixed_parts(place, heads, heads_other, weight_mine)
+    parts, end = backward_states(own, own_theirs, core, saved, parts)
+    parts = lax.all_to_all(parts, "tp", 0, 0, tiled=True)
+    sums = jnp.sum(parts.astype(F32), axis=0).astype(BF16)
+    kept, came = sums[:WIDTH], exchange(sums[WIDTH:], 1)
+    first, second = jnp.where(core == 0, kept, came), jnp.where(core == 0, came, kept)
+    mixed = jnp.concatenate(
+        [first[:, :WIDTH], second[:, :WIDTH], first[:, WIDTH:], second[:, WIDTH:]], axis=1
+    )
     query_grad, key_grad, value_grad, logit_grad = pull(
         place, queries, keys, beta_logit, reads, wy, state, end, head_grad
     )

time: 176 us -> 172 us (0.977)
  waiting for transfers between devices: 41.6 us -> 37 us
  Pallas kernels: 35.9 us -> 40.1 us
  local copies, waits for them, and re-layouts: 6.4 us -> 3.96 us
  starting transfers between devices: 64.9 us -> 63 us
    ppermute x12, waiting for transfers between devices: 35 us -> 28.3 us  [send(): return lax.ppermute(block, 'ctx', route)]
    pallas_call x3 -> x5, Pallas kernels: 17 us -> 21.2 us  [the longest x1 5.32 us: head_gradient(): call(head_grad_kernel, STEPS, [whole(8, WIDTH, 512), whole(8, WIDTH, 512)...]
    ppermute x9 -> x10, waiting for transfers between devices: 6.54 us -> 8.72 us  [exchange(): return lax.ppermute(block, 'ctx', route)]
    ppermute x9 -> x10, starting transfers between devices: 19 us -> 17.1 us  [exchange(): return lax.ppermute(block, 'ctx', route)]
  transfers between devices with their start and end apart: 25 -> 26, of which waited for: 11 -> 13; matrix products, arithmetic and copies ran while one was open for 6% -> 5% of each run, Pallas kernels for 17% -> 21%
where the time goes in v4:
time: 172 us; the launch traced here: 169 us
  starting transfers between devices  63 us (37%)
  Pallas kernels  40.1 us (23%)
  waiting for transfers between devices  37 us (22%)
  between operations  14.5 us (8%)
  other arithmetic  7.09 us (4%)
  local copies, waits for them, and re-layouts  3.96 us (2%)
  matrix products  3.71 us (2%)
    ppermute x12, starting transfers between devices, send(): return lax.ppermute(block, 'ctx', route)  36.8 us
    ppermute x12, waiting for transfers between devices, send(): return lax.ppermute(block, 'ctx', route)  28.3 us
    ppermute x10, starting transfers between devices, exchange(): return lax.ppermute(block, 'ctx', route)  17.1 us
    pallas_call x2, Pallas kernels, prepare(): pl.pallas_call(functools.partial(prepare_kernel, mine), grid_spec=pltpu.P...  12.7 us
    ppermute x10, waiting for transfers between devices, exchange(): return lax.ppermute(block, 'ctx', route)  8.72 us
    pallas_call x1, Pallas kernels, pull(): call(pull_kernel, 2, [by_columns(WIDTH), by_columns(PAIRS), whole(4, PAIR...  6.15 us
    pallas_call x1, Pallas kernels, head_gradient(): call(head_grad_kernel, STEPS, [whole(8, WIDTH, 512), whole(8, WIDTH, 512)...  5.32 us
    pallas_call x1, Pallas kernels, mixed_parts(): call(mixed_kernel, STEPS, [whole(WIDTH, 512), whole(WIDTH, 512), weight_t...  4.96 us
  transfers between devices with their start and end apart: 26, of which 13 were waited for; matrix products, arithmetic and copies ran while one was open for 5% of the time, Pallas kernels for 21%

profile of v4, /device:TPU:1, one launch (start us, length us, event | category | flops | bytes accessed | tf_op | source)
XLA Modules:
  0.0 169.3 jit_solution(4798915251102627533)
XLA Ops:
  7.2 3.7 %collective-permute-start = (bf16[128,512]{1,0:T(8,128)(2,1)}, bf16[128,512]{1,0:T(8,128)(2,1)S(1)}, u32[]{:S(2)}, u32[]{:S(2)}) collective-permute-start(bf16[128,512]{1,0:T(8,128)(2,1)} %param.10), channel_id=1, source_target_pairs={{0,128},{8,136},{16,144},{24,152},{32,160},{40,168},{48,176},{56,1... | collective-permute-start | bytes 393224 | tf_op jit(solution)/shard_map/ppermute | solution.py:26
  11.4 6.3 %shard_map.109 = (bf16[2,128,256]{2,1,0:T(8,128)(2,1)}, f32[4,256,256]{2,1,0:T(8,128)}, f32[4,256,256]{2,1,0:T(8,128)}, f32[4,128,128]{2,1,0:T(8,128)}, f32[4,128,128]{2,1,0:T(8,128)}) custom-call(s32[2]{0:T(128)} %pad_add_fusion.refs_0_.place, bf16[128,512]{1,0:T(8,128)(2,1)} %q_ref.1, bf16[128,1024]{1,0:T(8,128)(2,1)} %k_ref.1, bf16[128,1024]{1,0:T(8,128)(2,1)} %refs_3_.2, ...), custom_call_target="tpu_custom_call" | custom-call | flops 104857600 | bytes 16777216 | tf_op jit(solution)/shard_map/pallas_call | solution.py:172
  17.7 1.6 pad_maximum_fusion
  20.4 6.4 %shard_map.110 = (bf16[2,128,256]{2,1,0:T(8,128)(2,1)}, f32[4,256,256]{2,1,0:T(8,128)}, f32[4,256,256]{2,1,0:T(8,128)}, f32[4,128,128]{2,1,0:T(8,128)}, f32[4,128,128]{2,1,0:T(8,128)}) custom-call(s32[2]{0:T(128)} %pad_add_fusion.refs_0_.place, bf16[128,512]{1,0:T(8,128)(2,1)} %q_ref.1, ...), custom_call_target="tpu_custom_call", output_to_operand_aliasing={{1}: (5, {}), {2}: (6, {}), {3}: (7, {}), {4}: (8, {})} | custom-call | flops 1048576 | bytes 65536 | tf_op jit(solution)/shard_map/pallas_call | solution.py:172
  28.4 4.9 %collective-permute-start.3 = (bf16[2,128,256]{2,1,0:T(8,128)(2,1)S(1)}, bf16[2,128,256]{2,1,0:T(8,128)(2,1)S(1)}, u32[]{:S(2)}, u32[]{:S(2)}) collective-permute-start(bf16[2,128,256]{2,1,0:T(8,128)(2,1)S(1)} %pad_maximum_fusion.1), channel_id=1, source_target_pairs={{0,32},{8,40},{16,48},{24,56},{32,64},{40,72},{48,80},{56,88},{64,... | collective-permute-start | bytes 393224 | tf_op jit(solution)/shard_map/ppermute | solution.py:21
  33.3 3.6 %collective-permute-start.2 = (bf16[2,128,256]{2,1,0:T(8,128)(2,1)S(1)}, bf16[2,128,256]{2,1,0:T(8,128)(2,1)S(1)}, u32[]{:S(2)}, u32[]{:S(2)}) collective-permute-start(bf16[2,128,256]{2,1,0:T(8,128)(2,1)S(1)} %pad_maximum_fusion.1), channel_id=1, source_target_pairs={{0,16},{8,24},{16,32},{24,40},{32,48},{40,56},{48,64},{56,72},{64,... | collective-permute-start | bytes 393224 | tf_op jit(solution)/shard_map/ppermute | solution.py:21
  37.9 4.2 %all-to-all-start = ((bf16[8,128,512]{2,1,0:T(8,128)(2,1)}), bf16[8,128,512]{2,1,0:T(8,128)(2,1)S(1)}, u32[]{:S(2)}, u32[]{:S(2)}) async-start(bf16[8,128,512]{2,1,0:T(8,128)(2,1)} %broadcast_in_dim.2), calls=%async_computation | async-start | bytes 2097152 | tf_op jit(solution)/shard_map/all_to_all | solution.py:529
  42.2 3.3 %collective-permute-done.2 = bf16[2,128,256]{2,1,0:T(8,128)(2,1)S(1)} collective-permute-done((bf16[2,128,256]{2,1,0:T(8,128)(2,1)S(1)}, bf16[2,128,256]{2,1,0:T(8,128)(2,1)S(1)}, u32[]{:S(2)}, u32[]{:S(2)}) %collective-permute-start.2) | collective-permute-done | bytes 131104 | tf_op jit(solution)/shard_map/ppermute | solution.py:21
  45.8 8.0 %collective-permute-start.4 = (bf16[2,128,256]{2,1,0:T(8,128)(2,1)S(1)}, bf16[2,128,256]{2,1,0:T(8,128)(2,1)S(1)}, u32[]{:S(2)}, u32[]{:S(2)}) collective-permute-start(bf16[2,128,256]{2,1,0:T(8,128)(2,1)S(1)} %pad_maximum_fusion.2), channel_id=1, source_target_pairs={{0,32},{8,40},{16,48},{24,56},{32,64},{40,72},{48,80},{56,88},{64,... | collective-permute-start | bytes 393224 | tf_op jit(solution)/shard_map/ppermute | solution.py:21
  53.8 8.5 %collective-permute-done.4 = bf16[2,128,256]{2,1,0:T(8,128)(2,1)S(1)} collective-permute-done((bf16[2,128,256]{2,1,0:T(8,128)(2,1)S(1)}, bf16[2,128,256]{2,1,0:T(8,128)(2,1)S(1)}, u32[]{:S(2)}, u32[]{:S(2)}) %collective-permute-start.4) | collective-permute-done | bytes 131104 | tf_op jit(solution)/shard_map/ppermute | solution.py:21
  62.5 9.5 %collective-permute-start.6 = (bf16[2,128,256]{2,1,0:T(8,128)(2,1)S(1)}, bf16[2,128,256]{2,1,0:T(8,128)(2,1)S(1)}, u32[]{:S(2)}, u32[]{:S(2)}) collective-permute-start(bf16[2,128,256]{2,1,0:T(8,128)(2,1)S(1)} %pad_maximum_fusion.3), channel_id=1, source_target_pairs={{0,128},{8,136},{16,144},{24,152},{32,160},{40,168},{48,176},{56,1... | collective-permute-start | bytes 393224 | tf_op jit(solution)/shard_map/ppermute | solution.py:21
  72.1 1.5 collective-permute-start.7
  74.7 1.6 collective-permute-start.5
  76.3 1.5 collective-permute-done.7
  78.0 2.8 %collective-permute-done.5 = bf16[2,128,256]{2,1,0:T(8,128)(2,1)S(1)} collective-permute-done((bf16[2,128,256]{2,1,0:T(8,128)(2,1)S(1)}, bf16[2,128,256]{2,1,0:T(8,128)(2,1)S(1)}, u32[]{:S(2)}, u32[]{:S(2)}) %collective-permute-start.5) | collective-permute-done | bytes 131104 | tf_op jit(solution)/shard_map/ppermute | solution.py:21
  83.7 2.6 %shard_map.111.heads_ref = bf16[128,512]{1,0:T(8,128)(2,1)} custom-call(s32[2]{0:T(128)} %pad_add_fusion.refs_0_.place, f32[4,128,128]{2,1,0:T(8,128)} %get-tuple-element.48.qt_ref, f32[4,128,128]{2,1,0:T(8,128)} %get-tuple-element.49.local_ref, bf16[4,128,128]{2,1,0:T(8,128)(2,1)} %pad_maximum_fusion.4.state_ref), custom_call_target="tpu_custom_call" | custom-call | flops 16777216 | bytes 1048576 | tf_op jit(solution)/shard_map/pallas_call | solution.py:239
  88.5 4.9 %shard_map.116 = bf16[8,256,512]{2,1,0:T(8,128)(2,1)} custom-call(s32[2]{0:T(128)} %pad_add_fusion.refs_0_.place, bf16[8,128,512]{2,1,0:T(8,128)(2,1)} %copy-done, bf16[8,128,512]{2,1,0:T(8,128)(2,1)} %collective-permute-done.10.other_ref, bf16[128,512]{1,0:T(8,128)(2,1)} %shard_map.111.heads_ref, bf16[128,512]{1,0:T(8,128)(2,1)} %copy-done.1), custom_call_target="tpu_custom_call" | custom-call | flops 536870912 | bytes 5242880 | tf_op jit(solution)/shard_map/pallas_call | solution.py:263
  93.5 5.3 %shard_map.113 = (f32[128,512]{1,0:T(8,128)}, f32[128,512]{1,0:T(8,128)}) custom-call(s32[2]{0:T(128)} %pad_add_fusion.refs_0_.place, bf16[8,128,512]{2,1,0:T(8,128)(2,1)} %copy-done, bf16[8,128,512]{2,1,0:T(8,128)(2,1)} %collective-permute-done.10.other_ref, bf16[8,2,128,512]{3,2,1,0:T(8,128)(2,1)} %bitcast.22), custom_call_target="tpu_custom_call" | custom-call | flops 536870912 | bytes 5242880 | tf_op jit(solution)/shard_map/pallas_call | solution.py:320
  99.1 1.4 collective-permute-done.11.came_ref
  101.2 3.4 %shard_map.114 = (f32[128,512]{1,0:T(8,128)}, bf16[2,128,128]{2,1,0:T(8,128)(2,1)}, bf16[2,128,128]{2,1,0:T(8,128)(2,1)}) custom-call(s32[2]{0:T(128)} %pad_add_fusion.refs_0_.place, f32[128,512]{1,0:T(8,128)} %get-tuple-element.57.kept_ref, f32[128,512]{1,0:T(8,128)} %copy-done.7, f32[4,128,128]{2,1,0:T(8,128)} %get-tuple-element.48.qt_ref), custom_call_target="tpu_custom_call" | custom-call | flops 16777216 | bytes 1048576 | tf_op jit(solution)/shard_map/pallas_call | solution.py:348
  107.5 1.3 collective-permute-start.13
  108.8 5.0 %shard_map.112 = bf16[8,256,256]{2,1,0:T(8,128)(2,1)} custom-call(s32[2]{0:T(128)} %pad_add_fusion.refs_0_.place, bf16[128,512]{1,0:T(8,128)(2,1)} %shard_map.111.heads_ref, bf16[128,512]{1,0:T(8,128)(2,1)} %copy-done.1, bf16[8,2,128,512]{3,2,1,0:T(8,128)(2,1)} %bitcast.23), custom_call_target="tpu_custom_call" | custom-call | flops 536870912 | bytes 3145728 | tf_op jit(solution)/shard_map/pallas_call | solution.py:288
  115.5 4.8 %all-to-all-start.1 = ((bf16[8,256,256]{2,1,0:T(8,128)(2,1)}), bf16[8,256,256]{2,1,0:T(8,128)(2,1)S(1)}, u32[]{:S(2)}, u32[]{:S(2)}) async-start(bf16[8,256,256]{2,1,0:T(8,128)(2,1)} %shard_map.112), calls=%async_computation.1 | async-start | bytes 2097152 | tf_op jit(solution)/shard_map/all_to_all | solution.py:547
  123.6 1.3 collective-permute-start.19
  124.9 1.3 collective-permute-start.17
  126.2 1.3 collective-permute-start.16
  127.5 10.8 %collective-permute-done.18 = bf16[2,128,128]{2,1,0:T(8,128)(2,1)S(1)} collective-permute-done((bf16[2,128,128]{2,1,0:T(8,128)(2,1)S(1)}, bf16[2,128,128]{2,1,0:T(8,128)(2,1)S(1)}, u32[]{:S(2)}, u32[]{:S(2)}) %collective-permute-start.18) | collective-permute-done | bytes 65568 | tf_op jit(solution)/shard_map/ppermute | solution.py:21
  138.6 3.8 %collective-permute-start.20 = (bf16[2,128,128]{2,1,0:T(8,128)(2,1)S(1)}, bf16[2,128,128]{2,1,0:T(8,128)(2,1)S(1)}, u32[]{:S(2)}, u32[]{:S(2)}) collective-permute-start(bf16[2,128,128]{2,1,0:T(8,128)(2,1)S(1)} %get-tuple-element.75), channel_id=1, source_target_pairs={{0,8},{8,0},{16,24},{24,16},{32,40},{40,32},{48,56},{56,48},{64,72... | collective-permute-start | bytes 196616 | tf_op jit(solution)/shard_map/ppermute | solution.py:26
  144.6 6.1 %shard_map.115 = (bf16[128,512]{1,0:T(8,128)(2,1)}, bf16[128,1024]{1,0:T(8,128)(2,1)}, bf16[128,1024]{1,0:T(8,128)(2,1)}, f32[4,256]{1,0:T(4,128)}) custom-call(s32[2]{0:T(128)} %pad_add_fusion.refs_0_.place, bf16[128,512]{1,0:T(8,128)(2,1)} %q_ref.1, bf16[128,1024]{1,0:T(8,128)(2,1)} %k_ref.1, f32[4,256]{1,0:T(4,128)} %logit_ref.1, ...), custom_call_target="tpu_custom_call" | custom-call | flops 1879048192 | bytes 5242880 | tf_op jit(solution)/shard_map/pallas_call | solution.py:420
  151.7 5.3 %collective-permute-start.21 = (bf16[128,512]{1,0:T(8,128)(2,1)S(1)}, bf16[128,512]{1,0:T(8,128)(2,1)S(1)}, u32[]{:S(2)}, u32[]{:S(2)}) collective-permute-start(bf16[128,512]{1,0:T(8,128)(2,1)S(1)} %slice_bitcast_fusion), channel_id=1, source_target_pairs={{0,128},{8,136},{16,144},{24,152},{32,160},{40,168},{48,176},{56,1... | collective-permute-start | bytes 393224 | tf_op jit(solution)/shard_map/ppermute | solution.py:26
  157.7 3.1 %collective-permute-done.21 = bf16[128,512]{1,0:T(8,128)(2,1)S(1)} collective-permute-done((bf16[128,512]{1,0:T(8,128)(2,1)S(1)}, bf16[128,512]{1,0:T(8,128)(2,1)S(1)}, u32[]{:S(2)}, u32[]{:S(2)}) %collective-permute-start.21) | collective-permute-done | bytes 131104 | tf_op jit(solution)/shard_map/ppermute | solution.py:26
  160.9 1.6 convert_add_fusion
  (90 shorter events, 24.0 us)
Async XLA Ops:
  7.2 74.3 %all-gather.3.cloned.1.call-start = ((), (), s32[]{:S(2)}) async-start(), calls=%async_computation.4 | async-start | bytes 2359296 | tf_op jit(solution)/shard_map/all_gather | solution.py:528
  7.2 10.5 %collective-permute-start = (bf16[128,512]{1,0:T(8,128)(2,1)}, bf16[128,512]{1,0:T(8,128)(2,1)S(1)}, u32[]{:S(2)}, u32[]{:S(2)}) collective-permute-start(bf16[128,512]{1,0:T(8,128)(2,1)} %param.10), channel_id=1, source_target_pairs={{0,128},{8,136},{16,144},{24,152},{32,160},{40,168},{48,176},{56,1... | collective-permute-start | bytes 393224 | tf_op jit(solution)/shard_map/ppermute | solution.py:26
  19.4 7.4 %collective-permute-start.1 = (bf16[2,128,256]{2,1,0:T(8,128)(2,1)}, bf16[2,128,256]{2,1,0:T(8,128)(2,1)S(1)}, u32[]{:S(2)}, u32[]{:S(2)}) collective-permute-start(bf16[2,128,256]{2,1,0:T(8,128)(2,1)} %get-tuple-element.50), channel_id=1, source_target_pairs={{0,8},{8,0},{16,24},{24,16},{32,40},{40,32},{48,56},{56,48},{64,72... | collective-permute-start | bytes 393224 | tf_op jit(solution)/shard_map/ppermute | solution.py:26
  20.4 16.5 %copy-start.8 = (bf16[128,512]{1,0:T(8,128)(2,1)S(1)}, bf16[128,512]{1,0:T(8,128)(2,1)}, u32[]{:S(2)}) copy-start(bf16[128,512]{1,0:T(8,128)(2,1)} %param.11) | copy-start | bytes 393220
  28.4 13.8 %collective-permute-start.3 = (bf16[2,128,256]{2,1,0:T(8,128)(2,1)S(1)}, bf16[2,128,256]{2,1,0:T(8,128)(2,1)S(1)}, u32[]{:S(2)}, u32[]{:S(2)}) collective-permute-start(bf16[2,128,256]{2,1,0:T(8,128)(2,1)S(1)} %pad_maximum_fusion.1), channel_id=1, source_target_pairs={{0,32},{8,40},{16,48},{24,56},{32,64},{40,72},{48,80},{56,88},{64,... | collective-permute-start | bytes 393224 | tf_op jit(solution)/shard_map/ppermute | solution.py:21
  33.3 12.2 %collective-permute-start.2 = (bf16[2,128,256]{2,1,0:T(8,128)(2,1)S(1)}, bf16[2,128,256]{2,1,0:T(8,128)(2,1)S(1)}, u32[]{:S(2)}, u32[]{:S(2)}) collective-permute-start(bf16[2,128,256]{2,1,0:T(8,128)(2,1)S(1)} %pad_maximum_fusion.1), channel_id=1, source_target_pairs={{0,16},{8,24},{16,32},{24,40},{32,48},{40,56},{48,64},{56,72},{64,... | collective-permute-start | bytes 393224 | tf_op jit(solution)/shard_map/ppermute | solution.py:21
  37.9 24.6 %all-to-all-start = ((bf16[8,128,512]{2,1,0:T(8,128)(2,1)}), bf16[8,128,512]{2,1,0:T(8,128)(2,1)S(1)}, u32[]{:S(2)}, u32[]{:S(2)}) async-start(bf16[8,128,512]{2,1,0:T(8,128)(2,1)} %broadcast_in_dim.2), calls=%async_computation | async-start | bytes 2097152 | tf_op jit(solution)/shard_map/all_to_all | solution.py:529
  42.2 108.6 %reduce-scatter.2.cloned.1.call-start = ((), (), s32[]{:S(2)}) async-start(), calls=%async_computation.3 | async-start | bytes 2359296 | tf_op jit(solution)/shard_map/reduce_scatter | solution.py:539
  45.8 16.5 %collective-permute-start.4 = (bf16[2,128,256]{2,1,0:T(8,128)(2,1)S(1)}, bf16[2,128,256]{2,1,0:T(8,128)(2,1)S(1)}, u32[]{:S(2)}, u32[]{:S(2)}) collective-permute-start(bf16[2,128,256]{2,1,0:T(8,128)(2,1)S(1)} %pad_maximum_fusion.2), channel_id=1, source_target_pairs={{0,32},{8,40},{16,48},{24,56},{32,64},{40,72},{48,80},{56,88},{64,... | collective-permute-start | bytes 393224 | tf_op jit(solution)/shard_map/ppermute | solution.py:21
  62.5 25.4 %copy-start = (bf16[8,128,512]{2,1,0:T(8,128)(2,1)}, bf16[8,128,512]{2,1,0:T(8,128)(2,1)S(1)}, u32[]{:S(2)}) copy-start(bf16[8,128,512]{2,1,0:T(8,128)(2,1)S(1)} %all-to-all-done.own_ref) | copy-start | bytes 3145732
  62.5 15.3 %collective-permute-start.6 = (bf16[2,128,256]{2,1,0:T(8,128)(2,1)S(1)}, bf16[2,128,256]{2,1,0:T(8,128)(2,1)S(1)}, u32[]{:S(2)}, u32[]{:S(2)}) collective-permute-start(bf16[2,128,256]{2,1,0:T(8,128)(2,1)S(1)} %pad_maximum_fusion.3), channel_id=1, source_target_pairs={{0,128},{8,136},{16,144},{24,152},{32,160},{40,168},{48,176},{56,1... | collective-permute-start | bytes 393224 | tf_op jit(solution)/shard_map/ppermute | solution.py:21
  72.1 5.8 %collective-permute-start.7 = (bf16[2,128,128]{2,1,0:T(8,128)(2,1)S(1)}, bf16[2,128,128]{2,1,0:T(8,128)(2,1)S(1)}, u32[]{:S(2)}, u32[]{:S(2)}) collective-permute-start(bf16[2,128,128]{2,1,0:T(8,128)(2,1)S(1)} %fusion.30), channel_id=1, source_target_pairs={{0,192},{8,200},{16,208},{24,216},{32,224},{40,232},{48,240},{56,2... | collective-permute-start | bytes 196616 | tf_op jit(solution)/shard_map/ppermute | solution.py:21
  73.6 13.1 %collective-permute-start.10 = (bf16[8,128,512]{2,1,0:T(8,128)(2,1)S(1)}, bf16[8,128,512]{2,1,0:T(8,128)(2,1)}, u32[]{:S(2)}, u32[]{:S(2)}) collective-permute-start(bf16[8,128,512]{2,1,0:T(8,128)(2,1)S(1)} %all-to-all-done.own_ref), channel_id=1, source_target_pairs={{0,8},{8,0},{16,24},{24,16},{32,40},{40,32},{48,56},{56,48},{64,72... | collective-permute-start | bytes 3145736 | tf_op jit(solution)/shard_map/ppermute | solution.py:26
  74.7 6.0 %collective-permute-start.5 = (bf16[2,128,256]{2,1,0:T(8,128)(2,1)S(1)}, bf16[2,128,256]{2,1,0:T(8,128)(2,1)S(1)}, u32[]{:S(2)}, u32[]{:S(2)}) collective-permute-start(bf16[2,128,256]{2,1,0:T(8,128)(2,1)S(1)} %pad_maximum_fusion.3), channel_id=1, source_target_pairs={{0,64},{8,72},{16,80},{24,88},{32,96},{40,104},{48,112},{56,120},{... | collective-permute-start | bytes 393224 | tf_op jit(solution)/shard_map/ppermute | solution.py:21
  81.4 1.6 collective-permute-start.8
  86.3 1.6 collective-permute-start.9
  98.8 1.7 %collective-permute-start.11 = (f32[128,512]{1,0:T(8,128)}, f32[128,512]{1,0:T(8,128)S(1)}, u32[]{:S(2)}, u32[]{:S(2)}) collective-permute-start(f32[128,512]{1,0:T(8,128)} %get-tuple-element.58), channel_id=1, source_target_pairs={{0,8},{8,0},{16,24},{24,16},{32,40},{40,32},{48,56},{56,48},{64,72... | collective-permute-start | bytes 786440 | tf_op jit(solution)/shard_map/ppermute | solution.py:26
  104.7 1.5 collective-permute-start.12
  107.2 8.1 %copy-start.10 = (bf16[2,128,256]{2,1,0:T(8,128)(2,1)S(1)}, bf16[2,128,256]{2,1,0:T(8,128)(2,1)}, u32[]{:S(2)}) copy-start(bf16[2,128,256]{2,1,0:T(8,128)(2,1)} %copy-done.9) | copy-start | bytes 393220
  107.5 6.3 %collective-permute-start.13 = (bf16[2,128,128]{2,1,0:T(8,128)(2,1)S(1)}, bf16[2,128,128]{2,1,0:T(8,128)(2,1)S(1)}, u32[]{:S(2)}, u32[]{:S(2)}) collective-permute-start(bf16[2,128,128]{2,1,0:T(8,128)(2,1)S(1)} %convolution_convert_fusion.6), channel_id=1, source_target_pairs={{16,0},{24,8},{32,16},{40,24},{48,32},{56,40},{64,48},{72,56},{80,... | collective-permute-start | bytes 196616 | tf_op jit(solution)/shard_map/ppermute | solution.py:21
  113.7 9.5 %copy-start.5 = (bf16[2,128,256]{2,1,0:T(8,128)(2,1)S(1)}, bf16[2,128,256]{2,1,0:T(8,128)(2,1)}, u32[]{:S(2)}) copy-start(bf16[2,128,256]{2,1,0:T(8,128)(2,1)} %copy-done.4) | copy-start | bytes 393220
  113.7 24.6 %copy-start.3 = (bf16[2,128,256]{2,1,0:T(8,128)(2,1)S(1)}, bf16[2,128,256]{2,1,0:T(8,128)(2,1)}, u32[]{:S(2)}) copy-start(bf16[2,128,256]{2,1,0:T(8,128)(2,1)} %copy-done.2) | copy-start | bytes 393220
  113.7 24.6 %copy-start.6 = (bf16[2,128,128]{2,1,0:T(8,128)(2,1)S(1)}, bf16[2,128,128]{2,1,0:T(8,128)(2,1)}, u32[]{:S(2)}) copy-start(bf16[2,128,128]{2,1,0:T(8,128)(2,1)} %get-tuple-element.59) | copy-start | bytes 196612
  114.0 7.5 %collective-permute-start.15 = (bf16[2,128,128]{2,1,0:T(8,128)(2,1)S(1)}, bf16[2,128,128]{2,1,0:T(8,128)(2,1)S(1)}, u32[]{:S(2)}, u32[]{:S(2)}) collective-permute-start(bf16[2,128,128]{2,1,0:T(8,128)(2,1)S(1)} %convolution_convert_fusion.5), channel_id=1, source_target_pairs={{32,0},{40,8},{48,16},{56,24},{64,32},{72,40},{80,48},{88,56},{96,... | collective-permute-start | bytes 196616 | tf_op jit(solution)/shard_map/ppermute | solution.py:21
  115.5 28.5 %all-to-all-start.1 = ((bf16[8,256,256]{2,1,0:T(8,128)(2,1)}), bf16[8,256,256]{2,1,0:T(8,128)(2,1)S(1)}, u32[]{:S(2)}, u32[]{:S(2)}) async-start(bf16[8,256,256]{2,1,0:T(8,128)(2,1)} %shard_map.112), calls=%async_computation.1 | async-start | bytes 2097152 | tf_op jit(solution)/shard_map/all_to_all | solution.py:547
  121.7 16.6 %collective-permute-start.18 = (bf16[2,128,128]{2,1,0:T(8,128)(2,1)S(1)}, bf16[2,128,128]{2,1,0:T(8,128)(2,1)S(1)}, u32[]{:S(2)}, u32[]{:S(2)}) collective-permute-start(bf16[2,128,128]{2,1,0:T(8,128)(2,1)S(1)} %convolution_convert_fusion.2), channel_id=1, source_target_pairs={{144,0},{152,8},{160,16},{168,24},{176,32},{184,40},{192,48},{200,... | collective-permute-start | bytes 196616 | tf_op jit(solution)/shard_map/ppermute | solution.py:21
  123.6 14.7 %collective-permute-start.19 = (bf16[2,128,128]{2,1,0:T(8,128)(2,1)S(1)}, bf16[2,128,128]{2,1,0:T(8,128)(2,1)S(1)}, u32[]{:S(2)}, u32[]{:S(2)}) collective-permute-start(bf16[2,128,128]{2,1,0:T(8,128)(2,1)S(1)} %convolution_convert_fusion), channel_id=1, source_target_pairs={{208,0},{216,8},{224,16},{232,24},{240,32},{248,40},{209,1},{217,9... | collective-permute-start | bytes 196616 | tf_op jit(solution)/shard_map/ppermute | solution.py:21
  124.9 13.4 %collective-permute-start.17 = (bf16[2,128,128]{2,1,0:T(8,128)(2,1)S(1)}, bf16[2,128,128]{2,1,0:T(8,128)(2,1)S(1)}, u32[]{:S(2)}, u32[]{:S(2)}) collective-permute-start(bf16[2,128,128]{2,1,0:T(8,128)(2,1)S(1)} %convolution_convert_fusion.4), channel_id=1, source_target_pairs={{80,0},{88,8},{96,16},{104,24},{112,32},{120,40},{128,48},{136,56}... | collective-permute-start | bytes 196616 | tf_op jit(solution)/shard_map/ppermute | solution.py:21
  126.2 12.2 %collective-permute-start.16 = (bf16[2,128,128]{2,1,0:T(8,128)(2,1)S(1)}, bf16[2,128,128]{2,1,0:T(8,128)(2,1)S(1)}, u32[]{:S(2)}, u32[]{:S(2)}) collective-permute-start(bf16[2,128,128]{2,1,0:T(8,128)(2,1)S(1)} %add_convert_fusion.2), channel_id=1, source_target_pairs={{16,0},{24,8},{32,16},{40,24},{48,32},{56,40},{64,48},{72,56},{80,... | collective-permute-start | bytes 196616 | tf_op jit(solution)/shard_map/ppermute | solution.py:21
  138.6 4.7 %collective-permute-start.20 = (bf16[2,128,128]{2,1,0:T(8,128)(2,1)S(1)}, bf16[2,128,128]{2,1,0:T(8,128)(2,1)S(1)}, u32[]{:S(2)}, u32[]{:S(2)}) collective-permute-start(bf16[2,128,128]{2,1,0:T(8,128)(2,1)S(1)} %get-tuple-element.75), channel_id=1, source_target_pairs={{0,8},{8,0},{16,24},{24,16},{32,40},{40,32},{48,56},{56,48},{64,72... | collective-permute-start | bytes 196616 | tf_op jit(solution)/shard_map/ppermute | solution.py:26
  144.1 6.6 %collective-permute-start.14 = (bf16[128,256]{1,0:T(8,128)(2,1)S(1)}, bf16[128,256]{1,0:T(8,128)(2,1)S(1)}, u32[]{:S(2)}, u32[]{:S(2)}) collective-permute-start(bf16[128,256]{1,0:T(8,128)(2,1)S(1)} %slice.118), channel_id=1, source_target_pairs={{0,8},{8,0},{16,24},{24,16},{32,40},{40,32},{48,56},{56,48},{64,72... | collective-permute-start | bytes 196616 | tf_op jit(solution)/shard_map/ppermute | solution.py:26
  151.7 9.1 %collective-permute-start.21 = (bf16[128,512]{1,0:T(8,128)(2,1)S(1)}, bf16[128,512]{1,0:T(8,128)(2,1)S(1)}, u32[]{:S(2)}, u32[]{:S(2)}) collective-permute-start(bf16[128,512]{1,0:T(8,128)(2,1)S(1)} %slice_bitcast_fusion), channel_id=1, source_target_pairs={{0,128},{8,136},{16,144},{24,152},{32,160},{40,168},{48,176},{56,1... | collective-permute-start | bytes 393224 | tf_op jit(solution)/shard_map/ppermute | solution.py:26
  (5 other events, 5.9 us)
Sparse Core Ops, SparseCore 0:
  19.5 51.5 all-gather.2
  93.6 41.1 reduce-scatter.1

commit v5 on v4

--- a/solution.py
+++ b/solution.py
@@ -454,7 +454,7 @@
     return x[:, :, :WIDTH], x[:, :, WIDTH:]
 
 
-def forward_states(mine, theirs, core, grad_full, gate):
+def forward_states(place, mine, theirs, core, grad_full, weight):
     theirs = exchange(theirs, 1)
     even = jnp.where(core == 0, mine, theirs)
     odd = jnp.where(core == 0, theirs, mine)
@@ -478,6 +478,12 @@
     near_a, near_b = halves(send(both, 8))
     mid_a, mid_b = halves(send(both, 16))
     far_b = send(rounded, 24)
+    grad_other = exchange(grad_full, 1)
+    kept_grad, given_grad = head_gradient(place, grad_full, grad_other, weight)
+    kept_grad, given_grad, near_a, near_b, mid_a, mid_b, far_b = lax.optimization_barrier(
+        (kept_grad, given_grad, near_a, near_b, mid_a, mid_b, far_b)
+    )
+    head_grad = (kept_grad, exchange(given_grad, 1))
     inner = (mid_b.astype(F32) + mul(mid_a, far_b)).astype(BF16)
     inner = (near_b.astype(F32) + mul(near_a, inner)).astype(BF16)
     first = (state + mul(window4, inner)).astype(BF16)
@@ -486,9 +492,8 @@
     second = (mul(even_a, first) + even_b.astype(F32)).astype(BF16)
     kept = jnp.where(core == 0, first, second)
     given = jnp.where(core == 0, second, first)
-    gate, given = lax.optimization_barrier((gate, given))
     state_in = jnp.concatenate([kept, exchange(given, 1)], axis=0)
-    return grad_full, gate, state_in, (even_a, odd_a, window1, window2, window4, window8, window12)
+    return grad_full, grad_other, head_grad, state_in, (even_a, odd_a, window1, window2, window4, window8, window12)
 
 
 def backward_states(mine, theirs, core, saved, gate):
@@ -529,21 +534,20 @@
     grad_full = lax.all_to_all(
         jnp.broadcast_to(out_grad[None], (8, WIDTH, 512)), "tp", 0, 0, tiled=True
     )
-    grad_full, weight_mine, state, saved = forward_states(
-        mine, theirs, core, grad_full, weight_mine
-    )
-    grad_other = exchange(grad_full, 1)
+    grad_full, grad_other, head_grad, state, saved = forward_states(
+        place, mine, theirs, core, grad_full, weight_mine
+    )
     heads = head_outputs(place, qt, local_out, state)
     heads_other = exchange(heads, 1)
     terms = weight_terms(place, grad_full, grad_other, heads, heads_other)
     ring_sum = lax.psum_scatter(
         terms, "ctx", scatter_dimension=0, axis_index_groups=rings
     ).reshape(2, WIDTH, 512)
-    weight_grad = ring_sum[0].astype(F32) + exchange(ring_sum[1], 16).astype(F32)
-    kept, given = head_gradient(place, grad_full, grad_other, weight_mine)
-    head_grad, own, own_theirs = own_cotangent(place, kept, exchange(given, 1), qt)
+    head_grad, own, own_theirs = own_cotangent(place, *head_grad, qt)
     parts = mixed_parts(place, heads, heads_other, weight_mine)
     parts, end = backward_states(own, own_theirs, core, saved, parts)
+    end, ring_sum = lax.optimization_barrier((end, ring_sum))
+    weight_grad = ring_sum[0].astype(F32) + exchange(ring_sum[1], 16).astype(F32)
     parts = lax.all_to_all(parts, "tp", 0, 0, tiled=True)
     sums = jnp.sum(parts.astype(F32), axis=0).astype(BF16)
     kept, came = sums[:WIDTH], exchange(sums[WIDTH:], 1)

time: 172 us -> 172 us (level)
  waiting for transfers between devices: 37 us -> 32.6 us
  local copies, waits for them, and re-layouts: 3.96 us -> 6.04 us
  starting transfers between devices: 63 us -> 64.9 us
  matrix products: 3.71 us -> 5.45 us
    ppermute x10, waiting for transfers between devices: 8.72 us -> 5.06 us  [exchange(): return lax.ppermute(block, 'ctx', route)]
  transfers between devices with their start and end apart: 26 -> 26, of which waited for: 13 -> 10; matrix products, arithmetic and copies ran while one was open for 5% -> 5% of each run, Pallas kernels for 21% -> 19%
where the time goes in v5:
time: 172 us; the launch traced here: 170 us
  starting transfers between devices  64.9 us (38%)
  Pallas kernels  40.3 us (23%)
  waiting for transfers between devices  32.6 us (19%)
  between operations  14.4 us (8%)
  other arithmetic  6.28 us (4%)
  local copies, waits for them, and re-layouts  6.04 us (4%)
  matrix products  5.45 us (3%)
    ppermute x12, starting transfers between devices, send(): return lax.ppermute(block, 'ctx', route)  37.5 us
    ppermute x12, waiting for transfers between devices, send(): return lax.ppermute(block, 'ctx', route)  27.5 us
    ppermute x10, starting transfers between devices, exchange(): return lax.ppermute(block, 'ctx', route)  17.4 us
    pallas_call x2, Pallas kernels, prepare(): pl.pallas_call(functools.partial(prepare_kernel, mine), grid_spec=pltpu.P...  12.7 us
    pallas_call x1, Pallas kernels, pull(): call(pull_kernel, 2, [by_columns(WIDTH), by_columns(PAIRS), whole(4, PAIR...  6.29 us
    all_to_all x1, starting transfers between devices, local(): parts = lax.all_to_all(parts, 'tp', 0, 0, tiled=True)  5.69 us
    pallas_call x1, Pallas kernels, head_gradient(): call(head_grad_kernel, STEPS, [whole(8, WIDTH, 512), whole(8, WIDTH, 512)...  5.34 us
    ppermute x10, waiting for transfers between devices, exchange(): return lax.ppermute(block, 'ctx', route)  5.06 us
  transfers between devices with their start and end apart: 26, of which 10 were waited for; matrix products, arithmetic and copies ran while one was open for 5% of the time, Pallas kernels for 19%

profile of v5, /device:TPU:1, one launch (start us, length us, event | category | flops | bytes accessed | tf_op | source)
XLA Modules:
  0.0 170.1 jit_solution(5723019297211989807)
XLA Ops:
  7.2 3.7 %collective-permute-start = (bf16[128,512]{1,0:T(8,128)(2,1)}, bf16[128,512]{1,0:T(8,128)(2,1)S(1)}, u32[]{:S(2)}, u32[]{:S(2)}) collective-permute-start(bf16[128,512]{1,0:T(8,128)(2,1)} %param.10), channel_id=1, source_target_pairs={{0,128},{8,136},{16,144},{24,152},{32,160},{40,168},{48,176},{56,1... | collective-permute-start | bytes 393224 | tf_op jit(solution)/shard_map/ppermute | solution.py:26
  11.5 6.3 %shard_map.109 = (bf16[2,128,256]{2,1,0:T(8,128)(2,1)}, f32[4,256,256]{2,1,0:T(8,128)}, f32[4,256,256]{2,1,0:T(8,128)}, f32[4,128,128]{2,1,0:T(8,128)}, f32[4,128,128]{2,1,0:T(8,128)}) custom-call(s32[2]{0:T(128)} %pad_add_fusion.refs_0_.place, bf16[128,512]{1,0:T(8,128)(2,1)} %q_ref.1, bf16[128,1024]{1,0:T(8,128)(2,1)} %k_ref.1, bf16[128,1024]{1,0:T(8,128)(2,1)} %refs_3_.2, ...), custom_call_target="tpu_custom_call" | custom-call | flops 104857600 | bytes 16777216 | tf_op jit(solution)/shard_map/pallas_call | solution.py:172
  17.8 1.6 pad_maximum_fusion
  20.5 6.4 %shard_map.110 = (bf16[2,128,256]{2,1,0:T(8,128)(2,1)}, f32[4,256,256]{2,1,0:T(8,128)}, f32[4,256,256]{2,1,0:T(8,128)}, f32[4,128,128]{2,1,0:T(8,128)}, f32[4,128,128]{2,1,0:T(8,128)}) custom-call(s32[2]{0:T(128)} %pad_add_fusion.refs_0_.place, bf16[128,512]{1,0:T(8,128)(2,1)} %q_ref.1, ...), custom_call_target="tpu_custom_call", output_to_operand_aliasing={{1}: (5, {}), {2}: (6, {}), {3}: (7, {}), {4}: (8, {})} | custom-call | flops 1048576 | bytes 65536 | tf_op jit(solution)/shard_map/pallas_call | solution.py:172
  28.5 4.9 %collective-permute-start.3 = (bf16[2,128,256]{2,1,0:T(8,128)(2,1)S(1)}, bf16[2,128,256]{2,1,0:T(8,128)(2,1)S(1)}, u32[]{:S(2)}, u32[]{:S(2)}) collective-permute-start(bf16[2,128,256]{2,1,0:T(8,128)(2,1)S(1)} %pad_maximum_fusion.1), channel_id=1, source_target_pairs={{0,32},{8,40},{16,48},{24,56},{32,64},{40,72},{48,80},{56,88},{64,... | collective-permute-start | bytes 393224 | tf_op jit(solution)/shard_map/ppermute | solution.py:21
  33.4 3.5 %collective-permute-start.2 = (bf16[2,128,256]{2,1,0:T(8,128)(2,1)S(1)}, bf16[2,128,256]{2,1,0:T(8,128)(2,1)S(1)}, u32[]{:S(2)}, u32[]{:S(2)}) collective-permute-start(bf16[2,128,256]{2,1,0:T(8,128)(2,1)S(1)} %pad_maximum_fusion.1), channel_id=1, source_target_pairs={{0,16},{8,24},{16,32},{24,40},{32,48},{40,56},{48,64},{56,72},{64,... | collective-permute-start | bytes 393224 | tf_op jit(solution)/shard_map/ppermute | solution.py:21
  38.1 4.2 %all-to-all-start = ((bf16[8,128,512]{2,1,0:T(8,128)(2,1)}), bf16[8,128,512]{2,1,0:T(8,128)(2,1)S(1)}, u32[]{:S(2)}, u32[]{:S(2)}) async-start(bf16[8,128,512]{2,1,0:T(8,128)(2,1)} %broadcast_in_dim.2), calls=%async_computation | async-start | bytes 2097152 | tf_op jit(solution)/shard_map/all_to_all | solution.py:534
  42.3 3.3 %collective-permute-done.2 = bf16[2,128,256]{2,1,0:T(8,128)(2,1)S(1)} collective-permute-done((bf16[2,128,256]{2,1,0:T(8,128)(2,1)S(1)}, bf16[2,128,256]{2,1,0:T(8,128)(2,1)S(1)}, u32[]{:S(2)}, u32[]{:S(2)}) %collective-permute-start.2) | collective-permute-done | bytes 131104 | tf_op jit(solution)/shard_map/ppermute | solution.py:21
  45.9 8.0 %collective-permute-start.4 = (bf16[2,128,256]{2,1,0:T(8,128)(2,1)S(1)}, bf16[2,128,256]{2,1,0:T(8,128)(2,1)S(1)}, u32[]{:S(2)}, u32[]{:S(2)}) collective-permute-start(bf16[2,128,256]{2,1,0:T(8,128)(2,1)S(1)} %pad_maximum_fusion.2), channel_id=1, source_target_pairs={{0,32},{8,40},{16,48},{24,56},{32,64},{40,72},{48,80},{56,88},{64,... | collective-permute-start | bytes 393224 | tf_op jit(solution)/shard_map/ppermute | solution.py:21
  53.9 8.5 %collective-permute-done.4 = bf16[2,128,256]{2,1,0:T(8,128)(2,1)S(1)} collective-permute-done((bf16[2,128,256]{2,1,0:T(8,128)(2,1)S(1)}, bf16[2,128,256]{2,1,0:T(8,128)(2,1)S(1)}, u32[]{:S(2)}, u32[]{:S(2)}) %collective-permute-start.4) | collective-permute-done | bytes 131104 | tf_op jit(solution)/shard_map/ppermute | solution.py:21
  63.4 9.8 %collective-permute-start.7 = (bf16[2,128,256]{2,1,0:T(8,128)(2,1)S(1)}, bf16[2,128,256]{2,1,0:T(8,128)(2,1)S(1)}, u32[]{:S(2)}, u32[]{:S(2)}) collective-permute-start(bf16[2,128,256]{2,1,0:T(8,128)(2,1)S(1)} %pad_maximum_fusion.3), channel_id=1, source_target_pairs={{0,128},{8,136},{16,144},{24,152},{32,160},{40,168},{48,176},{56,1... | collective-permute-start | bytes 393224 | tf_op jit(solution)/shard_map/ppermute | solution.py:21
  73.2 2.0 %collective-permute-start.8 = (bf16[2,128,128]{2,1,0:T(8,128)(2,1)S(1)}, bf16[2,128,128]{2,1,0:T(8,128)(2,1)}, u32[]{:S(2)}, u32[]{:S(2)}) collective-permute-start(bf16[2,128,128]{2,1,0:T(8,128)(2,1)S(1)} %fusion.20), channel_id=1, source_target_pairs={{0,192},{8,200},{16,208},{24,216},{32,224},{40,232},{48,240},{56,2... | collective-permute-start | bytes 196616 | tf_op jit(solution)/shard_map/ppermute | solution.py:21
  75.1 1.6 collective-permute-start.6
  77.4 4.6 %collective-permute-done.6 = bf16[2,128,256]{2,1,0:T(8,128)(2,1)S(1)} collective-permute-done((bf16[2,128,256]{2,1,0:T(8,128)(2,1)S(1)}, bf16[2,128,256]{2,1,0:T(8,128)(2,1)S(1)}, u32[]{:S(2)}, u32[]{:S(2)}) %collective-permute-start.6) | collective-permute-done | bytes 131104 | tf_op jit(solution)/shard_map/ppermute | solution.py:21
  82.6 5.3 %shard_map.111 = (f32[128,512]{1,0:T(8,128)}, f32[128,512]{1,0:T(8,128)}) custom-call(s32[2]{0:T(128)} %pad_add_fusion.refs_0_.place, bf16[8,128,512]{2,1,0:T(8,128)(2,1)} %copy-done, bf16[8,128,512]{2,1,0:T(8,128)(2,1)} %collective-permute-done.5.other_ref, bf16[8,2,128,512]{3,2,1,0:T(8,128)(2,1)} %bitcast.25), custom_call_target="tpu_custom_call" | custom-call | flops 536870912 | bytes 5242880 | tf_op jit(solution)/shard_map/pallas_call | solution.py:320
  92.4 2.6 %shard_map.112.heads_ref = bf16[128,512]{1,0:T(8,128)(2,1)} custom-call(s32[2]{0:T(128)} %pad_add_fusion.refs_0_.place, f32[4,128,128]{2,1,0:T(8,128)} %get-tuple-element.55.qt_ref, f32[4,128,128]{2,1,0:T(8,128)} %get-tuple-element.56.local_ref, bf16[4,128,128]{2,1,0:T(8,128)(2,1)} %pad_maximum_fusion.4.state_ref), custom_call_target="tpu_custom_call" | custom-call | flops 16777216 | bytes 1048576 | tf_op jit(solution)/shard_map/pallas_call | solution.py:239
  95.4 1.2 collective-permute-done.10.heads_other_ref
  97.2 4.9 %shard_map.115 = bf16[8,256,512]{2,1,0:T(8,128)(2,1)} custom-call(s32[2]{0:T(128)} %pad_add_fusion.refs_0_.place, bf16[8,128,512]{2,1,0:T(8,128)(2,1)} %copy-done, bf16[8,128,512]{2,1,0:T(8,128)(2,1)} %collective-permute-done.5.other_ref, bf16[128,512]{1,0:T(8,128)(2,1)} %shard_map.112.heads_ref, bf16[128,512]{1,0:T(8,128)(2,1)} %copy-done.1), custom_call_target="tpu_custom_call" | custom-call | flops 536870912 | bytes 5242880 | tf_op jit(solution)/shard_map/pallas_call | solution.py:263
  103.4 1.2 collective-permute-done.11.came_ref
  105.3 3.5 %shard_map.114 = (f32[128,512]{1,0:T(8,128)}, bf16[2,128,128]{2,1,0:T(8,128)(2,1)}, bf16[2,128,128]{2,1,0:T(8,128)(2,1)}) custom-call(s32[2]{0:T(128)} %pad_add_fusion.refs_0_.place, f32[128,512]{1,0:T(8,128)} %get-tuple-element.69.kept_ref, f32[128,512]{1,0:T(8,128)} %copy-done.6, f32[4,128,128]{2,1,0:T(8,128)} %get-tuple-element.55.qt_ref), custom_call_target="tpu_custom_call" | custom-call | flops 16777216 | bytes 1048576 | tf_op jit(solution)/shard_map/pallas_call | solution.py:348
  111.6 1.3 collective-permute-start.13
  112.9 5.0 %shard_map.113 = bf16[8,256,256]{2,1,0:T(8,128)(2,1)} custom-call(s32[2]{0:T(128)} %pad_add_fusion.refs_0_.place, bf16[128,512]{1,0:T(8,128)(2,1)} %shard_map.112.heads_ref, bf16[128,512]{1,0:T(8,128)(2,1)} %copy-done.1, bf16[8,2,128,512]{3,2,1,0:T(8,128)(2,1)} %bitcast.26), custom_call_target="tpu_custom_call" | custom-call | flops 536870912 | bytes 3145728 | tf_op jit(solution)/shard_map/pallas_call | solution.py:288
  118.6 1.3 collective-permute-start.15
  120.1 5.7 %all-to-all-start.1 = ((bf16[8,256,256]{2,1,0:T(8,128)(2,1)}), bf16[8,256,256]{2,1,0:T(8,128)(2,1)S(1)}, u32[]{:S(2)}, u32[]{:S(2)}) async-start(bf16[8,256,256]{2,1,0:T(8,128)(2,1)} %shard_map.113), calls=%async_computation.1 | async-start | bytes 2097152 | tf_op jit(solution)/shard_map/all_to_all | solution.py:551
  126.6 1.3 collective-permute-start.18
  127.9 1.3 collective-permute-start.19
  129.2 1.3 collective-permute-start.17
  130.5 1.3 collective-permute-start.16
  131.8 10.6 %collective-permute-done.18 = bf16[2,128,128]{2,1,0:T(8,128)(2,1)S(1)} collective-permute-done((bf16[2,128,128]{2,1,0:T(8,128)(2,1)S(1)}, bf16[2,128,128]{2,1,0:T(8,128)(2,1)S(1)}, u32[]{:S(2)}, u32[]{:S(2)}) %collective-permute-start.18) | collective-permute-done | bytes 65568 | tf_op jit(solution)/shard_map/ppermute | solution.py:21
  142.7 4.5 %collective-permute-start.20 = (bf16[2,128,128]{2,1,0:T(8,128)(2,1)S(1)}, bf16[2,128,128]{2,1,0:T(8,128)(2,1)S(1)}, u32[]{:S(2)}, u32[]{:S(2)}) collective-permute-start(bf16[2,128,128]{2,1,0:T(8,128)(2,1)S(1)} %get-tuple-element.89), channel_id=1, source_target_pairs={{0,8},{8,0},{16,24},{24,16},{32,40},{40,32},{48,56},{56,48},{64,72... | collective-permute-start | bytes 196616 | tf_op jit(solution)/shard_map/ppermute | solution.py:26
  150.5 5.7 %collective-permute-start.21 = (bf16[128,512]{1,0:T(8,128)(2,1)S(1)}, bf16[128,512]{1,0:T(8,128)(2,1)S(1)}, u32[]{:S(2)}, u32[]{:S(2)}) collective-permute-start(bf16[128,512]{1,0:T(8,128)(2,1)S(1)} %slice_bitcast_fusion), channel_id=1, source_target_pairs={{0,128},{8,136},{16,144},{24,152},{32,160},{40,168},{48,176},{56,1... | collective-permute-start | bytes 393224 | tf_op jit(solution)/shard_map/ppermute | solution.py:26
  156.2 6.3 %shard_map.116 = (bf16[128,512]{1,0:T(8,128)(2,1)}, bf16[128,1024]{1,0:T(8,128)(2,1)}, bf16[128,1024]{1,0:T(8,128)(2,1)}, f32[4,256]{1,0:T(4,128)}) custom-call(s32[2]{0:T(128)} %pad_add_fusion.refs_0_.place, bf16[128,512]{1,0:T(8,128)(2,1)} %q_ref.1, bf16[128,1024]{1,0:T(8,128)(2,1)} %k_ref.1, f32[4,256]{1,0:T(4,128)} %logit_ref.1, ...), custom_call_target="tpu_custom_call" | custom-call | flops 1879048192 | bytes 5242880 | tf_op jit(solution)/shard_map/pallas_call | solution.py:420
  (88 shorter events, 22.9 us)
Async XLA Ops:
  7.2 75.5 %all-gather.3.cloned.1.call-start = ((), (), s32[]{:S(2)}) async-start(), calls=%async_computation.4 | async-start | bytes 2359296 | tf_op jit(solution)/shard_map/all_gather | solution.py:533
  7.2 10.6 %collective-permute-start = (bf16[128,512]{1,0:T(8,128)(2,1)}, bf16[128,512]{1,0:T(8,128)(2,1)S(1)}, u32[]{:S(2)}, u32[]{:S(2)}) collective-permute-start(bf16[128,512]{1,0:T(8,128)(2,1)} %param.10), channel_id=1, source_target_pairs={{0,128},{8,136},{16,144},{24,152},{32,160},{40,168},{48,176},{56,1... | collective-permute-start | bytes 393224 | tf_op jit(solution)/shard_map/ppermute | solution.py:26
  19.5 7.4 %collective-permute-start.1 = (bf16[2,128,256]{2,1,0:T(8,128)(2,1)}, bf16[2,128,256]{2,1,0:T(8,128)(2,1)S(1)}, u32[]{:S(2)}, u32[]{:S(2)}) collective-permute-start(bf16[2,128,256]{2,1,0:T(8,128)(2,1)} %get-tuple-element.57), channel_id=1, source_target_pairs={{0,8},{8,0},{16,24},{24,16},{32,40},{40,32},{48,56},{56,48},{64,72... | collective-permute-start | bytes 393224 | tf_op jit(solution)/shard_map/ppermute | solution.py:26
  20.5 16.5 %copy-start.7 = (bf16[128,512]{1,0:T(8,128)(2,1)S(1)}, bf16[128,512]{1,0:T(8,128)(2,1)}, u32[]{:S(2)}) copy-start(bf16[128,512]{1,0:T(8,128)(2,1)} %param.11) | copy-start | bytes 393220
  28.5 13.8 %collective-permute-start.3 = (bf16[2,128,256]{2,1,0:T(8,128)(2,1)S(1)}, bf16[2,128,256]{2,1,0:T(8,128)(2,1)S(1)}, u32[]{:S(2)}, u32[]{:S(2)}) collective-permute-start(bf16[2,128,256]{2,1,0:T(8,128)(2,1)S(1)} %pad_maximum_fusion.1), channel_id=1, source_target_pairs={{0,32},{8,40},{16,48},{24,56},{32,64},{40,72},{48,80},{56,88},{64,... | collective-permute-start | bytes 393224 | tf_op jit(solution)/shard_map/ppermute | solution.py:21
  33.4 12.2 %collective-permute-start.2 = (bf16[2,128,256]{2,1,0:T(8,128)(2,1)S(1)}, bf16[2,128,256]{2,1,0:T(8,128)(2,1)S(1)}, u32[]{:S(2)}, u32[]{:S(2)}) collective-permute-start(bf16[2,128,256]{2,1,0:T(8,128)(2,1)S(1)} %pad_maximum_fusion.1), channel_id=1, source_target_pairs={{0,16},{8,24},{16,32},{24,40},{32,48},{40,56},{48,64},{56,72},{64,... | collective-permute-start | bytes 393224 | tf_op jit(solution)/shard_map/ppermute | solution.py:21
  38.1 24.6 %all-to-all-start = ((bf16[8,128,512]{2,1,0:T(8,128)(2,1)}), bf16[8,128,512]{2,1,0:T(8,128)(2,1)S(1)}, u32[]{:S(2)}, u32[]{:S(2)}) async-start(bf16[8,128,512]{2,1,0:T(8,128)(2,1)} %broadcast_in_dim.2), calls=%async_computation | async-start | bytes 2097152 | tf_op jit(solution)/shard_map/all_to_all | solution.py:534
  42.3 107.3 %reduce-scatter.2.cloned.1.call-start = ((), (), s32[]{:S(2)}) async-start(), calls=%async_computation.3 | async-start | bytes 2359296 | tf_op jit(solution)/shard_map/reduce_scatter | solution.py:543
  45.9 16.5 %collective-permute-start.4 = (bf16[2,128,256]{2,1,0:T(8,128)(2,1)S(1)}, bf16[2,128,256]{2,1,0:T(8,128)(2,1)S(1)}, u32[]{:S(2)}, u32[]{:S(2)}) collective-permute-start(bf16[2,128,256]{2,1,0:T(8,128)(2,1)S(1)} %pad_maximum_fusion.2), channel_id=1, source_target_pairs={{0,32},{8,40},{16,48},{24,56},{32,64},{40,72},{48,80},{56,88},{64,... | collective-permute-start | bytes 393224 | tf_op jit(solution)/shard_map/ppermute | solution.py:21
  62.6 20.0 %copy-start = (bf16[8,128,512]{2,1,0:T(8,128)(2,1)}, bf16[8,128,512]{2,1,0:T(8,128)(2,1)S(1)}, u32[]{:S(2)}) copy-start(bf16[8,128,512]{2,1,0:T(8,128)(2,1)S(1)} %all-to-all-done.own_ref) | copy-start | bytes 3145732
  62.6 20.0 %collective-permute-start.5 = (bf16[8,128,512]{2,1,0:T(8,128)(2,1)S(1)}, bf16[8,128,512]{2,1,0:T(8,128)(2,1)}, u32[]{:S(2)}, u32[]{:S(2)}) collective-permute-start(bf16[8,128,512]{2,1,0:T(8,128)(2,1)S(1)} %all-to-all-done.own_ref), channel_id=1, source_target_pairs={{0,8},{8,0},{16,24},{24,16},{32,40},{40,32},{48,56},{56,48},{64,72... | collective-permute-start | bytes 3145736 | tf_op jit(solution)/shard_map/ppermute | solution.py:26
  63.4 13.3 %collective-permute-start.7 = (bf16[2,128,256]{2,1,0:T(8,128)(2,1)S(1)}, bf16[2,128,256]{2,1,0:T(8,128)(2,1)S(1)}, u32[]{:S(2)}, u32[]{:S(2)}) collective-permute-start(bf16[2,128,256]{2,1,0:T(8,128)(2,1)S(1)} %pad_maximum_fusion.3), channel_id=1, source_target_pairs={{0,128},{8,136},{16,144},{24,152},{32,160},{40,168},{48,176},{56,1... | collective-permute-start | bytes 393224 | tf_op jit(solution)/shard_map/ppermute | solution.py:21
  73.2 14.8 %collective-permute-start.8 = (bf16[2,128,128]{2,1,0:T(8,128)(2,1)S(1)}, bf16[2,128,128]{2,1,0:T(8,128)(2,1)}, u32[]{:S(2)}, u32[]{:S(2)}) collective-permute-start(bf16[2,128,128]{2,1,0:T(8,128)(2,1)S(1)} %fusion.20), channel_id=1, source_target_pairs={{0,192},{8,200},{16,208},{24,216},{32,224},{40,232},{48,240},{56,2... | collective-permute-start | bytes 196616 | tf_op jit(solution)/shard_map/ppermute | solution.py:21
  75.1 6.8 %collective-permute-start.6 = (bf16[2,128,256]{2,1,0:T(8,128)(2,1)S(1)}, bf16[2,128,256]{2,1,0:T(8,128)(2,1)S(1)}, u32[]{:S(2)}, u32[]{:S(2)}) collective-permute-start(bf16[2,128,256]{2,1,0:T(8,128)(2,1)S(1)} %pad_maximum_fusion.3), channel_id=1, source_target_pairs={{0,64},{8,72},{16,80},{24,88},{32,96},{40,104},{48,112},{56,120},{... | collective-permute-start | bytes 393224 | tf_op jit(solution)/shard_map/ppermute | solution.py:21
  90.3 1.4 collective-permute-start.9
  95.0 1.6 collective-permute-start.10
  102.1 0.9 copy-start.8
  103.1 1.5 collective-permute-start.11
  108.8 1.5 collective-permute-start.12
  111.6 6.9 %collective-permute-start.13 = (bf16[2,128,128]{2,1,0:T(8,128)(2,1)S(1)}, bf16[2,128,128]{2,1,0:T(8,128)(2,1)S(1)}, u32[]{:S(2)}, u32[]{:S(2)}) collective-permute-start(bf16[2,128,128]{2,1,0:T(8,128)(2,1)S(1)} %convolution_convert_fusion.6), channel_id=1, source_target_pairs={{16,0},{24,8},{32,16},{40,24},{48,32},{56,40},{64,48},{72,56},{80,... | collective-permute-start | bytes 196616 | tf_op jit(solution)/shard_map/ppermute | solution.py:21
  117.9 24.6 %copy-start.3 = (bf16[2,128,256]{2,1,0:T(8,128)(2,1)S(1)}, bf16[2,128,256]{2,1,0:T(8,128)(2,1)}, u32[]{:S(2)}) copy-start(bf16[2,128,256]{2,1,0:T(8,128)(2,1)} %copy-done.2) | copy-start | bytes 393220
  117.9 24.6 %copy-start.4 = (bf16[2,128,128]{2,1,0:T(8,128)(2,1)S(1)}, bf16[2,128,128]{2,1,0:T(8,128)(2,1)}, u32[]{:S(2)}) copy-start(bf16[2,128,128]{2,1,0:T(8,128)(2,1)} %get-tuple-element.71) | copy-start | bytes 196612
  118.6 7.2 %collective-permute-start.15 = (bf16[2,128,128]{2,1,0:T(8,128)(2,1)S(1)}, bf16[2,128,128]{2,1,0:T(8,128)(2,1)S(1)}, u32[]{:S(2)}, u32[]{:S(2)}) collective-permute-start(bf16[2,128,128]{2,1,0:T(8,128)(2,1)S(1)} %convolution_convert_fusion.5), channel_id=1, source_target_pairs={{32,0},{40,8},{48,16},{56,24},{64,32},{72,40},{80,48},{88,56},{96,... | collective-permute-start | bytes 196616 | tf_op jit(solution)/shard_map/ppermute | solution.py:21
  120.1 27.2 %all-to-all-start.1 = ((bf16[8,256,256]{2,1,0:T(8,128)(2,1)}), bf16[8,256,256]{2,1,0:T(8,128)(2,1)S(1)}, u32[]{:S(2)}, u32[]{:S(2)}) async-start(bf16[8,256,256]{2,1,0:T(8,128)(2,1)} %shard_map.113), calls=%async_computation.1 | async-start | bytes 2097152 | tf_op jit(solution)/shard_map/all_to_all | solution.py:551
  126.6 15.8 %collective-permute-start.18 = (bf16[2,128,128]{2,1,0:T(8,128)(2,1)S(1)}, bf16[2,128,128]{2,1,0:T(8,128)(2,1)S(1)}, u32[]{:S(2)}, u32[]{:S(2)}) collective-permute-start(bf16[2,128,128]{2,1,0:T(8,128)(2,1)S(1)} %convolution_convert_fusion.2), channel_id=1, source_target_pairs={{144,0},{152,8},{160,16},{168,24},{176,32},{184,40},{192,48},{200,... | collective-permute-start | bytes 196616 | tf_op jit(solution)/shard_map/ppermute | solution.py:21
  127.9 14.5 %collective-permute-start.19 = (bf16[2,128,128]{2,1,0:T(8,128)(2,1)S(1)}, bf16[2,128,128]{2,1,0:T(8,128)(2,1)S(1)}, u32[]{:S(2)}, u32[]{:S(2)}) collective-permute-start(bf16[2,128,128]{2,1,0:T(8,128)(2,1)S(1)} %convolution_convert_fusion), channel_id=1, source_target_pairs={{208,0},{216,8},{224,16},{232,24},{240,32},{248,40},{209,1},{217,9... | collective-permute-start | bytes 196616 | tf_op jit(solution)/shard_map/ppermute | solution.py:21
  129.2 13.3 %collective-permute-start.17 = (bf16[2,128,128]{2,1,0:T(8,128)(2,1)S(1)}, bf16[2,128,128]{2,1,0:T(8,128)(2,1)S(1)}, u32[]{:S(2)}, u32[]{:S(2)}) collective-permute-start(bf16[2,128,128]{2,1,0:T(8,128)(2,1)S(1)} %convolution_convert_fusion.4), channel_id=1, source_target_pairs={{80,0},{88,8},{96,16},{104,24},{112,32},{120,40},{128,48},{136,56}... | collective-permute-start | bytes 196616 | tf_op jit(solution)/shard_map/ppermute | solution.py:21
  130.5 12.0 %collective-permute-start.16 = (bf16[2,128,128]{2,1,0:T(8,128)(2,1)S(1)}, bf16[2,128,128]{2,1,0:T(8,128)(2,1)S(1)}, u32[]{:S(2)}, u32[]{:S(2)}) collective-permute-start(bf16[2,128,128]{2,1,0:T(8,128)(2,1)S(1)} %add_convert_fusion.2), channel_id=1, source_target_pairs={{16,0},{24,8},{32,16},{40,24},{48,32},{56,40},{64,48},{72,56},{80,... | collective-permute-start | bytes 196616 | tf_op jit(solution)/shard_map/ppermute | solution.py:21
  142.7 5.4 %collective-permute-start.20 = (bf16[2,128,128]{2,1,0:T(8,128)(2,1)S(1)}, bf16[2,128,128]{2,1,0:T(8,128)(2,1)S(1)}, u32[]{:S(2)}, u32[]{:S(2)}) collective-permute-start(bf16[2,128,128]{2,1,0:T(8,128)(2,1)S(1)} %get-tuple-element.89), channel_id=1, source_target_pairs={{0,8},{8,0},{16,24},{24,16},{32,40},{40,32},{48,56},{56,48},{64,72... | collective-permute-start | bytes 196616 | tf_op jit(solution)/shard_map/ppermute | solution.py:26
  147.4 1.4 collective-permute-start.14
  150.5 12.0 %collective-permute-start.21 = (bf16[128,512]{1,0:T(8,128)(2,1)S(1)}, bf16[128,512]{1,0:T(8,128)(2,1)S(1)}, u32[]{:S(2)}, u32[]{:S(2)}) collective-permute-start(bf16[128,512]{1,0:T(8,128)(2,1)S(1)} %slice_bitcast_fusion), channel_id=1, source_target_pairs={{0,128},{8,136},{16,144},{24,152},{32,160},{40,168},{48,176},{56,1... | collective-permute-start | bytes 393224 | tf_op jit(solution)/shard_map/ppermute | solution.py:26
  156.2 6.3 %copy-start.5 = (bf16[1,256,512]{2,1,0:T(8,128)(2,1)S(1)}, bf16[1,256,512]{2,1,0:T(8,128)(2,1)}, u32[]{:S(2)}) copy-start(bf16[1,256,512]{2,1,0:T(8,128)(2,1)} %reduce-scatter.2.cloned.1.call-done) | copy-start | bytes 786436
  (3 other events, 2.0 us)
Sparse Core Ops, SparseCore 0:
  19.6 51.5 all-gather.2
  102.3 45.0 reduce-scatter.1

commit v6 on v5

--- a/solution.py
+++ b/solution.py
@@ -332,7 +332,7 @@
     grad_ref[...] = kept_ref[...] + came_ref[...]
     for head in range(4):
         grad = grad_ref[:, head * WIDTH : (head + 1) * WIDTH]
-        own = dot(qt_ref[head], grad, 0, 0).astype(BF16)
+        own = dot(qt_ref[head], grad, 0, 0, passes=1).astype(BF16)
 
         @pl.when(place[0] == head // 2)
         def _():
@@ -475,14 +475,14 @@
     rounded = state.astype(BF16)
     both = jnp.concatenate([window4, rounded], axis=2)
     grad_full, both = lax.optimization_barrier((grad_full, both))
-    near_a, near_b = halves(send(both, 8))
-    mid_a, mid_b = halves(send(both, 16))
-    far_b = send(rounded, 24)
+    near, mid, far_b = send(both, 8), send(both, 16), send(rounded, 24)
     grad_other = exchange(grad_full, 1)
     kept_grad, given_grad = head_gradient(place, grad_full, grad_other, weight)
-    kept_grad, given_grad, near_a, near_b, mid_a, mid_b, far_b = lax.optimization_barrier(
-        (kept_grad, given_grad, near_a, near_b, mid_a, mid_b, far_b)
-    )
+    kept_grad, given_grad, near, mid, far_b = lax.optimization_barrier(
+        (kept_grad, given_grad, near, mid, far_b)
+    )
+    near_a, near_b = halves(near)
+    mid_a, mid_b = halves(mid)
     head_grad = (kept_grad, exchange(given_grad, 1))
     inner = (mid_b.astype(F32) + mul(mid_a, far_b)).astype(BF16)
     inner = (near_b.astype(F32) + mul(near_a, inner)).astype(BF16)

time: 172 us -> 167 us (0.971)
  waiting for transfers between devices: 32.6 us -> 26.6 us
  matrix products: 5.45 us -> 7.19 us
    ppermute x12, waiting for transfers between devices: 27.5 us -> 21.5 us  [send(): return lax.ppermute(block, 'ctx', route)]
  transfers between devices with their start and end apart: 26 -> 26, of which waited for: 10 -> 9; matrix products, arithmetic and copies ran while one was open for 5% -> 6% of each run, Pallas kernels for 19% -> 20%
where the time goes in v6:
time: 167 us; the launch traced here: 166 us
  starting transfers between devices  66.4 us (40%)
  Pallas kernels  40.2 us (24%)
  waiting for transfers between devices  26.6 us (16%)
  between operations  14.4 us (9%)
  matrix products  7.19 us (4%)
  other arithmetic  6.94 us (4%)
  local copies, waits for them, and re-layouts  4.36 us (3%)
    ppermute x12, starting transfers between devices, send(): return lax.ppermute(block, 'ctx', route)  38.9 us
    ppermute x12, waiting for transfers between devices, send(): return lax.ppermute(block, 'ctx', route)  21.5 us
    ppermute x10, starting transfers between devices, exchange(): return lax.ppermute(block, 'ctx', route)  17.6 us
    pallas_call x2, Pallas kernels, prepare(): pl.pallas_call(functools.partial(prepare_kernel, mine), grid_spec=pltpu.P...  12.7 us
    pallas_call x1, Pallas kernels, pull(): call(pull_kernel, 2, [by_columns(WIDTH), by_columns(PAIRS), whole(4, PAIR...  6.27 us
    all_to_all x1, starting transfers between devices, local(): parts = lax.all_to_all(parts, 'tp', 0, 0, tiled=True)  5.66 us
    pallas_call x1, Pallas kernels, head_gradient(): call(head_grad_kernel, STEPS, [whole(8, WIDTH, 512), whole(8, WIDTH, 512)...  5.34 us
    ppermute x10, waiting for transfers between devices, exchange(): return lax.ppermute(block, 'ctx', route)  5.07 us
  transfers between devices with their start and end apart: 26, of which 9 were waited for; matrix products, arithmetic and copies ran while one was open for 6% of the time, Pallas kernels for 20%

profile of v6, /device:TPU:1, one launch (start us, length us, event | category | flops | bytes accessed | tf_op | source)
XLA Modules:
  0.0 166.1 jit_solution(16275595368219194230)
XLA Ops:
  7.2 3.7 %collective-permute-start = (bf16[128,512]{1,0:T(8,128)(2,1)}, bf16[128,512]{1,0:T(8,128)(2,1)S(1)}, u32[]{:S(2)}, u32[]{:S(2)}) collective-permute-start(bf16[128,512]{1,0:T(8,128)(2,1)} %param.10), channel_id=1, source_target_pairs={{0,128},{8,136},{16,144},{24,152},{32,160},{40,168},{48,176},{56,1... | collective-permute-start | bytes 393224 | tf_op jit(solution)/shard_map/ppermute | solution.py:26
  11.5 6.3 %shard_map.109 = (bf16[2,128,256]{2,1,0:T(8,128)(2,1)}, f32[4,256,256]{2,1,0:T(8,128)}, f32[4,256,256]{2,1,0:T(8,128)}, f32[4,128,128]{2,1,0:T(8,128)}, f32[4,128,128]{2,1,0:T(8,128)}) custom-call(s32[2]{0:T(128)} %pad_add_fusion.refs_0_.place, bf16[128,512]{1,0:T(8,128)(2,1)} %q_ref.1, bf16[128,1024]{1,0:T(8,128)(2,1)} %k_ref.1, bf16[128,1024]{1,0:T(8,128)(2,1)} %refs_3_.2, ...), custom_call_target="tpu_custom_call" | custom-call | flops 104857600 | bytes 16777216 | tf_op jit(solution)/shard_map/pallas_call | solution.py:172
  17.8 1.6 pad_maximum_fusion
  20.5 6.4 %shard_map.110 = (bf16[2,128,256]{2,1,0:T(8,128)(2,1)}, f32[4,256,256]{2,1,0:T(8,128)}, f32[4,256,256]{2,1,0:T(8,128)}, f32[4,128,128]{2,1,0:T(8,128)}, f32[4,128,128]{2,1,0:T(8,128)}) custom-call(s32[2]{0:T(128)} %pad_add_fusion.refs_0_.place, bf16[128,512]{1,0:T(8,128)(2,1)} %q_ref.1, ...), custom_call_target="tpu_custom_call", output_to_operand_aliasing={{1}: (5, {}), {2}: (6, {}), {3}: (7, {}), {4}: (8, {})} | custom-call | flops 1048576 | bytes 65536 | tf_op jit(solution)/shard_map/pallas_call | solution.py:172
  28.1 4.9 %collective-permute-start.3 = (bf16[2,128,256]{2,1,0:T(8,128)(2,1)S(1)}, bf16[2,128,256]{2,1,0:T(8,128)(2,1)S(1)}, u32[]{:S(2)}, u32[]{:S(2)}) collective-permute-start(bf16[2,128,256]{2,1,0:T(8,128)(2,1)S(1)} %pad_maximum_fusion.1), channel_id=1, source_target_pairs={{0,32},{8,40},{16,48},{24,56},{32,64},{40,72},{48,80},{56,88},{64,... | collective-permute-start | bytes 393224 | tf_op jit(solution)/shard_map/ppermute | solution.py:21
  33.0 3.5 %collective-permute-start.2 = (bf16[2,128,256]{2,1,0:T(8,128)(2,1)S(1)}, bf16[2,128,256]{2,1,0:T(8,128)(2,1)S(1)}, u32[]{:S(2)}, u32[]{:S(2)}) collective-permute-start(bf16[2,128,256]{2,1,0:T(8,128)(2,1)S(1)} %pad_maximum_fusion.1), channel_id=1, source_target_pairs={{0,16},{8,24},{16,32},{24,40},{32,48},{40,56},{48,64},{56,72},{64,... | collective-permute-start | bytes 393224 | tf_op jit(solution)/shard_map/ppermute | solution.py:21
  37.7 4.2 %all-to-all-start = ((bf16[8,128,512]{2,1,0:T(8,128)(2,1)}), bf16[8,128,512]{2,1,0:T(8,128)(2,1)S(1)}, u32[]{:S(2)}, u32[]{:S(2)}) async-start(bf16[8,128,512]{2,1,0:T(8,128)(2,1)} %broadcast_in_dim.2), calls=%async_computation | async-start | bytes 2097152 | tf_op jit(solution)/shard_map/all_to_all | solution.py:534
  41.9 3.7 %collective-permute-done.2 = bf16[2,128,256]{2,1,0:T(8,128)(2,1)S(1)} collective-permute-done((bf16[2,128,256]{2,1,0:T(8,128)(2,1)S(1)}, bf16[2,128,256]{2,1,0:T(8,128)(2,1)S(1)}, u32[]{:S(2)}, u32[]{:S(2)}) %collective-permute-start.2) | collective-permute-done | bytes 131104 | tf_op jit(solution)/shard_map/ppermute | solution.py:21
  45.9 7.5 %collective-permute-start.4 = (bf16[2,128,256]{2,1,0:T(8,128)(2,1)S(1)}, bf16[2,128,256]{2,1,0:T(8,128)(2,1)S(1)}, u32[]{:S(2)}, u32[]{:S(2)}) collective-permute-start(bf16[2,128,256]{2,1,0:T(8,128)(2,1)S(1)} %pad_maximum_fusion.2), channel_id=1, source_target_pairs={{0,32},{8,40},{16,48},{24,56},{32,64},{40,72},{48,80},{56,88},{64,... | collective-permute-start | bytes 393224 | tf_op jit(solution)/shard_map/ppermute | solution.py:21
  53.4 8.7 %collective-permute-done.4 = bf16[2,128,256]{2,1,0:T(8,128)(2,1)S(1)} collective-permute-done((bf16[2,128,256]{2,1,0:T(8,128)(2,1)S(1)}, bf16[2,128,256]{2,1,0:T(8,128)(2,1)S(1)}, u32[]{:S(2)}, u32[]{:S(2)}) %collective-permute-start.4) | collective-permute-done | bytes 131104 | tf_op jit(solution)/shard_map/ppermute | solution.py:21
  63.7 10.1 %collective-permute-start.7 = (bf16[2,128,256]{2,1,0:T(8,128)(2,1)}, bf16[2,128,256]{2,1,0:T(8,128)(2,1)}, u32[]{:S(2)}, u32[]{:S(2)}) collective-permute-start(bf16[2,128,256]{2,1,0:T(8,128)(2,1)} %pad_maximum_fusion.3), channel_id=1, source_target_pairs={{0,128},{8,136},{16,144},{24,152},{32,160},{40,168},{48,176},{56,1... | collective-permute-start | bytes 393224 | tf_op jit(solution)/shard_map/ppermute | solution.py:21
  73.8 3.2 %collective-permute-start.6 = (bf16[2,128,256]{2,1,0:T(8,128)(2,1)}, bf16[2,128,256]{2,1,0:T(8,128)(2,1)}, u32[]{:S(2)}, u32[]{:S(2)}) collective-permute-start(bf16[2,128,256]{2,1,0:T(8,128)(2,1)} %pad_maximum_fusion.3), channel_id=1, source_target_pairs={{0,64},{8,72},{16,80},{24,88},{32,96},{40,104},{48,112},{56,120},{... | collective-permute-start | bytes 393224 | tf_op jit(solution)/shard_map/ppermute | solution.py:21
  77.0 1.9 %collective-permute-start.8 = (bf16[2,128,128]{2,1,0:T(8,128)(2,1)S(1)}, bf16[2,128,128]{2,1,0:T(8,128)(2,1)}, u32[]{:S(2)}, u32[]{:S(2)}) collective-permute-start(bf16[2,128,128]{2,1,0:T(8,128)(2,1)S(1)} %fusion.30), channel_id=1, source_target_pairs={{0,192},{8,200},{16,208},{24,216},{32,224},{40,232},{48,240},{56,2... | collective-permute-start | bytes 196616 | tf_op jit(solution)/shard_map/ppermute | solution.py:21
  78.9 5.3 %shard_map.111 = (f32[128,512]{1,0:T(8,128)}, f32[128,512]{1,0:T(8,128)}) custom-call(s32[2]{0:T(128)} %pad_add_fusion.refs_0_.place, bf16[8,128,512]{2,1,0:T(8,128)(2,1)} %copy-done, bf16[8,128,512]{2,1,0:T(8,128)(2,1)} %collective-permute-done.5.other_ref, bf16[8,2,128,512]{3,2,1,0:T(8,128)(2,1)} %bitcast.21), custom_call_target="tpu_custom_call" | custom-call | flops 536870912 | bytes 5242880 | tf_op jit(solution)/shard_map/pallas_call | solution.py:320
  85.3 1.2 fusion
  88.9 2.6 %shard_map.112.heads_ref = bf16[128,512]{1,0:T(8,128)(2,1)} custom-call(s32[2]{0:T(128)} %pad_add_fusion.refs_0_.place, f32[4,128,128]{2,1,0:T(8,128)} %get-tuple-element.53.qt_ref, f32[4,128,128]{2,1,0:T(8,128)} %get-tuple-element.54.local_ref, bf16[4,128,128]{2,1,0:T(8,128)(2,1)} %pad_maximum_fusion.4.state_ref), custom_call_target="tpu_custom_call" | custom-call | flops 16777216 | bytes 1048576 | tf_op jit(solution)/shard_map/pallas_call | solution.py:239
  91.9 1.2 collective-permute-done.10.heads_other_ref
  93.7 4.9 %shard_map.115 = bf16[8,256,512]{2,1,0:T(8,128)(2,1)} custom-call(s32[2]{0:T(128)} %pad_add_fusion.refs_0_.place, bf16[8,128,512]{2,1,0:T(8,128)(2,1)} %copy-done, bf16[8,128,512]{2,1,0:T(8,128)(2,1)} %collective-permute-done.5.other_ref, bf16[128,512]{1,0:T(8,128)(2,1)} %shard_map.112.heads_ref, bf16[128,512]{1,0:T(8,128)(2,1)} %copy-done.1), custom_call_target="tpu_custom_call" | custom-call | flops 536870912 | bytes 5242880 | tf_op jit(solution)/shard_map/pallas_call | solution.py:263
  99.9 1.2 collective-permute-done.11.came_ref
  101.8 3.3 %shard_map.114 = (f32[128,512]{1,0:T(8,128)}, bf16[2,128,128]{2,1,0:T(8,128)(2,1)}, bf16[2,128,128]{2,1,0:T(8,128)(2,1)}) custom-call(s32[2]{0:T(128)} %pad_add_fusion.refs_0_.place, f32[128,512]{1,0:T(8,128)} %get-tuple-element.65.kept_ref, f32[128,512]{1,0:T(8,128)} %copy-done.4, f32[4,128,128]{2,1,0:T(8,128)} %get-tuple-element.53.qt_ref), custom_call_target="tpu_custom_call" | custom-call | flops 16777216 | bytes 1048576 | tf_op jit(solution)/shard_map/pallas_call | solution.py:348
  107.9 1.3 collective-permute-start.13
  109.2 5.0 %shard_map.113 = bf16[8,256,256]{2,1,0:T(8,128)(2,1)} custom-call(s32[2]{0:T(128)} %pad_add_fusion.refs_0_.place, bf16[128,512]{1,0:T(8,128)(2,1)} %shard_map.112.heads_ref, bf16[128,512]{1,0:T(8,128)(2,1)} %copy-done.1, bf16[8,2,128,512]{3,2,1,0:T(8,128)(2,1)} %bitcast.22), custom_call_target="tpu_custom_call" | custom-call | flops 536870912 | bytes 3145728 | tf_op jit(solution)/shard_map/pallas_call | solution.py:288
  114.9 1.3 collective-permute-start.15
  117.2 5.7 %all-to-all-start.1 = ((bf16[8,256,256]{2,1,0:T(8,128)(2,1)}), bf16[8,256,256]{2,1,0:T(8,128)(2,1)S(1)}, u32[]{:S(2)}, u32[]{:S(2)}) async-start(bf16[8,256,256]{2,1,0:T(8,128)(2,1)} %shard_map.113), calls=%async_computation.1 | async-start | bytes 2097152 | tf_op jit(solution)/shard_map/all_to_all | solution.py:551
  124.5 1.3 collective-permute-start.18
  125.8 1.3 collective-permute-start.19
  127.1 1.3 collective-permute-start.17
  128.4 1.3 collective-permute-start.16
  129.7 8.6 %collective-permute-done.18 = bf16[2,128,128]{2,1,0:T(8,128)(2,1)S(1)} collective-permute-done((bf16[2,128,128]{2,1,0:T(8,128)(2,1)S(1)}, bf16[2,128,128]{2,1,0:T(8,128)(2,1)S(1)}, u32[]{:S(2)}, u32[]{:S(2)}) %collective-permute-start.18) | collective-permute-done | bytes 65568 | tf_op jit(solution)/shard_map/ppermute | solution.py:21
  138.6 2.5 %collective-permute-start.20 = (bf16[2,128,128]{2,1,0:T(8,128)(2,1)S(1)}, bf16[2,128,128]{2,1,0:T(8,128)(2,1)S(1)}, u32[]{:S(2)}, u32[]{:S(2)}) collective-permute-start(bf16[2,128,128]{2,1,0:T(8,128)(2,1)S(1)} %get-tuple-element.85), channel_id=1, source_target_pairs={{0,8},{8,0},{16,24},{24,16},{32,40},{40,32},{48,56},{56,48},{64,72... | collective-permute-start | bytes 196616 | tf_op jit(solution)/shard_map/ppermute | solution.py:26
  144.3 7.9 %collective-permute-start.21 = (bf16[128,512]{1,0:T(8,128)(2,1)S(1)}, bf16[128,512]{1,0:T(8,128)(2,1)S(1)}, u32[]{:S(2)}, u32[]{:S(2)}) collective-permute-start(bf16[128,512]{1,0:T(8,128)(2,1)S(1)} %slice_bitcast_fusion), channel_id=1, source_target_pairs={{0,128},{8,136},{16,144},{24,152},{32,160},{40,168},{48,176},{56,1... | collective-permute-start | bytes 393224 | tf_op jit(solution)/shard_map/ppermute | solution.py:26
  152.2 6.3 %shard_map.116 = (bf16[128,512]{1,0:T(8,128)(2,1)}, bf16[128,1024]{1,0:T(8,128)(2,1)}, bf16[128,1024]{1,0:T(8,128)(2,1)}, f32[4,256]{1,0:T(4,128)}) custom-call(s32[2]{0:T(128)} %pad_add_fusion.refs_0_.place, bf16[128,512]{1,0:T(8,128)(2,1)} %q_ref.1, bf16[128,1024]{1,0:T(8,128)(2,1)} %k_ref.1, f32[4,256]{1,0:T(4,128)} %logit_ref.1, ...), custom_call_target="tpu_custom_call" | custom-call | flops 1879048192 | bytes 5242880 | tf_op jit(solution)/shard_map/pallas_call | solution.py:420
  (82 shorter events, 22.5 us)
Async XLA Ops:
  7.2 71.7 %all-gather.3.cloned.1.call-start = ((), (), s32[]{:S(2)}) async-start(), calls=%async_computation.4 | async-start | bytes 2359296 | tf_op jit(solution)/shard_map/all_gather | solution.py:533
  7.2 10.6 %collective-permute-start = (bf16[128,512]{1,0:T(8,128)(2,1)}, bf16[128,512]{1,0:T(8,128)(2,1)S(1)}, u32[]{:S(2)}, u32[]{:S(2)}) collective-permute-start(bf16[128,512]{1,0:T(8,128)(2,1)} %param.10), channel_id=1, source_target_pairs={{0,128},{8,136},{16,144},{24,152},{32,160},{40,168},{48,176},{56,1... | collective-permute-start | bytes 393224 | tf_op jit(solution)/shard_map/ppermute | solution.py:26
  19.5 7.4 %collective-permute-start.1 = (bf16[2,128,256]{2,1,0:T(8,128)(2,1)}, bf16[2,128,256]{2,1,0:T(8,128)(2,1)S(1)}, u32[]{:S(2)}, u32[]{:S(2)}) collective-permute-start(bf16[2,128,256]{2,1,0:T(8,128)(2,1)} %get-tuple-element.55), channel_id=1, source_target_pairs={{0,8},{8,0},{16,24},{24,16},{32,40},{40,32},{48,56},{56,48},{64,72... | collective-permute-start | bytes 393224 | tf_op jit(solution)/shard_map/ppermute | solution.py:26
  20.5 16.0 %copy-start.5 = (bf16[128,512]{1,0:T(8,128)(2,1)S(1)}, bf16[128,512]{1,0:T(8,128)(2,1)}, u32[]{:S(2)}) copy-start(bf16[128,512]{1,0:T(8,128)(2,1)} %param.11) | copy-start | bytes 393220
  28.1 13.8 %collective-permute-start.3 = (bf16[2,128,256]{2,1,0:T(8,128)(2,1)S(1)}, bf16[2,128,256]{2,1,0:T(8,128)(2,1)S(1)}, u32[]{:S(2)}, u32[]{:S(2)}) collective-permute-start(bf16[2,128,256]{2,1,0:T(8,128)(2,1)S(1)} %pad_maximum_fusion.1), channel_id=1, source_target_pairs={{0,32},{8,40},{16,48},{24,56},{32,64},{40,72},{48,80},{56,88},{64,... | collective-permute-start | bytes 393224 | tf_op jit(solution)/shard_map/ppermute | solution.py:21
  33.0 12.7 %collective-permute-start.2 = (bf16[2,128,256]{2,1,0:T(8,128)(2,1)S(1)}, bf16[2,128,256]{2,1,0:T(8,128)(2,1)S(1)}, u32[]{:S(2)}, u32[]{:S(2)}) collective-permute-start(bf16[2,128,256]{2,1,0:T(8,128)(2,1)S(1)} %pad_maximum_fusion.1), channel_id=1, source_target_pairs={{0,16},{8,24},{16,32},{24,40},{32,48},{40,56},{48,64},{56,72},{64,... | collective-permute-start | bytes 393224 | tf_op jit(solution)/shard_map/ppermute | solution.py:21
  37.7 25.3 %all-to-all-start = ((bf16[8,128,512]{2,1,0:T(8,128)(2,1)}), bf16[8,128,512]{2,1,0:T(8,128)(2,1)S(1)}, u32[]{:S(2)}, u32[]{:S(2)}) async-start(bf16[8,128,512]{2,1,0:T(8,128)(2,1)} %broadcast_in_dim.2), calls=%async_computation | async-start | bytes 2097152 | tf_op jit(solution)/shard_map/all_to_all | solution.py:534
  41.9 101.5 %reduce-scatter.2.cloned.1.call-start = ((), (), s32[]{:S(2)}) async-start(), calls=%async_computation.3 | async-start | bytes 2359296 | tf_op jit(solution)/shard_map/reduce_scatter | solution.py:543
  45.9 16.2 %collective-permute-start.4 = (bf16[2,128,256]{2,1,0:T(8,128)(2,1)S(1)}, bf16[2,128,256]{2,1,0:T(8,128)(2,1)S(1)}, u32[]{:S(2)}, u32[]{:S(2)}) collective-permute-start(bf16[2,128,256]{2,1,0:T(8,128)(2,1)S(1)} %pad_maximum_fusion.2), channel_id=1, source_target_pairs={{0,32},{8,40},{16,48},{24,56},{32,64},{40,72},{48,80},{56,88},{64,... | collective-permute-start | bytes 393224 | tf_op jit(solution)/shard_map/ppermute | solution.py:21
  63.0 15.9 %copy-start = (bf16[8,128,512]{2,1,0:T(8,128)(2,1)}, bf16[8,128,512]{2,1,0:T(8,128)(2,1)S(1)}, u32[]{:S(2)}) copy-start(bf16[8,128,512]{2,1,0:T(8,128)(2,1)S(1)} %all-to-all-done.own_ref) | copy-start | bytes 3145732
  63.0 15.9 %collective-permute-start.5 = (bf16[8,128,512]{2,1,0:T(8,128)(2,1)S(1)}, bf16[8,128,512]{2,1,0:T(8,128)(2,1)}, u32[]{:S(2)}, u32[]{:S(2)}) collective-permute-start(bf16[8,128,512]{2,1,0:T(8,128)(2,1)S(1)} %all-to-all-done.own_ref), channel_id=1, source_target_pairs={{0,8},{8,0},{16,24},{24,16},{32,40},{40,32},{48,56},{56,48},{64,72... | collective-permute-start | bytes 3145736 | tf_op jit(solution)/shard_map/ppermute | solution.py:26
  63.7 20.6 %collective-permute-start.7 = (bf16[2,128,256]{2,1,0:T(8,128)(2,1)}, bf16[2,128,256]{2,1,0:T(8,128)(2,1)}, u32[]{:S(2)}, u32[]{:S(2)}) collective-permute-start(bf16[2,128,256]{2,1,0:T(8,128)(2,1)} %pad_maximum_fusion.3), channel_id=1, source_target_pairs={{0,128},{8,136},{16,144},{24,152},{32,160},{40,168},{48,176},{56,1... | collective-permute-start | bytes 393224 | tf_op jit(solution)/shard_map/ppermute | solution.py:21
  73.8 10.5 %collective-permute-start.6 = (bf16[2,128,256]{2,1,0:T(8,128)(2,1)}, bf16[2,128,256]{2,1,0:T(8,128)(2,1)}, u32[]{:S(2)}, u32[]{:S(2)}) collective-permute-start(bf16[2,128,256]{2,1,0:T(8,128)(2,1)} %pad_maximum_fusion.3), channel_id=1, source_target_pairs={{0,64},{8,72},{16,80},{24,88},{32,96},{40,104},{48,112},{56,120},{... | collective-permute-start | bytes 393224 | tf_op jit(solution)/shard_map/ppermute | solution.py:21
  77.0 7.2 %collective-permute-start.8 = (bf16[2,128,128]{2,1,0:T(8,128)(2,1)S(1)}, bf16[2,128,128]{2,1,0:T(8,128)(2,1)}, u32[]{:S(2)}, u32[]{:S(2)}) collective-permute-start(bf16[2,128,128]{2,1,0:T(8,128)(2,1)S(1)} %fusion.30), channel_id=1, source_target_pairs={{0,192},{8,200},{16,208},{24,216},{32,224},{40,232},{48,240},{56,2... | collective-permute-start | bytes 196616 | tf_op jit(solution)/shard_map/ppermute | solution.py:21
  86.7 1.6 collective-permute-start.9
  91.5 1.6 collective-permute-start.10
  98.6 0.9 copy-start.6
  99.6 1.5 collective-permute-start.11
  101.1 0.7 copy-start.4
  105.1 1.5 collective-permute-start.12
  107.9 6.8 %collective-permute-start.13 = (bf16[2,128,128]{2,1,0:T(8,128)(2,1)S(1)}, bf16[2,128,128]{2,1,0:T(8,128)(2,1)S(1)}, u32[]{:S(2)}, u32[]{:S(2)}) collective-permute-start(bf16[2,128,128]{2,1,0:T(8,128)(2,1)S(1)} %convolution_convert_fusion.6), channel_id=1, source_target_pairs={{16,0},{24,8},{32,16},{40,24},{48,32},{56,40},{64,48},{72,56},{80,... | collective-permute-start | bytes 196616 | tf_op jit(solution)/shard_map/ppermute | solution.py:21
  114.2 24.1 %copy-start.2 = (bf16[2,128,128]{2,1,0:T(8,128)(2,1)S(1)}, bf16[2,128,128]{2,1,0:T(8,128)(2,1)}, u32[]{:S(2)}) copy-start(bf16[2,128,128]{2,1,0:T(8,128)(2,1)} %get-tuple-element.67) | copy-start | bytes 196612
  114.9 8.0 %collective-permute-start.15 = (bf16[2,128,128]{2,1,0:T(8,128)(2,1)S(1)}, bf16[2,128,128]{2,1,0:T(8,128)(2,1)S(1)}, u32[]{:S(2)}, u32[]{:S(2)}) collective-permute-start(bf16[2,128,128]{2,1,0:T(8,128)(2,1)S(1)} %convolution_convert_fusion.5), channel_id=1, source_target_pairs={{32,0},{40,8},{48,16},{56,24},{64,32},{72,40},{80,48},{88,56},{96,... | collective-permute-start | bytes 196616 | tf_op jit(solution)/shard_map/ppermute | solution.py:21
  117.2 23.9 %all-to-all-start.1 = ((bf16[8,256,256]{2,1,0:T(8,128)(2,1)}), bf16[8,256,256]{2,1,0:T(8,128)(2,1)S(1)}, u32[]{:S(2)}, u32[]{:S(2)}) async-start(bf16[8,256,256]{2,1,0:T(8,128)(2,1)} %shard_map.113), calls=%async_computation.1 | async-start | bytes 2097152 | tf_op jit(solution)/shard_map/all_to_all | solution.py:551
  124.5 13.8 %collective-permute-start.18 = (bf16[2,128,128]{2,1,0:T(8,128)(2,1)S(1)}, bf16[2,128,128]{2,1,0:T(8,128)(2,1)S(1)}, u32[]{:S(2)}, u32[]{:S(2)}) collective-permute-start(bf16[2,128,128]{2,1,0:T(8,128)(2,1)S(1)} %convolution_convert_fusion.2), channel_id=1, source_target_pairs={{144,0},{152,8},{160,16},{168,24},{176,32},{184,40},{192,48},{200,... | collective-permute-start | bytes 196616 | tf_op jit(solution)/shard_map/ppermute | solution.py:21
  125.8 12.5 %collective-permute-start.19 = (bf16[2,128,128]{2,1,0:T(8,128)(2,1)S(1)}, bf16[2,128,128]{2,1,0:T(8,128)(2,1)S(1)}, u32[]{:S(2)}, u32[]{:S(2)}) collective-permute-start(bf16[2,128,128]{2,1,0:T(8,128)(2,1)S(1)} %convolution_convert_fusion), channel_id=1, source_target_pairs={{208,0},{216,8},{224,16},{232,24},{240,32},{248,40},{209,1},{217,9... | collective-permute-start | bytes 196616 | tf_op jit(solution)/shard_map/ppermute | solution.py:21
  127.1 11.2 %collective-permute-start.17 = (bf16[2,128,128]{2,1,0:T(8,128)(2,1)S(1)}, bf16[2,128,128]{2,1,0:T(8,128)(2,1)S(1)}, u32[]{:S(2)}, u32[]{:S(2)}) collective-permute-start(bf16[2,128,128]{2,1,0:T(8,128)(2,1)S(1)} %convolution_convert_fusion.4), channel_id=1, source_target_pairs={{80,0},{88,8},{96,16},{104,24},{112,32},{120,40},{128,48},{136,56}... | collective-permute-start | bytes 196616 | tf_op jit(solution)/shard_map/ppermute | solution.py:21
  128.4 9.9 %collective-permute-start.16 = (bf16[2,128,128]{2,1,0:T(8,128)(2,1)S(1)}, bf16[2,128,128]{2,1,0:T(8,128)(2,1)S(1)}, u32[]{:S(2)}, u32[]{:S(2)}) collective-permute-start(bf16[2,128,128]{2,1,0:T(8,128)(2,1)S(1)} %add_convert_fusion.2), channel_id=1, source_target_pairs={{16,0},{24,8},{32,16},{40,24},{48,32},{56,40},{64,48},{72,56},{80,... | collective-permute-start | bytes 196616 | tf_op jit(solution)/shard_map/ppermute | solution.py:21
  138.6 3.4 %collective-permute-start.20 = (bf16[2,128,128]{2,1,0:T(8,128)(2,1)S(1)}, bf16[2,128,128]{2,1,0:T(8,128)(2,1)S(1)}, u32[]{:S(2)}, u32[]{:S(2)}) collective-permute-start(bf16[2,128,128]{2,1,0:T(8,128)(2,1)S(1)} %get-tuple-element.85), channel_id=1, source_target_pairs={{0,8},{8,0},{16,24},{24,16},{32,40},{40,32},{48,56},{56,48},{64,72... | collective-permute-start | bytes 196616 | tf_op jit(solution)/shard_map/ppermute | solution.py:26
  141.3 1.4 collective-permute-start.14
  144.3 14.2 %collective-permute-start.21 = (bf16[128,512]{1,0:T(8,128)(2,1)S(1)}, bf16[128,512]{1,0:T(8,128)(2,1)S(1)}, u32[]{:S(2)}, u32[]{:S(2)}) collective-permute-start(bf16[128,512]{1,0:T(8,128)(2,1)S(1)} %slice_bitcast_fusion), channel_id=1, source_target_pairs={{0,128},{8,136},{16,144},{24,152},{32,160},{40,168},{48,176},{56,1... | collective-permute-start | bytes 393224 | tf_op jit(solution)/shard_map/ppermute | solution.py:26
  152.2 6.3 %copy-start.3 = (bf16[1,256,512]{2,1,0:T(8,128)(2,1)S(1)}, bf16[1,256,512]{2,1,0:T(8,128)(2,1)}, u32[]{:S(2)}) copy-start(bf16[1,256,512]{2,1,0:T(8,128)(2,1)} %reduce-scatter.2.cloned.1.call-done) | copy-start | bytes 786436
  (1 other events, 0.7 us)
Sparse Core Ops, SparseCore 0:
  19.6 51.3 all-gather.2
  98.8 42.5 reduce-scatter.1

commit v7 on v6

--- a/solution.py
+++ b/solution.py
@@ -199,33 +199,53 @@
         input_output_aliases={5 + i: 1 + i for i in range(len(filled))},
         compiler_params=pltpu.CompilerParams(vmem_limit_bytes=VMEM),
         cost_estimate=pl.CostEstimate(
-            flops=(1 if mine else 100) << 20, bytes_accessed=1 << (16 if mine else 24), transcendentals=0
+            flops=1 << 20, bytes_accessed=1 << 16, transcendentals=0
         ),
     )(place, queries, keys, values, logits, *filled)
 
 
 STEPS = 4
-BLOCKS = [(z, row) for z in range(2) for row in range(2)]
-
-
-def grad_rows(place, step, own_ref, other_ref):
-    def block(ref, z, row):
-        column = pl.multiple_of(z * 256 + place[0] * 128, 128)
-        return ref[(row ^ place[1]) * 4 + step, :, pl.ds(column, 128)]
-
-    rows = [
-        jnp.concatenate([block(ref, *place_of) for place_of in BLOCKS], axis=1)
-        for ref in (own_ref, other_ref)
+
+
+def feature_columns(ref, place, owner):
+    blocks = [ref[owner, :, pl.ds(pl.multiple_of(z * 256 + place[0] * 128, 128), 128)] for z in range(2)]
+    return jnp.concatenate(blocks, axis=1)
+
+
+def pack_kernel(place, own_ref, other_ref, out_ref):
+    owner = (1 - place[1]) * 4 + pl.program_id(0)
+    out_ref[0, 0] = feature_columns(own_ref, place, owner)
+    out_ref[0, 1] = feature_columns(other_ref, place, owner)
+
+
+def pack(place, grad_full, grad_other):
+    return call(
+        pack_kernel,
+        STEPS,
+        [whole(8, WIDTH, 512), whole(8, WIDTH, 512)],
+        pl.BlockSpec((1, 2, WIDTH, 256), lambda step, place: (step, 0, 0, 0)),
+        arr(BF16, 4, 2, WIDTH, 256),
+        1 << 20,
+        3 << 20,
+    )(place, grad_full, grad_other)
+
+
+def grad_rows(place, own_ref, other_ref, across_ref):
+    owner = place[1] * 4 + pl.program_id(0)
+    rows = [feature_columns(ref, place, owner) for ref in (own_ref, other_ref)]
+    return jnp.concatenate(rows + [across_ref[0, 0], across_ref[0, 1]], axis=0)
+
+
+def grad_specs():
+    return [
+        whole(8, WIDTH, 512),
+        whole(8, WIDTH, 512),
+        pl.BlockSpec((1, 2, WIDTH, 256), lambda step, place: (step, 0, 0, 0)),
     ]
-    return jnp.concatenate(rows, axis=0)
-
-
-def weight_rows(ref):
-    return jnp.concatenate([ref[z, row] for z, row in BLOCKS], axis=0)
 
 
 def weight_tile():
-    return pl.BlockSpec((2, 2, WIDTH, 512), lambda step, place: (step, 0, 0, 0))
+    return pl.BlockSpec((2, WIDTH, 512), lambda step, place: (step, 0, 0))
 
 
 def heads_kernel(place, qt_ref, local_ref, state_ref, heads_ref):
@@ -247,89 +267,94 @@
     )(place, qt, local, state)
 
 
-def weight_terms_kernel(place, own_ref, other_ref, heads_ref, heads_other_ref, out_ref):
+def weight_terms_kernel(place, own_ref, other_ref, across_ref, heads_ref, heads_across_ref, out_ref):
     product = lax.dot_general(
-        grad_rows(place, pl.program_id(0), own_ref, other_ref),
-        jnp.concatenate([heads_ref[...], heads_other_ref[...]], axis=0),
+        grad_rows(place, own_ref, other_ref, across_ref),
+        jnp.concatenate([heads_ref[0], heads_ref[1], heads_across_ref[0], heads_across_ref[1]], axis=0),
         (((0,), (0,)), ((), ())),
         preferred_element_type=F32,
     )
     product = (product * (1.0 / 64.0)).astype(BF16)
-    for z in range(2):
-        out_ref[z] = product[z * 256 : z * 256 + 256]
-
-
-def weight_terms(place, grad_full, grad_other, heads, heads_other):
+    out_ref[0] = product[:WIDTH]
+    out_ref[1] = product[WIDTH:]
+
+
+def weight_terms(place, grads, heads, heads_across):
     return call(
         weight_terms_kernel,
         STEPS,
-        [whole(8, WIDTH, 512), whole(8, WIDTH, 512), whole(WIDTH, 512), whole(WIDTH, 512)],
-        pl.BlockSpec((2, 256, 512), lambda step, place: (step, 0, 0)),
-        arr(BF16, 8, 256, 512),
+        grad_specs() + [whole(2, WIDTH, 512), whole(2, WIDTH, 512)],
+        weight_tile(),
+        arr(BF16, 8, WIDTH, 512),
         2 * 128 * 512 * 4096,
-        5 << 20,
-    )(place, grad_full, grad_other, heads, heads_other)
-
-
-def mixed_kernel(place, heads_ref, heads_other_ref, weight_ref, out_ref):
+        4 << 20,
+    )(place, *grads, heads, heads_across)
+
+
+def mixed_kernel(place, heads_ref, weight_ref, across_ref, out_ref):
     step = pl.program_id(0)
+    rows = [ref[z] for ref in (weight_ref, across_ref) for z in range(2)]
     product = lax.dot_general(
-        jnp.concatenate([heads_ref[...], heads_other_ref[...]], axis=0),
-        weight_rows(weight_ref),
+        jnp.concatenate([heads_ref[0], heads_ref[1]], axis=0),
+        jnp.concatenate(rows, axis=0),
         (((1,), (1,)), ((), ())),
         preferred_element_type=F32,
     ).astype(BF16)
-    for i, (z, row) in enumerate(BLOCKS):
-        owner = (row ^ place[1]) * 4 + step
-        out_ref[owner, :, z * 128 : z * 128 + 128] = product[:, i * WIDTH : (i + 1) * WIDTH]
-
-
-def mixed_parts(place, heads, heads_other, weight):
+    out_ref[place[1] * 4 + step] = product[:, :256]
+    out_ref[(1 - place[1]) * 4 + step] = product[:, 256:]
+
+
+def mixed_parts(place, heads, weight, weight_across):
     return call(
         mixed_kernel,
         STEPS,
-        [whole(WIDTH, 512), whole(WIDTH, 512), weight_tile()],
+        [whole(2, WIDTH, 512), weight_tile(), weight_tile()],
         whole(8, 256, 256),
         arr(BF16, 8, 256, 256),
         2 * 128 * 512 * 4096,
         3 << 20,
-    )(place, heads, heads_other, weight)
-
-
-def head_grad_kernel(place, own_ref, other_ref, weight_ref, kept_ref, given_ref):
+    )(place, heads, weight, weight_across)
+
+
+def head_grad_kernel(place, own_ref, other_ref, across_ref, weight_ref, kept_ref, given_ref):
     step = pl.program_id(0)
     total = jnp.dot(
-        grad_rows(place, step, own_ref, other_ref),
-        weight_rows(weight_ref),
+        grad_rows(place, own_ref, other_ref, across_ref),
+        jnp.concatenate([weight_ref[0], weight_ref[1]], axis=0),
         preferred_element_type=F32,
     )
+    parts = [total[i * WIDTH : (i + 1) * WIDTH] for i in range(4)]
 
     @pl.when(step == 0)
     def _():
-        kept_ref[...] = total[:WIDTH]
-        given_ref[...] = total[WIDTH:]
+        kept_ref[0] = parts[0]
+        kept_ref[1] = parts[2]
+        given_ref[0] = parts[1]
+        given_ref[1] = parts[3]
 
     @pl.when(step > 0)
     def _():
-        kept_ref[...] += total[:WIDTH]
-        given_ref[...] += total[WIDTH:]
-
-
-def head_gradient(place, grad_full, grad_other, weight):
-    part = arr(F32, WIDTH, 512)
+        kept_ref[0] += parts[0]
+        kept_ref[1] += parts[2]
+        given_ref[0] += parts[1]
+        given_ref[1] += parts[3]
+
+
+def head_gradient(place, grads, weight):
+    part = arr(F32, 2, WIDTH, 512)
     return call(
         head_grad_kernel,
         STEPS,
-        [whole(8, WIDTH, 512), whole(8, WIDTH, 512), weight_tile()],
-        [whole(WIDTH, 512), whole(WIDTH, 512)],
+        grad_specs() + [weight_tile()],
+        [whole(2, WIDTH, 512), whole(2, WIDTH, 512)],
         [part, part],
         2 * 128 * 512 * 4096,
-        5 << 20,
-    )(place, grad_full, grad_other, weight)
+        4 << 20,
+    )(place, *grads, weight)
 
 
 def own_kernel(place, kept_ref, came_ref, qt_ref, grad_ref, mine_ref, theirs_ref):
-    grad_ref[...] = kept_ref[...] + came_ref[...]
+    grad_ref[...] = kept_ref[...] + came_ref[...].astype(F32)
     for head in range(4):
         grad = grad_ref[:, head * WIDTH : (head + 1) * WIDTH]
         own = dot(qt_ref[head], grad, 0, 0, passes=1).astype(BF16)
@@ -464,7 +489,10 @@
     chip = jnp.concatenate(
         [joined[:, :, :WIDTH], joined[:, :, WIDTH:] + odd_b.astype(F32)], axis=2
     ).astype(BF16)
+    grad_full, chip = lax.optimization_barrier((grad_full, chip))
     one, two = send(chip, 2), send(chip, 4)
+    grad_other = exchange(grad_full, 1)
+    grads = (grad_full, grad_other, exchange(pack(place, grad_full, grad_other), 16))
     window1, state = halves(one)
     step = mul(window1, two)
     state = state.astype(F32) + step[:, :, WIDTH:]
@@ -474,16 +502,16 @@
     window4 = step[:, :, :WIDTH].astype(BF16)
     rounded = state.astype(BF16)
     both = jnp.concatenate([window4, rounded], axis=2)
-    grad_full, both = lax.optimization_barrier((grad_full, both))
     near, mid, far_b = send(both, 8), send(both, 16), send(rounded, 24)
-    grad_other = exchange(grad_full, 1)
-    kept_grad, given_grad = head_gradient(place, grad_full, grad_other, weight)
+    kept_grad, given_grad = head_gradient(place, grads, weight)
     kept_grad, given_grad, near, mid, far_b = lax.optimization_barrier(
         (kept_grad, given_grad, near, mid, far_b)
     )
     near_a, near_b = halves(near)
     mid_a, mid_b = halves(mid)
-    head_grad = (kept_grad, exchange(given_grad, 1))
+    given_grad = exchange(given_grad, 1)
+    across_grad = exchange((kept_grad[1] + given_grad[1]).astype(BF16), 16)
+    head_grad = (kept_grad[0] + given_grad[0], across_grad)
     inner = (mid_b.astype(F32) + mul(mid_a, far_b)).astype(BF16)
     inner = (near_b.astype(F32) + mul(near_a, inner)).astype(BF16)
     first = (state + mul(window4, inner)).astype(BF16)
@@ -493,7 +521,7 @@
     kept = jnp.where(core == 0, first, second)
     given = jnp.where(core == 0, second, first)
     state_in = jnp.concatenate([kept, exchange(given, 1)], axis=0)
-    return grad_full, grad_other, head_grad, state_in, (even_a, odd_a, window1, window2, window4, window8, window12)
+    return grads, head_grad, state_in, (even_a, odd_a, window1, window2, window4, window8, window12)
 
 
 def backward_states(mine, theirs, core, saved, gate):
@@ -524,30 +552,22 @@
     place = jnp.stack([core, index >> 4]).astype(jnp.int32)
     rings = [[(half * 8 + z) * 2 + c for z in range(8)] for half in range(2) for c in range(2)]
     operands = (queries, keys, values, beta_logit)
-    across = exchange(out_weight, 16)
-    theirs, *filled = prepare(place, *operands, False)
-    across, theirs = lax.optimization_barrier((across, theirs))
-    weight_pair = jnp.stack([out_weight, across])
-    weight_pair, *operands = lax.optimization_barrier((weight_pair, *operands))
-    mine, reads, wy, qt, local_out = prepare(place, *operands, True, filled)
-    weight_mine = lax.all_gather(weight_pair, "ctx", axis=0, axis_index_groups=rings)
     grad_full = lax.all_to_all(
         jnp.broadcast_to(out_grad[None], (8, WIDTH, 512)), "tp", 0, 0, tiled=True
     )
-    grad_full, grad_other, head_grad, state, saved = forward_states(
-        place, mine, theirs, core, grad_full, weight_mine
-    )
+    weight = lax.all_gather(out_weight, "ctx", axis=0, axis_index_groups=rings)
+    theirs, *filled = prepare(place, *operands, False)
+    mine, reads, wy, qt, local_out = prepare(place, *operands, True, filled)
+    grads, head_grad, state, saved = forward_states(place, mine, theirs, core, grad_full, weight)
+    head_grad, own, own_theirs = own_cotangent(place, *head_grad, qt)
     heads = head_outputs(place, qt, local_out, state)
-    heads_other = exchange(heads, 1)
-    terms = weight_terms(place, grad_full, grad_other, heads, heads_other)
-    ring_sum = lax.psum_scatter(
+    heads = jnp.stack([heads, exchange(heads, 1)])
+    terms = weight_terms(place, grads, heads, exchange(heads, 16))
+    weight_grad = lax.psum_scatter(
         terms, "ctx", scatter_dimension=0, axis_index_groups=rings
-    ).reshape(2, WIDTH, 512)
-    head_grad, own, own_theirs = own_cotangent(place, *head_grad, qt)
-    parts = mixed_parts(place, heads, heads_other, weight_mine)
+    ).astype(F32)
+    parts = mixed_parts(place, heads, weight, exchange(weight, 16))
     parts, end = backward_states(own, own_theirs, core, saved, parts)
-    end, ring_sum = lax.optimization_barrier((end, ring_sum))
-    weight_grad = ring_sum[0].astype(F32) + exchange(ring_sum[1], 16).astype(F32)
     parts = lax.all_to_all(parts, "tp", 0, 0, tiled=True)
     sums = jnp.sum(parts.astype(F32), axis=0).astype(BF16)
     kept, came = sums[:WIDTH], exchange(sums[WIDTH:], 1)

time: 167 us -> 204 us (1.22)
  the two profiles are of different devices: /device:TPU:1 before, /device:TPU:4 now
where the time goes in v7:
time: 204 us; the launch traced here: 202 us
  waiting for transfers between devices  70.7 us (35%)
  starting transfers between devices  49.6 us (24%)
  Pallas kernels  44.4 us (22%)
  between operations  14.5 us (7%)
  matrix products  9.21 us (5%)
  other arithmetic  8.7 us (4%)
  local copies, waits for them, and re-layouts  5.23 us (3%)
    ppermute x12, starting transfers between devices, send(): return lax.ppermute(block, 'ctx', route)  36.2 us
    ppermute x12, waiting for transfers between devices, exchange(): return lax.ppermute(block, 'ctx', route)  27.8 us
    ppermute x12, waiting for transfers between devices, send(): return lax.ppermute(block, 'ctx', route)  25.5 us
    pallas_call x2, Pallas kernels, prepare(): pl.pallas_call(functools.partial(prepare_kernel, mine), grid_spec=pltpu.P...  12.6 us
    reduce_scatter x1, waiting for transfers between devices, local(): lax.psum_scatter(terms, 'ctx', scatter_dimension=0, axis_index_groups=rings)  8.94 us
    all_to_all x1, waiting for transfers between devices, local(): lax.all_to_all(jnp.broadcast_to(out_grad[None], (8, WIDTH, 512)), 'tp', 0...  7.72 us
    pallas_call x1, Pallas kernels, pull(): call(pull_kernel, 2, [by_columns(WIDTH), by_columns(PAIRS), whole(4, PAIR...  6.15 us
    pallas_call x1, Pallas kernels, head_gradient(): call(head_grad_kernel, STEPS, grad_specs() + [weight_tile()], [whole(2, W...  5.7 us
  transfers between devices with their start and end apart: 28, of which 9 were waited for; matrix products, arithmetic and copies ran while one was open for 8% of the time, Pallas kernels for 19%

profile of v7, /device:TPU:4, one launch (start us, length us, event | category | flops | bytes accessed | tf_op | source)
XLA Modules:
  0.0 202.4 jit_solution(7508755946953151206)
XLA Ops:
  7.8 6.4 %shard_map.109 = (bf16[2,128,256]{2,1,0:T(8,128)(2,1)}, f32[4,256,256]{2,1,0:T(8,128)}, f32[4,256,256]{2,1,0:T(8,128)}, f32[4,128,128]{2,1,0:T(8,128)}, f32[4,128,128]{2,1,0:T(8,128)}) custom-call(s32[2]{0:T(128)} %pad_add_fusion.refs_0_.place, bf16[128,512]{1,0:T(8,128)(2,1)} %q_ref.1, bf16[128,1024]{1,0:T(8,128)(2,1)} %k_ref.1, bf16[128,1024]{1,0:T(8,128)(2,1)} %refs_3_.3, ...), custom_call_target="tpu_custom_call" | custom-call | flops 1048576 | bytes 65536 | tf_op jit(solution)/shard_map/pallas_call | solution.py:172
  15.3 5.1 %all-to-all-start = ((bf16[8,128,512]{2,1,0:T(8,128)(2,1)}), bf16[8,128,512]{2,1,0:T(8,128)(2,1)S(1)}, u32[]{:S(2)}, u32[]{:S(2)}) async-start(bf16[8,128,512]{2,1,0:T(8,128)(2,1)} %broadcast_in_dim.2), calls=%async_computation | async-start | bytes 2097152 | tf_op jit(solution)/shard_map/all_to_all | solution.py:555
  21.2 6.2 %shard_map.110 = (bf16[2,128,256]{2,1,0:T(8,128)(2,1)}, f32[4,256,256]{2,1,0:T(8,128)}, f32[4,256,256]{2,1,0:T(8,128)}, f32[4,128,128]{2,1,0:T(8,128)}, f32[4,128,128]{2,1,0:T(8,128)}) custom-call(s32[2]{0:T(128)} %pad_add_fusion.refs_0_.place, bf16[128,512]{1,0:T(8,128)(2,1)} %q_ref.1, ...), custom_call_target="tpu_custom_call", output_to_operand_aliasing={{1}: (5, {}), {2}: (6, {}), {3}: (7, {}), {4}: (8, {})} | custom-call | flops 1048576 | bytes 65536 | tf_op jit(solution)/shard_map/pallas_call | solution.py:172
  29.1 7.7 %all-to-all-done.own_ref = bf16[8,128,512]{2,1,0:T(8,128)(2,1)S(1)} async-done(((bf16[8,128,512]{2,1,0:T(8,128)(2,1)}), bf16[8,128,512]{2,1,0:T(8,128)(2,1)S(1)}, u32[]{:S(2)}, u32[]{:S(2)}) %all-to-all-start) | async-done | bytes 1048608 | tf_op jit(solution)/shard_map/all_to_all | solution.py:555
  36.8 3.8 %collective-permute-start.1 = (bf16[2,128,256]{2,1,0:T(8,128)(2,1)S(1)}, bf16[2,128,256]{2,1,0:T(8,128)(2,1)S(1)}, u32[]{:S(2)}, u32[]{:S(2)}) collective-permute-start(bf16[2,128,256]{2,1,0:T(8,128)(2,1)S(1)} %pad_maximum_fusion.1), channel_id=1, source_target_pairs={{0,16},{8,24},{16,32},{24,40},{32,48},{40,56},{48,64},{56,72},{64,... | collective-permute-start | bytes 393224 | tf_op jit(solution)/shard_map/ppermute | solution.py:21
  40.6 5.2 %collective-permute-start.2 = (bf16[2,128,256]{2,1,0:T(8,128)(2,1)S(1)}, bf16[2,128,256]{2,1,0:T(8,128)(2,1)S(1)}, u32[]{:S(2)}, u32[]{:S(2)}) collective-permute-start(bf16[2,128,256]{2,1,0:T(8,128)(2,1)S(1)} %pad_maximum_fusion.1), channel_id=1, source_target_pairs={{0,32},{8,40},{16,48},{24,56},{32,64},{40,72},{48,80},{56,88},{64,... | collective-permute-start | bytes 393224 | tf_op jit(solution)/shard_map/ppermute | solution.py:21
  45.8 5.1 %collective-permute-done.1 = bf16[2,128,256]{2,1,0:T(8,128)(2,1)S(1)} collective-permute-done((bf16[2,128,256]{2,1,0:T(8,128)(2,1)S(1)}, bf16[2,128,256]{2,1,0:T(8,128)(2,1)S(1)}, u32[]{:S(2)}, u32[]{:S(2)}) %collective-permute-start.1) | collective-permute-done | bytes 131104 | tf_op jit(solution)/shard_map/ppermute | solution.py:21
  50.9 8.1 %collective-permute-done.2 = bf16[2,128,256]{2,1,0:T(8,128)(2,1)S(1)} collective-permute-done((bf16[2,128,256]{2,1,0:T(8,128)(2,1)S(1)}, bf16[2,128,256]{2,1,0:T(8,128)(2,1)S(1)}, u32[]{:S(2)}, u32[]{:S(2)}) %collective-permute-start.2) | collective-permute-done | bytes 131104 | tf_op jit(solution)/shard_map/ppermute | solution.py:21
  59.3 1.9 collective-permute-start.3
  61.2 3.6 %shard_map.111 = bf16[4,2,128,256]{3,2,1,0:T(8,128)(2,1)} custom-call(s32[2]{0:T(128)} %pad_add_fusion.refs_0_.place, bf16[8,128,512]{2,1,0:T(8,128)(2,1)} %copy-done, bf16[8,128,512]{2,1,0:T(8,128)(2,1)} %collective-permute-done.4.other_ref), custom_call_target="tpu_custom_call" | custom-call | flops 1048576 | bytes 3145728 | tf_op jit(solution)/shard_map/pallas_call | solution.py:222
  64.9 7.9 %collective-permute-done.3 = bf16[2,128,256]{2,1,0:T(8,128)(2,1)S(1)} collective-permute-done((bf16[2,128,256]{2,1,0:T(8,128)(2,1)S(1)}, bf16[2,128,256]{2,1,0:T(8,128)(2,1)S(1)}, u32[]{:S(2)}, u32[]{:S(2)}) %collective-permute-start.3) | collective-permute-done | bytes 131104 | tf_op jit(solution)/shard_map/ppermute | solution.py:21
  73.7 1.9 collective-permute-start.6
  75.6 1.3 collective-permute-start.7
  76.9 1.3 collective-permute-start.8
  78.2 4.1 %collective-permute-done.5.across_ref = bf16[4,2,128,256]{3,2,1,0:T(8,128)(2,1)S(1)} collective-permute-done((bf16[4,2,128,256]{3,2,1,0:T(8,128)(2,1)}, bf16[4,2,128,256]{3,2,1,0:T(8,128)(2,1)S(1)}, u32[]{:S(2)}, u32[]{:S(2)}) %collective-permute-start.5) | collective-permute-done | bytes 524320 | tf_op jit(solution)/shard_map/ppermute | solution.py:26
  83.1 5.7 %shard_map.112 = (f32[2,128,512]{2,1,0:T(8,128)}, f32[2,128,512]{2,1,0:T(8,128)}) custom-call(s32[2]{0:T(128)} %pad_add_fusion.refs_0_.place, bf16[8,128,512]{2,1,0:T(8,128)(2,1)} %copy-done, bf16[8,128,512]{2,1,0:T(8,128)(2,1)} %collective-permute-done.4.other_ref, bf16[4,2,128,256]{3,2,1,0:T(8,128)(2,1)} %copy-done.3, bf16[8,128,512]{2,1,0:T(8,128)(2,1)} %bitcast.22), custom_call_target="tpu_custom_call" | custom-call | flops 536870912 | bytes 4194304 | tf_op jit(solution)/shard_map/pallas_call | solution.py:345
  92.7 2.8 %collective-permute-start.13 = (bf16[128,512]{1,0:T(8,128)(2,1)S(1)}, bf16[128,512]{1,0:T(8,128)(2,1)S(1)}, u32[]{:S(2)}, u32[]{:S(2)}) collective-permute-start(bf16[128,512]{1,0:T(8,128)(2,1)S(1)} %get-tuple-element.62), channel_id=1, source_target_pairs={{0,128},{8,136},{16,144},{24,152},{32,160},{40,168},{48,176},{56,1... | collective-permute-start | bytes 393224 | tf_op jit(solution)/shard_map/ppermute | solution.py:26
  96.4 22.5 %collective-permute-done.13.came_ref = bf16[128,512]{1,0:T(8,128)(2,1)S(1)} collective-permute-done((bf16[128,512]{1,0:T(8,128)(2,1)S(1)}, bf16[128,512]{1,0:T(8,128)(2,1)S(1)}, u32[]{:S(2)}, u32[]{:S(2)}) %collective-permute-start.13) | collective-permute-done | bytes 131104 | tf_op jit(solution)/shard_map/ppermute | solution.py:26
  119.5 3.3 %shard_map.115 = (f32[128,512]{1,0:T(8,128)}, bf16[2,128,128]{2,1,0:T(8,128)(2,1)}, bf16[2,128,128]{2,1,0:T(8,128)(2,1)}) custom-call(s32[2]{0:T(128)} %pad_add_fusion.refs_0_.place, f32[128,512]{1,0:T(8,128)} %get-tuple-element.63.kept_ref, bf16[128,512]{1,0:T(8,128)(2,1)} %copy-done.14, f32[4,128,128]{2,1,0:T(8,128)} %get-tuple-element.38.qt_ref), custom_call_target="tpu_custom_call" | custom-call | flops 16777216 | bytes 1048576 | tf_op jit(solution)/shard_map/pallas_call | solution.py:373
  122.8 1.5 pad_maximum_fusion.4.state_ref
  124.3 2.7 %shard_map.113 = bf16[128,512]{1,0:T(8,128)(2,1)} custom-call(s32[2]{0:T(128)} %pad_add_fusion.refs_0_.place, f32[4,128,128]{2,1,0:T(8,128)} %get-tuple-element.38.qt_ref, f32[4,128,128]{2,1,0:T(8,128)} %get-tuple-element.39.local_ref, bf16[4,128,128]{2,1,0:T(8,128)(2,1)} %pad_maximum_fusion.4.state_ref), custom_call_target="tpu_custom_call" | custom-call | flops 16777216 | bytes 1048576 | tf_op jit(solution)/shard_map/pallas_call | solution.py:259
  130.4 5.2 %collective-permute-start.15 = (bf16[2,128,128]{2,1,0:T(8,128)(2,1)}, bf16[2,128,128]{2,1,0:T(8,128)(2,1)}, u32[]{:S(2)}, u32[]{:S(2)}) collective-permute-start(bf16[2,128,128]{2,1,0:T(8,128)(2,1)} %convolution_convert_fusion.6), channel_id=1, source_target_pairs={{16,0},{24,8},{32,16},{40,24},{48,32},{56,40},{64,48},{72,56},{80,... | collective-permute-start | bytes 196616 | tf_op jit(solution)/shard_map/ppermute | solution.py:21
  136.3 4.9 %shard_map.114 = bf16[8,256,256]{2,1,0:T(8,128)(2,1)} custom-call(s32[2]{0:T(128)} %pad_add_fusion.refs_0_.place, bf16[2,128,512]{2,1,0:T(8,128)(2,1)} %copy-done.2, bf16[8,128,512]{2,1,0:T(8,128)(2,1)} %bitcast.23, bf16[8,128,512]{2,1,0:T(8,128)(2,1)} %collective-permute-done.11.across_ref), custom_call_target="tpu_custom_call" | custom-call | flops 536870912 | bytes 3145728 | tf_op jit(solution)/shard_map/pallas_call | solution.py:308
  142.3 4.9 %collective-permute-start.17 = (bf16[2,128,128]{2,1,0:T(8,128)(2,1)S(1)}, bf16[2,128,128]{2,1,0:T(8,128)(2,1)S(1)}, u32[]{:S(2)}, u32[]{:S(2)}) collective-permute-start(bf16[2,128,128]{2,1,0:T(8,128)(2,1)S(1)} %convolution_convert_fusion.5), channel_id=1, source_target_pairs={{32,0},{40,8},{48,16},{56,24},{64,32},{72,40},{80,48},{88,56},{96,... | collective-permute-start | bytes 196616 | tf_op jit(solution)/shard_map/ppermute | solution.py:21
  148.2 5.4 %shard_map.117 = bf16[8,128,512]{2,1,0:T(8,128)(2,1)} custom-call(s32[2]{0:T(128)} %pad_add_fusion.refs_0_.place, bf16[8,128,512]{2,1,0:T(8,128)(2,1)} %copy-done, bf16[8,128,512]{2,1,0:T(8,128)(2,1)} %collective-permute-done.4.other_ref, bf16[4,2,128,256]{3,2,1,0:T(8,128)(2,1)} %copy-done.3, bf16[2,128,512]{2,1,0:T(8,128)(2,1)} %copy-done.2, ...), custom_call_target="tpu_custom_call" | custom-call | flops 536870912 | bytes 4194304 | tf_op jit(solution)/shard_map/pallas_call | solution.py:283
  153.6 3.6 %all-to-all-start.1 = ((bf16[8,256,256]{2,1,0:T(8,128)(2,1)}), bf16[8,256,256]{2,1,0:T(8,128)(2,1)S(1)}, u32[]{:S(2)}, u32[]{:S(2)}) async-start(bf16[8,256,256]{2,1,0:T(8,128)(2,1)} %shard_map.114), calls=%async_computation.1 | async-start | bytes 2097152 | tf_op jit(solution)/shard_map/all_to_all | solution.py:571
  159.5 5.5 %collective-permute-start.19 = (bf16[2,128,128]{2,1,0:T(8,128)(2,1)S(1)}, bf16[2,128,128]{2,1,0:T(8,128)(2,1)S(1)}, u32[]{:S(2)}, u32[]{:S(2)}) collective-permute-start(bf16[2,128,128]{2,1,0:T(8,128)(2,1)S(1)} %convolution_convert_fusion.4), channel_id=1, source_target_pairs={{80,0},{88,8},{96,16},{104,24},{112,32},{120,40},{128,48},{136,56}... | collective-permute-start | bytes 196616 | tf_op jit(solution)/shard_map/ppermute | solution.py:21
  166.4 3.9 %collective-permute-start.18 = (bf16[2,128,128]{2,1,0:T(8,128)(2,1)S(1)}, bf16[2,128,128]{2,1,0:T(8,128)(2,1)S(1)}, u32[]{:S(2)}, u32[]{:S(2)}) collective-permute-start(bf16[2,128,128]{2,1,0:T(8,128)(2,1)S(1)} %add_convert_fusion.2), channel_id=1, source_target_pairs={{16,0},{24,8},{32,16},{40,24},{48,32},{56,40},{64,48},{72,56},{80,... | collective-permute-start | bytes 196616 | tf_op jit(solution)/shard_map/ppermute | solution.py:21
  170.3 4.3 %collective-permute-done.18 = bf16[2,128,128]{2,1,0:T(8,128)(2,1)S(1)} collective-permute-done((bf16[2,128,128]{2,1,0:T(8,128)(2,1)S(1)}, bf16[2,128,128]{2,1,0:T(8,128)(2,1)S(1)}, u32[]{:S(2)}, u32[]{:S(2)}) %collective-permute-start.18) | collective-permute-done | bytes 65568 | tf_op jit(solution)/shard_map/ppermute | solution.py:21
  178.1 6.1 %shard_map.116 = (bf16[128,512]{1,0:T(8,128)(2,1)}, bf16[128,1024]{1,0:T(8,128)(2,1)}, bf16[128,1024]{1,0:T(8,128)(2,1)}, f32[4,256]{1,0:T(4,128)}) custom-call(s32[2]{0:T(128)} %pad_add_fusion.refs_0_.place, bf16[128,512]{1,0:T(8,128)(2,1)} %q_ref.1, bf16[128,1024]{1,0:T(8,128)(2,1)} %k_ref.1, f32[4,256]{1,0:T(4,128)} %logit_ref.1, ...), custom_call_target="tpu_custom_call" | custom-call | flops 1879048192 | bytes 5242880 | tf_op jit(solution)/shard_map/pallas_call | solution.py:445
  184.9 8.9 %reduce-scatter.2.cloned.1.call-done = bf16[1,128,512]{2,1,0:T(8,128)(2,1)} async-done(((bf16[8,128,512]{2,1,0:T(8,128)(2,1)}), bf16[1,128,512]{2,1,0:T(8,128)(2,1)}) %reduce-scatter.2.cloned.1.call-update) | async-done | bytes 131088 | tf_op jit(solution)/shard_map/reduce_scatter | solution.py:566
  193.9 1.6 bitcast_convert_fusion
  (103 shorter events, 25.2 us)
Async XLA Ops:
  7.8 6.4 %copy-start.13 = (bf16[128,512]{1,0:T(8,128)(2,1)S(1)}, bf16[128,512]{1,0:T(8,128)(2,1)}, u32[]{:S(2)}) copy-start(bf16[128,512]{1,0:T(8,128)(2,1)} %param.11) | copy-start | bytes 393220
  14.2 13.2 %collective-permute-start = (bf16[2,128,256]{2,1,0:T(8,128)(2,1)}, bf16[2,128,256]{2,1,0:T(8,128)(2,1)S(1)}, u32[]{:S(2)}, u32[]{:S(2)}) collective-permute-start(bf16[2,128,256]{2,1,0:T(8,128)(2,1)} %get-tuple-element.40), channel_id=1, source_target_pairs={{0,8},{8,0},{16,24},{24,16},{32,40},{40,32},{48,56},{56,48},{64,72... | collective-permute-start | bytes 393224 | tf_op jit(solution)/shard_map/ppermute | solution.py:26
  15.3 21.5 %all-to-all-start = ((bf16[8,128,512]{2,1,0:T(8,128)(2,1)}), bf16[8,128,512]{2,1,0:T(8,128)(2,1)S(1)}, u32[]{:S(2)}, u32[]{:S(2)}) async-start(bf16[8,128,512]{2,1,0:T(8,128)(2,1)} %broadcast_in_dim.2), calls=%async_computation | async-start | bytes 2097152 | tf_op jit(solution)/shard_map/all_to_all | solution.py:555
  20.4 57.8 %all-gather.3.cloned.1.call-start = ((), (), s32[]{:S(2)}) async-start(), calls=%async_computation.4 | async-start | bytes 1179648 | tf_op jit(solution)/shard_map/all_gather | solution.py:558
  21.1 172.8 %reduce-scatter.2.cloned.1.call-start = ((), (), s32[]{:S(2)}) async-start(), calls=%async_computation.3 | async-start | bytes 1179648 | tf_op jit(solution)/shard_map/reduce_scatter | solution.py:566
  36.8 24.4 %copy-start = (bf16[8,128,512]{2,1,0:T(8,128)(2,1)}, bf16[8,128,512]{2,1,0:T(8,128)(2,1)S(1)}, u32[]{:S(2)}) copy-start(bf16[8,128,512]{2,1,0:T(8,128)(2,1)S(1)} %all-to-all-done.own_ref) | copy-start | bytes 3145732
  36.8 24.4 %collective-permute-start.4 = (bf16[8,128,512]{2,1,0:T(8,128)(2,1)S(1)}, bf16[8,128,512]{2,1,0:T(8,128)(2,1)}, u32[]{:S(2)}, u32[]{:S(2)}) collective-permute-start(bf16[8,128,512]{2,1,0:T(8,128)(2,1)S(1)} %all-to-all-done.own_ref), channel_id=1, source_target_pairs={{0,8},{8,0},{16,24},{24,16},{32,40},{40,32},{48,56},{56,48},{64,72... | collective-permute-start | bytes 3145736 | tf_op jit(solution)/shard_map/ppermute | solution.py:26
  36.8 14.1 %collective-permute-start.1 = (bf16[2,128,256]{2,1,0:T(8,128)(2,1)S(1)}, bf16[2,128,256]{2,1,0:T(8,128)(2,1)S(1)}, u32[]{:S(2)}, u32[]{:S(2)}) collective-permute-start(bf16[2,128,256]{2,1,0:T(8,128)(2,1)S(1)} %pad_maximum_fusion.1), channel_id=1, source_target_pairs={{0,16},{8,24},{16,32},{24,40},{32,48},{40,56},{48,64},{56,72},{64,... | collective-permute-start | bytes 393224 | tf_op jit(solution)/shard_map/ppermute | solution.py:21
  40.6 18.4 %collective-permute-start.2 = (bf16[2,128,256]{2,1,0:T(8,128)(2,1)S(1)}, bf16[2,128,256]{2,1,0:T(8,128)(2,1)S(1)}, u32[]{:S(2)}, u32[]{:S(2)}) collective-permute-start(bf16[2,128,256]{2,1,0:T(8,128)(2,1)S(1)} %pad_maximum_fusion.1), channel_id=1, source_target_pairs={{0,32},{8,40},{16,48},{24,56},{32,64},{40,72},{48,80},{56,88},{64,... | collective-permute-start | bytes 393224 | tf_op jit(solution)/shard_map/ppermute | solution.py:21
  59.3 13.5 %collective-permute-start.3 = (bf16[2,128,256]{2,1,0:T(8,128)(2,1)S(1)}, bf16[2,128,256]{2,1,0:T(8,128)(2,1)S(1)}, u32[]{:S(2)}, u32[]{:S(2)}) collective-permute-start(bf16[2,128,256]{2,1,0:T(8,128)(2,1)S(1)} %pad_maximum_fusion.2), channel_id=1, source_target_pairs={{0,32},{8,40},{16,48},{24,56},{32,64},{40,72},{48,80},{56,88},{64,... | collective-permute-start | bytes 393224 | tf_op jit(solution)/shard_map/ppermute | solution.py:21
  64.9 17.4 %collective-permute-start.5 = (bf16[4,2,128,256]{3,2,1,0:T(8,128)(2,1)}, bf16[4,2,128,256]{3,2,1,0:T(8,128)(2,1)S(1)}, u32[]{:S(2)}, u32[]{:S(2)}) collective-permute-start(bf16[4,2,128,256]{3,2,1,0:T(8,128)(2,1)} %shard_map.111), channel_id=1, source_target_pairs={{0,128},{8,136},{16,144},{24,152},{32,160},{40,168},{48,176},{56,1... | collective-permute-start | bytes 1572872 | tf_op jit(solution)/shard_map/ppermute | solution.py:26
  73.7 15.1 %collective-permute-start.6 = (bf16[2,128,256]{2,1,0:T(8,128)(2,1)}, bf16[2,128,256]{2,1,0:T(8,128)(2,1)}, u32[]{:S(2)}, u32[]{:S(2)}) collective-permute-start(bf16[2,128,256]{2,1,0:T(8,128)(2,1)} %pad_maximum_fusion.3), channel_id=1, source_target_pairs={{0,64},{8,72},{16,80},{24,88},{32,96},{40,104},{48,112},{56,120},{... | collective-permute-start | bytes 393224 | tf_op jit(solution)/shard_map/ppermute | solution.py:21
  75.6 13.2 %collective-permute-start.7 = (bf16[2,128,256]{2,1,0:T(8,128)(2,1)}, bf16[2,128,256]{2,1,0:T(8,128)(2,1)S(1)}, u32[]{:S(2)}, u32[]{:S(2)}) collective-permute-start(bf16[2,128,256]{2,1,0:T(8,128)(2,1)} %pad_maximum_fusion.3), channel_id=1, source_target_pairs={{0,128},{8,136},{16,144},{24,152},{32,160},{40,168},{48,176},{56,1... | collective-permute-start | bytes 393224 | tf_op jit(solution)/shard_map/ppermute | solution.py:21
  76.9 11.9 %collective-permute-start.8 = (bf16[2,128,128]{2,1,0:T(8,128)(2,1)S(1)}, bf16[2,128,128]{2,1,0:T(8,128)(2,1)}, u32[]{:S(2)}, u32[]{:S(2)}) collective-permute-start(bf16[2,128,128]{2,1,0:T(8,128)(2,1)S(1)} %fusion.33), channel_id=1, source_target_pairs={{0,192},{8,200},{16,208},{24,216},{32,224},{40,232},{48,240},{56,2... | collective-permute-start | bytes 196616 | tf_op jit(solution)/shard_map/ppermute | solution.py:21
  88.9 3.1 %collective-permute-start.12 = (f32[2,128,512]{2,1,0:T(8,128)}, f32[2,128,512]{2,1,0:T(8,128)S(1)}, u32[]{:S(2)}, u32[]{:S(2)}) collective-permute-start(f32[2,128,512]{2,1,0:T(8,128)} %get-tuple-element.50), channel_id=1, source_target_pairs={{0,8},{8,0},{16,24},{24,16},{32,40},{40,32},{48,56},{56,48},{64,72... | collective-permute-start | bytes 1572872 | tf_op jit(solution)/shard_map/ppermute | solution.py:26
  89.0 46.7 %collective-permute-start.11 = (bf16[8,128,512]{2,1,0:T(8,128)(2,1)S(1)}, bf16[8,128,512]{2,1,0:T(8,128)(2,1)}, u32[]{:S(2)}, u32[]{:S(2)}) collective-permute-start(bf16[8,128,512]{2,1,0:T(8,128)(2,1)S(1)} %bitcast.24), channel_id=1, source_target_pairs={{0,128},{8,136},{16,144},{24,152},{32,160},{40,168},{48,176},{56,1... | collective-permute-start | bytes 3145736 | tf_op jit(solution)/shard_map/ppermute | solution.py:26
  92.7 26.1 %collective-permute-start.13 = (bf16[128,512]{1,0:T(8,128)(2,1)S(1)}, bf16[128,512]{1,0:T(8,128)(2,1)S(1)}, u32[]{:S(2)}, u32[]{:S(2)}) collective-permute-start(bf16[128,512]{1,0:T(8,128)(2,1)S(1)} %get-tuple-element.62), channel_id=1, source_target_pairs={{0,128},{8,136},{16,144},{24,152},{32,160},{40,168},{48,176},{56,1... | collective-permute-start | bytes 393224 | tf_op jit(solution)/shard_map/ppermute | solution.py:26
  96.4 26.5 %collective-permute-start.9 = (bf16[2,128,128]{2,1,0:T(8,128)(2,1)}, bf16[2,128,128]{2,1,0:T(8,128)(2,1)}, u32[]{:S(2)}, u32[]{:S(2)}) collective-permute-start(bf16[2,128,128]{2,1,0:T(8,128)(2,1)} %get-tuple-element.71), channel_id=1, source_target_pairs={{0,8},{8,0},{16,24},{24,16},{32,40},{40,32},{48,56},{56,48},{64,72... | collective-permute-start | bytes 196616 | tf_op jit(solution)/shard_map/ppermute | solution.py:26
  122.8 4.8 %collective-permute-start.14 = (bf16[2,128,128]{2,1,0:T(8,128)(2,1)}, bf16[2,128,128]{2,1,0:T(8,128)(2,1)}, u32[]{:S(2)}, u32[]{:S(2)}) collective-permute-start(bf16[2,128,128]{2,1,0:T(8,128)(2,1)} %get-tuple-element.52), channel_id=1, source_target_pairs={{0,8},{8,0},{16,24},{24,16},{32,40},{40,32},{48,56},{56,48},{64,72... | collective-permute-start | bytes 196616 | tf_op jit(solution)/shard_map/ppermute | solution.py:26
  127.1 8.5 %collective-permute-start.10 = (bf16[128,512]{1,0:T(8,128)(2,1)}, bf16[128,512]{1,0:T(8,128)(2,1)S(1)}, u32[]{:S(2)}, u32[]{:S(2)}) collective-permute-start(bf16[128,512]{1,0:T(8,128)(2,1)} %shard_map.113), channel_id=1, source_target_pairs={{0,8},{8,0},{16,24},{24,16},{32,40},{40,32},{48,56},{56,48},{64,72... | collective-permute-start | bytes 393224 | tf_op jit(solution)/shard_map/ppermute | solution.py:26
  130.4 10.9 %collective-permute-start.15 = (bf16[2,128,128]{2,1,0:T(8,128)(2,1)}, bf16[2,128,128]{2,1,0:T(8,128)(2,1)}, u32[]{:S(2)}, u32[]{:S(2)}) collective-permute-start(bf16[2,128,128]{2,1,0:T(8,128)(2,1)} %convolution_convert_fusion.6), channel_id=1, source_target_pairs={{16,0},{24,8},{32,16},{40,24},{48,32},{56,40},{64,48},{72,56},{80,... | collective-permute-start | bytes 196616 | tf_op jit(solution)/shard_map/ppermute | solution.py:21
  135.6 12.6 %collective-permute-start.23 = (bf16[2,128,512]{2,1,0:T(8,128)(2,1)S(1)}, bf16[2,128,512]{2,1,0:T(8,128)(2,1)}, u32[]{:S(2)}, u32[]{:S(2)}) collective-permute-start(bf16[2,128,512]{2,1,0:T(8,128)(2,1)S(1)} %pad_maximum_fusion.heads_ref), channel_id=1, source_target_pairs={{0,128},{8,136},{16,144},{24,152},{32,160},{40,168},{48,176},{56,1... | collective-permute-start | bytes 786440 | tf_op jit(solution)/shard_map/ppermute | solution.py:26
  142.3 14.9 %collective-permute-start.17 = (bf16[2,128,128]{2,1,0:T(8,128)(2,1)S(1)}, bf16[2,128,128]{2,1,0:T(8,128)(2,1)S(1)}, u32[]{:S(2)}, u32[]{:S(2)}) collective-permute-start(bf16[2,128,128]{2,1,0:T(8,128)(2,1)S(1)} %convolution_convert_fusion.5), channel_id=1, source_target_pairs={{32,0},{40,8},{48,16},{56,24},{64,32},{72,40},{80,48},{88,56},{96,... | collective-permute-start | bytes 196616 | tf_op jit(solution)/shard_map/ppermute | solution.py:21
  153.6 24.0 %all-to-all-start.1 = ((bf16[8,256,256]{2,1,0:T(8,128)(2,1)}), bf16[8,256,256]{2,1,0:T(8,128)(2,1)S(1)}, u32[]{:S(2)}, u32[]{:S(2)}) async-start(bf16[8,256,256]{2,1,0:T(8,128)(2,1)} %shard_map.114), calls=%async_computation.1 | async-start | bytes 2097152 | tf_op jit(solution)/shard_map/all_to_all | solution.py:571
  159.2 15.4 %copy-start.5 = (bf16[2,128,256]{2,1,0:T(8,128)(2,1)S(1)}, bf16[2,128,256]{2,1,0:T(8,128)(2,1)}, u32[]{:S(2)}) copy-start(bf16[2,128,256]{2,1,0:T(8,128)(2,1)} %copy-done.4) | copy-start | bytes 393220
  159.2 15.4 %copy-start.12 = (bf16[2,128,128]{2,1,0:T(8,128)(2,1)S(1)}, bf16[2,128,128]{2,1,0:T(8,128)(2,1)}, u32[]{:S(2)}) copy-start(bf16[2,128,128]{2,1,0:T(8,128)(2,1)} %get-tuple-element.51) | copy-start | bytes 196612
  159.5 10.7 %collective-permute-start.19 = (bf16[2,128,128]{2,1,0:T(8,128)(2,1)S(1)}, bf16[2,128,128]{2,1,0:T(8,128)(2,1)S(1)}, u32[]{:S(2)}, u32[]{:S(2)}) collective-permute-start(bf16[2,128,128]{2,1,0:T(8,128)(2,1)S(1)} %convolution_convert_fusion.4), channel_id=1, source_target_pairs={{80,0},{88,8},{96,16},{104,24},{112,32},{120,40},{128,48},{136,56}... | collective-permute-start | bytes 196616 | tf_op jit(solution)/shard_map/ppermute | solution.py:21
  165.0 5.2 %collective-permute-start.20 = (bf16[2,128,128]{2,1,0:T(8,128)(2,1)S(1)}, bf16[2,128,128]{2,1,0:T(8,128)(2,1)S(1)}, u32[]{:S(2)}, u32[]{:S(2)}) collective-permute-start(bf16[2,128,128]{2,1,0:T(8,128)(2,1)S(1)} %convolution_convert_fusion.2), channel_id=1, source_target_pairs={{144,0},{152,8},{160,16},{168,24},{176,32},{184,40},{192,48},{200,... | collective-permute-start | bytes 196616 | tf_op jit(solution)/shard_map/ppermute | solution.py:21
  165.7 4.6 %collective-permute-start.21 = (bf16[2,128,128]{2,1,0:T(8,128)(2,1)S(1)}, bf16[2,128,128]{2,1,0:T(8,128)(2,1)S(1)}, u32[]{:S(2)}, u32[]{:S(2)}) collective-permute-start(bf16[2,128,128]{2,1,0:T(8,128)(2,1)S(1)} %convolution_convert_fusion), channel_id=1, source_target_pairs={{208,0},{216,8},{224,16},{232,24},{240,32},{248,40},{209,1},{217,9... | collective-permute-start | bytes 196616 | tf_op jit(solution)/shard_map/ppermute | solution.py:21
  166.4 8.2 %collective-permute-start.18 = (bf16[2,128,128]{2,1,0:T(8,128)(2,1)S(1)}, bf16[2,128,128]{2,1,0:T(8,128)(2,1)S(1)}, u32[]{:S(2)}, u32[]{:S(2)}) collective-permute-start(bf16[2,128,128]{2,1,0:T(8,128)(2,1)S(1)} %add_convert_fusion.2), channel_id=1, source_target_pairs={{16,0},{24,8},{32,16},{40,24},{48,32},{56,40},{64,48},{72,56},{80,... | collective-permute-start | bytes 196616 | tf_op jit(solution)/shard_map/ppermute | solution.py:21
  175.6 1.3 collective-permute-start.22
  177.8 6.4 %collective-permute-start.16 = (bf16[128,256]{1,0:T(8,128)(2,1)S(1)}, bf16[128,256]{1,0:T(8,128)(2,1)S(1)}, u32[]{:S(2)}, u32[]{:S(2)}) collective-permute-start(bf16[128,256]{1,0:T(8,128)(2,1)S(1)} %slice.122), channel_id=1, source_target_pairs={{0,8},{8,0},{16,24},{24,16},{32,40},{40,32},{48,56},{56,48},{64,72... | collective-permute-start | bytes 196616 | tf_op jit(solution)/shard_map/ppermute | solution.py:26
  (11 other events, 24.8 us)
Sparse Core Ops, SparseCore 0:
  23.0 43.3 all-gather.2
  153.7 40.1 reduce-scatter.1

commit v8 on v6

--- a/solution.py
+++ b/solution.py
@@ -464,14 +464,19 @@
     chip = jnp.concatenate(
         [joined[:, :, :WIDTH], joined[:, :, WIDTH:] + odd_b.astype(F32)], axis=2
     ).astype(BF16)
-    one, two = send(chip, 2), send(chip, 4)
+    one, two, three, four = [send(chip, 2 * k) for k in range(1, 5)]
     window1, state = halves(one)
-    step = mul(window1, two)
-    state = state.astype(F32) + step[:, :, WIDTH:]
-    window2 = step[:, :, :WIDTH].astype(BF16)
-    step = mul(window2, send(jnp.concatenate([window2, state.astype(BF16)], axis=2), 4))
-    state = state + step[:, :, WIDTH:]
+    third, inner = halves(three)
+    outer = mul(window1, two)
+    state = state.astype(F32) + outer[:, :, WIDTH:]
+    window2 = outer[:, :, :WIDTH].astype(BF16)
+    step = mul(third, four)
+    inner = (inner.astype(F32) + step[:, :, WIDTH:]).astype(BF16)
+    step = jnp.concatenate([step[:, :, :WIDTH].astype(BF16), inner, third], axis=2)
+    step = mul(window2, step)
     window4 = step[:, :, :WIDTH].astype(BF16)
+    state = state + step[:, :, WIDTH : 2 * WIDTH]
+    window3 = step[:, :, 2 * WIDTH :].astype(BF16)
     rounded = state.astype(BF16)
     both = jnp.concatenate([window4, rounded], axis=2)
     grad_full, both = lax.optimization_barrier((grad_full, both))
@@ -493,20 +498,18 @@
     kept = jnp.where(core == 0, first, second)
     given = jnp.where(core == 0, second, first)
     state_in = jnp.concatenate([kept, exchange(given, 1)], axis=0)
-    return grad_full, grad_other, head_grad, state_in, (even_a, odd_a, window1, window2, window4, window8, window12)
+    return grad_full, grad_other, head_grad, state_in, (even_a, odd_a, (window1, window2, window3), window4, window8, window12)
 
 
 def backward_states(mine, theirs, core, saved, gate):
-    even_a, odd_a, window1, window2, window4, window8, window12 = saved
+    even_a, odd_a, near_windows, window4, window8, window12 = saved
     theirs = exchange(theirs, 1)
     even = jnp.where(core == 0, mine, theirs)
     odd = jnp.where(core == 0, theirs, mine)
     total = even.astype(F32) + mul_t(even_a, odd)
-    for window, distance in ((window1, 2), (window2, 4)):
-        passed = mul_t(window, total.astype(BF16)).astype(BF16)
-        if distance == 4:
-            gate, passed = lax.optimization_barrier((gate, passed))
-        total = total + send(passed, -distance).astype(F32)
+    rounded = total.astype(BF16)
+    for k, window in enumerate(near_windows):
+        total = total + send(mul_t(window, rounded).astype(BF16), -2 * k - 2).astype(F32)
     rounded = total.astype(BF16)
     second = send(rounded, -2).astype(F32)
     for window, distance in ((window4, 10), (window8, 18), (window12, 26)):

time: 167 us -> 178 us (1.066)
  waiting for transfers between devices: 26.6 us -> 37.6 us
  starting transfers between devices: 66.4 us -> 63.1 us
    ppermute x12 -> x14, waiting for transfers between devices: 21.5 us -> 32.5 us  [send(): return lax.ppermute(block, 'ctx', route)]
    ppermute x10, starting transfers between devices: 17.6 us -> 15.7 us  [exchange(): return lax.ppermute(block, 'ctx', route)]
    ppermute x12 -> x14, starting transfers between devices: 38.9 us -> 38 us  [send(): return lax.ppermute(block, 'ctx', route)]
    dot_general x7 -> x8, matrix products: 3.29 us -> 3.58 us  [mul_t(): return jnp.einsum('hji,hjk->hik', a, b, preferred_element_type=F32)]
    dot_general x7 -> x8, matrix products: 3.89 us -> 4.14 us  [mul(): return jnp.einsum('hij,hjk->hik', a, b, preferred_element_type=F32)]
  transfers between devices with their start and end apart: 26 -> 28, of which waited for: 9 -> 10; matrix products, arithmetic and copies ran while one was open for 6% -> 7% of each run, Pallas kernels for 20% -> 19%
where the time goes in v8:
time: 178 us; the launch traced here: 176 us
  starting transfers between devices  63.1 us (35%)
  Pallas kernels  40.2 us (23%)
  waiting for transfers between devices  37.6 us (21%)
  between operations  14.4 us (8%)
  other arithmetic  8.33 us (5%)
  matrix products  7.71 us (4%)
  local copies, waits for them, and re-layouts  4.76 us (3%)
    ppermute x14, starting transfers between devices, send(): return lax.ppermute(block, 'ctx', route)  38 us
    ppermute x14, waiting for transfers between devices, send(): return lax.ppermute(block, 'ctx', route)  32.5 us
    ppermute x10, starting transfers between devices, exchange(): return lax.ppermute(block, 'ctx', route)  15.7 us
    pallas_call x2, Pallas kernels, prepare(): pl.pallas_call(functools.partial(prepare_kernel, mine), grid_spec=pltpu.P...  12.7 us
    pallas_call x1, Pallas kernels, pull(): call(pull_kernel, 2, [by_columns(WIDTH), by_columns(PAIRS), whole(4, PAIR...  6.3 us
    pallas_call x1, Pallas kernels, head_gradient(): call(head_grad_kernel, STEPS, [whole(8, WIDTH, 512), whole(8, WIDTH, 512)...  5.34 us
    pallas_call x1, Pallas kernels, mixed_parts(): call(mixed_kernel, STEPS, [whole(WIDTH, 512), whole(WIDTH, 512), weight_t...  5.1 us
    all_to_all x1, starting transfers between devices, local(): parts = lax.all_to_all(parts, 'tp', 0, 0, tiled=True)  5.08 us
  transfers between devices with their start and end apart: 28, of which 10 were waited for; matrix products, arithmetic and copies ran while one was open for 7% of the time, Pallas kernels for 19%

profile of v8, /device:TPU:1, one launch (start us, length us, event | category | flops | bytes accessed | tf_op | source)
XLA Modules:
  0.0 176.2 jit_solution(7531524861649875532)
XLA Ops:
  7.2 3.7 %collective-permute-start = (bf16[128,512]{1,0:T(8,128)(2,1)}, bf16[128,512]{1,0:T(8,128)(2,1)S(1)}, u32[]{:S(2)}, u32[]{:S(2)}) collective-permute-start(bf16[128,512]{1,0:T(8,128)(2,1)} %param.10), channel_id=1, source_target_pairs={{0,128},{8,136},{16,144},{24,152},{32,160},{40,168},{48,176},{56,1... | collective-permute-start | bytes 393224 | tf_op jit(solution)/shard_map/ppermute | solution.py:26
  11.5 6.3 %shard_map.109 = (bf16[2,128,256]{2,1,0:T(8,128)(2,1)}, f32[4,256,256]{2,1,0:T(8,128)}, f32[4,256,256]{2,1,0:T(8,128)}, f32[4,128,128]{2,1,0:T(8,128)}, f32[4,128,128]{2,1,0:T(8,128)}) custom-call(s32[2]{0:T(128)} %pad_add_fusion.refs_0_.place, bf16[128,512]{1,0:T(8,128)(2,1)} %q_ref.1, bf16[128,1024]{1,0:T(8,128)(2,1)} %k_ref.1, bf16[128,1024]{1,0:T(8,128)(2,1)} %refs_3_.2, ...), custom_call_target="tpu_custom_call" | custom-call | flops 104857600 | bytes 16777216 | tf_op jit(solution)/shard_map/pallas_call | solution.py:172
  17.8 1.6 pad_maximum_fusion
  20.5 6.4 %shard_map.110 = (bf16[2,128,256]{2,1,0:T(8,128)(2,1)}, f32[4,256,256]{2,1,0:T(8,128)}, f32[4,256,256]{2,1,0:T(8,128)}, f32[4,128,128]{2,1,0:T(8,128)}, f32[4,128,128]{2,1,0:T(8,128)}) custom-call(s32[2]{0:T(128)} %pad_add_fusion.refs_0_.place, bf16[128,512]{1,0:T(8,128)(2,1)} %q_ref.1, ...), custom_call_target="tpu_custom_call", output_to_operand_aliasing={{1}: (5, {}), {2}: (6, {}), {3}: (7, {}), {4}: (8, {})} | custom-call | flops 1048576 | bytes 65536 | tf_op jit(solution)/shard_map/pallas_call | solution.py:172
  28.5 8.8 %collective-permute-start.5 = (bf16[2,128,256]{2,1,0:T(8,128)(2,1)S(1)}, bf16[2,128,256]{2,1,0:T(8,128)(2,1)S(1)}, u32[]{:S(2)}, u32[]{:S(2)}) collective-permute-start(bf16[2,128,256]{2,1,0:T(8,128)(2,1)S(1)} %pad_maximum_fusion.1), channel_id=1, source_target_pairs={{0,64},{8,72},{16,80},{24,88},{32,96},{40,104},{48,112},{56,120},{... | collective-permute-start | bytes 393224 | tf_op jit(solution)/shard_map/ppermute | solution.py:21
  37.3 3.6 %collective-permute-start.4 = (bf16[2,128,256]{2,1,0:T(8,128)(2,1)S(1)}, bf16[2,128,256]{2,1,0:T(8,128)(2,1)S(1)}, u32[]{:S(2)}, u32[]{:S(2)}) collective-permute-start(bf16[2,128,256]{2,1,0:T(8,128)(2,1)S(1)} %pad_maximum_fusion.1), channel_id=1, source_target_pairs={{0,48},{8,56},{16,64},{24,72},{32,80},{40,88},{48,96},{56,104},{64... | collective-permute-start | bytes 393224 | tf_op jit(solution)/shard_map/ppermute | solution.py:21
  42.0 4.2 %all-to-all-start = ((bf16[8,128,512]{2,1,0:T(8,128)(2,1)}), bf16[8,128,512]{2,1,0:T(8,128)(2,1)S(1)}, u32[]{:S(2)}, u32[]{:S(2)}) async-start(bf16[8,128,512]{2,1,0:T(8,128)(2,1)} %broadcast_in_dim.2), calls=%async_computation | async-start | bytes 2097152 | tf_op jit(solution)/shard_map/all_to_all | solution.py:537
  46.2 1.3 collective-permute-start.3
  47.5 3.4 %collective-permute-start.2 = (bf16[2,128,256]{2,1,0:T(8,128)(2,1)S(1)}, bf16[2,128,256]{2,1,0:T(8,128)(2,1)S(1)}, u32[]{:S(2)}, u32[]{:S(2)}) collective-permute-start(bf16[2,128,256]{2,1,0:T(8,128)(2,1)S(1)} %pad_maximum_fusion.1), channel_id=1, source_target_pairs={{0,16},{8,24},{16,32},{24,40},{32,48},{40,56},{48,64},{56,72},{64,... | collective-permute-start | bytes 393224 | tf_op jit(solution)/shard_map/ppermute | solution.py:21
  51.0 5.0 %collective-permute-done.4 = bf16[2,128,256]{2,1,0:T(8,128)(2,1)S(1)} collective-permute-done((bf16[2,128,256]{2,1,0:T(8,128)(2,1)S(1)}, bf16[2,128,256]{2,1,0:T(8,128)(2,1)S(1)}, u32[]{:S(2)}, u32[]{:S(2)}) %collective-permute-start.4) | collective-permute-done | bytes 131104 | tf_op jit(solution)/shard_map/ppermute | solution.py:21
  56.3 7.6 %collective-permute-done.3 = bf16[2,128,256]{2,1,0:T(8,128)(2,1)S(1)} collective-permute-done((bf16[2,128,256]{2,1,0:T(8,128)(2,1)S(1)}, bf16[2,128,256]{2,1,0:T(8,128)(2,1)S(1)}, u32[]{:S(2)}, u32[]{:S(2)}) %collective-permute-start.3) | collective-permute-done | bytes 131104 | tf_op jit(solution)/shard_map/ppermute | solution.py:21
  63.8 5.3 %collective-permute-done.2 = bf16[2,128,256]{2,1,0:T(8,128)(2,1)S(1)} collective-permute-done((bf16[2,128,256]{2,1,0:T(8,128)(2,1)S(1)}, bf16[2,128,256]{2,1,0:T(8,128)(2,1)S(1)}, u32[]{:S(2)}, u32[]{:S(2)}) %collective-permute-start.2) | collective-permute-done | bytes 131104 | tf_op jit(solution)/shard_map/ppermute | solution.py:21
  70.2 1.5 pad_maximum_fusion.2
  72.9 6.0 %collective-permute-start.8 = (bf16[2,128,256]{2,1,0:T(8,128)(2,1)}, bf16[2,128,256]{2,1,0:T(8,128)(2,1)}, u32[]{:S(2)}, u32[]{:S(2)}) collective-permute-start(bf16[2,128,256]{2,1,0:T(8,128)(2,1)} %pad_maximum_fusion.2), channel_id=1, source_target_pairs={{0,128},{8,136},{16,144},{24,152},{32,160},{40,168},{48,176},{56,1... | collective-permute-start | bytes 393224 | tf_op jit(solution)/shard_map/ppermute | solution.py:21
  78.9 3.9 %collective-permute-start.7 = (bf16[2,128,256]{2,1,0:T(8,128)(2,1)}, bf16[2,128,256]{2,1,0:T(8,128)(2,1)}, u32[]{:S(2)}, u32[]{:S(2)}) collective-permute-start(bf16[2,128,256]{2,1,0:T(8,128)(2,1)} %pad_maximum_fusion.2), channel_id=1, source_target_pairs={{0,64},{8,72},{16,80},{24,88},{32,96},{40,104},{48,112},{56,120},{... | collective-permute-start | bytes 393224 | tf_op jit(solution)/shard_map/ppermute | solution.py:21
  82.8 1.9 %collective-permute-start.9 = (bf16[2,128,128]{2,1,0:T(8,128)(2,1)}, bf16[2,128,128]{2,1,0:T(8,128)(2,1)}, u32[]{:S(2)}, u32[]{:S(2)}) collective-permute-start(bf16[2,128,128]{2,1,0:T(8,128)(2,1)} %fusion.36), channel_id=1, source_target_pairs={{0,192},{8,200},{16,208},{24,216},{32,224},{40,232},{48,240},{56,2... | collective-permute-start | bytes 196616 | tf_op jit(solution)/shard_map/ppermute | solution.py:21
  84.7 5.3 %shard_map.111 = (f32[128,512]{1,0:T(8,128)}, f32[128,512]{1,0:T(8,128)}) custom-call(s32[2]{0:T(128)} %pad_add_fusion.refs_0_.place, bf16[8,128,512]{2,1,0:T(8,128)(2,1)} %copy-done, bf16[8,128,512]{2,1,0:T(8,128)(2,1)} %collective-permute-done.6.other_ref, bf16[8,2,128,512]{3,2,1,0:T(8,128)(2,1)} %bitcast.24), custom_call_target="tpu_custom_call" | custom-call | flops 536870912 | bytes 5242880 | tf_op jit(solution)/shard_map/pallas_call | solution.py:320
  94.9 2.6 %shard_map.112.heads_ref = bf16[128,512]{1,0:T(8,128)(2,1)} custom-call(s32[2]{0:T(128)} %pad_add_fusion.refs_0_.place, f32[4,128,128]{2,1,0:T(8,128)} %get-tuple-element.51.qt_ref, f32[4,128,128]{2,1,0:T(8,128)} %get-tuple-element.52.local_ref, bf16[4,128,128]{2,1,0:T(8,128)(2,1)} %pad_maximum_fusion.3.state_ref), custom_call_target="tpu_custom_call" | custom-call | flops 16777216 | bytes 1048576 | tf_op jit(solution)/shard_map/pallas_call | solution.py:239
  99.8 4.9 %shard_map.115 = bf16[8,256,512]{2,1,0:T(8,128)(2,1)} custom-call(s32[2]{0:T(128)} %pad_add_fusion.refs_0_.place, bf16[8,128,512]{2,1,0:T(8,128)(2,1)} %copy-done, bf16[8,128,512]{2,1,0:T(8,128)(2,1)} %collective-permute-done.6.other_ref, bf16[128,512]{1,0:T(8,128)(2,1)} %shard_map.112.heads_ref, bf16[128,512]{1,0:T(8,128)(2,1)} %copy-done.1), custom_call_target="tpu_custom_call" | custom-call | flops 536870912 | bytes 5242880 | tf_op jit(solution)/shard_map/pallas_call | solution.py:263
  107.8 3.3 %shard_map.114 = (f32[128,512]{1,0:T(8,128)}, bf16[2,128,128]{2,1,0:T(8,128)(2,1)}, bf16[2,128,128]{2,1,0:T(8,128)(2,1)}) custom-call(s32[2]{0:T(128)} %pad_add_fusion.refs_0_.place, f32[128,512]{1,0:T(8,128)} %get-tuple-element.65.kept_ref, f32[128,512]{1,0:T(8,128)} %copy-done.8, f32[4,128,128]{2,1,0:T(8,128)} %get-tuple-element.51.qt_ref), custom_call_target="tpu_custom_call" | custom-call | flops 16777216 | bytes 1048576 | tf_op jit(solution)/shard_map/pallas_call | solution.py:348
  114.0 1.3 collective-permute-start.17
  119.3 5.1 %shard_map.113 = bf16[8,256,256]{2,1,0:T(8,128)(2,1)} custom-call(s32[2]{0:T(128)} %pad_add_fusion.refs_0_.place, bf16[128,512]{1,0:T(8,128)(2,1)} %shard_map.112.heads_ref, bf16[128,512]{1,0:T(8,128)(2,1)} %copy-done.1, bf16[8,2,128,512]{3,2,1,0:T(8,128)(2,1)} %bitcast.25), custom_call_target="tpu_custom_call" | custom-call | flops 536870912 | bytes 3145728 | tf_op jit(solution)/shard_map/pallas_call | solution.py:288
  124.4 5.1 %all-to-all-start.1 = ((bf16[8,256,256]{2,1,0:T(8,128)(2,1)}), bf16[8,256,256]{2,1,0:T(8,128)(2,1)S(1)}, u32[]{:S(2)}, u32[]{:S(2)}) async-start(bf16[8,256,256]{2,1,0:T(8,128)(2,1)} %shard_map.113), calls=%async_computation.1 | async-start | bytes 2097152 | tf_op jit(solution)/shard_map/all_to_all | solution.py:554
  131.2 1.3 collective-permute-start.20
  132.5 1.3 collective-permute-start.21
  133.8 1.3 collective-permute-start.19
  135.1 1.3 collective-permute-start.18
  136.4 10.0 %collective-permute-done.20 = bf16[2,128,128]{2,1,0:T(8,128)(2,1)S(1)} collective-permute-done((bf16[2,128,128]{2,1,0:T(8,128)(2,1)S(1)}, bf16[2,128,128]{2,1,0:T(8,128)(2,1)S(1)}, u32[]{:S(2)}, u32[]{:S(2)}) %collective-permute-start.20) | collective-permute-done | bytes 65568 | tf_op jit(solution)/shard_map/ppermute | solution.py:21
  146.4 4.5 %collective-permute-done.21 = bf16[2,128,128]{2,1,0:T(8,128)(2,1)S(1)} collective-permute-done((bf16[2,128,128]{2,1,0:T(8,128)(2,1)S(1)}, bf16[2,128,128]{2,1,0:T(8,128)(2,1)S(1)}, u32[]{:S(2)}, u32[]{:S(2)}) %collective-permute-start.21) | collective-permute-done | bytes 65568 | tf_op jit(solution)/shard_map/ppermute | solution.py:21
  151.2 2.9 %collective-permute-start.22 = (bf16[2,128,128]{2,1,0:T(8,128)(2,1)S(1)}, bf16[2,128,128]{2,1,0:T(8,128)(2,1)S(1)}, u32[]{:S(2)}, u32[]{:S(2)}) collective-permute-start(bf16[2,128,128]{2,1,0:T(8,128)(2,1)S(1)} %get-tuple-element.81), channel_id=1, source_target_pairs={{0,8},{8,0},{16,24},{24,16},{32,40},{40,32},{48,56},{56,48},{64,72... | collective-permute-start | bytes 196616 | tf_op jit(solution)/shard_map/ppermute | solution.py:26
  157.4 4.9 %collective-permute-start.23 = (bf16[128,512]{1,0:T(8,128)(2,1)S(1)}, bf16[128,512]{1,0:T(8,128)(2,1)S(1)}, u32[]{:S(2)}, u32[]{:S(2)}) collective-permute-start(bf16[128,512]{1,0:T(8,128)(2,1)S(1)} %slice_bitcast_fusion), channel_id=1, source_target_pairs={{0,128},{8,136},{16,144},{24,152},{32,160},{40,168},{48,176},{56,1... | collective-permute-start | bytes 393224 | tf_op jit(solution)/shard_map/ppermute | solution.py:26
  162.3 6.3 %shard_map.116 = (bf16[128,512]{1,0:T(8,128)(2,1)}, bf16[128,1024]{1,0:T(8,128)(2,1)}, bf16[128,1024]{1,0:T(8,128)(2,1)}, f32[4,256]{1,0:T(4,128)}) custom-call(s32[2]{0:T(128)} %pad_add_fusion.refs_0_.place, bf16[128,512]{1,0:T(8,128)(2,1)} %q_ref.1, bf16[128,1024]{1,0:T(8,128)(2,1)} %k_ref.1, f32[4,256]{1,0:T(4,128)} %logit_ref.1, ...), custom_call_target="tpu_custom_call" | custom-call | flops 1879048192 | bytes 5242880 | tf_op jit(solution)/shard_map/pallas_call | solution.py:420
  (95 shorter events, 29.7 us)
Async XLA Ops:
  7.2 77.5 %all-gather.3.cloned.1.call-start = ((), (), s32[]{:S(2)}) async-start(), calls=%async_computation.4 | async-start | bytes 2359296 | tf_op jit(solution)/shard_map/all_gather | solution.py:536
  7.2 10.6 %collective-permute-start = (bf16[128,512]{1,0:T(8,128)(2,1)}, bf16[128,512]{1,0:T(8,128)(2,1)S(1)}, u32[]{:S(2)}, u32[]{:S(2)}) collective-permute-start(bf16[128,512]{1,0:T(8,128)(2,1)} %param.10), channel_id=1, source_target_pairs={{0,128},{8,136},{16,144},{24,152},{32,160},{40,168},{48,176},{56,1... | collective-permute-start | bytes 393224 | tf_op jit(solution)/shard_map/ppermute | solution.py:26
  19.4 7.5 %collective-permute-start.1 = (bf16[2,128,256]{2,1,0:T(8,128)(2,1)}, bf16[2,128,256]{2,1,0:T(8,128)(2,1)S(1)}, u32[]{:S(2)}, u32[]{:S(2)}) collective-permute-start(bf16[2,128,256]{2,1,0:T(8,128)(2,1)} %get-tuple-element.53), channel_id=1, source_target_pairs={{0,8},{8,0},{16,24},{24,16},{32,40},{40,32},{48,56},{56,48},{64,72... | collective-permute-start | bytes 393224 | tf_op jit(solution)/shard_map/ppermute | solution.py:26
  20.5 20.4 %copy-start.9 = (bf16[128,512]{1,0:T(8,128)(2,1)S(1)}, bf16[128,512]{1,0:T(8,128)(2,1)}, u32[]{:S(2)}) copy-start(bf16[128,512]{1,0:T(8,128)(2,1)} %param.11) | copy-start | bytes 393220
  28.5 22.5 %collective-permute-start.5 = (bf16[2,128,256]{2,1,0:T(8,128)(2,1)S(1)}, bf16[2,128,256]{2,1,0:T(8,128)(2,1)S(1)}, u32[]{:S(2)}, u32[]{:S(2)}) collective-permute-start(bf16[2,128,256]{2,1,0:T(8,128)(2,1)S(1)} %pad_maximum_fusion.1), channel_id=1, source_target_pairs={{0,64},{8,72},{16,80},{24,88},{32,96},{40,104},{48,112},{56,120},{... | collective-permute-start | bytes 393224 | tf_op jit(solution)/shard_map/ppermute | solution.py:21
  37.3 18.7 %collective-permute-start.4 = (bf16[2,128,256]{2,1,0:T(8,128)(2,1)S(1)}, bf16[2,128,256]{2,1,0:T(8,128)(2,1)S(1)}, u32[]{:S(2)}, u32[]{:S(2)}) collective-permute-start(bf16[2,128,256]{2,1,0:T(8,128)(2,1)S(1)} %pad_maximum_fusion.1), channel_id=1, source_target_pairs={{0,48},{8,56},{16,64},{24,72},{32,80},{40,88},{48,96},{56,104},{64... | collective-permute-start | bytes 393224 | tf_op jit(solution)/shard_map/ppermute | solution.py:21
  42.0 29.7 %all-to-all-start = ((bf16[8,128,512]{2,1,0:T(8,128)(2,1)}), bf16[8,128,512]{2,1,0:T(8,128)(2,1)S(1)}, u32[]{:S(2)}, u32[]{:S(2)}) async-start(bf16[8,128,512]{2,1,0:T(8,128)(2,1)} %broadcast_in_dim.2), calls=%async_computation | async-start | bytes 2097152 | tf_op jit(solution)/shard_map/all_to_all | solution.py:537
  46.2 110.2 %reduce-scatter.2.cloned.1.call-start = ((), (), s32[]{:S(2)}) async-start(), calls=%async_computation.3 | async-start | bytes 2359296 | tf_op jit(solution)/shard_map/reduce_scatter | solution.py:546
  46.2 17.6 %collective-permute-start.3 = (bf16[2,128,256]{2,1,0:T(8,128)(2,1)S(1)}, bf16[2,128,256]{2,1,0:T(8,128)(2,1)S(1)}, u32[]{:S(2)}, u32[]{:S(2)}) collective-permute-start(bf16[2,128,256]{2,1,0:T(8,128)(2,1)S(1)} %pad_maximum_fusion.1), channel_id=1, source_target_pairs={{0,32},{8,40},{16,48},{24,56},{32,64},{40,72},{48,80},{56,88},{64,... | collective-permute-start | bytes 393224 | tf_op jit(solution)/shard_map/ppermute | solution.py:21
  47.5 21.6 %collective-permute-start.2 = (bf16[2,128,256]{2,1,0:T(8,128)(2,1)S(1)}, bf16[2,128,256]{2,1,0:T(8,128)(2,1)S(1)}, u32[]{:S(2)}, u32[]{:S(2)}) collective-permute-start(bf16[2,128,256]{2,1,0:T(8,128)(2,1)S(1)} %pad_maximum_fusion.1), channel_id=1, source_target_pairs={{0,16},{8,24},{16,32},{24,40},{32,48},{40,56},{48,64},{56,72},{64,... | collective-permute-start | bytes 393224 | tf_op jit(solution)/shard_map/ppermute | solution.py:21
  71.7 13.0 %copy-start = (bf16[8,128,512]{2,1,0:T(8,128)(2,1)}, bf16[8,128,512]{2,1,0:T(8,128)(2,1)S(1)}, u32[]{:S(2)}) copy-start(bf16[8,128,512]{2,1,0:T(8,128)(2,1)S(1)} %all-to-all-done.own_ref) | copy-start | bytes 3145732
  71.7 13.0 %collective-permute-start.6 = (bf16[8,128,512]{2,1,0:T(8,128)(2,1)S(1)}, bf16[8,128,512]{2,1,0:T(8,128)(2,1)}, u32[]{:S(2)}, u32[]{:S(2)}) collective-permute-start(bf16[8,128,512]{2,1,0:T(8,128)(2,1)S(1)} %all-to-all-done.own_ref), channel_id=1, source_target_pairs={{0,8},{8,0},{16,24},{24,16},{32,40},{40,32},{48,56},{56,48},{64,72... | collective-permute-start | bytes 3145736 | tf_op jit(solution)/shard_map/ppermute | solution.py:26
  72.9 17.2 %collective-permute-start.8 = (bf16[2,128,256]{2,1,0:T(8,128)(2,1)}, bf16[2,128,256]{2,1,0:T(8,128)(2,1)}, u32[]{:S(2)}, u32[]{:S(2)}) collective-permute-start(bf16[2,128,256]{2,1,0:T(8,128)(2,1)} %pad_maximum_fusion.2), channel_id=1, source_target_pairs={{0,128},{8,136},{16,144},{24,152},{32,160},{40,168},{48,176},{56,1... | collective-permute-start | bytes 393224 | tf_op jit(solution)/shard_map/ppermute | solution.py:21
  78.9 11.2 %collective-permute-start.7 = (bf16[2,128,256]{2,1,0:T(8,128)(2,1)}, bf16[2,128,256]{2,1,0:T(8,128)(2,1)}, u32[]{:S(2)}, u32[]{:S(2)}) collective-permute-start(bf16[2,128,256]{2,1,0:T(8,128)(2,1)} %pad_maximum_fusion.2), channel_id=1, source_target_pairs={{0,64},{8,72},{16,80},{24,88},{32,96},{40,104},{48,112},{56,120},{... | collective-permute-start | bytes 393224 | tf_op jit(solution)/shard_map/ppermute | solution.py:21
  82.8 7.3 %collective-permute-start.9 = (bf16[2,128,128]{2,1,0:T(8,128)(2,1)}, bf16[2,128,128]{2,1,0:T(8,128)(2,1)}, u32[]{:S(2)}, u32[]{:S(2)}) collective-permute-start(bf16[2,128,128]{2,1,0:T(8,128)(2,1)} %fusion.36), channel_id=1, source_target_pairs={{0,192},{8,200},{16,208},{24,216},{32,224},{40,232},{48,240},{56,2... | collective-permute-start | bytes 196616 | tf_op jit(solution)/shard_map/ppermute | solution.py:21
  92.5 1.8 %collective-permute-start.10 = (bf16[2,128,128]{2,1,0:T(8,128)(2,1)S(1)}, bf16[2,128,128]{2,1,0:T(8,128)(2,1)S(1)}, u32[]{:S(2)}, u32[]{:S(2)}) collective-permute-start(bf16[2,128,128]{2,1,0:T(8,128)(2,1)S(1)} %get-tuple-element.83), channel_id=1, source_target_pairs={{0,8},{8,0},{16,24},{24,16},{32,40},{40,32},{48,56},{56,48},{64,72... | collective-permute-start | bytes 196616 | tf_op jit(solution)/shard_map/ppermute | solution.py:26
  97.6 1.6 collective-permute-start.11
  104.6 10.6 %copy-start.5 = (bf16[2,128,256]{2,1,0:T(8,128)(2,1)S(1)}, bf16[2,128,256]{2,1,0:T(8,128)(2,1)}, u32[]{:S(2)}) copy-start(bf16[2,128,256]{2,1,0:T(8,128)(2,1)} %copy-done.4) | copy-start | bytes 393220
  105.6 1.5 collective-permute-start.13
  111.1 1.5 collective-permute-start.14
  114.0 15.5 %collective-permute-start.17 = (bf16[2,128,128]{2,1,0:T(8,128)(2,1)S(1)}, bf16[2,128,128]{2,1,0:T(8,128)(2,1)S(1)}, u32[]{:S(2)}, u32[]{:S(2)}) collective-permute-start(bf16[2,128,128]{2,1,0:T(8,128)(2,1)S(1)} %convolution_convert_fusion.5), channel_id=1, source_target_pairs={{48,0},{56,8},{64,16},{72,24},{80,32},{88,40},{96,48},{104,56},{11... | collective-permute-start | bytes 196616 | tf_op jit(solution)/shard_map/ppermute | solution.py:21
  115.5 14.0 %collective-permute-start.15 = (bf16[2,128,128]{2,1,0:T(8,128)(2,1)S(1)}, bf16[2,128,128]{2,1,0:T(8,128)(2,1)S(1)}, u32[]{:S(2)}, u32[]{:S(2)}) collective-permute-start(bf16[2,128,128]{2,1,0:T(8,128)(2,1)S(1)} %convolution_convert_fusion.7), channel_id=1, source_target_pairs={{16,0},{24,8},{32,16},{40,24},{48,32},{56,40},{64,48},{72,56},{80,... | collective-permute-start | bytes 196616 | tf_op jit(solution)/shard_map/ppermute | solution.py:21
  117.0 12.5 %collective-permute-start.16 = (bf16[2,128,128]{2,1,0:T(8,128)(2,1)S(1)}, bf16[2,128,128]{2,1,0:T(8,128)(2,1)S(1)}, u32[]{:S(2)}, u32[]{:S(2)}) collective-permute-start(bf16[2,128,128]{2,1,0:T(8,128)(2,1)S(1)} %convolution_convert_fusion.6), channel_id=1, source_target_pairs={{32,0},{40,8},{48,16},{56,24},{64,32},{72,40},{80,48},{88,56},{96,... | collective-permute-start | bytes 196616 | tf_op jit(solution)/shard_map/ppermute | solution.py:21
  124.4 26.6 %copy-start.3 = (bf16[2,128,256]{2,1,0:T(8,128)(2,1)S(1)}, bf16[2,128,256]{2,1,0:T(8,128)(2,1)}, u32[]{:S(2)}) copy-start(bf16[2,128,256]{2,1,0:T(8,128)(2,1)} %copy-done.2) | copy-start | bytes 393220
  124.4 29.7 %all-to-all-start.1 = ((bf16[8,256,256]{2,1,0:T(8,128)(2,1)}), bf16[8,256,256]{2,1,0:T(8,128)(2,1)S(1)}, u32[]{:S(2)}, u32[]{:S(2)}) async-start(bf16[8,256,256]{2,1,0:T(8,128)(2,1)} %shard_map.113), calls=%async_computation.1 | async-start | bytes 2097152 | tf_op jit(solution)/shard_map/all_to_all | solution.py:554
  131.2 15.2 %collective-permute-start.20 = (bf16[2,128,128]{2,1,0:T(8,128)(2,1)S(1)}, bf16[2,128,128]{2,1,0:T(8,128)(2,1)S(1)}, u32[]{:S(2)}, u32[]{:S(2)}) collective-permute-start(bf16[2,128,128]{2,1,0:T(8,128)(2,1)S(1)} %convolution_convert_fusion.2), channel_id=1, source_target_pairs={{144,0},{152,8},{160,16},{168,24},{176,32},{184,40},{192,48},{200,... | collective-permute-start | bytes 196616 | tf_op jit(solution)/shard_map/ppermute | solution.py:21
  132.5 18.5 %collective-permute-start.21 = (bf16[2,128,128]{2,1,0:T(8,128)(2,1)S(1)}, bf16[2,128,128]{2,1,0:T(8,128)(2,1)S(1)}, u32[]{:S(2)}, u32[]{:S(2)}) collective-permute-start(bf16[2,128,128]{2,1,0:T(8,128)(2,1)S(1)} %convolution_convert_fusion), channel_id=1, source_target_pairs={{208,0},{216,8},{224,16},{232,24},{240,32},{248,40},{209,1},{217,9... | collective-permute-start | bytes 196616 | tf_op jit(solution)/shard_map/ppermute | solution.py:21
  133.8 17.2 %collective-permute-start.19 = (bf16[2,128,128]{2,1,0:T(8,128)(2,1)S(1)}, bf16[2,128,128]{2,1,0:T(8,128)(2,1)S(1)}, u32[]{:S(2)}, u32[]{:S(2)}) collective-permute-start(bf16[2,128,128]{2,1,0:T(8,128)(2,1)S(1)} %convolution_convert_fusion.4), channel_id=1, source_target_pairs={{80,0},{88,8},{96,16},{104,24},{112,32},{120,40},{128,48},{136,56}... | collective-permute-start | bytes 196616 | tf_op jit(solution)/shard_map/ppermute | solution.py:21
  135.1 15.9 %collective-permute-start.18 = (bf16[2,128,128]{2,1,0:T(8,128)(2,1)S(1)}, bf16[2,128,128]{2,1,0:T(8,128)(2,1)S(1)}, u32[]{:S(2)}, u32[]{:S(2)}) collective-permute-start(bf16[2,128,128]{2,1,0:T(8,128)(2,1)S(1)} %add_convert_fusion.2), channel_id=1, source_target_pairs={{16,0},{24,8},{32,16},{40,24},{48,32},{56,40},{64,48},{72,56},{80,... | collective-permute-start | bytes 196616 | tf_op jit(solution)/shard_map/ppermute | solution.py:21
  151.2 3.8 %collective-permute-start.22 = (bf16[2,128,128]{2,1,0:T(8,128)(2,1)S(1)}, bf16[2,128,128]{2,1,0:T(8,128)(2,1)S(1)}, u32[]{:S(2)}, u32[]{:S(2)}) collective-permute-start(bf16[2,128,128]{2,1,0:T(8,128)(2,1)S(1)} %get-tuple-element.81), channel_id=1, source_target_pairs={{0,8},{8,0},{16,24},{24,16},{32,40},{40,32},{48,56},{56,48},{64,72... | collective-permute-start | bytes 196616 | tf_op jit(solution)/shard_map/ppermute | solution.py:26
  154.3 1.4 collective-permute-start.12
  157.4 11.2 %collective-permute-start.23 = (bf16[128,512]{1,0:T(8,128)(2,1)S(1)}, bf16[128,512]{1,0:T(8,128)(2,1)S(1)}, u32[]{:S(2)}, u32[]{:S(2)}) collective-permute-start(bf16[128,512]{1,0:T(8,128)(2,1)S(1)} %slice_bitcast_fusion), channel_id=1, source_target_pairs={{0,128},{8,136},{16,144},{24,152},{32,160},{40,168},{48,176},{56,1... | collective-permute-start | bytes 393224 | tf_op jit(solution)/shard_map/ppermute | solution.py:26
  (7 other events, 20.5 us)
Sparse Core Ops, SparseCore 0:
  19.6 60.0 all-gather.2
  104.8 47.7 reduce-scatter.1

commit v9 on v6

--- a/solution.py
+++ b/solution.py
@@ -351,8 +351,8 @@
         [whole(WIDTH, 512), whole(WIDTH, 512), whole(4, WIDTH, WIDTH)],
         [whole(WIDTH, 512), whole(2, WIDTH, WIDTH), whole(2, WIDTH, WIDTH)],
         [arr(F32, WIDTH, 512), pair, pair],
-        2 * 4 * 128**3,
-        1 << 20,
+        1 << 10,
+        1 << 10,
     )(place, kept, came, qt)
 
 
@@ -454,7 +454,7 @@
     return x[:, :, :WIDTH], x[:, :, WIDTH:]
 
 
-def forward_states(place, mine, theirs, core, grad_full, weight):
+def forward_states(place, mine, theirs, core, grad_full, weight, qt):
     theirs = exchange(theirs, 1)
     even = jnp.where(core == 0, mine, theirs)
     odd = jnp.where(core == 0, theirs, mine)
@@ -475,24 +475,24 @@
     rounded = state.astype(BF16)
     both = jnp.concatenate([window4, rounded], axis=2)
     grad_full, both = lax.optimization_barrier((grad_full, both))
-    near, mid, far_b = send(both, 8), send(both, 16), send(rounded, 24)
+    near = send(both, 8)
     grad_other = exchange(grad_full, 1)
     kept_grad, given_grad = head_gradient(place, grad_full, grad_other, weight)
-    kept_grad, given_grad, near, mid, far_b = lax.optimization_barrier(
-        (kept_grad, given_grad, near, mid, far_b)
-    )
-    near_a, near_b = halves(near)
-    mid_a, mid_b = halves(mid)
-    head_grad = (kept_grad, exchange(given_grad, 1))
-    inner = (mid_b.astype(F32) + mul(mid_a, far_b)).astype(BF16)
-    inner = (near_b.astype(F32) + mul(near_a, inner)).astype(BF16)
-    first = (state + mul(window4, inner)).astype(BF16)
-    window8 = mul(window4, near_a).astype(BF16)
-    window12 = mul(window8, mid_a).astype(BF16)
+    kept_grad, given_grad, near = lax.optimization_barrier((kept_grad, given_grad, near))
+    step = mul(window4, near)
+    window8 = step[:, :, :WIDTH].astype(BF16)
+    state = state + step[:, :, WIDTH:]
+    far = send(jnp.concatenate([window4, state.astype(BF16)], axis=2), 16)
+    head_grad, own, own_theirs = own_cotangent(place, kept_grad, exchange(given_grad, 1), qt)
+    head_grad, own, own_theirs, far = lax.optimization_barrier((head_grad, own, own_theirs, far))
+    step = mul(window8, far)
+    window12 = step[:, :, :WIDTH].astype(BF16)
+    first = (state + step[:, :, WIDTH:]).astype(BF16)
     second = (mul(even_a, first) + even_b.astype(F32)).astype(BF16)
     kept = jnp.where(core == 0, first, second)
     given = jnp.where(core == 0, second, first)
     state_in = jnp.concatenate([kept, exchange(given, 1)], axis=0)
+    head_grad = (head_grad, own, own_theirs)
     return grad_full, grad_other, head_grad, state_in, (even_a, odd_a, window1, window2, window4, window8, window12)
 
 
@@ -504,9 +504,10 @@
     total = even.astype(F32) + mul_t(even_a, odd)
     for window, distance in ((window1, 2), (window2, 4)):
         passed = mul_t(window, total.astype(BF16)).astype(BF16)
-        if distance == 4:
-            gate, passed = lax.optimization_barrier((gate, passed))
-        total = total + send(passed, -distance).astype(F32)
+        came = send(passed, -distance)
+        if distance == 2:
+            gate, came = lax.optimization_barrier((gate, came))
+        total = total + came.astype(F32)
     rounded = total.astype(BF16)
     second = send(rounded, -2).astype(F32)
     for window, distance in ((window4, 10), (window8, 18), (window12, 26)):
@@ -535,7 +536,7 @@
         jnp.broadcast_to(out_grad[None], (8, WIDTH, 512)), "tp", 0, 0, tiled=True
     )
     grad_full, grad_other, head_grad, state, saved = forward_states(
-        place, mine, theirs, core, grad_full, weight_mine
+        place, mine, theirs, core, grad_full, weight_mine, qt
     )
     heads = head_outputs(place, qt, local_out, state)
     heads_other = exchange(heads, 1)
@@ -543,7 +544,7 @@
     ring_sum = lax.psum_scatter(
         terms, "ctx", scatter_dimension=0, axis_index_groups=rings
     ).reshape(2, WIDTH, 512)
-    head_grad, own, own_theirs = own_cotangent(place, *head_grad, qt)
+    head_grad, own, own_theirs = head_grad
     parts = mixed_parts(place, heads, heads_other, weight_mine)
     parts, end = backward_states(own, own_theirs, core, saved, parts)
     end, ring_sum = lax.optimization_barrier((end, ring_sum))

time: 167 us -> 170 us (1.018)
  the two profiles are of different devices: /device:TPU:1 before, /device:TPU:8 now
where the time goes in v9:
time: 170 us; the launch traced here: 169 us
  starting transfers between devices  66.9 us (39%)
  Pallas kernels  40.1 us (24%)
  waiting for transfers between devices  33.4 us (20%)
  between operations  14.4 us (8%)
  other arithmetic  6.94 us (4%)
  local copies, waits for them, and re-layouts  4.24 us (2%)
  matrix products  3.4 us (2%)
    ppermute x11, starting transfers between devices, send(): return lax.ppermute(block, 'ctx', route)  43.9 us
    ppermute x11, waiting for transfers between devices, send(): return lax.ppermute(block, 'ctx', route)  28.8 us
    ppermute x10, starting transfers between devices, exchange(): return lax.ppermute(block, 'ctx', route)  12.9 us
    pallas_call x2, Pallas kernels, prepare(): pl.pallas_call(functools.partial(prepare_kernel, mine), grid_spec=pltpu.P...  12.7 us
    pallas_call x1, Pallas kernels, pull(): call(pull_kernel, 2, [by_columns(WIDTH), by_columns(PAIRS), whole(4, PAIR...  6.28 us
    pallas_call x1, Pallas kernels, head_gradient(): call(head_grad_kernel, STEPS, [whole(8, WIDTH, 512), whole(8, WIDTH, 512)...  5.32 us
    all_to_all x1, starting transfers between devices, local(): parts = lax.all_to_all(parts, 'tp', 0, 0, tiled=True)  5.17 us
    pallas_call x1, Pallas kernels, mixed_parts(): call(mixed_kernel, STEPS, [whole(WIDTH, 512), whole(WIDTH, 512), weight_t...  4.96 us
  transfers between devices with their start and end apart: 25, of which 11 were waited for; matrix products, arithmetic and copies ran while one was open for 4% of the time, Pallas kernels for 19%

profile of v9, /device:TPU:8, one launch (start us, length us, event | category | flops | bytes accessed | tf_op | source)
XLA Modules:
  0.0 169.4 jit_solution(17030239411432476997)
XLA Ops:
  7.2 3.1 %collective-permute-start = (bf16[128,512]{1,0:T(8,128)(2,1)}, bf16[128,512]{1,0:T(8,128)(2,1)S(1)}, u32[]{:S(2)}, u32[]{:S(2)}) collective-permute-start(bf16[128,512]{1,0:T(8,128)(2,1)} %param.10), channel_id=1, source_target_pairs={{0,128},{8,136},{16,144},{24,152},{32,160},{40,168},{48,176},{56,1... | collective-permute-start | bytes 393224 | tf_op jit(solution)/shard_map/ppermute | solution.py:26
  10.9 6.3 %shard_map.109 = (bf16[2,128,256]{2,1,0:T(8,128)(2,1)}, f32[4,256,256]{2,1,0:T(8,128)}, f32[4,256,256]{2,1,0:T(8,128)}, f32[4,128,128]{2,1,0:T(8,128)}, f32[4,128,128]{2,1,0:T(8,128)}) custom-call(s32[2]{0:T(128)} %pad_add_fusion.refs_0_.place, bf16[128,512]{1,0:T(8,128)(2,1)} %q_ref.1, bf16[128,1024]{1,0:T(8,128)(2,1)} %k_ref.1, bf16[128,1024]{1,0:T(8,128)(2,1)} %refs_3_.2, ...), custom_call_target="tpu_custom_call" | custom-call | flops 104857600 | bytes 16777216 | tf_op jit(solution)/shard_map/pallas_call | solution.py:172
  17.2 1.6 pad_maximum_fusion
  19.0 6.4 %shard_map.110 = (bf16[2,128,256]{2,1,0:T(8,128)(2,1)}, f32[4,256,256]{2,1,0:T(8,128)}, f32[4,256,256]{2,1,0:T(8,128)}, f32[4,128,128]{2,1,0:T(8,128)}, f32[4,128,128]{2,1,0:T(8,128)}) custom-call(s32[2]{0:T(128)} %pad_add_fusion.refs_0_.place, bf16[128,512]{1,0:T(8,128)(2,1)} %q_ref.1, ...), custom_call_target="tpu_custom_call", output_to_operand_aliasing={{1}: (5, {}), {2}: (6, {}), {3}: (7, {}), {4}: (8, {})} | custom-call | flops 1048576 | bytes 65536 | tf_op jit(solution)/shard_map/pallas_call | solution.py:172
  26.6 5.2 %collective-permute-start.3 = (bf16[2,128,256]{2,1,0:T(8,128)(2,1)S(1)}, bf16[2,128,256]{2,1,0:T(8,128)(2,1)S(1)}, u32[]{:S(2)}, u32[]{:S(2)}) collective-permute-start(bf16[2,128,256]{2,1,0:T(8,128)(2,1)S(1)} %pad_maximum_fusion.3), channel_id=1, source_target_pairs={{0,32},{8,40},{16,48},{24,56},{32,64},{40,72},{48,80},{56,88},{64,... | collective-permute-start | bytes 393224 | tf_op jit(solution)/shard_map/ppermute | solution.py:21
  31.8 3.8 %collective-permute-start.2 = (bf16[2,128,256]{2,1,0:T(8,128)(2,1)S(1)}, bf16[2,128,256]{2,1,0:T(8,128)(2,1)S(1)}, u32[]{:S(2)}, u32[]{:S(2)}) collective-permute-start(bf16[2,128,256]{2,1,0:T(8,128)(2,1)S(1)} %pad_maximum_fusion.3), channel_id=1, source_target_pairs={{0,16},{8,24},{16,32},{24,40},{32,48},{40,56},{48,64},{56,72},{64,... | collective-permute-start | bytes 393224 | tf_op jit(solution)/shard_map/ppermute | solution.py:21
  36.7 4.9 %all-to-all-start = ((bf16[8,128,512]{2,1,0:T(8,128)(2,1)}), bf16[8,128,512]{2,1,0:T(8,128)(2,1)S(1)}, u32[]{:S(2)}, u32[]{:S(2)}) async-start(bf16[8,128,512]{2,1,0:T(8,128)(2,1)} %broadcast_in_dim.2), calls=%async_computation | async-start | bytes 2097152 | tf_op jit(solution)/shard_map/all_to_all | solution.py:535
  41.7 3.2 %collective-permute-done.2 = bf16[2,128,256]{2,1,0:T(8,128)(2,1)S(1)} collective-permute-done((bf16[2,128,256]{2,1,0:T(8,128)(2,1)S(1)}, bf16[2,128,256]{2,1,0:T(8,128)(2,1)S(1)}, u32[]{:S(2)}, u32[]{:S(2)}) %collective-permute-start.2) | collective-permute-done | bytes 131104 | tf_op jit(solution)/shard_map/ppermute | solution.py:21
  45.1 7.7 %collective-permute-start.4 = (bf16[2,128,256]{2,1,0:T(8,128)(2,1)S(1)}, bf16[2,128,256]{2,1,0:T(8,128)(2,1)S(1)}, u32[]{:S(2)}, u32[]{:S(2)}) collective-permute-start(bf16[2,128,256]{2,1,0:T(8,128)(2,1)S(1)} %pad_maximum_fusion.4), channel_id=1, source_target_pairs={{0,32},{8,40},{16,48},{24,56},{32,64},{40,72},{48,80},{56,88},{64,... | collective-permute-start | bytes 393224 | tf_op jit(solution)/shard_map/ppermute | solution.py:21
  52.8 8.3 %collective-permute-done.4 = bf16[2,128,256]{2,1,0:T(8,128)(2,1)S(1)} collective-permute-done((bf16[2,128,256]{2,1,0:T(8,128)(2,1)S(1)}, bf16[2,128,256]{2,1,0:T(8,128)(2,1)S(1)}, u32[]{:S(2)}, u32[]{:S(2)}) %collective-permute-start.4) | collective-permute-done | bytes 131104 | tf_op jit(solution)/shard_map/ppermute | solution.py:21
  62.1 10.7 %collective-permute-start.6 = (bf16[2,128,256]{2,1,0:T(8,128)(2,1)}, bf16[2,128,256]{2,1,0:T(8,128)(2,1)}, u32[]{:S(2)}, u32[]{:S(2)}) collective-permute-start(bf16[2,128,256]{2,1,0:T(8,128)(2,1)} %pad_maximum_fusion.2), channel_id=1, source_target_pairs={{0,64},{8,72},{16,80},{24,88},{32,96},{40,104},{48,112},{56,120},{... | collective-permute-start | bytes 393224 | tf_op jit(solution)/shard_map/ppermute | solution.py:21
  72.8 5.3 %shard_map.111 = (f32[128,512]{1,0:T(8,128)}, f32[128,512]{1,0:T(8,128)}) custom-call(s32[2]{0:T(128)} %pad_add_fusion.refs_0_.place, bf16[8,128,512]{2,1,0:T(8,128)(2,1)} %copy-done, bf16[8,128,512]{2,1,0:T(8,128)(2,1)} %collective-permute-done.5.other_ref, bf16[8,2,128,512]{3,2,1,0:T(8,128)(2,1)} %bitcast.19), custom_call_target="tpu_custom_call" | custom-call | flops 536870912 | bytes 5242880 | tf_op jit(solution)/shard_map/pallas_call | solution.py:320
  79.6 8.7 %collective-permute-start.8 = (bf16[2,128,256]{2,1,0:T(8,128)(2,1)S(1)}, bf16[2,128,256]{2,1,0:T(8,128)(2,1)S(1)}, u32[]{:S(2)}, u32[]{:S(2)}) collective-permute-start(bf16[2,128,256]{2,1,0:T(8,128)(2,1)S(1)} %pad_maximum_fusion.1), channel_id=1, source_target_pairs={{0,128},{8,136},{16,144},{24,152},{32,160},{40,168},{48,176},{56,1... | collective-permute-start | bytes 393224 | tf_op jit(solution)/shard_map/ppermute | solution.py:21
  88.9 3.3 %shard_map.112 = (f32[128,512]{1,0:T(8,128)}, bf16[2,128,128]{2,1,0:T(8,128)(2,1)}, bf16[2,128,128]{2,1,0:T(8,128)(2,1)}) custom-call(s32[2]{0:T(128)} %pad_add_fusion.refs_0_.place, f32[128,512]{1,0:T(8,128)} %get-tuple-element.65.kept_ref, f32[128,512]{1,0:T(8,128)} %copy-done.6, f32[4,128,128]{2,1,0:T(8,128)} %get-tuple-element.55.qt_ref), custom_call_target="tpu_custom_call" | custom-call | flops 1024 | bytes 1024 | tf_op jit(solution)/shard_map/pallas_call | solution.py:348
  92.9 1.1 collective-permute-done.9
  94.6 2.6 %shard_map.113.heads_ref = bf16[128,512]{1,0:T(8,128)(2,1)} custom-call(s32[2]{0:T(128)} %pad_add_fusion.refs_0_.place, f32[4,128,128]{2,1,0:T(8,128)} %get-tuple-element.55.qt_ref, f32[4,128,128]{2,1,0:T(8,128)} %get-tuple-element.56.local_ref, bf16[4,128,128]{2,1,0:T(8,128)(2,1)} %pad_maximum_fusion.5.state_ref), custom_call_target="tpu_custom_call" | custom-call | flops 16777216 | bytes 1048576 | tf_op jit(solution)/shard_map/pallas_call | solution.py:239
  97.4 1.4 collective-permute-done.10.heads_other_ref
  99.5 4.9 %shard_map.115 = bf16[8,256,512]{2,1,0:T(8,128)(2,1)} custom-call(s32[2]{0:T(128)} %pad_add_fusion.refs_0_.place, bf16[8,128,512]{2,1,0:T(8,128)(2,1)} %copy-done, bf16[8,128,512]{2,1,0:T(8,128)(2,1)} %collective-permute-done.5.other_ref, bf16[128,512]{1,0:T(8,128)(2,1)} %shard_map.113.heads_ref, bf16[128,512]{1,0:T(8,128)(2,1)} %copy-done.1), custom_call_target="tpu_custom_call" | custom-call | flops 536870912 | bytes 5242880 | tf_op jit(solution)/shard_map/pallas_call | solution.py:263
  106.9 1.3 collective-permute-start.12
  108.2 5.0 %shard_map.114 = bf16[8,256,256]{2,1,0:T(8,128)(2,1)} custom-call(s32[2]{0:T(128)} %pad_add_fusion.refs_0_.place, bf16[128,512]{1,0:T(8,128)(2,1)} %shard_map.113.heads_ref, bf16[128,512]{1,0:T(8,128)(2,1)} %copy-done.1, bf16[8,2,128,512]{3,2,1,0:T(8,128)(2,1)} %bitcast.20), custom_call_target="tpu_custom_call" | custom-call | flops 536870912 | bytes 3145728 | tf_op jit(solution)/shard_map/pallas_call | solution.py:288
  113.4 1.3 collective-permute-start.14
  114.7 5.2 %all-to-all-start.1 = ((bf16[8,256,256]{2,1,0:T(8,128)(2,1)}), bf16[8,256,256]{2,1,0:T(8,128)(2,1)S(1)}, u32[]{:S(2)}, u32[]{:S(2)}) async-start(bf16[8,256,256]{2,1,0:T(8,128)(2,1)} %shard_map.114), calls=%async_computation.1 | async-start | bytes 2097152 | tf_op jit(solution)/shard_map/all_to_all | solution.py:552
  119.8 2.9 %collective-permute-done.14 = bf16[2,128,128]{2,1,0:T(8,128)(2,1)S(1)} collective-permute-done((bf16[2,128,128]{2,1,0:T(8,128)(2,1)S(1)}, bf16[2,128,128]{2,1,0:T(8,128)(2,1)S(1)}, u32[]{:S(2)}, u32[]{:S(2)}) %collective-permute-start.14) | collective-permute-done | bytes 65568 | tf_op jit(solution)/shard_map/ppermute | solution.py:21
  123.5 1.3 collective-permute-start.16
  124.8 1.3 collective-permute-start.17
  126.1 1.3 collective-permute-start.18
  127.4 1.3 collective-permute-start.15
  128.7 4.5 %collective-permute-done.16 = bf16[2,128,128]{2,1,0:T(8,128)(2,1)S(1)} collective-permute-done((bf16[2,128,128]{2,1,0:T(8,128)(2,1)S(1)}, bf16[2,128,128]{2,1,0:T(8,128)(2,1)S(1)}, u32[]{:S(2)}, u32[]{:S(2)}) %collective-permute-start.16) | collective-permute-done | bytes 65568 | tf_op jit(solution)/shard_map/ppermute | solution.py:21
  133.1 4.5 %collective-permute-done.17 = bf16[2,128,128]{2,1,0:T(8,128)(2,1)S(1)} collective-permute-done((bf16[2,128,128]{2,1,0:T(8,128)(2,1)S(1)}, bf16[2,128,128]{2,1,0:T(8,128)(2,1)S(1)}, u32[]{:S(2)}, u32[]{:S(2)}) %collective-permute-start.17) | collective-permute-done | bytes 65568 | tf_op jit(solution)/shard_map/ppermute | solution.py:21
  137.7 5.4 %collective-permute-done.18 = bf16[2,128,128]{2,1,0:T(8,128)(2,1)S(1)} collective-permute-done((bf16[2,128,128]{2,1,0:T(8,128)(2,1)S(1)}, bf16[2,128,128]{2,1,0:T(8,128)(2,1)S(1)}, u32[]{:S(2)}, u32[]{:S(2)}) %collective-permute-start.18) | collective-permute-done | bytes 65568 | tf_op jit(solution)/shard_map/ppermute | solution.py:21
  147.4 8.1 %collective-permute-start.20 = (bf16[128,512]{1,0:T(8,128)(2,1)S(1)}, bf16[128,512]{1,0:T(8,128)(2,1)S(1)}, u32[]{:S(2)}, u32[]{:S(2)}) collective-permute-start(bf16[128,512]{1,0:T(8,128)(2,1)S(1)} %slice_bitcast_fusion), channel_id=1, source_target_pairs={{0,128},{8,136},{16,144},{24,152},{32,160},{40,168},{48,176},{56,1... | collective-permute-start | bytes 393224 | tf_op jit(solution)/shard_map/ppermute | solution.py:26
  155.5 6.3 %shard_map.116 = (bf16[128,512]{1,0:T(8,128)(2,1)}, bf16[128,1024]{1,0:T(8,128)(2,1)}, bf16[128,1024]{1,0:T(8,128)(2,1)}, f32[4,256]{1,0:T(4,128)}) custom-call(s32[2]{0:T(128)} %pad_add_fusion.refs_0_.place, bf16[128,512]{1,0:T(8,128)(2,1)} %q_ref.1, bf16[128,1024]{1,0:T(8,128)(2,1)} %k_ref.1, f32[4,256]{1,0:T(4,128)} %logit_ref.1, ...), custom_call_target="tpu_custom_call" | custom-call | flops 1879048192 | bytes 5242880 | tf_op jit(solution)/shard_map/pallas_call | solution.py:420
  (85 shorter events, 16.7 us)
Async XLA Ops:
  7.2 65.6 %all-gather.3.cloned.1.call-start = ((), (), s32[]{:S(2)}) async-start(), calls=%async_computation.4 | async-start | bytes 2359296 | tf_op jit(solution)/shard_map/all_gather | solution.py:534
  7.2 10.0 %collective-permute-start = (bf16[128,512]{1,0:T(8,128)(2,1)}, bf16[128,512]{1,0:T(8,128)(2,1)S(1)}, u32[]{:S(2)}, u32[]{:S(2)}) collective-permute-start(bf16[128,512]{1,0:T(8,128)(2,1)} %param.10), channel_id=1, source_target_pairs={{0,128},{8,136},{16,144},{24,152},{32,160},{40,168},{48,176},{56,1... | collective-permute-start | bytes 393224 | tf_op jit(solution)/shard_map/ppermute | solution.py:26
  18.9 6.5 %collective-permute-start.1 = (bf16[2,128,256]{2,1,0:T(8,128)(2,1)}, bf16[2,128,256]{2,1,0:T(8,128)(2,1)S(1)}, u32[]{:S(2)}, u32[]{:S(2)}) collective-permute-start(bf16[2,128,256]{2,1,0:T(8,128)(2,1)} %get-tuple-element.57), channel_id=1, source_target_pairs={{0,8},{8,0},{16,24},{24,16},{32,40},{40,32},{48,56},{56,48},{64,72... | collective-permute-start | bytes 393224 | tf_op jit(solution)/shard_map/ppermute | solution.py:26
  19.0 16.6 %copy-start.7 = (bf16[128,512]{1,0:T(8,128)(2,1)S(1)}, bf16[128,512]{1,0:T(8,128)(2,1)}, u32[]{:S(2)}) copy-start(bf16[128,512]{1,0:T(8,128)(2,1)} %param.11) | copy-start | bytes 393220
  26.6 15.1 %collective-permute-start.3 = (bf16[2,128,256]{2,1,0:T(8,128)(2,1)S(1)}, bf16[2,128,256]{2,1,0:T(8,128)(2,1)S(1)}, u32[]{:S(2)}, u32[]{:S(2)}) collective-permute-start(bf16[2,128,256]{2,1,0:T(8,128)(2,1)S(1)} %pad_maximum_fusion.3), channel_id=1, source_target_pairs={{0,32},{8,40},{16,48},{24,56},{32,64},{40,72},{48,80},{56,88},{64,... | collective-permute-start | bytes 393224 | tf_op jit(solution)/shard_map/ppermute | solution.py:21
  31.8 13.0 %collective-permute-start.2 = (bf16[2,128,256]{2,1,0:T(8,128)(2,1)S(1)}, bf16[2,128,256]{2,1,0:T(8,128)(2,1)S(1)}, u32[]{:S(2)}, u32[]{:S(2)}) collective-permute-start(bf16[2,128,256]{2,1,0:T(8,128)(2,1)S(1)} %pad_maximum_fusion.3), channel_id=1, source_target_pairs={{0,16},{8,24},{16,32},{24,40},{32,48},{40,56},{48,64},{56,72},{64,... | collective-permute-start | bytes 393224 | tf_op jit(solution)/shard_map/ppermute | solution.py:21
  36.7 25.3 %all-to-all-start = ((bf16[8,128,512]{2,1,0:T(8,128)(2,1)}), bf16[8,128,512]{2,1,0:T(8,128)(2,1)S(1)}, u32[]{:S(2)}, u32[]{:S(2)}) async-start(bf16[8,128,512]{2,1,0:T(8,128)(2,1)} %broadcast_in_dim.2), calls=%async_computation | async-start | bytes 2097152 | tf_op jit(solution)/shard_map/all_to_all | solution.py:535
  41.7 104.8 %reduce-scatter.2.cloned.1.call-start = ((), (), s32[]{:S(2)}) async-start(), calls=%async_computation.3 | async-start | bytes 2359296 | tf_op jit(solution)/shard_map/reduce_scatter | solution.py:544
  44.8 28.0 %copy-start.2 = (bf16[2,128,256]{2,1,0:T(8,128)(2,1)}, bf16[2,128,256]{2,1,0:T(8,128)(2,1)S(1)}, u32[]{:S(2)}) copy-start(bf16[2,128,256]{2,1,0:T(8,128)(2,1)S(1)} %collective-permute-done.2) | copy-start | bytes 393220
  45.1 16.1 %collective-permute-start.4 = (bf16[2,128,256]{2,1,0:T(8,128)(2,1)S(1)}, bf16[2,128,256]{2,1,0:T(8,128)(2,1)S(1)}, u32[]{:S(2)}, u32[]{:S(2)}) collective-permute-start(bf16[2,128,256]{2,1,0:T(8,128)(2,1)S(1)} %pad_maximum_fusion.4), channel_id=1, source_target_pairs={{0,32},{8,40},{16,48},{24,56},{32,64},{40,72},{48,80},{56,88},{64,... | collective-permute-start | bytes 393224 | tf_op jit(solution)/shard_map/ppermute | solution.py:21
  62.1 10.8 %copy-start = (bf16[8,128,512]{2,1,0:T(8,128)(2,1)}, bf16[8,128,512]{2,1,0:T(8,128)(2,1)S(1)}, u32[]{:S(2)}) copy-start(bf16[8,128,512]{2,1,0:T(8,128)(2,1)S(1)} %all-to-all-done.own_ref) | copy-start | bytes 3145732
  62.1 10.7 %collective-permute-start.5 = (bf16[8,128,512]{2,1,0:T(8,128)(2,1)S(1)}, bf16[8,128,512]{2,1,0:T(8,128)(2,1)}, u32[]{:S(2)}, u32[]{:S(2)}) collective-permute-start(bf16[8,128,512]{2,1,0:T(8,128)(2,1)S(1)} %all-to-all-done.own_ref), channel_id=1, source_target_pairs={{0,8},{8,0},{16,24},{24,16},{32,40},{40,32},{48,56},{56,48},{64,72... | collective-permute-start | bytes 3145736 | tf_op jit(solution)/shard_map/ppermute | solution.py:26
  62.1 16.1 %collective-permute-start.6 = (bf16[2,128,256]{2,1,0:T(8,128)(2,1)}, bf16[2,128,256]{2,1,0:T(8,128)(2,1)}, u32[]{:S(2)}, u32[]{:S(2)}) collective-permute-start(bf16[2,128,256]{2,1,0:T(8,128)(2,1)} %pad_maximum_fusion.2), channel_id=1, source_target_pairs={{0,64},{8,72},{16,80},{24,88},{32,96},{40,104},{48,112},{56,120},{... | collective-permute-start | bytes 393224 | tf_op jit(solution)/shard_map/ppermute | solution.py:21
  79.2 9.0 %collective-permute-start.7 = (f32[128,512]{1,0:T(8,128)}, f32[128,512]{1,0:T(8,128)S(1)}, u32[]{:S(2)}, u32[]{:S(2)}) collective-permute-start(f32[128,512]{1,0:T(8,128)} %get-tuple-element.66), channel_id=1, source_target_pairs={{0,8},{8,0},{16,24},{24,16},{32,40},{40,32},{48,56},{56,48},{64,72... | collective-permute-start | bytes 786440 | tf_op jit(solution)/shard_map/ppermute | solution.py:26
  79.6 12.7 %collective-permute-start.8 = (bf16[2,128,256]{2,1,0:T(8,128)(2,1)S(1)}, bf16[2,128,256]{2,1,0:T(8,128)(2,1)S(1)}, u32[]{:S(2)}, u32[]{:S(2)}) collective-permute-start(bf16[2,128,256]{2,1,0:T(8,128)(2,1)S(1)} %pad_maximum_fusion.1), channel_id=1, source_target_pairs={{0,128},{8,136},{16,144},{24,152},{32,160},{40,168},{48,176},{56,1... | collective-permute-start | bytes 393224 | tf_op jit(solution)/shard_map/ppermute | solution.py:21
  92.6 1.3 collective-permute-start.9
  97.2 1.6 collective-permute-start.10
  104.3 0.8 copy-start.8
  104.3 2.1 %copy-start.4 = (bf16[2,128,128]{2,1,0:T(8,128)(2,1)S(1)}, bf16[2,128,128]{2,1,0:T(8,128)(2,1)}, u32[]{:S(2)}) copy-start(bf16[2,128,128]{2,1,0:T(8,128)(2,1)} %get-tuple-element.71) | copy-start | bytes 196612
  104.3 2.3 %copy-start.3 = (bf16[2,128,256]{2,1,0:T(8,128)(2,1)S(1)}, bf16[2,128,256]{2,1,0:T(8,128)(2,1)}, u32[]{:S(2)}) copy-start(bf16[2,128,256]{2,1,0:T(8,128)(2,1)} %copy-done.2) | copy-start | bytes 393220
  105.2 1.3 collective-permute-start.11
  106.9 6.3 %collective-permute-start.12 = (bf16[2,128,128]{2,1,0:T(8,128)(2,1)S(1)}, bf16[2,128,128]{2,1,0:T(8,128)(2,1)S(1)}, u32[]{:S(2)}, u32[]{:S(2)}) collective-permute-start(bf16[2,128,128]{2,1,0:T(8,128)(2,1)S(1)} %convolution_convert_fusion.4), channel_id=1, source_target_pairs={{16,0},{24,8},{32,16},{40,24},{48,32},{56,40},{64,48},{72,56},{80,... | collective-permute-start | bytes 196616 | tf_op jit(solution)/shard_map/ppermute | solution.py:21
  113.4 9.4 %collective-permute-start.14 = (bf16[2,128,128]{2,1,0:T(8,128)(2,1)S(1)}, bf16[2,128,128]{2,1,0:T(8,128)(2,1)S(1)}, u32[]{:S(2)}, u32[]{:S(2)}) collective-permute-start(bf16[2,128,128]{2,1,0:T(8,128)(2,1)S(1)} %convolution_convert_fusion.3), channel_id=1, source_target_pairs={{32,0},{40,8},{48,16},{56,24},{64,32},{72,40},{80,48},{88,56},{96,... | collective-permute-start | bytes 196616 | tf_op jit(solution)/shard_map/ppermute | solution.py:21
  114.7 28.7 %all-to-all-start.1 = ((bf16[8,256,256]{2,1,0:T(8,128)(2,1)}), bf16[8,256,256]{2,1,0:T(8,128)(2,1)S(1)}, u32[]{:S(2)}, u32[]{:S(2)}) async-start(bf16[8,256,256]{2,1,0:T(8,128)(2,1)} %shard_map.114), calls=%async_computation.1 | async-start | bytes 2097152 | tf_op jit(solution)/shard_map/all_to_all | solution.py:552
  123.5 9.7 %collective-permute-start.16 = (bf16[2,128,128]{2,1,0:T(8,128)(2,1)S(1)}, bf16[2,128,128]{2,1,0:T(8,128)(2,1)S(1)}, u32[]{:S(2)}, u32[]{:S(2)}) collective-permute-start(bf16[2,128,128]{2,1,0:T(8,128)(2,1)S(1)} %convolution_convert_fusion.2), channel_id=1, source_target_pairs={{80,0},{88,8},{96,16},{104,24},{112,32},{120,40},{128,48},{136,56}... | collective-permute-start | bytes 196616 | tf_op jit(solution)/shard_map/ppermute | solution.py:21
  124.8 12.9 %collective-permute-start.17 = (bf16[2,128,128]{2,1,0:T(8,128)(2,1)S(1)}, bf16[2,128,128]{2,1,0:T(8,128)(2,1)S(1)}, u32[]{:S(2)}, u32[]{:S(2)}) collective-permute-start(bf16[2,128,128]{2,1,0:T(8,128)(2,1)S(1)} %convolution_convert_fusion.1), channel_id=1, source_target_pairs={{144,0},{152,8},{160,16},{168,24},{176,32},{184,40},{192,48},{200,... | collective-permute-start | bytes 196616 | tf_op jit(solution)/shard_map/ppermute | solution.py:21
  126.1 17.0 %collective-permute-start.18 = (bf16[2,128,128]{2,1,0:T(8,128)(2,1)S(1)}, bf16[2,128,128]{2,1,0:T(8,128)(2,1)S(1)}, u32[]{:S(2)}, u32[]{:S(2)}) collective-permute-start(bf16[2,128,128]{2,1,0:T(8,128)(2,1)S(1)} %convolution_convert_fusion), channel_id=1, source_target_pairs={{208,0},{216,8},{224,16},{232,24},{240,32},{248,40},{209,1},{217,9... | collective-permute-start | bytes 196616 | tf_op jit(solution)/shard_map/ppermute | solution.py:21
  127.4 15.7 %collective-permute-start.15 = (bf16[2,128,128]{2,1,0:T(8,128)(2,1)S(1)}, bf16[2,128,128]{2,1,0:T(8,128)(2,1)S(1)}, u32[]{:S(2)}, u32[]{:S(2)}) collective-permute-start(bf16[2,128,128]{2,1,0:T(8,128)(2,1)S(1)} %add_convert_fusion.2), channel_id=1, source_target_pairs={{16,0},{24,8},{32,16},{40,24},{48,32},{56,40},{64,48},{72,56},{80,... | collective-permute-start | bytes 196616 | tf_op jit(solution)/shard_map/ppermute | solution.py:21
  143.3 1.3 collective-permute-start.19
  143.6 1.7 %collective-permute-start.13 = (bf16[128,256]{1,0:T(8,128)(2,1)S(1)}, bf16[128,256]{1,0:T(8,128)(2,1)S(1)}, u32[]{:S(2)}, u32[]{:S(2)}) collective-permute-start(bf16[128,256]{1,0:T(8,128)(2,1)S(1)} %slice.117), channel_id=1, source_target_pairs={{0,8},{8,0},{16,24},{24,16},{32,40},{40,32},{48,56},{56,48},{64,72... | collective-permute-start | bytes 196616 | tf_op jit(solution)/shard_map/ppermute | solution.py:26
  147.4 14.4 %collective-permute-start.20 = (bf16[128,512]{1,0:T(8,128)(2,1)S(1)}, bf16[128,512]{1,0:T(8,128)(2,1)S(1)}, u32[]{:S(2)}, u32[]{:S(2)}) collective-permute-start(bf16[128,512]{1,0:T(8,128)(2,1)S(1)} %slice_bitcast_fusion), channel_id=1, source_target_pairs={{0,128},{8,136},{16,144},{24,152},{32,160},{40,168},{48,176},{56,1... | collective-permute-start | bytes 393224 | tf_op jit(solution)/shard_map/ppermute | solution.py:26
  155.5 6.3 %copy-start.5 = (bf16[1,256,512]{2,1,0:T(8,128)(2,1)S(1)}, bf16[1,256,512]{2,1,0:T(8,128)(2,1)}, u32[]{:S(2)}) copy-start(bf16[1,256,512]{2,1,0:T(8,128)(2,1)} %reduce-scatter.2.cloned.1.call-done) | copy-start | bytes 786436
  (2 other events, 1.4 us)
Sparse Core Ops, SparseCore 0:
  19.0 53.1 all-gather.2
  104.5 41.9 reduce-scatter.1

commit v10 on v6

--- a/solution.py
+++ b/solution.py
@@ -454,7 +454,7 @@
     return x[:, :, :WIDTH], x[:, :, WIDTH:]
 
 
-def forward_states(place, mine, theirs, core, grad_full, weight):
+def forward_states(place, mine, theirs, index, core, grad_full, weight):
     theirs = exchange(theirs, 1)
     even = jnp.where(core == 0, mine, theirs)
     odd = jnp.where(core == 0, theirs, mine)
@@ -464,53 +464,61 @@
     chip = jnp.concatenate(
         [joined[:, :, :WIDTH], joined[:, :, WIDTH:] + odd_b.astype(F32)], axis=2
     ).astype(BF16)
-    one, two = send(chip, 2), send(chip, 4)
-    window1, state = halves(one)
-    step = mul(window1, two)
-    state = state.astype(F32) + step[:, :, WIDTH:]
-    window2 = step[:, :, :WIDTH].astype(BF16)
-    step = mul(window2, send(jnp.concatenate([window2, state.astype(BF16)], axis=2), 4))
-    state = state + step[:, :, WIDTH:]
-    window4 = step[:, :, :WIDTH].astype(BF16)
-    rounded = state.astype(BF16)
-    both = jnp.concatenate([window4, rounded], axis=2)
-    grad_full, both = lax.optimization_barrier((grad_full, both))
-    near, mid, far_b = send(both, 8), send(both, 16), send(rounded, 24)
-    grad_other = exchange(grad_full, 1)
+    total, levels = chip, []
+    diagonal = jnp.broadcast_to(jnp.eye(WIDTH, dtype=BF16), (2, WIDTH, WIDTH))
+    for bit in (2, 4, 8):
+        came = exchange(total, bit)
+        if bit == 8:
+            grad_other, came = lax.optimization_barrier((exchange(grad_full, 1), came))
+        upper = (index & bit) != 0
+        left, right = jnp.where(upper, came, total), jnp.where(upper, total, came)
+        right_a, right_b = halves(right)
+        step = mul(right_a, left)
+        total = jnp.concatenate(
+            [step[:, :, :WIDTH], step[:, :, WIDTH:] + right_b.astype(F32)], axis=2
+        ).astype(BF16)
+        came_a, came_b = halves(came)
+        if not levels:
+            levels.append((bit, left[:, :, :WIDTH], None))
+            before, state = jnp.where(upper, came_a, diagonal), jnp.where(upper, came_b, 0.0)
+            state = state.astype(F32)
+            after = jnp.where(upper, diagonal, came_a)
+        else:
+            levels.append((bit, left[:, :, :WIDTH], after))
+            step = mul(before, came)
+            before = jnp.where(upper, step[:, :, :WIDTH].astype(BF16), before)
+            state = jnp.where(upper, state + step[:, :, WIDTH:], state)
+            after = jnp.where(upper, after, mul(came_a, after).astype(BF16))
+    weight, total = lax.optimization_barrier((weight, total))
+    far = send(total[:, :, WIDTH:], 16)
     kept_grad, given_grad = head_gradient(place, grad_full, grad_other, weight)
-    kept_grad, given_grad, near, mid, far_b = lax.optimization_barrier(
-        (kept_grad, given_grad, near, mid, far_b)
-    )
-    near_a, near_b = halves(near)
-    mid_a, mid_b = halves(mid)
+    kept_grad, given_grad, far = lax.optimization_barrier((kept_grad, given_grad, far))
     head_grad = (kept_grad, exchange(given_grad, 1))
-    inner = (mid_b.astype(F32) + mul(mid_a, far_b)).astype(BF16)
-    inner = (near_b.astype(F32) + mul(near_a, inner)).astype(BF16)
-    first = (state + mul(window4, inner)).astype(BF16)
-    window8 = mul(window4, near_a).astype(BF16)
-    window12 = mul(window8, mid_a).astype(BF16)
+    first = (state + mul(before, far)).astype(BF16)
     second = (mul(even_a, first) + even_b.astype(F32)).astype(BF16)
     kept = jnp.where(core == 0, first, second)
     given = jnp.where(core == 0, second, first)
     state_in = jnp.concatenate([kept, exchange(given, 1)], axis=0)
-    return grad_full, grad_other, head_grad, state_in, (even_a, odd_a, window1, window2, window4, window8, window12)
-
-
-def backward_states(mine, theirs, core, saved, gate):
-    even_a, odd_a, window1, window2, window4, window8, window12 = saved
+    return grad_full, grad_other, head_grad, state_in, (even_a, odd_a, levels, after)
+
+
+def backward_states(mine, theirs, index, core, saved, gate):
+    even_a, odd_a, levels, after = saved
     theirs = exchange(theirs, 1)
     even = jnp.where(core == 0, mine, theirs)
     odd = jnp.where(core == 0, theirs, mine)
-    total = even.astype(F32) + mul_t(even_a, odd)
-    for window, distance in ((window1, 2), (window2, 4)):
-        passed = mul_t(window, total.astype(BF16)).astype(BF16)
-        if distance == 4:
-            gate, passed = lax.optimization_barrier((gate, passed))
-        total = total + send(passed, -distance).astype(F32)
-    rounded = total.astype(BF16)
-    second = send(rounded, -2).astype(F32)
-    for window, distance in ((window4, 10), (window8, 18), (window12, 26)):
-        second += send(mul_t(window, rounded).astype(BF16), -distance).astype(F32)
+    total = (even.astype(F32) + mul_t(even_a, odd)).astype(BF16)
+    for bit, left_a, window in levels:
+        came = exchange(total, bit)
+        upper = (index & bit) != 0
+        if window is None:
+            gate, came = lax.optimization_barrier((gate, came))
+            second = jnp.where(upper, 0.0, came.astype(F32))
+        else:
+            second = jnp.where(upper, second, second + mul_t(window, came))
+        left, right = jnp.where(upper, came, total), jnp.where(upper, total, came)
+        total = (left.astype(F32) + mul_t(left_a, right)).astype(BF16)
+    second = second + mul_t(after, send(total, -16))
     second = second.astype(BF16)
     first = (odd.astype(F32) + mul_t(odd_a, second)).astype(BF16)
     kept = jnp.where(core == 0, first, second)
@@ -535,7 +543,7 @@
         jnp.broadcast_to(out_grad[None], (8, WIDTH, 512)), "tp", 0, 0, tiled=True
     )
     grad_full, grad_other, head_grad, state, saved = forward_states(
-        place, mine, theirs, core, grad_full, weight_mine
+        place, mine, theirs, index, core, grad_full, weight_mine
     )
     heads = head_outputs(place, qt, local_out, state)
     heads_other = exchange(heads, 1)
@@ -545,7 +553,7 @@
     ).reshape(2, WIDTH, 512)
     head_grad, own, own_theirs = own_cotangent(place, *head_grad, qt)
     parts = mixed_parts(place, heads, heads_other, weight_mine)
-    parts, end = backward_states(own, own_theirs, core, saved, parts)
+    parts, end = backward_states(own, own_theirs, index, core, saved, parts)
     end, ring_sum = lax.optimization_barrier((end, ring_sum))
     weight_grad = ring_sum[0].astype(F32) + exchange(ring_sum[1], 16).astype(F32)
     parts = lax.all_to_all(parts, "tp", 0, 0, tiled=True)

time: 167 us -> 160 us (0.958)
  starting transfers between devices: 66.4 us -> 43.3 us
  waiting for transfers between devices: 26.6 us -> 43.2 us
    ppermute x12 -> x2, starting transfers between devices: 38.9 us -> 5.43 us  [send(): return lax.ppermute(block, 'ctx', route)]
    ppermute x10 -> x16, waiting for transfers between devices: 5.07 us -> 32 us  [exchange(): return lax.ppermute(block, 'ctx', route)]
    ppermute x12 -> x2, waiting for transfers between devices: 21.5 us -> 6.05 us  [send(): return lax.ppermute(block, 'ctx', route)]
    ppermute x10 -> x16, starting transfers between devices: 17.6 us -> 29 us  [exchange(): return lax.ppermute(block, 'ctx', route)]
    all_gather x1, waiting for transfers between devices: 0.01 us -> 2.93 us  [local(): lax.all_gather(weight_pair, 'ctx', axis=0, axis_index_groups=rings)]
    all_to_all x1, waiting for transfers between devices: 0.01 us -> 2.16 us  [local(): lax.all_to_all(jnp.broadcast_to(out_grad[None], (8, WIDTH, 512)), 'tp', 0...]
    dot_general x7 -> x9, matrix products: 3.89 us -> 3.29 us  [mul(): return jnp.einsum('hij,hjk->hik', a, b, preferred_element_type=F32)]
  transfers between devices with their start and end apart: 26 -> 22, of which waited for: 9 -> 12; matrix products, arithmetic and copies ran while one was open for 6% -> 7% of each run, Pallas kernels for 20% -> 20%
where the time goes in v10:
time: 160 us; the launch traced here: 159 us
  starting transfers between devices  43.3 us (27%)
  waiting for transfers between devices  43.2 us (27%)
  Pallas kernels  40.1 us (25%)
  between operations  14.4 us (9%)
  other arithmetic  6.37 us (4%)
  matrix products  6.1 us (4%)
  local copies, waits for them, and re-layouts  5.97 us (4%)
    ppermute x16, waiting for transfers between devices, exchange(): return lax.ppermute(block, 'ctx', route)  32 us
    ppermute x16, starting transfers between devices, exchange(): return lax.ppermute(block, 'ctx', route)  29 us
    pallas_call x2, Pallas kernels, prepare(): pl.pallas_call(functools.partial(prepare_kernel, mine), grid_spec=pltpu.P...  12.7 us
    pallas_call x1, Pallas kernels, pull(): call(pull_kernel, 2, [by_columns(WIDTH), by_columns(PAIRS), whole(4, PAIR...  6.29 us
    ppermute x2, waiting for transfers between devices, send(): return lax.ppermute(block, 'ctx', route)  6.05 us
    ppermute x2, starting transfers between devices, send(): return lax.ppermute(block, 'ctx', route)  5.43 us
    pallas_call x1, Pallas kernels, head_gradient(): call(head_grad_kernel, STEPS, [whole(8, WIDTH, 512), whole(8, WIDTH, 512)...  5.34 us
    pallas_call x1, Pallas kernels, mixed_parts(): call(mixed_kernel, STEPS, [whole(WIDTH, 512), whole(WIDTH, 512), weight_t...  4.97 us
  transfers between devices with their start and end apart: 22, of which 12 were waited for; matrix products, arithmetic and copies ran while one was open for 7% of the time, Pallas kernels for 20%

profile of v10, /device:TPU:1, one launch (start us, length us, event | category | flops | bytes accessed | tf_op | source)
XLA Modules:
  0.0 159.4 jit_solution(4335528355727825060)
XLA Ops:
  7.2 3.7 %collective-permute-start = (bf16[128,512]{1,0:T(8,128)(2,1)}, bf16[128,512]{1,0:T(8,128)(2,1)S(1)}, u32[]{:S(2)}, u32[]{:S(2)}) collective-permute-start(bf16[128,512]{1,0:T(8,128)(2,1)} %param.10), channel_id=1, source_target_pairs={{0,128},{8,136},{16,144},{24,152},{32,160},{40,168},{48,176},{56,1... | collective-permute-start | bytes 393224 | tf_op jit(solution)/shard_map/ppermute | solution.py:26
  11.4 6.3 %shard_map.109 = (bf16[2,128,256]{2,1,0:T(8,128)(2,1)}, f32[4,256,256]{2,1,0:T(8,128)}, f32[4,256,256]{2,1,0:T(8,128)}, f32[4,128,128]{2,1,0:T(8,128)}, f32[4,128,128]{2,1,0:T(8,128)}) custom-call(s32[2]{0:T(128)} %pad_add_fusion.refs_0_.place, bf16[128,512]{1,0:T(8,128)(2,1)} %q_ref.1, bf16[128,1024]{1,0:T(8,128)(2,1)} %k_ref.1, bf16[128,1024]{1,0:T(8,128)(2,1)} %refs_3_.2, ...), custom_call_target="tpu_custom_call" | custom-call | flops 104857600 | bytes 16777216 | tf_op jit(solution)/shard_map/pallas_call | solution.py:172
  18.7 1.6 %pad_maximum_fusion = bf16[2,128,512]{2,1,0:T(8,128)(2,1)} fusion(bf16[1,128,512]{2,1,0:T(8,128)(2,1)S(1)} %bitcast.31, bf16[1,128,512]{2,1,0:T(8,128)(2,1)} %bitcast.30), kind=kLoop, calls=%fused_computation.13 | loop fusion | flops 131072 | bytes 524288 | tf_op jit(solution)/shard_map/stack | solution.py:538
  20.3 6.4 %shard_map.110 = (bf16[2,128,256]{2,1,0:T(8,128)(2,1)}, f32[4,256,256]{2,1,0:T(8,128)}, f32[4,256,256]{2,1,0:T(8,128)}, f32[4,128,128]{2,1,0:T(8,128)}, f32[4,128,128]{2,1,0:T(8,128)}) custom-call(s32[2]{0:T(128)} %pad_add_fusion.refs_0_.place, bf16[128,512]{1,0:T(8,128)(2,1)} %q_ref.1, ...), custom_call_target="tpu_custom_call", output_to_operand_aliasing={{1}: (5, {}), {2}: (6, {}), {3}: (7, {}), {4}: (8, {})} | custom-call | flops 1048576 | bytes 65536 | tf_op jit(solution)/shard_map/pallas_call | solution.py:172
  27.9 1.7 %collective-permute-start.2 = (bf16[2,128,256]{2,1,0:T(8,128)(2,1)S(1)}, bf16[2,128,256]{2,1,0:T(8,128)(2,1)S(1)}, u32[]{:S(2)}, u32[]{:S(2)}) collective-permute-start(bf16[2,128,256]{2,1,0:T(8,128)(2,1)S(1)} %pad_maximum_fusion.1), channel_id=1, source_target_pairs={{0,16},{8,24},{16,0},{24,8},{32,48},{40,56},{48,32},{56,40},{64,80... | collective-permute-start | bytes 393224 | tf_op jit(solution)/shard_map/ppermute | solution.py:26
  30.7 4.2 %all-to-all-start = ((bf16[8,128,512]{2,1,0:T(8,128)(2,1)}), bf16[8,128,512]{2,1,0:T(8,128)(2,1)S(1)}, u32[]{:S(2)}, u32[]{:S(2)}) async-start(bf16[8,128,512]{2,1,0:T(8,128)(2,1)} %broadcast_in_dim.21), calls=%async_computation | async-start | bytes 2097152 | tf_op jit(solution)/shard_map/all_to_all | solution.py:542
  35.3 3.1 %collective-permute-start.3 = (bf16[2,128,256]{2,1,0:T(8,128)(2,1)S(1)}, bf16[2,128,256]{2,1,0:T(8,128)(2,1)S(1)}, u32[]{:S(2)}, u32[]{:S(2)}) collective-permute-start(bf16[2,128,256]{2,1,0:T(8,128)(2,1)S(1)} %pad_maximum_fusion.2), channel_id=1, source_target_pairs={{0,32},{8,40},{16,48},{24,56},{32,0},{40,8},{48,16},{56,24},{64,96... | collective-permute-start | bytes 393224 | tf_op jit(solution)/shard_map/ppermute | solution.py:26
  38.4 9.6 %collective-permute-done.3 = bf16[2,128,256]{2,1,0:T(8,128)(2,1)S(1)} collective-permute-done((bf16[2,128,256]{2,1,0:T(8,128)(2,1)S(1)}, bf16[2,128,256]{2,1,0:T(8,128)(2,1)S(1)}, u32[]{:S(2)}, u32[]{:S(2)}) %collective-permute-start.3) | collective-permute-done | bytes 131104 | tf_op jit(solution)/shard_map/ppermute | solution.py:26
  48.0 2.2 %all-to-all-done.own_ref = bf16[8,128,512]{2,1,0:T(8,128)(2,1)S(1)} async-done(((bf16[8,128,512]{2,1,0:T(8,128)(2,1)}), bf16[8,128,512]{2,1,0:T(8,128)(2,1)S(1)}, u32[]{:S(2)}, u32[]{:S(2)}) %all-to-all-start) | async-done | bytes 1048608 | tf_op jit(solution)/shard_map/all_to_all | solution.py:542
  50.2 1.4 collective-permute-start.4
  51.9 6.1 %collective-permute-start.5 = (bf16[2,128,256]{2,1,0:T(8,128)(2,1)S(1)}, bf16[2,128,256]{2,1,0:T(8,128)(2,1)S(1)}, u32[]{:S(2)}, u32[]{:S(2)}) collective-permute-start(bf16[2,128,256]{2,1,0:T(8,128)(2,1)S(1)} %pad_maximum_fusion.3), channel_id=1, source_target_pairs={{0,64},{8,72},{16,80},{24,88},{32,96},{40,104},{48,112},{56,120},{... | collective-permute-start | bytes 393224 | tf_op jit(solution)/shard_map/ppermute | solution.py:26
  58.2 7.6 %collective-permute-done.5 = bf16[2,128,256]{2,1,0:T(8,128)(2,1)S(1)} collective-permute-done((bf16[2,128,256]{2,1,0:T(8,128)(2,1)S(1)}, bf16[2,128,256]{2,1,0:T(8,128)(2,1)S(1)}, u32[]{:S(2)}, u32[]{:S(2)}) %collective-permute-start.5) | collective-permute-done | bytes 131104 | tf_op jit(solution)/shard_map/ppermute | solution.py:26
  67.1 2.9 %all-gather.3.cloned.1.call-done = bf16[16,128,512]{2,1,0:T(8,128)(2,1)} async-done(((bf16[2,128,512]{2,1,0:T(8,128)(2,1)}), bf16[16,128,512]{2,1,0:T(8,128)(2,1)}) %all-gather.3.cloned.1.call-update) | async-done | bytes 2097168 | tf_op jit(solution)/shard_map/all_gather | solution.py:541
  70.7 4.1 %collective-permute-start.6 = (bf16[2,128,128]{2,1,0:T(8,128)(2,1)}, bf16[2,128,128]{2,1,0:T(8,128)(2,1)}, u32[]{:S(2)}, u32[]{:S(2)}) collective-permute-start(bf16[2,128,128]{2,1,0:T(8,128)(2,1)} %slice.142), channel_id=1, source_target_pairs={{0,128},{8,136},{16,144},{24,152},{32,160},{40,168},{48,176},{56,1... | collective-permute-start | bytes 196616 | tf_op jit(solution)/shard_map/ppermute | solution.py:21
  75.7 5.3 %shard_map.111 = (f32[128,512]{1,0:T(8,128)}, f32[128,512]{1,0:T(8,128)}) custom-call(s32[2]{0:T(128)} %pad_add_fusion.refs_0_.place, bf16[8,128,512]{2,1,0:T(8,128)(2,1)} %copy-done, bf16[8,128,512]{2,1,0:T(8,128)(2,1)} %copy-done.1, bf16[8,2,128,512]{3,2,1,0:T(8,128)(2,1)} %bitcast.26), custom_call_target="tpu_custom_call" | custom-call | flops 536870912 | bytes 5242880 | tf_op jit(solution)/shard_map/pallas_call | solution.py:320
  81.1 1.3 fusion.9
  82.5 3.1 %collective-permute-start.7 = (bf16[2,128,128]{2,1,0:T(8,128)(2,1)S(1)}, bf16[2,128,128]{2,1,0:T(8,128)(2,1)S(1)}, u32[]{:S(2)}, u32[]{:S(2)}) collective-permute-start(bf16[2,128,128]{2,1,0:T(8,128)(2,1)S(1)} %get-tuple-element.93), channel_id=1, source_target_pairs={{0,8},{8,0},{16,24},{24,16},{32,40},{40,32},{48,56},{56,48},{64,72... | collective-permute-start | bytes 196616 | tf_op jit(solution)/shard_map/ppermute | solution.py:26
  87.1 2.6 %shard_map.112.heads_ref = bf16[128,512]{1,0:T(8,128)(2,1)} custom-call(s32[2]{0:T(128)} %pad_add_fusion.refs_0_.place, f32[4,128,128]{2,1,0:T(8,128)} %get-tuple-element.53.qt_ref, f32[4,128,128]{2,1,0:T(8,128)} %get-tuple-element.54.local_ref, bf16[4,128,128]{2,1,0:T(8,128)(2,1)} %pad_maximum_fusion.5.state_ref), custom_call_target="tpu_custom_call" | custom-call | flops 16777216 | bytes 1048576 | tf_op jit(solution)/shard_map/pallas_call | solution.py:239
  90.1 1.2 collective-permute-done.8.heads_other_ref
  92.0 4.9 %shard_map.115 = bf16[8,256,512]{2,1,0:T(8,128)(2,1)} custom-call(s32[2]{0:T(128)} %pad_add_fusion.refs_0_.place, bf16[8,128,512]{2,1,0:T(8,128)(2,1)} %copy-done, bf16[8,128,512]{2,1,0:T(8,128)(2,1)} %copy-done.1, bf16[128,512]{1,0:T(8,128)(2,1)} %shard_map.112.heads_ref, bf16[128,512]{1,0:T(8,128)(2,1)} %copy-done.2), custom_call_target="tpu_custom_call" | custom-call | flops 536870912 | bytes 5242880 | tf_op jit(solution)/shard_map/pallas_call | solution.py:263
  98.1 1.2 collective-permute-done.9.came_ref
  100.0 3.3 %shard_map.114 = (f32[128,512]{1,0:T(8,128)}, bf16[2,128,128]{2,1,0:T(8,128)(2,1)}, bf16[2,128,128]{2,1,0:T(8,128)(2,1)}) custom-call(s32[2]{0:T(128)} %pad_add_fusion.refs_0_.place, f32[128,512]{1,0:T(8,128)} %get-tuple-element.65.kept_ref, f32[128,512]{1,0:T(8,128)} %copy-done.8, f32[4,128,128]{2,1,0:T(8,128)} %get-tuple-element.53.qt_ref), custom_call_target="tpu_custom_call" | custom-call | flops 16777216 | bytes 1048576 | tf_op jit(solution)/shard_map/pallas_call | solution.py:348
  107.0 5.0 %shard_map.113 = bf16[8,256,256]{2,1,0:T(8,128)(2,1)} custom-call(s32[2]{0:T(128)} %pad_add_fusion.refs_0_.place, bf16[128,512]{1,0:T(8,128)(2,1)} %shard_map.112.heads_ref, bf16[128,512]{1,0:T(8,128)(2,1)} %copy-done.2, bf16[8,2,128,512]{3,2,1,0:T(8,128)(2,1)} %bitcast.27), custom_call_target="tpu_custom_call" | custom-call | flops 536870912 | bytes 3145728 | tf_op jit(solution)/shard_map/pallas_call | solution.py:288
  113.1 6.6 %collective-permute-done.13 = bf16[2,128,128]{2,1,0:T(8,128)(2,1)S(1)} collective-permute-done((bf16[2,128,128]{2,1,0:T(8,128)(2,1)S(1)}, bf16[2,128,128]{2,1,0:T(8,128)(2,1)S(1)}, u32[]{:S(2)}, u32[]{:S(2)}) %collective-permute-start.13) | collective-permute-done | bytes 65568 | tf_op jit(solution)/shard_map/ppermute | solution.py:26
  119.9 1.4 collective-permute-start.14
  121.4 4.5 %all-to-all-start.1 = ((bf16[8,256,256]{2,1,0:T(8,128)(2,1)}), bf16[8,256,256]{2,1,0:T(8,128)(2,1)S(1)}, u32[]{:S(2)}, u32[]{:S(2)}) async-start(bf16[8,256,256]{2,1,0:T(8,128)(2,1)} %shard_map.113), calls=%async_computation.1 | async-start | bytes 2097152 | tf_op jit(solution)/shard_map/all_to_all | solution.py:559
  125.9 3.5 %collective-permute-done.14 = bf16[2,128,128]{2,1,0:T(8,128)(2,1)S(1)} collective-permute-done((bf16[2,128,128]{2,1,0:T(8,128)(2,1)S(1)}, bf16[2,128,128]{2,1,0:T(8,128)(2,1)S(1)}, u32[]{:S(2)}, u32[]{:S(2)}) %collective-permute-start.14) | collective-permute-done | bytes 65568 | tf_op jit(solution)/shard_map/ppermute | solution.py:26
  129.7 1.3 collective-permute-start.15
  131.2 6.0 %collective-permute-done.15 = bf16[2,128,128]{2,1,0:T(8,128)(2,1)S(1)} collective-permute-done((bf16[2,128,128]{2,1,0:T(8,128)(2,1)S(1)}, bf16[2,128,128]{2,1,0:T(8,128)(2,1)S(1)}, u32[]{:S(2)}, u32[]{:S(2)}) %collective-permute-start.15) | collective-permute-done | bytes 65568 | tf_op jit(solution)/shard_map/ppermute | solution.py:21
  138.1 2.3 %collective-permute-start.16 = (bf16[2,128,128]{2,1,0:T(8,128)(2,1)S(1)}, bf16[2,128,128]{2,1,0:T(8,128)(2,1)S(1)}, u32[]{:S(2)}, u32[]{:S(2)}) collective-permute-start(bf16[2,128,128]{2,1,0:T(8,128)(2,1)S(1)} %get-tuple-element.91), channel_id=1, source_target_pairs={{0,8},{8,0},{16,24},{24,16},{32,40},{40,32},{48,56},{56,48},{64,72... | collective-permute-start | bytes 196616 | tf_op jit(solution)/shard_map/ppermute | solution.py:26
  140.6 2.3 %collective-permute-start.12 = (bf16[128,256]{1,0:T(8,128)(2,1)S(1)}, bf16[128,256]{1,0:T(8,128)(2,1)S(1)}, u32[]{:S(2)}, u32[]{:S(2)}) collective-permute-start(bf16[128,256]{1,0:T(8,128)(2,1)S(1)} %slice.183), channel_id=1, source_target_pairs={{0,8},{8,0},{16,24},{24,16},{32,40},{40,32},{48,56},{56,48},{64,72... | collective-permute-start | bytes 196616 | tf_op jit(solution)/shard_map/ppermute | solution.py:26
  145.5 6.3 %shard_map.116 = (bf16[128,512]{1,0:T(8,128)(2,1)}, bf16[128,1024]{1,0:T(8,128)(2,1)}, bf16[128,1024]{1,0:T(8,128)(2,1)}, f32[4,256]{1,0:T(4,128)}) custom-call(s32[2]{0:T(128)} %pad_add_fusion.refs_0_.place, bf16[128,512]{1,0:T(8,128)(2,1)} %q_ref.1, bf16[128,1024]{1,0:T(8,128)(2,1)} %k_ref.1, f32[4,256]{1,0:T(4,128)} %logit_ref.1, ...), custom_call_target="tpu_custom_call" | custom-call | flops 1879048192 | bytes 5242880 | tf_op jit(solution)/shard_map/pallas_call | solution.py:420
  (94 shorter events, 21.9 us)
Async XLA Ops:
  7.2 62.9 %all-gather.3.cloned.1.call-start = ((), (), s32[]{:S(2)}) async-start(), calls=%async_computation.4 | async-start | bytes 2359296 | tf_op jit(solution)/shard_map/all_gather | solution.py:541
  7.2 10.5 %collective-permute-start = (bf16[128,512]{1,0:T(8,128)(2,1)}, bf16[128,512]{1,0:T(8,128)(2,1)S(1)}, u32[]{:S(2)}, u32[]{:S(2)}) collective-permute-start(bf16[128,512]{1,0:T(8,128)(2,1)} %param.10), channel_id=1, source_target_pairs={{0,128},{8,136},{16,144},{24,152},{32,160},{40,168},{48,176},{56,1... | collective-permute-start | bytes 393224 | tf_op jit(solution)/shard_map/ppermute | solution.py:26
  17.7 9.0 %collective-permute-start.1 = (bf16[2,128,256]{2,1,0:T(8,128)(2,1)}, bf16[2,128,256]{2,1,0:T(8,128)(2,1)S(1)}, u32[]{:S(2)}, u32[]{:S(2)}) collective-permute-start(bf16[2,128,256]{2,1,0:T(8,128)(2,1)} %get-tuple-element.55), channel_id=1, source_target_pairs={{0,8},{8,0},{16,24},{24,16},{32,40},{40,32},{48,56},{56,48},{64,72... | collective-permute-start | bytes 393224 | tf_op jit(solution)/shard_map/ppermute | solution.py:26
  20.3 9.4 %copy-start.9 = (bf16[128,512]{1,0:T(8,128)(2,1)S(1)}, bf16[128,512]{1,0:T(8,128)(2,1)}, u32[]{:S(2)}) copy-start(bf16[128,512]{1,0:T(8,128)(2,1)} %param.11) | copy-start | bytes 393220
  27.7 3.0 %copy-start.3 = (bf16[2,128,256]{2,1,0:T(8,128)(2,1)}, bf16[2,128,256]{2,1,0:T(8,128)(2,1)S(1)}, u32[]{:S(2)}) copy-start(bf16[2,128,256]{2,1,0:T(8,128)(2,1)S(1)} %get-tuple-element.86) | copy-start | bytes 393220
  27.9 7.1 %collective-permute-start.2 = (bf16[2,128,256]{2,1,0:T(8,128)(2,1)S(1)}, bf16[2,128,256]{2,1,0:T(8,128)(2,1)S(1)}, u32[]{:S(2)}, u32[]{:S(2)}) collective-permute-start(bf16[2,128,256]{2,1,0:T(8,128)(2,1)S(1)} %pad_maximum_fusion.1), channel_id=1, source_target_pairs={{0,16},{8,24},{16,0},{24,8},{32,48},{40,56},{48,32},{56,40},{64,80... | collective-permute-start | bytes 393224 | tf_op jit(solution)/shard_map/ppermute | solution.py:26
  30.7 19.5 %all-to-all-start = ((bf16[8,128,512]{2,1,0:T(8,128)(2,1)}), bf16[8,128,512]{2,1,0:T(8,128)(2,1)S(1)}, u32[]{:S(2)}, u32[]{:S(2)}) async-start(bf16[8,128,512]{2,1,0:T(8,128)(2,1)} %broadcast_in_dim.21), calls=%async_computation | async-start | bytes 2097152 | tf_op jit(solution)/shard_map/all_to_all | solution.py:542
  35.0 109.6 %reduce-scatter.2.cloned.1.call-start = ((), (), s32[]{:S(2)}) async-start(), calls=%async_computation.3 | async-start | bytes 2359296 | tf_op jit(solution)/shard_map/reduce_scatter | solution.py:551
  35.3 12.7 %collective-permute-start.3 = (bf16[2,128,256]{2,1,0:T(8,128)(2,1)S(1)}, bf16[2,128,256]{2,1,0:T(8,128)(2,1)S(1)}, u32[]{:S(2)}, u32[]{:S(2)}) collective-permute-start(bf16[2,128,256]{2,1,0:T(8,128)(2,1)S(1)} %pad_maximum_fusion.2), channel_id=1, source_target_pairs={{0,32},{8,40},{16,48},{24,56},{32,0},{40,8},{48,16},{56,24},{64,96... | collective-permute-start | bytes 393224 | tf_op jit(solution)/shard_map/ppermute | solution.py:26
  50.2 25.5 %copy-start = (bf16[8,128,512]{2,1,0:T(8,128)(2,1)}, bf16[8,128,512]{2,1,0:T(8,128)(2,1)S(1)}, u32[]{:S(2)}) copy-start(bf16[8,128,512]{2,1,0:T(8,128)(2,1)S(1)} %all-to-all-done.own_ref) | copy-start | bytes 3145732
  50.2 15.6 %collective-permute-start.4 = (bf16[8,128,512]{2,1,0:T(8,128)(2,1)S(1)}, bf16[8,128,512]{2,1,0:T(8,128)(2,1)S(1)}, u32[]{:S(2)}, u32[]{:S(2)}) collective-permute-start(bf16[8,128,512]{2,1,0:T(8,128)(2,1)S(1)} %all-to-all-done.own_ref), channel_id=1, source_target_pairs={{0,8},{8,0},{16,24},{24,16},{32,40},{40,32},{48,56},{56,48},{64,72... | collective-permute-start | bytes 3145736 | tf_op jit(solution)/shard_map/ppermute | solution.py:26
  51.9 14.0 %collective-permute-start.5 = (bf16[2,128,256]{2,1,0:T(8,128)(2,1)S(1)}, bf16[2,128,256]{2,1,0:T(8,128)(2,1)S(1)}, u32[]{:S(2)}, u32[]{:S(2)}) collective-permute-start(bf16[2,128,256]{2,1,0:T(8,128)(2,1)S(1)} %pad_maximum_fusion.3), channel_id=1, source_target_pairs={{0,64},{8,72},{16,80},{24,88},{32,96},{40,104},{48,112},{56,120},{... | collective-permute-start | bytes 393224 | tf_op jit(solution)/shard_map/ppermute | solution.py:26
  58.2 7.7 %copy-start.5 = (f32[2,128,256]{2,1,0:T(8,128)}, f32[2,128,256]{2,1,0:T(8,128)S(1)}, u32[]{:S(2)}) copy-start(f32[2,128,256]{2,1,0:T(8,128)S(1)} %fusion.61) | copy-start | bytes 786436
  58.2 16.6 %copy-start.6 = (bf16[2,128,128]{2,1,0:T(8,128)(2,1)}, bf16[2,128,128]{2,1,0:T(8,128)(2,1)S(1)}, u32[]{:S(2)}) copy-start(bf16[2,128,128]{2,1,0:T(8,128)(2,1)S(1)} %fusion.14) | copy-start | bytes 196612
  65.9 1.0 copy-start.1
  70.7 10.4 %collective-permute-start.6 = (bf16[2,128,128]{2,1,0:T(8,128)(2,1)}, bf16[2,128,128]{2,1,0:T(8,128)(2,1)}, u32[]{:S(2)}, u32[]{:S(2)}) collective-permute-start(bf16[2,128,128]{2,1,0:T(8,128)(2,1)} %slice.142), channel_id=1, source_target_pairs={{0,128},{8,136},{16,144},{24,152},{32,160},{40,168},{48,176},{56,1... | collective-permute-start | bytes 196616 | tf_op jit(solution)/shard_map/ppermute | solution.py:21
  82.5 4.0 %collective-permute-start.7 = (bf16[2,128,128]{2,1,0:T(8,128)(2,1)S(1)}, bf16[2,128,128]{2,1,0:T(8,128)(2,1)S(1)}, u32[]{:S(2)}, u32[]{:S(2)}) collective-permute-start(bf16[2,128,128]{2,1,0:T(8,128)(2,1)S(1)} %get-tuple-element.93), channel_id=1, source_target_pairs={{0,8},{8,0},{16,24},{24,16},{32,40},{40,32},{48,56},{56,48},{64,72... | collective-permute-start | bytes 196616 | tf_op jit(solution)/shard_map/ppermute | solution.py:26
  89.7 1.6 collective-permute-start.8
  96.9 0.9 copy-start.10
  97.8 1.5 collective-permute-start.9
  103.3 1.5 collective-permute-start.10
  105.9 6.1 %collective-permute-start.11 = (bf16[2,128,128]{2,1,0:T(8,128)(2,1)S(1)}, bf16[2,128,128]{2,1,0:T(8,128)(2,1)S(1)}, u32[]{:S(2)}, u32[]{:S(2)}) collective-permute-start(bf16[2,128,128]{2,1,0:T(8,128)(2,1)S(1)} %add_convert_fusion.4), channel_id=1, source_target_pairs={{0,16},{8,24},{16,0},{24,8},{32,48},{40,56},{48,32},{56,40},{64,80... | collective-permute-start | bytes 196616 | tf_op jit(solution)/shard_map/ppermute | solution.py:26
  112.2 25.6 %copy-start.4 = (bf16[2,128,256]{2,1,0:T(8,128)(2,1)S(1)}, bf16[2,128,256]{2,1,0:T(8,128)(2,1)}, u32[]{:S(2)}) copy-start(bf16[2,128,256]{2,1,0:T(8,128)(2,1)} %copy-done.3) | copy-start | bytes 393220
  112.2 25.6 %copy-start.11 = (bf16[2,128,128]{2,1,0:T(8,128)(2,1)S(1)}, bf16[2,128,128]{2,1,0:T(8,128)(2,1)}, u32[]{:S(2)}) copy-start(bf16[2,128,128]{2,1,0:T(8,128)(2,1)} %get-tuple-element.67) | copy-start | bytes 196612
  112.3 7.4 %collective-permute-start.13 = (bf16[2,128,128]{2,1,0:T(8,128)(2,1)S(1)}, bf16[2,128,128]{2,1,0:T(8,128)(2,1)S(1)}, u32[]{:S(2)}, u32[]{:S(2)}) collective-permute-start(bf16[2,128,128]{2,1,0:T(8,128)(2,1)S(1)} %add_convert_fusion.3), channel_id=1, source_target_pairs={{0,32},{8,40},{16,48},{24,56},{32,0},{40,8},{48,16},{56,24},{64,96... | collective-permute-start | bytes 196616 | tf_op jit(solution)/shard_map/ppermute | solution.py:26
  119.9 9.6 %collective-permute-start.14 = (bf16[2,128,128]{2,1,0:T(8,128)(2,1)S(1)}, bf16[2,128,128]{2,1,0:T(8,128)(2,1)S(1)}, u32[]{:S(2)}, u32[]{:S(2)}) collective-permute-start(bf16[2,128,128]{2,1,0:T(8,128)(2,1)S(1)} %add_convert_fusion.2), channel_id=1, source_target_pairs={{0,64},{8,72},{16,80},{24,88},{32,96},{40,104},{48,112},{56,120},{... | collective-permute-start | bytes 196616 | tf_op jit(solution)/shard_map/ppermute | solution.py:26
  121.4 19.0 %all-to-all-start.1 = ((bf16[8,256,256]{2,1,0:T(8,128)(2,1)}), bf16[8,256,256]{2,1,0:T(8,128)(2,1)S(1)}, u32[]{:S(2)}, u32[]{:S(2)}) async-start(bf16[8,256,256]{2,1,0:T(8,128)(2,1)} %shard_map.113), calls=%async_computation.1 | async-start | bytes 2097152 | tf_op jit(solution)/shard_map/all_to_all | solution.py:559
  129.7 7.6 %collective-permute-start.15 = (bf16[2,128,128]{2,1,0:T(8,128)(2,1)S(1)}, bf16[2,128,128]{2,1,0:T(8,128)(2,1)S(1)}, u32[]{:S(2)}, u32[]{:S(2)}) collective-permute-start(bf16[2,128,128]{2,1,0:T(8,128)(2,1)S(1)} %add_convert_fusion.1), channel_id=1, source_target_pairs={{128,0},{136,8},{144,16},{152,24},{160,32},{168,40},{176,48},{184,... | collective-permute-start | bytes 196616 | tf_op jit(solution)/shard_map/ppermute | solution.py:21
  138.1 4.8 %collective-permute-start.16 = (bf16[2,128,128]{2,1,0:T(8,128)(2,1)S(1)}, bf16[2,128,128]{2,1,0:T(8,128)(2,1)S(1)}, u32[]{:S(2)}, u32[]{:S(2)}) collective-permute-start(bf16[2,128,128]{2,1,0:T(8,128)(2,1)S(1)} %get-tuple-element.91), channel_id=1, source_target_pairs={{0,8},{8,0},{16,24},{24,16},{32,40},{40,32},{48,56},{56,48},{64,72... | collective-permute-start | bytes 196616 | tf_op jit(solution)/shard_map/ppermute | solution.py:26
  140.6 3.2 %collective-permute-start.12 = (bf16[128,256]{1,0:T(8,128)(2,1)S(1)}, bf16[128,256]{1,0:T(8,128)(2,1)S(1)}, u32[]{:S(2)}, u32[]{:S(2)}) collective-permute-start(bf16[128,256]{1,0:T(8,128)(2,1)S(1)} %slice.183), channel_id=1, source_target_pairs={{0,8},{8,0},{16,24},{24,16},{32,40},{40,32},{48,56},{56,48},{64,72... | collective-permute-start | bytes 196616 | tf_op jit(solution)/shard_map/ppermute | solution.py:26
  145.4 6.4 %collective-permute-start.17 = (bf16[128,512]{1,0:T(8,128)(2,1)S(1)}, bf16[128,512]{1,0:T(8,128)(2,1)S(1)}, u32[]{:S(2)}, u32[]{:S(2)}) collective-permute-start(bf16[128,512]{1,0:T(8,128)(2,1)S(1)} %slice_bitcast_fusion), channel_id=1, source_target_pairs={{0,128},{8,136},{16,144},{24,152},{32,160},{40,168},{48,176},{56,1... | collective-permute-start | bytes 393224 | tf_op jit(solution)/shard_map/ppermute | solution.py:26
  145.5 6.3 %copy-start.7 = (bf16[1,256,512]{2,1,0:T(8,128)(2,1)S(1)}, bf16[1,256,512]{2,1,0:T(8,128)(2,1)}, u32[]{:S(2)}) copy-start(bf16[1,256,512]{2,1,0:T(8,128)(2,1)} %reduce-scatter.2.cloned.1.call-done) | copy-start | bytes 786436
  (2 other events, 1.4 us)
Sparse Core Ops, SparseCore 0:
  20.4 49.5 all-gather.2
  97.0 38.8 reduce-scatter.1

commit v11 on v10

--- a/solution.py
+++ b/solution.py
@@ -208,18 +208,26 @@
 BLOCKS = [(z, row) for z in range(2) for row in range(2)]
 
 
-def grad_rows(place, step, own_ref, other_ref):
-    def block(ref, z, row):
-        column = pl.multiple_of(z * 256 + place[0] * 128, 128)
-        return ref[(row ^ place[1]) * 4 + step, :, pl.ds(column, 128)]
+def grad_rows(place, refs):
+    def block(ref, z):
+        return ref[0, :, pl.ds(pl.multiple_of(z * 256 + place[0] * 128, 128), 128)]
 
     rows = [
-        jnp.concatenate([block(ref, *place_of) for place_of in BLOCKS], axis=1)
-        for ref in (own_ref, other_ref)
+        jnp.concatenate([block(refs[2 * core + row], z) for z, row in BLOCKS], axis=1)
+        for core in range(2)
     ]
     return jnp.concatenate(rows, axis=0)
 
 
+def grad_specs():
+    def tile(row):
+        return pl.BlockSpec(
+            (1, WIDTH, 512), lambda step, place: ((row ^ place[1]) * 4 + step, 0, 0)
+        )
+
+    return [tile(0), tile(1), tile(0), tile(1)]
+
+
 def weight_rows(ref):
     return jnp.concatenate([ref[z, row] for z, row in BLOCKS], axis=0)
 
@@ -228,28 +236,43 @@
     return pl.BlockSpec((2, 2, WIDTH, 512), lambda step, place: (step, 0, 0, 0))
 
 
-def heads_kernel(place, qt_ref, local_ref, state_ref, heads_ref):
+def heads_kernel(
+    place, qt_ref, local_ref, state_ref, kept_ref, came_ref,
+    heads_ref, grad_ref, mine_ref, theirs_ref,
+):
+    grad_ref[...] = kept_ref[...] + came_ref[...]
     for head in range(4):
+        columns = slice(head * WIDTH, (head + 1) * WIDTH)
         result = dot(qt_ref[head], state_ref[slot(head, place)]) + local_ref[head]
-        heads_ref[:, head * WIDTH : (head + 1) * WIDTH] = result.astype(BF16)
-
-
-def head_outputs(place, qt, local, state):
-    square = whole(4, WIDTH, WIDTH)
+        heads_ref[:, columns] = result.astype(BF16)
+        own = dot(qt_ref[head], grad_ref[:, columns], 0, 0, passes=1).astype(BF16)
+
+        @pl.when(place[0] == head // 2)
+        def _():
+            mine_ref[head % 2] = own
+
+        @pl.when(place[0] != head // 2)
+        def _():
+            theirs_ref[head % 2] = own
+
+
+def head_outputs(place, qt, local, state, kept, came):
+    square, pair = whole(4, WIDTH, WIDTH), arr(BF16, 2, WIDTH, WIDTH)
     return call(
         heads_kernel,
         1,
-        [square, square, square],
-        whole(WIDTH, 512),
-        arr(BF16, WIDTH, 512),
-        2 * 4 * 128**3,
-        1 << 20,
-    )(place, qt, local, state)
-
-
-def weight_terms_kernel(place, own_ref, other_ref, heads_ref, heads_other_ref, out_ref):
+        [square, square, square, whole(WIDTH, 512), whole(WIDTH, 512)],
+        [whole(WIDTH, 512), whole(WIDTH, 512), whole(2, WIDTH, WIDTH), whole(2, WIDTH, WIDTH)],
+        [arr(BF16, WIDTH, 512), arr(F32, WIDTH, 512), pair, pair],
+        2 * 8 * 128**3,
+        2 << 20,
+    )(place, qt, local, state, kept, came)
+
+
+def weight_terms_kernel(place, *refs):
+    heads_ref, heads_other_ref, out_ref = refs[4:]
     product = lax.dot_general(
-        grad_rows(place, pl.program_id(0), own_ref, other_ref),
+        grad_rows(place, refs[:4]),
         jnp.concatenate([heads_ref[...], heads_other_ref[...]], axis=0),
         (((0,), (0,)), ((), ())),
         preferred_element_type=F32,
@@ -263,12 +286,12 @@
     return call(
         weight_terms_kernel,
         STEPS,
-        [whole(8, WIDTH, 512), whole(8, WIDTH, 512), whole(WIDTH, 512), whole(WIDTH, 512)],
+        grad_specs() + [whole(WIDTH, 512), whole(WIDTH, 512)],
         pl.BlockSpec((2, 256, 512), lambda step, place: (step, 0, 0)),
         arr(BF16, 8, 256, 512),
         2 * 128 * 512 * 4096,
         5 << 20,
-    )(place, grad_full, grad_other, heads, heads_other)
+    )(place, grad_full, grad_full, grad_other, grad_other, heads, heads_other)
 
 
 def mixed_kernel(place, heads_ref, heads_other_ref, weight_ref, out_ref):
@@ -296,10 +319,11 @@
     )(place, heads, heads_other, weight)
 
 
-def head_grad_kernel(place, own_ref, other_ref, weight_ref, kept_ref, given_ref):
+def head_grad_kernel(place, *refs):
     step = pl.program_id(0)
+    weight_ref, kept_ref, given_ref = refs[4:]
     total = jnp.dot(
-        grad_rows(place, step, own_ref, other_ref),
+        grad_rows(place, refs[:4]),
         weight_rows(weight_ref),
         preferred_element_type=F32,
     )
@@ -320,40 +344,12 @@
     return call(
         head_grad_kernel,
         STEPS,
-        [whole(8, WIDTH, 512), whole(8, WIDTH, 512), weight_tile()],
+        grad_specs() + [weight_tile()],
         [whole(WIDTH, 512), whole(WIDTH, 512)],
         [part, part],
         2 * 128 * 512 * 4096,
         5 << 20,
-    )(place, grad_full, grad_other, weight)
-
-
-def own_kernel(place, kept_ref, came_ref, qt_ref, grad_ref, mine_ref, theirs_ref):
-    grad_ref[...] = kept_ref[...] + came_ref[...]
-    for head in range(4):
-        grad = grad_ref[:, head * WIDTH : (head + 1) * WIDTH]
-        own = dot(qt_ref[head], grad, 0, 0, passes=1).astype(BF16)
-
-        @pl.when(place[0] == head // 2)
-        def _():
-            mine_ref[head % 2] = own
-
-        @pl.when(place[0] != head // 2)
-        def _():
-            theirs_ref[head % 2] = own
-
-
-def own_cotangent(place, kept, came, qt):
-    pair = arr(BF16, 2, WIDTH, WIDTH)
-    return call(
-        own_kernel,
-        1,
-        [whole(WIDTH, 512), whole(WIDTH, 512), whole(4, WIDTH, WIDTH)],
-        [whole(WIDTH, 512), whole(2, WIDTH, WIDTH), whole(2, WIDTH, WIDTH)],
-        [arr(F32, WIDTH, 512), pair, pair],
-        2 * 4 * 128**3,
-        1 << 20,
-    )(place, kept, came, qt)
+    )(place, grad_full, grad_full, grad_other, grad_other, weight)
 
 
 def pull_kernel(
@@ -502,7 +498,7 @@
     return grad_full, grad_other, head_grad, state_in, (even_a, odd_a, levels, after)
 
 
-def backward_states(mine, theirs, index, core, saved, gate):
+def backward_states(mine, theirs, index, core, saved, gate, last):
     even_a, odd_a, levels, after = saved
     theirs = exchange(theirs, 1)
     even = jnp.where(core == 0, mine, theirs)
@@ -523,7 +519,8 @@
     first = (odd.astype(F32) + mul_t(odd_a, second)).astype(BF16)
     kept = jnp.where(core == 0, first, second)
     given = jnp.where(core == 0, second, first)
-    return gate, jnp.concatenate([kept, exchange(given, 1)], axis=0)
+    last, given = lax.optimization_barrier((last, given))
+    return gate, last, jnp.concatenate([kept, exchange(given, 1)], axis=0)
 
 
 def local(queries, keys, values, beta_logit, out_weight, out_grad):
@@ -545,16 +542,14 @@
     grad_full, grad_other, head_grad, state, saved = forward_states(
         place, mine, theirs, index, core, grad_full, weight_mine
     )
-    heads = head_outputs(place, qt, local_out, state)
+    heads, head_grad, own, own_theirs = head_outputs(place, qt, local_out, state, *head_grad)
     heads_other = exchange(heads, 1)
     terms = weight_terms(place, grad_full, grad_other, heads, heads_other)
     ring_sum = lax.psum_scatter(
         terms, "ctx", scatter_dimension=0, axis_index_groups=rings
     ).reshape(2, WIDTH, 512)
-    head_grad, own, own_theirs = own_cotangent(place, *head_grad, qt)
     parts = mixed_parts(place, heads, heads_other, weight_mine)
-    parts, end = backward_states(own, own_theirs, index, core, saved, parts)
-    end, ring_sum = lax.optimization_barrier((end, ring_sum))
+    parts, ring_sum, end = backward_states(own, own_theirs, index, core, saved, parts, ring_sum)
     weight_grad = ring_sum[0].astype(F32) + exchange(ring_sum[1], 16).astype(F32)
     parts = lax.all_to_all(parts, "tp", 0, 0, tiled=True)
     sums = jnp.sum(parts.astype(F32), axis=0).astype(BF16)

time: 160 us -> 159 us (level)
  Pallas kernels: 40.1 us -> 37.9 us
  waiting for transfers between devices: 43.2 us -> 45.4 us
    all_to_all x1, waiting for transfers between devices: 0.01 us -> 2.62 us  [local(): parts = lax.all_to_all(parts, 'tp', 0, 0, tiled=True)]
    pallas_call x4 -> x3, Pallas kernels: 16.1 us -> 13.9 us  [the longest x1 5.3 us: weight_terms(): call(weight_terms_kernel, STEPS, grad_specs() + [whole(WIDTH, 512), whole...]
  transfers between devices with their start and end apart: 22 -> 22, of which waited for: 12 -> 12; matrix products, arithmetic and copies ran while one was open for 7% -> 8% of each run, Pallas kernels for 20% -> 18%
where the time goes in v11:
time: 159 us; the launch traced here: 158 us
  waiting for transfers between devices  45.4 us (29%)
  starting transfers between devices  43 us (27%)
  Pallas kernels  37.9 us (24%)
  between operations  14.4 us (9%)
  other arithmetic  6.39 us (4%)
  local copies, waits for them, and re-layouts  5.85 us (4%)
  matrix products  5.19 us (3%)
    ppermute x16, waiting for transfers between devices, exchange(): return lax.ppermute(block, 'ctx', route)  32.2 us
    ppermute x16, starting transfers between devices, exchange(): return lax.ppermute(block, 'ctx', route)  29.2 us
    pallas_call x2, Pallas kernels, prepare(): pl.pallas_call(functools.partial(prepare_kernel, mine), grid_spec=pltpu.P...  12.7 us
    pallas_call x1, Pallas kernels, pull(): call(pull_kernel, 2, [by_columns(WIDTH), by_columns(PAIRS), whole(4, PAIR...  6.27 us
    ppermute x2, starting transfers between devices, send(): return lax.ppermute(block, 'ctx', route)  5.42 us
    ppermute x2, waiting for transfers between devices, send(): return lax.ppermute(block, 'ctx', route)  5.42 us
    pallas_call x1, Pallas kernels, weight_terms(): call(weight_terms_kernel, STEPS, grad_specs() + [whole(WIDTH, 512), whole...  5.3 us
    pallas_call x1, Pallas kernels, head_gradient(): call(head_grad_kernel, STEPS, grad_specs() + [weight_tile()], [whole(WIDT...  5.19 us
  transfers between devices with their start and end apart: 22, of which 12 were waited for; matrix products, arithmetic and copies ran while one was open for 8% of the time, Pallas kernels for 18%

profile of v11, /device:TPU:1, one launch (start us, length us, event | category | flops | bytes accessed | tf_op | source)
XLA Modules:
  0.0 158.1 jit_solution(5668769488688248649)
XLA Ops:
  7.2 3.7 %collective-permute-start = (bf16[128,512]{1,0:T(8,128)(2,1)}, bf16[128,512]{1,0:T(8,128)(2,1)S(1)}, u32[]{:S(2)}, u32[]{:S(2)}) collective-permute-start(bf16[128,512]{1,0:T(8,128)(2,1)} %param.10), channel_id=1, source_target_pairs={{0,128},{8,136},{16,144},{24,152},{32,160},{40,168},{48,176},{56,1... | collective-permute-start | bytes 393224 | tf_op jit(solution)/shard_map/ppermute | solution.py:26
  11.5 6.3 %shard_map.109 = (bf16[2,128,256]{2,1,0:T(8,128)(2,1)}, f32[4,256,256]{2,1,0:T(8,128)}, f32[4,256,256]{2,1,0:T(8,128)}, f32[4,128,128]{2,1,0:T(8,128)}, f32[4,128,128]{2,1,0:T(8,128)}) custom-call(s32[2]{0:T(128)} %pad_add_fusion.refs_0_.place, bf16[128,512]{1,0:T(8,128)(2,1)} %q_ref.1, bf16[128,1024]{1,0:T(8,128)(2,1)} %k_ref.1, bf16[128,1024]{1,0:T(8,128)(2,1)} %refs_3_.2, ...), custom_call_target="tpu_custom_call" | custom-call | flops 104857600 | bytes 16777216 | tf_op jit(solution)/shard_map/pallas_call | solution.py:172
  18.7 1.6 %pad_maximum_fusion = bf16[2,128,512]{2,1,0:T(8,128)(2,1)} fusion(bf16[1,128,512]{2,1,0:T(8,128)(2,1)S(1)} %bitcast.31, bf16[1,128,512]{2,1,0:T(8,128)(2,1)} %bitcast.30), kind=kLoop, calls=%fused_computation.13 | loop fusion | flops 131072 | bytes 524288 | tf_op jit(solution)/shard_map/stack | solution.py:535
  20.4 6.4 %shard_map.110 = (bf16[2,128,256]{2,1,0:T(8,128)(2,1)}, f32[4,256,256]{2,1,0:T(8,128)}, f32[4,256,256]{2,1,0:T(8,128)}, f32[4,128,128]{2,1,0:T(8,128)}, f32[4,128,128]{2,1,0:T(8,128)}) custom-call(s32[2]{0:T(128)} %pad_add_fusion.refs_0_.place, bf16[128,512]{1,0:T(8,128)(2,1)} %q_ref.1, ...), custom_call_target="tpu_custom_call", output_to_operand_aliasing={{1}: (5, {}), {2}: (6, {}), {3}: (7, {}), {4}: (8, {})} | custom-call | flops 1048576 | bytes 65536 | tf_op jit(solution)/shard_map/pallas_call | solution.py:172
  28.0 1.7 %collective-permute-start.2 = (bf16[2,128,256]{2,1,0:T(8,128)(2,1)S(1)}, bf16[2,128,256]{2,1,0:T(8,128)(2,1)S(1)}, u32[]{:S(2)}, u32[]{:S(2)}) collective-permute-start(bf16[2,128,256]{2,1,0:T(8,128)(2,1)S(1)} %pad_maximum_fusion.1), channel_id=1, source_target_pairs={{0,16},{8,24},{16,0},{24,8},{32,48},{40,56},{48,32},{56,40},{64,80... | collective-permute-start | bytes 393224 | tf_op jit(solution)/shard_map/ppermute | solution.py:26
  30.8 4.2 %all-to-all-start = ((bf16[8,128,512]{2,1,0:T(8,128)(2,1)}), bf16[8,128,512]{2,1,0:T(8,128)(2,1)S(1)}, u32[]{:S(2)}, u32[]{:S(2)}) async-start(bf16[8,128,512]{2,1,0:T(8,128)(2,1)} %broadcast_in_dim.21), calls=%async_computation | async-start | bytes 2097152 | tf_op jit(solution)/shard_map/all_to_all | solution.py:539
  35.4 3.1 %collective-permute-start.3 = (bf16[2,128,256]{2,1,0:T(8,128)(2,1)S(1)}, bf16[2,128,256]{2,1,0:T(8,128)(2,1)S(1)}, u32[]{:S(2)}, u32[]{:S(2)}) collective-permute-start(bf16[2,128,256]{2,1,0:T(8,128)(2,1)S(1)} %pad_maximum_fusion.2), channel_id=1, source_target_pairs={{0,32},{8,40},{16,48},{24,56},{32,0},{40,8},{48,16},{56,24},{64,96... | collective-permute-start | bytes 393224 | tf_op jit(solution)/shard_map/ppermute | solution.py:26
  38.5 9.6 %collective-permute-done.3 = bf16[2,128,256]{2,1,0:T(8,128)(2,1)S(1)} collective-permute-done((bf16[2,128,256]{2,1,0:T(8,128)(2,1)S(1)}, bf16[2,128,256]{2,1,0:T(8,128)(2,1)S(1)}, u32[]{:S(2)}, u32[]{:S(2)}) %collective-permute-start.3) | collective-permute-done | bytes 131104 | tf_op jit(solution)/shard_map/ppermute | solution.py:26
  48.1 2.2 %all-to-all-done.refs_0_.refs_1_ = bf16[8,128,512]{2,1,0:T(8,128)(2,1)S(1)} async-done(((bf16[8,128,512]{2,1,0:T(8,128)(2,1)}), bf16[8,128,512]{2,1,0:T(8,128)(2,1)S(1)}, u32[]{:S(2)}, u32[]{:S(2)}) %all-to-all-start) | async-done | bytes 1048608 | tf_op jit(solution)/shard_map/all_to_all | solution.py:539
  50.2 1.4 collective-permute-start.4
  51.9 6.1 %collective-permute-start.5 = (bf16[2,128,256]{2,1,0:T(8,128)(2,1)S(1)}, bf16[2,128,256]{2,1,0:T(8,128)(2,1)S(1)}, u32[]{:S(2)}, u32[]{:S(2)}) collective-permute-start(bf16[2,128,256]{2,1,0:T(8,128)(2,1)S(1)} %pad_maximum_fusion.3), channel_id=1, source_target_pairs={{0,64},{8,72},{16,80},{24,88},{32,96},{40,104},{48,112},{56,120},{... | collective-permute-start | bytes 393224 | tf_op jit(solution)/shard_map/ppermute | solution.py:26
  58.2 7.6 %collective-permute-done.5 = bf16[2,128,256]{2,1,0:T(8,128)(2,1)S(1)} collective-permute-done((bf16[2,128,256]{2,1,0:T(8,128)(2,1)S(1)}, bf16[2,128,256]{2,1,0:T(8,128)(2,1)S(1)}, u32[]{:S(2)}, u32[]{:S(2)}) %collective-permute-start.5) | collective-permute-done | bytes 131104 | tf_op jit(solution)/shard_map/ppermute | solution.py:26
  67.2 2.9 %all-gather.3.cloned.1.call-done = bf16[16,128,512]{2,1,0:T(8,128)(2,1)} async-done(((bf16[2,128,512]{2,1,0:T(8,128)(2,1)}), bf16[16,128,512]{2,1,0:T(8,128)(2,1)}) %all-gather.3.cloned.1.call-update) | async-done | bytes 2097168 | tf_op jit(solution)/shard_map/all_gather | solution.py:538
  70.7 4.1 %collective-permute-start.6 = (bf16[2,128,128]{2,1,0:T(8,128)(2,1)}, bf16[2,128,128]{2,1,0:T(8,128)(2,1)}, u32[]{:S(2)}, u32[]{:S(2)}) collective-permute-start(bf16[2,128,128]{2,1,0:T(8,128)(2,1)} %slice.142), channel_id=1, source_target_pairs={{0,128},{8,136},{16,144},{24,152},{32,160},{40,168},{48,176},{56,1... | collective-permute-start | bytes 196616 | tf_op jit(solution)/shard_map/ppermute | solution.py:21
  75.8 5.2 %shard_map.111 = (f32[128,512]{1,0:T(8,128)}, f32[128,512]{1,0:T(8,128)}) custom-call(s32[2]{0:T(128)} %pad_add_fusion.refs_0_.place, bf16[8,128,512]{2,1,0:T(8,128)(2,1)} %copy-done, bf16[8,128,512]{2,1,0:T(8,128)(2,1)} %copy-done, bf16[8,128,512]{2,1,0:T(8,128)(2,1)} %copy-done.1, bf16[8,128,512]{2,1,0:T(8,128)(2,1)} %copy-done.1, ...), custom_call_target="tpu_custom_call" | custom-call | flops 536870912 | bytes 5242880 | tf_op jit(solution)/shard_map/pallas_call | solution.py:344
  81.0 3.0 %collective-permute-start.8 = (f32[128,512]{1,0:T(8,128)}, f32[128,512]{1,0:T(8,128)S(1)}, u32[]{:S(2)}, u32[]{:S(2)}) collective-permute-start(f32[128,512]{1,0:T(8,128)} %get-tuple-element.67), channel_id=1, source_target_pairs={{0,8},{8,0},{16,24},{24,16},{32,40},{40,32},{48,56},{56,48},{64,72... | collective-permute-start | bytes 786440 | tf_op jit(solution)/shard_map/ppermute | solution.py:26
  84.0 1.2 fusion.9
  85.5 1.2 collective-permute-done.7
  88.1 3.4 %shard_map.112 = (bf16[128,512]{1,0:T(8,128)(2,1)}, f32[128,512]{1,0:T(8,128)}, bf16[2,128,128]{2,1,0:T(8,128)(2,1)}, bf16[2,128,128]{2,1,0:T(8,128)(2,1)}) custom-call(s32[2]{0:T(128)} %pad_add_fusion.refs_0_.place, f32[4,128,128]{2,1,0:T(8,128)} %get-tuple-element.54.qt_ref, f32[4,128,128]{2,1,0:T(8,128)} %get-tuple-element.55.local_ref, ...), custom_call_target="tpu_custom_call" | custom-call | flops 33554432 | bytes 2097152 | tf_op jit(solution)/shard_map/pallas_call | solution.py:261
  91.7 1.4 collective-permute-done.9.heads_other_ref.refs_5_
  93.8 5.3 %shard_map.114 = bf16[8,256,512]{2,1,0:T(8,128)(2,1)} custom-call(s32[2]{0:T(128)} %pad_add_fusion.refs_0_.place, bf16[8,128,512]{2,1,0:T(8,128)(2,1)} %copy-done, bf16[8,128,512]{2,1,0:T(8,128)(2,1)} %copy-done, bf16[8,128,512]{2,1,0:T(8,128)(2,1)} %copy-done.1, bf16[8,128,512]{2,1,0:T(8,128)(2,1)} %copy-done.1, ...), custom_call_target="tpu_custom_call" | custom-call | flops 536870912 | bytes 5242880 | tf_op jit(solution)/shard_map/pallas_call | solution.py:286
  102.5 5.0 %shard_map.113 = bf16[8,256,256]{2,1,0:T(8,128)(2,1)} custom-call(s32[2]{0:T(128)} %pad_add_fusion.refs_0_.place, bf16[128,512]{1,0:T(8,128)(2,1)} %get-tuple-element.68.heads_ref.refs_4_, bf16[128,512]{1,0:T(8,128)(2,1)} %copy-done.4, bf16[8,2,128,512]{3,2,1,0:T(8,128)(2,1)} %bitcast.27), custom_call_target="tpu_custom_call" | custom-call | flops 536870912 | bytes 3145728 | tf_op jit(solution)/shard_map/pallas_call | solution.py:311
  108.5 7.0 %collective-permute-done.13 = bf16[2,128,128]{2,1,0:T(8,128)(2,1)S(1)} collective-permute-done((bf16[2,128,128]{2,1,0:T(8,128)(2,1)S(1)}, bf16[2,128,128]{2,1,0:T(8,128)(2,1)S(1)}, u32[]{:S(2)}, u32[]{:S(2)}) %collective-permute-start.13) | collective-permute-done | bytes 65568 | tf_op jit(solution)/shard_map/ppermute | solution.py:26
  115.7 2.0 %collective-permute-start.14 = (bf16[2,128,128]{2,1,0:T(8,128)(2,1)S(1)}, bf16[2,128,128]{2,1,0:T(8,128)(2,1)S(1)}, u32[]{:S(2)}, u32[]{:S(2)}) collective-permute-start(bf16[2,128,128]{2,1,0:T(8,128)(2,1)S(1)} %add_convert_fusion.2), channel_id=1, source_target_pairs={{0,64},{8,72},{16,80},{24,88},{32,96},{40,104},{48,112},{56,120},{... | collective-permute-start | bytes 196616 | tf_op jit(solution)/shard_map/ppermute | solution.py:26
  117.8 4.1 %all-to-all-start.1 = ((bf16[8,256,256]{2,1,0:T(8,128)(2,1)}), bf16[8,256,256]{2,1,0:T(8,128)(2,1)S(1)}, u32[]{:S(2)}, u32[]{:S(2)}) async-start(bf16[8,256,256]{2,1,0:T(8,128)(2,1)} %shard_map.113), calls=%async_computation.1 | async-start | bytes 2097152 | tf_op jit(solution)/shard_map/all_to_all | solution.py:554
  121.9 3.6 %collective-permute-done.14 = bf16[2,128,128]{2,1,0:T(8,128)(2,1)S(1)} collective-permute-done((bf16[2,128,128]{2,1,0:T(8,128)(2,1)S(1)}, bf16[2,128,128]{2,1,0:T(8,128)(2,1)S(1)}, u32[]{:S(2)}, u32[]{:S(2)}) %collective-permute-start.14) | collective-permute-done | bytes 65568 | tf_op jit(solution)/shard_map/ppermute | solution.py:26
  125.7 1.3 collective-permute-start.15
  127.3 5.4 %collective-permute-done.15 = bf16[2,128,128]{2,1,0:T(8,128)(2,1)S(1)} collective-permute-done((bf16[2,128,128]{2,1,0:T(8,128)(2,1)S(1)}, bf16[2,128,128]{2,1,0:T(8,128)(2,1)S(1)}, u32[]{:S(2)}, u32[]{:S(2)}) %collective-permute-start.15) | collective-permute-done | bytes 65568 | tf_op jit(solution)/shard_map/ppermute | solution.py:21
  133.3 2.6 %all-to-all-done.1 = bf16[8,256,256]{2,1,0:T(8,128)(2,1)S(1)} async-done(((bf16[8,256,256]{2,1,0:T(8,128)(2,1)}), bf16[8,256,256]{2,1,0:T(8,128)(2,1)S(1)}, u32[]{:S(2)}, u32[]{:S(2)}) %all-to-all-start.1) | async-done | bytes 1048608 | tf_op jit(solution)/shard_map/all_to_all | solution.py:554
  136.1 2.8 %collective-permute-start.12 = (bf16[128,256]{1,0:T(8,128)(2,1)S(1)}, bf16[128,256]{1,0:T(8,128)(2,1)S(1)}, u32[]{:S(2)}, u32[]{:S(2)}) collective-permute-start(bf16[128,256]{1,0:T(8,128)(2,1)S(1)} %slice.183), channel_id=1, source_target_pairs={{0,8},{8,0},{16,24},{24,16},{32,40},{40,32},{48,56},{56,48},{64,72... | collective-permute-start | bytes 196616 | tf_op jit(solution)/shard_map/ppermute | solution.py:26
  141.8 1.7 %collective-permute-start.17 = (bf16[128,512]{1,0:T(8,128)(2,1)S(1)}, bf16[128,512]{1,0:T(8,128)(2,1)S(1)}, u32[]{:S(2)}, u32[]{:S(2)}) collective-permute-start(bf16[128,512]{1,0:T(8,128)(2,1)S(1)} %slice_bitcast_fusion), channel_id=1, source_target_pairs={{0,128},{8,136},{16,144},{24,152},{32,160},{40,168},{48,176},{56,1... | collective-permute-start | bytes 393224 | tf_op jit(solution)/shard_map/ppermute | solution.py:26
  144.2 6.3 %shard_map.115 = (bf16[128,512]{1,0:T(8,128)(2,1)}, bf16[128,1024]{1,0:T(8,128)(2,1)}, bf16[128,1024]{1,0:T(8,128)(2,1)}, f32[4,256]{1,0:T(4,128)}) custom-call(s32[2]{0:T(128)} %pad_add_fusion.refs_0_.place, bf16[128,512]{1,0:T(8,128)(2,1)} %q_ref.1, bf16[128,1024]{1,0:T(8,128)(2,1)} %k_ref.1, f32[4,256]{1,0:T(4,128)} %logit_ref.1, ...), custom_call_target="tpu_custom_call" | custom-call | flops 1879048192 | bytes 5242880 | tf_op jit(solution)/shard_map/pallas_call | solution.py:416
  (93 shorter events, 20.2 us)
Async XLA Ops:
  7.2 62.9 %all-gather.3.cloned.1.call-start = ((), (), s32[]{:S(2)}) async-start(), calls=%async_computation.4 | async-start | bytes 2359296 | tf_op jit(solution)/shard_map/all_gather | solution.py:538
  7.2 10.6 %collective-permute-start = (bf16[128,512]{1,0:T(8,128)(2,1)}, bf16[128,512]{1,0:T(8,128)(2,1)S(1)}, u32[]{:S(2)}, u32[]{:S(2)}) collective-permute-start(bf16[128,512]{1,0:T(8,128)(2,1)} %param.10), channel_id=1, source_target_pairs={{0,128},{8,136},{16,144},{24,152},{32,160},{40,168},{48,176},{56,1... | collective-permute-start | bytes 393224 | tf_op jit(solution)/shard_map/ppermute | solution.py:26
  17.8 9.0 %collective-permute-start.1 = (bf16[2,128,256]{2,1,0:T(8,128)(2,1)}, bf16[2,128,256]{2,1,0:T(8,128)(2,1)S(1)}, u32[]{:S(2)}, u32[]{:S(2)}) collective-permute-start(bf16[2,128,256]{2,1,0:T(8,128)(2,1)} %get-tuple-element.56), channel_id=1, source_target_pairs={{0,8},{8,0},{16,24},{24,16},{32,40},{40,32},{48,56},{56,48},{64,72... | collective-permute-start | bytes 393224 | tf_op jit(solution)/shard_map/ppermute | solution.py:26
  20.4 9.4 %copy-start.9 = (bf16[128,512]{1,0:T(8,128)(2,1)S(1)}, bf16[128,512]{1,0:T(8,128)(2,1)}, u32[]{:S(2)}) copy-start(bf16[128,512]{1,0:T(8,128)(2,1)} %param.11) | copy-start | bytes 393220
  27.7 3.0 %copy-start.2 = (bf16[2,128,256]{2,1,0:T(8,128)(2,1)}, bf16[2,128,256]{2,1,0:T(8,128)(2,1)S(1)}, u32[]{:S(2)}) copy-start(bf16[2,128,256]{2,1,0:T(8,128)(2,1)S(1)} %get-tuple-element.88) | copy-start | bytes 393220
  28.0 7.1 %collective-permute-start.2 = (bf16[2,128,256]{2,1,0:T(8,128)(2,1)S(1)}, bf16[2,128,256]{2,1,0:T(8,128)(2,1)S(1)}, u32[]{:S(2)}, u32[]{:S(2)}) collective-permute-start(bf16[2,128,256]{2,1,0:T(8,128)(2,1)S(1)} %pad_maximum_fusion.1), channel_id=1, source_target_pairs={{0,16},{8,24},{16,0},{24,8},{32,48},{40,56},{48,32},{56,40},{64,80... | collective-permute-start | bytes 393224 | tf_op jit(solution)/shard_map/ppermute | solution.py:26
  30.8 19.5 %all-to-all-start = ((bf16[8,128,512]{2,1,0:T(8,128)(2,1)}), bf16[8,128,512]{2,1,0:T(8,128)(2,1)S(1)}, u32[]{:S(2)}, u32[]{:S(2)}) async-start(bf16[8,128,512]{2,1,0:T(8,128)(2,1)} %broadcast_in_dim.21), calls=%async_computation | async-start | bytes 2097152 | tf_op jit(solution)/shard_map/all_to_all | solution.py:539
  35.0 105.5 %reduce-scatter.2.cloned.1.call-start = ((), (), s32[]{:S(2)}) async-start(), calls=%async_computation.3 | async-start | bytes 2359296 | tf_op jit(solution)/shard_map/reduce_scatter | solution.py:548
  35.4 12.7 %collective-permute-start.3 = (bf16[2,128,256]{2,1,0:T(8,128)(2,1)S(1)}, bf16[2,128,256]{2,1,0:T(8,128)(2,1)S(1)}, u32[]{:S(2)}, u32[]{:S(2)}) collective-permute-start(bf16[2,128,256]{2,1,0:T(8,128)(2,1)S(1)} %pad_maximum_fusion.2), channel_id=1, source_target_pairs={{0,32},{8,40},{16,48},{24,56},{32,0},{40,8},{48,16},{56,24},{64,96... | collective-permute-start | bytes 393224 | tf_op jit(solution)/shard_map/ppermute | solution.py:26
  50.2 25.5 %copy-start = (bf16[8,128,512]{2,1,0:T(8,128)(2,1)}, bf16[8,128,512]{2,1,0:T(8,128)(2,1)S(1)}, u32[]{:S(2)}) copy-start(bf16[8,128,512]{2,1,0:T(8,128)(2,1)S(1)} %all-to-all-done.refs_0_.refs_1_) | copy-start | bytes 3145732
  50.2 15.7 %collective-permute-start.4 = (bf16[8,128,512]{2,1,0:T(8,128)(2,1)S(1)}, bf16[8,128,512]{2,1,0:T(8,128)(2,1)S(1)}, u32[]{:S(2)}, u32[]{:S(2)}) collective-permute-start(bf16[8,128,512]{2,1,0:T(8,128)(2,1)S(1)} %all-to-all-done.refs_0_.refs_1_), channel_id=1, source_target_pairs={{0,8},{8,0},{16,24},{24,16},{32,40},{40,32},{48,56},{56,48},{64,72... | collective-permute-start | bytes 3145736 | tf_op jit(solution)/shard_map/ppermute | solution.py:26
  51.9 14.0 %collective-permute-start.5 = (bf16[2,128,256]{2,1,0:T(8,128)(2,1)S(1)}, bf16[2,128,256]{2,1,0:T(8,128)(2,1)S(1)}, u32[]{:S(2)}, u32[]{:S(2)}) collective-permute-start(bf16[2,128,256]{2,1,0:T(8,128)(2,1)S(1)} %pad_maximum_fusion.3), channel_id=1, source_target_pairs={{0,64},{8,72},{16,80},{24,88},{32,96},{40,104},{48,112},{56,120},{... | collective-permute-start | bytes 393224 | tf_op jit(solution)/shard_map/ppermute | solution.py:26
  58.2 7.7 %copy-start.5 = (f32[2,128,256]{2,1,0:T(8,128)}, f32[2,128,256]{2,1,0:T(8,128)S(1)}, u32[]{:S(2)}) copy-start(f32[2,128,256]{2,1,0:T(8,128)S(1)} %fusion.61) | copy-start | bytes 786436
  58.2 16.6 %copy-start.6 = (bf16[2,128,128]{2,1,0:T(8,128)(2,1)}, bf16[2,128,128]{2,1,0:T(8,128)(2,1)S(1)}, u32[]{:S(2)}) copy-start(bf16[2,128,128]{2,1,0:T(8,128)(2,1)S(1)} %fusion.14) | copy-start | bytes 196612
  65.9 1.0 copy-start.1
  70.7 10.2 %collective-permute-start.6 = (bf16[2,128,128]{2,1,0:T(8,128)(2,1)}, bf16[2,128,128]{2,1,0:T(8,128)(2,1)}, u32[]{:S(2)}, u32[]{:S(2)}) collective-permute-start(bf16[2,128,128]{2,1,0:T(8,128)(2,1)} %slice.142), channel_id=1, source_target_pairs={{0,128},{8,136},{16,144},{24,152},{32,160},{40,168},{48,176},{56,1... | collective-permute-start | bytes 196616 | tf_op jit(solution)/shard_map/ppermute | solution.py:21
  81.0 6.5 %collective-permute-start.8 = (f32[128,512]{1,0:T(8,128)}, f32[128,512]{1,0:T(8,128)S(1)}, u32[]{:S(2)}, u32[]{:S(2)}) collective-permute-start(f32[128,512]{1,0:T(8,128)} %get-tuple-element.67), channel_id=1, source_target_pairs={{0,8},{8,0},{16,24},{24,16},{32,40},{40,32},{48,56},{56,48},{64,72... | collective-permute-start | bytes 786440 | tf_op jit(solution)/shard_map/ppermute | solution.py:26
  85.4 1.3 collective-permute-start.7
  91.5 1.6 collective-permute-start.9
  99.1 0.8 copy-start.11
  99.1 2.1 %copy-start.10 = (bf16[2,128,128]{2,1,0:T(8,128)(2,1)S(1)}, bf16[2,128,128]{2,1,0:T(8,128)(2,1)}, u32[]{:S(2)}) copy-start(bf16[2,128,128]{2,1,0:T(8,128)(2,1)} %get-tuple-element.69) | copy-start | bytes 196612
  99.9 1.3 collective-permute-start.10
  101.4 6.1 %collective-permute-start.11 = (bf16[2,128,128]{2,1,0:T(8,128)(2,1)S(1)}, bf16[2,128,128]{2,1,0:T(8,128)(2,1)S(1)}, u32[]{:S(2)}, u32[]{:S(2)}) collective-permute-start(bf16[2,128,128]{2,1,0:T(8,128)(2,1)S(1)} %add_convert_fusion.4), channel_id=1, source_target_pairs={{0,16},{8,24},{16,0},{24,8},{32,48},{40,56},{48,32},{56,40},{64,80... | collective-permute-start | bytes 196616 | tf_op jit(solution)/shard_map/ppermute | solution.py:26
  107.7 7.8 %collective-permute-start.13 = (bf16[2,128,128]{2,1,0:T(8,128)(2,1)S(1)}, bf16[2,128,128]{2,1,0:T(8,128)(2,1)S(1)}, u32[]{:S(2)}, u32[]{:S(2)}) collective-permute-start(bf16[2,128,128]{2,1,0:T(8,128)(2,1)S(1)} %add_convert_fusion.3), channel_id=1, source_target_pairs={{0,32},{8,40},{16,48},{24,56},{32,0},{40,8},{48,16},{56,24},{64,96... | collective-permute-start | bytes 196616 | tf_op jit(solution)/shard_map/ppermute | solution.py:26
  115.7 9.8 %collective-permute-start.14 = (bf16[2,128,128]{2,1,0:T(8,128)(2,1)S(1)}, bf16[2,128,128]{2,1,0:T(8,128)(2,1)S(1)}, u32[]{:S(2)}, u32[]{:S(2)}) collective-permute-start(bf16[2,128,128]{2,1,0:T(8,128)(2,1)S(1)} %add_convert_fusion.2), channel_id=1, source_target_pairs={{0,64},{8,72},{16,80},{24,88},{32,96},{40,104},{48,112},{56,120},{... | collective-permute-start | bytes 196616 | tf_op jit(solution)/shard_map/ppermute | solution.py:26
  117.8 21.0 %copy-start.3 = (bf16[2,128,256]{2,1,0:T(8,128)(2,1)S(1)}, bf16[2,128,256]{2,1,0:T(8,128)(2,1)}, u32[]{:S(2)}) copy-start(bf16[2,128,256]{2,1,0:T(8,128)(2,1)} %copy-done.2) | copy-start | bytes 393220
  117.8 18.1 %all-to-all-start.1 = ((bf16[8,256,256]{2,1,0:T(8,128)(2,1)}), bf16[8,256,256]{2,1,0:T(8,128)(2,1)S(1)}, u32[]{:S(2)}, u32[]{:S(2)}) async-start(bf16[8,256,256]{2,1,0:T(8,128)(2,1)} %shard_map.113), calls=%async_computation.1 | async-start | bytes 2097152 | tf_op jit(solution)/shard_map/all_to_all | solution.py:554
  125.7 6.9 %collective-permute-start.15 = (bf16[2,128,128]{2,1,0:T(8,128)(2,1)S(1)}, bf16[2,128,128]{2,1,0:T(8,128)(2,1)S(1)}, u32[]{:S(2)}, u32[]{:S(2)}) collective-permute-start(bf16[2,128,128]{2,1,0:T(8,128)(2,1)S(1)} %add_convert_fusion.1), channel_id=1, source_target_pairs={{128,0},{136,8},{144,16},{152,24},{160,32},{168,40},{176,48},{184,... | collective-permute-start | bytes 196616 | tf_op jit(solution)/shard_map/ppermute | solution.py:21
  136.1 3.7 %collective-permute-start.12 = (bf16[128,256]{1,0:T(8,128)(2,1)S(1)}, bf16[128,256]{1,0:T(8,128)(2,1)S(1)}, u32[]{:S(2)}, u32[]{:S(2)}) collective-permute-start(bf16[128,256]{1,0:T(8,128)(2,1)S(1)} %slice.183), channel_id=1, source_target_pairs={{0,8},{8,0},{16,24},{24,16},{32,40},{40,32},{48,56},{56,48},{64,72... | collective-permute-start | bytes 196616 | tf_op jit(solution)/shard_map/ppermute | solution.py:26
  140.4 3.1 %collective-permute-start.16 = (bf16[2,128,128]{2,1,0:T(8,128)(2,1)S(1)}, bf16[2,128,128]{2,1,0:T(8,128)(2,1)S(1)}, u32[]{:S(2)}, u32[]{:S(2)}) collective-permute-start(bf16[2,128,128]{2,1,0:T(8,128)(2,1)S(1)} %get-tuple-element.75), channel_id=1, source_target_pairs={{0,8},{8,0},{16,24},{24,16},{32,40},{40,32},{48,56},{56,48},{64,72... | collective-permute-start | bytes 196616 | tf_op jit(solution)/shard_map/ppermute | solution.py:26
  141.8 8.7 %collective-permute-start.17 = (bf16[128,512]{1,0:T(8,128)(2,1)S(1)}, bf16[128,512]{1,0:T(8,128)(2,1)S(1)}, u32[]{:S(2)}, u32[]{:S(2)}) collective-permute-start(bf16[128,512]{1,0:T(8,128)(2,1)S(1)} %slice_bitcast_fusion), channel_id=1, source_target_pairs={{0,128},{8,136},{16,144},{24,152},{32,160},{40,168},{48,176},{56,1... | collective-permute-start | bytes 393224 | tf_op jit(solution)/shard_map/ppermute | solution.py:26
  144.2 6.3 %copy-start.7 = (bf16[1,256,512]{2,1,0:T(8,128)(2,1)S(1)}, bf16[1,256,512]{2,1,0:T(8,128)(2,1)}, u32[]{:S(2)}) copy-start(bf16[1,256,512]{2,1,0:T(8,128)(2,1)} %reduce-scatter.2.cloned.1.call-done) | copy-start | bytes 786436
  (2 other events, 1.4 us)
Sparse Core Ops, SparseCore 0:
  20.5 49.5 all-gather.2
  99.2 37.8 reduce-scatter.1

commit v12 on v11

--- a/solution.py
+++ b/solution.py
@@ -199,7 +199,7 @@
         input_output_aliases={5 + i: 1 + i for i in range(len(filled))},
         compiler_params=pltpu.CompilerParams(vmem_limit_bytes=VMEM),
         cost_estimate=pl.CostEstimate(
-            flops=(1 if mine else 100) << 20, bytes_accessed=1 << (16 if mine else 24), transcendentals=0
+            flops=1 << 10, bytes_accessed=1 << 10, transcendentals=0
         ),
     )(place, queries, keys, values, logits, *filled)
 
@@ -228,12 +228,12 @@
     return [tile(0), tile(1), tile(0), tile(1)]
 
 
-def weight_rows(ref):
-    return jnp.concatenate([ref[z, row] for z, row in BLOCKS], axis=0)
+def weight_rows(refs):
+    return jnp.concatenate([refs[row][z] for z, row in BLOCKS], axis=0)
 
 
 def weight_tile():
-    return pl.BlockSpec((2, 2, WIDTH, 512), lambda step, place: (step, 0, 0, 0))
+    return pl.BlockSpec((2, WIDTH, 512), lambda step, place: (step, 0, 0))
 
 
 def heads_kernel(
@@ -294,11 +294,11 @@
     )(place, grad_full, grad_full, grad_other, grad_other, heads, heads_other)
 
 
-def mixed_kernel(place, heads_ref, heads_other_ref, weight_ref, out_ref):
+def mixed_kernel(place, heads_ref, heads_other_ref, weight_ref, across_ref, out_ref):
     step = pl.program_id(0)
     product = lax.dot_general(
         jnp.concatenate([heads_ref[...], heads_other_ref[...]], axis=0),
-        weight_rows(weight_ref),
+        weight_rows((weight_ref, across_ref)),
         (((1,), (1,)), ((), ())),
         preferred_element_type=F32,
     ).astype(BF16)
@@ -307,24 +307,24 @@
         out_ref[owner, :, z * 128 : z * 128 + 128] = product[:, i * WIDTH : (i + 1) * WIDTH]
 
 
-def mixed_parts(place, heads, heads_other, weight):
+def mixed_parts(place, heads, heads_other, weight, across):
     return call(
         mixed_kernel,
         STEPS,
-        [whole(WIDTH, 512), whole(WIDTH, 512), weight_tile()],
+        [whole(WIDTH, 512), whole(WIDTH, 512), weight_tile(), weight_tile()],
         whole(8, 256, 256),
         arr(BF16, 8, 256, 256),
         2 * 128 * 512 * 4096,
         3 << 20,
-    )(place, heads, heads_other, weight)
+    )(place, heads, heads_other, weight, across)
 
 
 def head_grad_kernel(place, *refs):
     step = pl.program_id(0)
-    weight_ref, kept_ref, given_ref = refs[4:]
+    *weight_refs, kept_ref, given_ref = refs[4:]
     total = jnp.dot(
         grad_rows(place, refs[:4]),
-        weight_rows(weight_ref),
+        weight_rows(weight_refs),
         preferred_element_type=F32,
     )
 
@@ -339,17 +339,17 @@
         given_ref[...] += total[WIDTH:]
 
 
-def head_gradient(place, grad_full, grad_other, weight):
+def head_gradient(place, grad_full, grad_other, weight, across):
     part = arr(F32, WIDTH, 512)
     return call(
         head_grad_kernel,
         STEPS,
-        grad_specs() + [weight_tile()],
+        grad_specs() + [weight_tile(), weight_tile()],
         [whole(WIDTH, 512), whole(WIDTH, 512)],
         [part, part],
         2 * 128 * 512 * 4096,
         5 << 20,
-    )(place, grad_full, grad_full, grad_other, grad_other, weight)
+    )(place, grad_full, grad_full, grad_other, grad_other, weight, across)
 
 
 def pull_kernel(
@@ -464,6 +464,9 @@
     diagonal = jnp.broadcast_to(jnp.eye(WIDTH, dtype=BF16), (2, WIDTH, WIDTH))
     for bit in (2, 4, 8):
         came = exchange(total, bit)
+        if bit == 4:
+            weight, came = lax.optimization_barrier((weight, came))
+            across = exchange(weight, 16)
         if bit == 8:
             grad_other, came = lax.optimization_barrier((exchange(grad_full, 1), came))
         upper = (index & bit) != 0
@@ -485,9 +488,8 @@
             before = jnp.where(upper, step[:, :, :WIDTH].astype(BF16), before)
             state = jnp.where(upper, state + step[:, :, WIDTH:], state)
             after = jnp.where(upper, after, mul(came_a, after).astype(BF16))
-    weight, total = lax.optimization_barrier((weight, total))
     far = send(total[:, :, WIDTH:], 16)
-    kept_grad, given_grad = head_gradient(place, grad_full, grad_other, weight)
+    kept_grad, given_grad = head_gradient(place, grad_full, grad_other, weight, across)
     kept_grad, given_grad, far = lax.optimization_barrier((kept_grad, given_grad, far))
     head_grad = (kept_grad, exchange(given_grad, 1))
     first = (state + mul(before, far)).astype(BF16)
@@ -495,7 +497,8 @@
     kept = jnp.where(core == 0, first, second)
     given = jnp.where(core == 0, second, first)
     state_in = jnp.concatenate([kept, exchange(given, 1)], axis=0)
-    return grad_full, grad_other, head_grad, state_in, (even_a, odd_a, levels, after)
+    weights = (weight, across)
+    return weights, grad_full, grad_other, head_grad, state_in, (even_a, odd_a, levels, after)
 
 
 def backward_states(mine, theirs, index, core, saved, gate, last):
@@ -529,18 +532,14 @@
     place = jnp.stack([core, index >> 4]).astype(jnp.int32)
     rings = [[(half * 8 + z) * 2 + c for z in range(8)] for half in range(2) for c in range(2)]
     operands = (queries, keys, values, beta_logit)
-    across = exchange(out_weight, 16)
     theirs, *filled = prepare(place, *operands, False)
-    across, theirs = lax.optimization_barrier((across, theirs))
-    weight_pair = jnp.stack([out_weight, across])
-    weight_pair, *operands = lax.optimization_barrier((weight_pair, *operands))
     mine, reads, wy, qt, local_out = prepare(place, *operands, True, filled)
-    weight_mine = lax.all_gather(weight_pair, "ctx", axis=0, axis_index_groups=rings)
+    weight = lax.all_gather(out_weight, "ctx", axis=0, axis_index_groups=rings)
     grad_full = lax.all_to_all(
         jnp.broadcast_to(out_grad[None], (8, WIDTH, 512)), "tp", 0, 0, tiled=True
     )
-    grad_full, grad_other, head_grad, state, saved = forward_states(
-        place, mine, theirs, index, core, grad_full, weight_mine
+    weights, grad_full, grad_other, head_grad, state, saved = forward_states(
+        place, mine, theirs, index, core, grad_full, weight
     )
     heads, head_grad, own, own_theirs = head_outputs(place, qt, local_out, state, *head_grad)
     heads_other = exchange(heads, 1)
@@ -548,7 +547,7 @@
     ring_sum = lax.psum_scatter(
         terms, "ctx", scatter_dimension=0, axis_index_groups=rings
     ).reshape(2, WIDTH, 512)
-    parts = mixed_parts(place, heads, heads_other, weight_mine)
+    parts = mixed_parts(place, heads, heads_other, *weights)
     parts, ring_sum, end = backward_states(own, own_theirs, index, core, saved, parts, ring_sum)
     weight_grad = ring_sum[0].astype(F32) + exchange(ring_sum[1], 16).astype(F32)
     parts = lax.all_to_all(parts, "tp", 0, 0, tiled=True)

time: 159 us -> 169 us (1.063)
  starting transfers between devices: 43 us -> 48.6 us
  waiting for transfers between devices: 45.4 us -> 50.5 us
    ppermute x16, waiting for transfers between devices: 32.2 us -> 19.4 us  [exchange(): return lax.ppermute(block, 'ctx', route)]
    all_to_all x1, waiting for transfers between devices: 2.15 us -> 11.8 us  [local(): lax.all_to_all(jnp.broadcast_to(out_grad[None], (8, WIDTH, 512)), 'tp', 0...]
    ppermute x2, waiting for transfers between devices: 5.42 us -> 12.6 us  [send(): return lax.ppermute(block, 'ctx', route)]
    all_gather x1, waiting for transfers between devices: 2.93 us -> 6.72 us  [local(): weight = lax.all_gather(out_weight, 'ctx', axis=0, axis_index_groups=rings)]
    ppermute x16, starting transfers between devices: 29.2 us -> 32.2 us  [exchange(): return lax.ppermute(block, 'ctx', route)]
    all_to_all x1, waiting for transfers between devices: 2.62 us -> 0.01 us  [local(): parts = lax.all_to_all(parts, 'tp', 0, 0, tiled=True)]
  transfers between devices with their start and end apart: 22 -> 22, of which waited for: 12 -> 10; matrix products, arithmetic and copies ran while one was open for 8% -> 7% of each run, Pallas kernels for 18% -> 14%
where the time goes in v12:
time: 169 us; the launch traced here: 168 us
  waiting for transfers between devices  50.5 us (30%)
  starting transfers between devices  48.6 us (29%)
  Pallas kernels  37.9 us (22%)
  between operations  14.5 us (9%)
  matrix products  6.66 us (4%)
  local copies, waits for them, and re-layouts  5.31 us (3%)
  other arithmetic  4.74 us (3%)
    ppermute x16, starting transfers between devices, exchange(): return lax.ppermute(block, 'ctx', route)  32.2 us
    ppermute x16, waiting for transfers between devices, exchange(): return lax.ppermute(block, 'ctx', route)  19.4 us
    pallas_call x2, Pallas kernels, prepare(): pl.pallas_call(functools.partial(prepare_kernel, mine), grid_spec=pltpu.P...  12.7 us
    ppermute x2, waiting for transfers between devices, send(): return lax.ppermute(block, 'ctx', route)  12.6 us
    all_to_all x1, waiting for transfers between devices, local(): lax.all_to_all(jnp.broadcast_to(out_grad[None], (8, WIDTH, 512)), 'tp', 0...  11.8 us
    all_gather x1, waiting for transfers between devices, local(): weight = lax.all_gather(out_weight, 'ctx', axis=0, axis_index_groups=rings)  6.72 us
    ppermute x2, starting transfers between devices, send(): return lax.ppermute(block, 'ctx', route)  6.33 us
    pallas_call x1, Pallas kernels, pull(): call(pull_kernel, 2, [by_columns(WIDTH), by_columns(PAIRS), whole(4, PAIR...  6.3 us
  transfers between devices with their start and end apart: 22, of which 10 were waited for; matrix products, arithmetic and copies ran while one was open for 7% of the time, Pallas kernels for 14%

profile of v12, /device:TPU:1, one launch (start us, length us, event | category | flops | bytes accessed | tf_op | source)
XLA Modules:
  0.0 168.2 jit_solution(17646529711075083267)
XLA Ops:
  7.8 6.3 %shard_map.109 = (bf16[2,128,256]{2,1,0:T(8,128)(2,1)}, f32[4,256,256]{2,1,0:T(8,128)}, f32[4,256,256]{2,1,0:T(8,128)}, f32[4,128,128]{2,1,0:T(8,128)}, f32[4,128,128]{2,1,0:T(8,128)}) custom-call(s32[2]{0:T(128)} %pad_add_fusion.refs_0_.place, bf16[128,512]{1,0:T(8,128)(2,1)} %q_ref.1, bf16[128,1024]{1,0:T(8,128)(2,1)} %k_ref.1, bf16[128,1024]{1,0:T(8,128)(2,1)} %refs_3_.3, ...), custom_call_target="tpu_custom_call" | custom-call | flops 1024 | bytes 1024 | tf_op jit(solution)/shard_map/pallas_call | solution.py:172
  14.1 3.2 %collective-permute-start = (bf16[2,128,256]{2,1,0:T(8,128)(2,1)}, bf16[2,128,256]{2,1,0:T(8,128)(2,1)S(1)}, u32[]{:S(2)}, u32[]{:S(2)}) collective-permute-start(bf16[2,128,256]{2,1,0:T(8,128)(2,1)} %get-tuple-element.43), channel_id=1, source_target_pairs={{0,8},{8,0},{16,24},{24,16},{32,40},{40,32},{48,56},{56,48},{64,72... | collective-permute-start | bytes 393224 | tf_op jit(solution)/shard_map/ppermute | solution.py:26
  17.4 6.4 %shard_map.110 = (bf16[2,128,256]{2,1,0:T(8,128)(2,1)}, f32[4,256,256]{2,1,0:T(8,128)}, f32[4,256,256]{2,1,0:T(8,128)}, f32[4,128,128]{2,1,0:T(8,128)}, f32[4,128,128]{2,1,0:T(8,128)}) custom-call(s32[2]{0:T(128)} %pad_add_fusion.refs_0_.place, bf16[128,512]{1,0:T(8,128)(2,1)} %q_ref.1, ...), custom_call_target="tpu_custom_call", output_to_operand_aliasing={{1}: (5, {}), {2}: (6, {}), {3}: (7, {}), {4}: (8, {})} | custom-call | flops 1024 | bytes 1024 | tf_op jit(solution)/shard_map/pallas_call | solution.py:172
  25.1 1.1 broadcast_in_dim.21
  26.2 5.0 %all-to-all-start = ((bf16[8,128,512]{2,1,0:T(8,128)(2,1)}), bf16[8,128,512]{2,1,0:T(8,128)(2,1)S(1)}, u32[]{:S(2)}, u32[]{:S(2)}) async-start(bf16[8,128,512]{2,1,0:T(8,128)(2,1)} %broadcast_in_dim.21), calls=%async_computation | async-start | bytes 2097152 | tf_op jit(solution)/shard_map/all_to_all | solution.py:538
  31.5 3.1 %collective-permute-start.2 = (bf16[2,128,256]{2,1,0:T(8,128)(2,1)S(1)}, bf16[2,128,256]{2,1,0:T(8,128)(2,1)S(1)}, u32[]{:S(2)}, u32[]{:S(2)}) collective-permute-start(bf16[2,128,256]{2,1,0:T(8,128)(2,1)S(1)} %pad_maximum_fusion.1), channel_id=1, source_target_pairs={{0,32},{8,40},{16,48},{24,56},{32,0},{40,8},{48,16},{56,24},{64,96... | collective-permute-start | bytes 393224 | tf_op jit(solution)/shard_map/ppermute | solution.py:26
  34.6 11.8 %all-to-all-done.refs_0_.refs_1_ = bf16[8,128,512]{2,1,0:T(8,128)(2,1)S(1)} async-done(((bf16[8,128,512]{2,1,0:T(8,128)(2,1)}), bf16[8,128,512]{2,1,0:T(8,128)(2,1)S(1)}, u32[]{:S(2)}, u32[]{:S(2)}) %all-to-all-start) | async-done | bytes 1048608 | tf_op jit(solution)/shard_map/all_to_all | solution.py:538
  46.4 1.4 collective-permute-start.3
  47.9 6.7 %all-gather.3.cloned.1.call-done = bf16[1024,512]{1,0:T(8,128)(2,1)} async-done(((bf16[128,512]{1,0:T(8,128)(2,1)}), bf16[1024,512]{1,0:T(8,128)(2,1)}) %all-gather.3.cloned.1.call-update) | async-done | bytes 1048592 | tf_op jit(solution)/shard_map/all_gather | solution.py:537
  54.9 3.4 %collective-permute-start.4 = (bf16[2,128,256]{2,1,0:T(8,128)(2,1)S(1)}, bf16[2,128,256]{2,1,0:T(8,128)(2,1)S(1)}, u32[]{:S(2)}, u32[]{:S(2)}) collective-permute-start(bf16[2,128,256]{2,1,0:T(8,128)(2,1)S(1)} %pad_maximum_fusion.2), channel_id=1, source_target_pairs={{0,64},{8,72},{16,80},{24,88},{32,96},{40,104},{48,112},{56,120},{... | collective-permute-start | bytes 393224 | tf_op jit(solution)/shard_map/ppermute | solution.py:26
  58.2 2.1 %collective-permute-start.5 = (bf16[8,128,512]{2,1,0:T(8,128)(2,1)}, bf16[8,128,512]{2,1,0:T(8,128)(2,1)}, u32[]{:S(2)}, u32[]{:S(2)}) collective-permute-start(bf16[8,128,512]{2,1,0:T(8,128)(2,1)} %bitcast.23), channel_id=1, source_target_pairs={{0,128},{8,136},{16,144},{24,152},{32,160},{40,168},{48,176},{56,1... | collective-permute-start | bytes 3145736 | tf_op jit(solution)/shard_map/ppermute | solution.py:26
  61.6 1.1 collective-permute-done.4
  63.7 5.0 %collective-permute-start.6 = (bf16[2,128,128]{2,1,0:T(8,128)(2,1)}, bf16[2,128,128]{2,1,0:T(8,128)(2,1)}, u32[]{:S(2)}, u32[]{:S(2)}) collective-permute-start(bf16[2,128,128]{2,1,0:T(8,128)(2,1)} %fusion.5), channel_id=1, source_target_pairs={{0,128},{8,136},{16,144},{24,152},{32,160},{40,168},{48,176},{56,1... | collective-permute-start | bytes 196616 | tf_op jit(solution)/shard_map/ppermute | solution.py:21
  69.6 11.0 %collective-permute-done.5.refs_5_.across_ref = bf16[8,128,512]{2,1,0:T(8,128)(2,1)} collective-permute-done((bf16[8,128,512]{2,1,0:T(8,128)(2,1)}, bf16[8,128,512]{2,1,0:T(8,128)(2,1)}, u32[]{:S(2)}, u32[]{:S(2)}) %collective-permute-start.5) | collective-permute-done | bytes 1048608 | tf_op jit(solution)/shard_map/ppermute | solution.py:26
  80.6 5.2 %shard_map.111 = (f32[128,512]{1,0:T(8,128)}, f32[128,512]{1,0:T(8,128)}) custom-call(s32[2]{0:T(128)} %pad_add_fusion.refs_0_.place, bf16[8,128,512]{2,1,0:T(8,128)(2,1)} %copy-done, bf16[8,128,512]{2,1,0:T(8,128)(2,1)} %copy-done, bf16[8,128,512]{2,1,0:T(8,128)(2,1)} %copy-done.1, bf16[8,128,512]{2,1,0:T(8,128)(2,1)} %copy-done.1, ...), custom_call_target="tpu_custom_call" | custom-call | flops 536870912 | bytes 5242880 | tf_op jit(solution)/shard_map/pallas_call | solution.py:344
  85.9 5.3 %collective-permute-start.8 = (f32[128,512]{1,0:T(8,128)}, f32[128,512]{1,0:T(8,128)S(1)}, u32[]{:S(2)}, u32[]{:S(2)}) collective-permute-start(f32[128,512]{1,0:T(8,128)} %get-tuple-element.53), channel_id=1, source_target_pairs={{0,8},{8,0},{16,24},{24,16},{32,40},{40,32},{48,56},{56,48},{64,72... | collective-permute-start | bytes 786440 | tf_op jit(solution)/shard_map/ppermute | solution.py:26
  91.1 1.3 fusion.10
  92.7 1.2 collective-permute-done.7
  95.3 3.4 %shard_map.112 = (bf16[128,512]{1,0:T(8,128)(2,1)}, f32[128,512]{1,0:T(8,128)}, bf16[2,128,128]{2,1,0:T(8,128)(2,1)}, bf16[2,128,128]{2,1,0:T(8,128)(2,1)}) custom-call(s32[2]{0:T(128)} %pad_add_fusion.refs_0_.place, f32[4,128,128]{2,1,0:T(8,128)} %get-tuple-element.41.qt_ref, f32[4,128,128]{2,1,0:T(8,128)} %get-tuple-element.42.local_ref, ...), custom_call_target="tpu_custom_call" | custom-call | flops 33554432 | bytes 2097152 | tf_op jit(solution)/shard_map/pallas_call | solution.py:261
  98.9 1.4 collective-permute-done.9.heads_other_ref.refs_5_
  100.9 5.3 %shard_map.114 = bf16[8,256,512]{2,1,0:T(8,128)(2,1)} custom-call(s32[2]{0:T(128)} %pad_add_fusion.refs_0_.place, bf16[8,128,512]{2,1,0:T(8,128)(2,1)} %copy-done, bf16[8,128,512]{2,1,0:T(8,128)(2,1)} %copy-done, bf16[8,128,512]{2,1,0:T(8,128)(2,1)} %copy-done.1, bf16[8,128,512]{2,1,0:T(8,128)(2,1)} %copy-done.1, ...), custom_call_target="tpu_custom_call" | custom-call | flops 536870912 | bytes 5242880 | tf_op jit(solution)/shard_map/pallas_call | solution.py:286
  107.2 1.1 collective-permute-done.10
  108.6 5.0 %shard_map.113 = bf16[8,256,256]{2,1,0:T(8,128)(2,1)} custom-call(s32[2]{0:T(128)} %pad_add_fusion.refs_0_.place, bf16[128,512]{1,0:T(8,128)(2,1)} %get-tuple-element.54.heads_ref.refs_4_, bf16[128,512]{1,0:T(8,128)(2,1)} %copy-done.2, bf16[8,128,512]{2,1,0:T(8,128)(2,1)} %bitcast.25, bf16[8,128,512]{2,1,0:T(8,128)(2,1)} %collective-permute-done.5.refs_5_.across_ref), custom_call_target="tpu_custom_call" | custom-call | flops 536870912 | bytes 3145728 | tf_op jit(solution)/shard_map/pallas_call | solution.py:311
  113.9 2.3 %collective-permute-start.13 = (bf16[2,128,128]{2,1,0:T(8,128)(2,1)S(1)}, bf16[2,128,128]{2,1,0:T(8,128)(2,1)S(1)}, u32[]{:S(2)}, u32[]{:S(2)}) collective-permute-start(bf16[2,128,128]{2,1,0:T(8,128)(2,1)S(1)} %add_convert_fusion.3), channel_id=1, source_target_pairs={{0,32},{8,40},{16,48},{24,56},{32,0},{40,8},{48,16},{56,24},{64,96... | collective-permute-start | bytes 196616 | tf_op jit(solution)/shard_map/ppermute | solution.py:26
  116.2 2.8 %collective-permute-done.13 = bf16[2,128,128]{2,1,0:T(8,128)(2,1)S(1)} collective-permute-done((bf16[2,128,128]{2,1,0:T(8,128)(2,1)S(1)}, bf16[2,128,128]{2,1,0:T(8,128)(2,1)S(1)}, u32[]{:S(2)}, u32[]{:S(2)}) %collective-permute-start.13) | collective-permute-done | bytes 65568 | tf_op jit(solution)/shard_map/ppermute | solution.py:26
  119.2 5.2 %collective-permute-start.14 = (bf16[2,128,128]{2,1,0:T(8,128)(2,1)S(1)}, bf16[2,128,128]{2,1,0:T(8,128)(2,1)S(1)}, u32[]{:S(2)}, u32[]{:S(2)}) collective-permute-start(bf16[2,128,128]{2,1,0:T(8,128)(2,1)S(1)} %add_convert_fusion.2), channel_id=1, source_target_pairs={{0,64},{8,72},{16,80},{24,88},{32,96},{40,104},{48,112},{56,120},{... | collective-permute-start | bytes 196616 | tf_op jit(solution)/shard_map/ppermute | solution.py:26
  124.6 5.0 %all-to-all-start.1 = ((bf16[8,256,256]{2,1,0:T(8,128)(2,1)}), bf16[8,256,256]{2,1,0:T(8,128)(2,1)S(1)}, u32[]{:S(2)}, u32[]{:S(2)}) async-start(bf16[8,256,256]{2,1,0:T(8,128)(2,1)} %shard_map.113), calls=%async_computation.1 | async-start | bytes 2097152 | tf_op jit(solution)/shard_map/all_to_all | solution.py:553
  129.8 1.3 collective-permute-start.15
  132.2 12.5 %collective-permute-done.15 = bf16[2,128,128]{2,1,0:T(8,128)(2,1)S(1)} collective-permute-done((bf16[2,128,128]{2,1,0:T(8,128)(2,1)S(1)}, bf16[2,128,128]{2,1,0:T(8,128)(2,1)S(1)}, u32[]{:S(2)}, u32[]{:S(2)}) %collective-permute-start.15) | collective-permute-done | bytes 65568 | tf_op jit(solution)/shard_map/ppermute | solution.py:21
  145.5 2.4 %collective-permute-start.12 = (bf16[128,256]{1,0:T(8,128)(2,1)S(1)}, bf16[128,256]{1,0:T(8,128)(2,1)S(1)}, u32[]{:S(2)}, u32[]{:S(2)}) collective-permute-start(bf16[128,256]{1,0:T(8,128)(2,1)S(1)} %slice.180), channel_id=1, source_target_pairs={{0,8},{8,0},{16,24},{24,16},{32,40},{40,32},{48,56},{56,48},{64,72... | collective-permute-start | bytes 196616 | tf_op jit(solution)/shard_map/ppermute | solution.py:26
  150.9 2.7 %collective-permute-start.17 = (bf16[128,512]{1,0:T(8,128)(2,1)S(1)}, bf16[128,512]{1,0:T(8,128)(2,1)S(1)}, u32[]{:S(2)}, u32[]{:S(2)}) collective-permute-start(bf16[128,512]{1,0:T(8,128)(2,1)S(1)} %slice_bitcast_fusion), channel_id=1, source_target_pairs={{0,128},{8,136},{16,144},{24,152},{32,160},{40,168},{48,176},{56,1... | collective-permute-start | bytes 393224 | tf_op jit(solution)/shard_map/ppermute | solution.py:26
  154.3 6.3 %shard_map.115 = (bf16[128,512]{1,0:T(8,128)(2,1)}, bf16[128,1024]{1,0:T(8,128)(2,1)}, bf16[128,1024]{1,0:T(8,128)(2,1)}, f32[4,256]{1,0:T(4,128)}) custom-call(s32[2]{0:T(128)} %pad_add_fusion.refs_0_.place, bf16[128,512]{1,0:T(8,128)(2,1)} %q_ref.1, bf16[128,1024]{1,0:T(8,128)(2,1)} %k_ref.1, f32[4,256]{1,0:T(4,128)} %logit_ref.1, ...), custom_call_target="tpu_custom_call" | custom-call | flops 1879048192 | bytes 5242880 | tf_op jit(solution)/shard_map/pallas_call | solution.py:416
  (96 shorter events, 16.2 us)
Async XLA Ops:
  7.2 47.4 %all-gather.3.cloned.1.call-start = ((), (), s32[]{:S(2)}) async-start(), calls=%async_computation.4 | async-start | bytes 1179648 | tf_op jit(solution)/shard_map/all_gather | solution.py:537
  14.1 9.7 %collective-permute-start = (bf16[2,128,256]{2,1,0:T(8,128)(2,1)}, bf16[2,128,256]{2,1,0:T(8,128)(2,1)S(1)}, u32[]{:S(2)}, u32[]{:S(2)}) collective-permute-start(bf16[2,128,256]{2,1,0:T(8,128)(2,1)} %get-tuple-element.43), channel_id=1, source_target_pairs={{0,8},{8,0},{16,24},{24,16},{32,40},{40,32},{48,56},{56,48},{64,72... | collective-permute-start | bytes 393224 | tf_op jit(solution)/shard_map/ppermute | solution.py:26
  17.4 7.7 %copy-start.7 = (bf16[128,512]{1,0:T(8,128)(2,1)S(1)}, bf16[128,512]{1,0:T(8,128)(2,1)}, u32[]{:S(2)}) copy-start(bf16[128,512]{1,0:T(8,128)(2,1)} %param.11) | copy-start | bytes 393220
  25.0 6.2 %collective-permute-start.1 = (bf16[2,128,256]{2,1,0:T(8,128)(2,1)S(1)}, bf16[2,128,256]{2,1,0:T(8,128)(2,1)S(1)}, u32[]{:S(2)}, u32[]{:S(2)}) collective-permute-start(bf16[2,128,256]{2,1,0:T(8,128)(2,1)S(1)} %pad_maximum_fusion), channel_id=1, source_target_pairs={{0,16},{8,24},{16,0},{24,8},{32,48},{40,56},{48,32},{56,40},{64,80... | collective-permute-start | bytes 393224 | tf_op jit(solution)/shard_map/ppermute | solution.py:26
  26.2 20.3 %all-to-all-start = ((bf16[8,128,512]{2,1,0:T(8,128)(2,1)}), bf16[8,128,512]{2,1,0:T(8,128)(2,1)S(1)}, u32[]{:S(2)}, u32[]{:S(2)}) async-start(bf16[8,128,512]{2,1,0:T(8,128)(2,1)} %broadcast_in_dim.21), calls=%async_computation | async-start | bytes 2097152 | tf_op jit(solution)/shard_map/all_to_all | solution.py:538
  31.2 118.4 %reduce-scatter.2.cloned.1.call-start = ((), (), s32[]{:S(2)}) async-start(), calls=%async_computation.3 | async-start | bytes 2359296 | tf_op jit(solution)/shard_map/reduce_scatter | solution.py:547
  31.5 16.3 %collective-permute-start.2 = (bf16[2,128,256]{2,1,0:T(8,128)(2,1)S(1)}, bf16[2,128,256]{2,1,0:T(8,128)(2,1)S(1)}, u32[]{:S(2)}, u32[]{:S(2)}) collective-permute-start(bf16[2,128,256]{2,1,0:T(8,128)(2,1)S(1)} %pad_maximum_fusion.1), channel_id=1, source_target_pairs={{0,32},{8,40},{16,48},{24,56},{32,0},{40,8},{48,16},{56,24},{64,96... | collective-permute-start | bytes 393224 | tf_op jit(solution)/shard_map/ppermute | solution.py:26
  46.4 34.2 %copy-start = (bf16[8,128,512]{2,1,0:T(8,128)(2,1)}, bf16[8,128,512]{2,1,0:T(8,128)(2,1)S(1)}, u32[]{:S(2)}) copy-start(bf16[8,128,512]{2,1,0:T(8,128)(2,1)S(1)} %all-to-all-done.refs_0_.refs_1_) | copy-start | bytes 3145732
  46.4 14.2 %collective-permute-start.3 = (bf16[8,128,512]{2,1,0:T(8,128)(2,1)S(1)}, bf16[8,128,512]{2,1,0:T(8,128)(2,1)S(1)}, u32[]{:S(2)}, u32[]{:S(2)}) collective-permute-start(bf16[8,128,512]{2,1,0:T(8,128)(2,1)S(1)} %all-to-all-done.refs_0_.refs_1_), channel_id=1, source_target_pairs={{0,8},{8,0},{16,24},{24,16},{32,40},{40,32},{48,56},{56,48},{64,72... | collective-permute-start | bytes 3145736 | tf_op jit(solution)/shard_map/ppermute | solution.py:26
  54.9 7.9 %collective-permute-start.4 = (bf16[2,128,256]{2,1,0:T(8,128)(2,1)S(1)}, bf16[2,128,256]{2,1,0:T(8,128)(2,1)S(1)}, u32[]{:S(2)}, u32[]{:S(2)}) collective-permute-start(bf16[2,128,256]{2,1,0:T(8,128)(2,1)S(1)} %pad_maximum_fusion.2), channel_id=1, source_target_pairs={{0,64},{8,72},{16,80},{24,88},{32,96},{40,104},{48,112},{56,120},{... | collective-permute-start | bytes 393224 | tf_op jit(solution)/shard_map/ppermute | solution.py:26
  58.2 22.4 %collective-permute-start.5 = (bf16[8,128,512]{2,1,0:T(8,128)(2,1)}, bf16[8,128,512]{2,1,0:T(8,128)(2,1)}, u32[]{:S(2)}, u32[]{:S(2)}) collective-permute-start(bf16[8,128,512]{2,1,0:T(8,128)(2,1)} %bitcast.23), channel_id=1, source_target_pairs={{0,128},{8,136},{16,144},{24,152},{32,160},{40,168},{48,176},{56,1... | collective-permute-start | bytes 3145736 | tf_op jit(solution)/shard_map/ppermute | solution.py:26
  60.6 8.1 %copy-start.4 = (bf16[2,128,128]{2,1,0:T(8,128)(2,1)}, bf16[2,128,128]{2,1,0:T(8,128)(2,1)S(1)}, u32[]{:S(2)}) copy-start(bf16[2,128,128]{2,1,0:T(8,128)(2,1)S(1)} %fusion.14) | copy-start | bytes 196612
  62.9 6.7 %copy-start.8 = (bf16[2,128,256]{2,1,0:T(8,128)(2,1)}, bf16[2,128,256]{2,1,0:T(8,128)(2,1)S(1)}, u32[]{:S(2)}) copy-start(bf16[2,128,256]{2,1,0:T(8,128)(2,1)S(1)} %get-tuple-element.68) | copy-start | bytes 393220
  63.7 22.2 %collective-permute-start.6 = (bf16[2,128,128]{2,1,0:T(8,128)(2,1)}, bf16[2,128,128]{2,1,0:T(8,128)(2,1)}, u32[]{:S(2)}, u32[]{:S(2)}) collective-permute-start(bf16[2,128,128]{2,1,0:T(8,128)(2,1)} %fusion.5), channel_id=1, source_target_pairs={{0,128},{8,136},{16,144},{24,152},{32,160},{40,168},{48,176},{56,1... | collective-permute-start | bytes 196616 | tf_op jit(solution)/shard_map/ppermute | solution.py:21
  85.9 8.7 %collective-permute-start.8 = (f32[128,512]{1,0:T(8,128)}, f32[128,512]{1,0:T(8,128)S(1)}, u32[]{:S(2)}, u32[]{:S(2)}) collective-permute-start(f32[128,512]{1,0:T(8,128)} %get-tuple-element.53), channel_id=1, source_target_pairs={{0,8},{8,0},{16,24},{24,16},{32,40},{40,32},{48,56},{56,48},{64,72... | collective-permute-start | bytes 786440 | tf_op jit(solution)/shard_map/ppermute | solution.py:26
  92.5 1.3 collective-permute-start.7
  98.7 1.6 collective-permute-start.9
  107.0 1.3 collective-permute-start.10
  108.3 10.9 %copy-start.12 = (bf16[2,128,128]{2,1,0:T(8,128)(2,1)}, bf16[2,128,128]{2,1,0:T(8,128)(2,1)S(1)}, u32[]{:S(2)}) copy-start(bf16[2,128,128]{2,1,0:T(8,128)(2,1)S(1)} %collective-permute-done.10) | copy-start | bytes 196612
  108.5 5.1 %collective-permute-start.11 = (bf16[2,128,128]{2,1,0:T(8,128)(2,1)S(1)}, bf16[2,128,128]{2,1,0:T(8,128)(2,1)S(1)}, u32[]{:S(2)}, u32[]{:S(2)}) collective-permute-start(bf16[2,128,128]{2,1,0:T(8,128)(2,1)S(1)} %add_convert_fusion.4), channel_id=1, source_target_pairs={{0,16},{8,24},{16,0},{24,8},{32,48},{40,56},{48,32},{56,40},{64,80... | collective-permute-start | bytes 196616 | tf_op jit(solution)/shard_map/ppermute | solution.py:26
  113.6 16.0 %copy-start.9 = (bf16[2,128,256]{2,1,0:T(8,128)(2,1)S(1)}, bf16[2,128,256]{2,1,0:T(8,128)(2,1)}, u32[]{:S(2)}) copy-start(bf16[2,128,256]{2,1,0:T(8,128)(2,1)} %copy-done.8) | copy-start | bytes 393220
  113.6 11.0 %copy-start.14 = (bf16[2,128,128]{2,1,0:T(8,128)(2,1)}, bf16[2,128,128]{2,1,0:T(8,128)(2,1)S(1)}, u32[]{:S(2)}) copy-start(bf16[2,128,128]{2,1,0:T(8,128)(2,1)S(1)} %collective-permute-done.11) | copy-start | bytes 196612
  113.9 5.1 %collective-permute-start.13 = (bf16[2,128,128]{2,1,0:T(8,128)(2,1)S(1)}, bf16[2,128,128]{2,1,0:T(8,128)(2,1)S(1)}, u32[]{:S(2)}, u32[]{:S(2)}) collective-permute-start(bf16[2,128,128]{2,1,0:T(8,128)(2,1)S(1)} %add_convert_fusion.3), channel_id=1, source_target_pairs={{0,32},{8,40},{16,48},{24,56},{32,0},{40,8},{48,16},{56,24},{64,96... | collective-permute-start | bytes 196616 | tf_op jit(solution)/shard_map/ppermute | solution.py:26
  119.2 10.4 %collective-permute-start.14 = (bf16[2,128,128]{2,1,0:T(8,128)(2,1)S(1)}, bf16[2,128,128]{2,1,0:T(8,128)(2,1)S(1)}, u32[]{:S(2)}, u32[]{:S(2)}) collective-permute-start(bf16[2,128,128]{2,1,0:T(8,128)(2,1)S(1)} %add_convert_fusion.2), channel_id=1, source_target_pairs={{0,64},{8,72},{16,80},{24,88},{32,96},{40,104},{48,112},{56,120},{... | collective-permute-start | bytes 196616 | tf_op jit(solution)/shard_map/ppermute | solution.py:26
  124.6 23.4 %copy-start.11 = (bf16[2,128,128]{2,1,0:T(8,128)(2,1)S(1)}, bf16[2,128,128]{2,1,0:T(8,128)(2,1)}, u32[]{:S(2)}) copy-start(bf16[2,128,128]{2,1,0:T(8,128)(2,1)} %get-tuple-element.55) | copy-start | bytes 196612
  124.6 23.4 %copy-start.13 = (bf16[2,128,128]{2,1,0:T(8,128)(2,1)S(1)}, bf16[2,128,128]{2,1,0:T(8,128)(2,1)}, u32[]{:S(2)}) copy-start(bf16[2,128,128]{2,1,0:T(8,128)(2,1)} %copy-done.12) | copy-start | bytes 196612
  124.6 20.8 %all-to-all-start.1 = ((bf16[8,256,256]{2,1,0:T(8,128)(2,1)}), bf16[8,256,256]{2,1,0:T(8,128)(2,1)S(1)}, u32[]{:S(2)}, u32[]{:S(2)}) async-start(bf16[8,256,256]{2,1,0:T(8,128)(2,1)} %shard_map.113), calls=%async_computation.1 | async-start | bytes 2097152 | tf_op jit(solution)/shard_map/all_to_all | solution.py:553
  129.8 14.9 %collective-permute-start.15 = (bf16[2,128,128]{2,1,0:T(8,128)(2,1)S(1)}, bf16[2,128,128]{2,1,0:T(8,128)(2,1)S(1)}, u32[]{:S(2)}, u32[]{:S(2)}) collective-permute-start(bf16[2,128,128]{2,1,0:T(8,128)(2,1)S(1)} %add_convert_fusion.1), channel_id=1, source_target_pairs={{128,0},{136,8},{144,16},{152,24},{160,32},{168,40},{176,48},{184,... | collective-permute-start | bytes 196616 | tf_op jit(solution)/shard_map/ppermute | solution.py:21
  145.5 3.3 %collective-permute-start.12 = (bf16[128,256]{1,0:T(8,128)(2,1)S(1)}, bf16[128,256]{1,0:T(8,128)(2,1)S(1)}, u32[]{:S(2)}, u32[]{:S(2)}) collective-permute-start(bf16[128,256]{1,0:T(8,128)(2,1)S(1)} %slice.180), channel_id=1, source_target_pairs={{0,8},{8,0},{16,24},{24,16},{32,40},{40,32},{48,56},{56,48},{64,72... | collective-permute-start | bytes 196616 | tf_op jit(solution)/shard_map/ppermute | solution.py:26
  149.6 4.0 %collective-permute-start.16 = (bf16[2,128,128]{2,1,0:T(8,128)(2,1)S(1)}, bf16[2,128,128]{2,1,0:T(8,128)(2,1)S(1)}, u32[]{:S(2)}, u32[]{:S(2)}) collective-permute-start(bf16[2,128,128]{2,1,0:T(8,128)(2,1)S(1)} %get-tuple-element.61), channel_id=1, source_target_pairs={{0,8},{8,0},{16,24},{24,16},{32,40},{40,32},{48,56},{56,48},{64,72... | collective-permute-start | bytes 196616 | tf_op jit(solution)/shard_map/ppermute | solution.py:26
  150.9 9.7 %collective-permute-start.17 = (bf16[128,512]{1,0:T(8,128)(2,1)S(1)}, bf16[128,512]{1,0:T(8,128)(2,1)S(1)}, u32[]{:S(2)}, u32[]{:S(2)}) collective-permute-start(bf16[128,512]{1,0:T(8,128)(2,1)S(1)} %slice_bitcast_fusion), channel_id=1, source_target_pairs={{0,128},{8,136},{16,144},{24,152},{32,160},{40,168},{48,176},{56,1... | collective-permute-start | bytes 393224 | tf_op jit(solution)/shard_map/ppermute | solution.py:26
  154.3 6.3 %copy-start.5 = (bf16[1,256,512]{2,1,0:T(8,128)(2,1)S(1)}, bf16[1,256,512]{2,1,0:T(8,128)(2,1)}, u32[]{:S(2)}) copy-start(bf16[1,256,512]{2,1,0:T(8,128)(2,1)} %reduce-scatter.2.cloned.1.call-done) | copy-start | bytes 786436
  (6 other events, 7.6 us)
Sparse Core Ops, SparseCore 0:
  17.5 37.0 all-gather.2
  106.3 38.8 reduce-scatter.1

commit v13 on v11

--- a/solution.py
+++ b/solution.py
@@ -550,16 +550,18 @@
     ).reshape(2, WIDTH, 512)
     parts = mixed_parts(place, heads, heads_other, weight_mine)
     parts, ring_sum, end = backward_states(own, own_theirs, index, core, saved, parts, ring_sum)
-    weight_grad = ring_sum[0].astype(F32) + exchange(ring_sum[1], 16).astype(F32)
+    across = exchange(ring_sum[1], 16)
     parts = lax.all_to_all(parts, "tp", 0, 0, tiled=True)
+    query_grad, key_grad, value_grad, logit_grad = pull(
+        place, queries, keys, beta_logit, reads, wy, state, end, head_grad
+    )
+    parts, across, query_grad = lax.optimization_barrier((parts, across, query_grad))
+    weight_grad = ring_sum[0].astype(F32) + across.astype(F32)
     sums = jnp.sum(parts.astype(F32), axis=0).astype(BF16)
     kept, came = sums[:WIDTH], exchange(sums[WIDTH:], 1)
     first, second = jnp.where(core == 0, kept, came), jnp.where(core == 0, came, kept)
     mixed = jnp.concatenate(
         [first[:, :WIDTH], second[:, :WIDTH], first[:, WIDTH:], second[:, WIDTH:]], axis=1
-    )
-    query_grad, key_grad, value_grad, logit_grad = pull(
-        place, queries, keys, beta_logit, reads, wy, state, end, head_grad
     )
     return mixed, query_grad, key_grad, value_grad, logit_grad, weight_grad
 

time: 159 us -> 161 us (1.013)
    reduce_scatter x1, waiting for transfers between devices: 0.01 us -> 3.82 us  [local(): lax.psum_scatter(terms, 'ctx', scatter_dimension=0, axis_index_groups=rings)]
    all_to_all x1, waiting for transfers between devices: 2.62 us -> 0.01 us  [local(): parts = lax.all_to_all(parts, 'tp', 0, 0, tiled=True)]
    unnamed x24 -> x30, local copies, waits for them, and re-layouts: 3.17 us -> 3.6 us
where the time goes in v13:
time: 161 us; the launch traced here: 160 us
  waiting for transfers between devices  46.5 us (29%)
  starting transfers between devices  43.3 us (27%)
  Pallas kernels  37.9 us (24%)
  between operations  14.4 us (9%)
  other arithmetic  6.41 us (4%)
  local copies, waits for them, and re-layouts  6.28 us (4%)
  matrix products  5.19 us (3%)
    ppermute x16, waiting for transfers between devices, exchange(): return lax.ppermute(block, 'ctx', route)  32.3 us
    ppermute x16, starting transfers between devices, exchange(): return lax.ppermute(block, 'ctx', route)  29.6 us
    pallas_call x2, Pallas kernels, prepare(): pl.pallas_call(functools.partial(prepare_kernel, mine), grid_spec=pltpu.P...  12.7 us
    pallas_call x1, Pallas kernels, pull(): call(pull_kernel, 2, [by_columns(WIDTH), by_columns(PAIRS), whole(4, PAIR...  6.28 us
    ppermute x2, starting transfers between devices, send(): return lax.ppermute(block, 'ctx', route)  5.43 us
    pallas_call x1, Pallas kernels, weight_terms(): call(weight_terms_kernel, STEPS, grad_specs() + [whole(WIDTH, 512), whole...  5.29 us
    ppermute x2, waiting for transfers between devices, send(): return lax.ppermute(block, 'ctx', route)  5.29 us
    pallas_call x1, Pallas kernels, head_gradient(): call(head_grad_kernel, STEPS, grad_specs() + [weight_tile()], [whole(WIDT...  5.21 us
  transfers between devices with their start and end apart: 22, of which 12 were waited for; matrix products, arithmetic and copies ran while one was open for 8% of the time, Pallas kernels for 18%

profile of v13, /device:TPU:1, one launch (start us, length us, event | category | flops | bytes accessed | tf_op | source)
XLA Modules:
  0.0 160.0 jit_solution(9720255918453558435)
XLA Ops:
  7.2 3.7 %collective-permute-start = (bf16[128,512]{1,0:T(8,128)(2,1)}, bf16[128,512]{1,0:T(8,128)(2,1)S(1)}, u32[]{:S(2)}, u32[]{:S(2)}) collective-permute-start(bf16[128,512]{1,0:T(8,128)(2,1)} %param.10), channel_id=1, source_target_pairs={{0,128},{8,136},{16,144},{24,152},{32,160},{40,168},{48,176},{56,1... | collective-permute-start | bytes 393224 | tf_op jit(solution)/shard_map/ppermute | solution.py:26
  11.5 6.3 %shard_map.109 = (bf16[2,128,256]{2,1,0:T(8,128)(2,1)}, f32[4,256,256]{2,1,0:T(8,128)}, f32[4,256,256]{2,1,0:T(8,128)}, f32[4,128,128]{2,1,0:T(8,128)}, f32[4,128,128]{2,1,0:T(8,128)}) custom-call(s32[2]{0:T(128)} %pad_add_fusion.refs_0_.place, bf16[128,512]{1,0:T(8,128)(2,1)} %q_ref.1, bf16[128,1024]{1,0:T(8,128)(2,1)} %k_ref.1, bf16[128,1024]{1,0:T(8,128)(2,1)} %refs_3_.2, ...), custom_call_target="tpu_custom_call" | custom-call | flops 104857600 | bytes 16777216 | tf_op jit(solution)/shard_map/pallas_call | solution.py:172
  18.7 1.6 %pad_maximum_fusion = bf16[2,128,512]{2,1,0:T(8,128)(2,1)} fusion(bf16[1,128,512]{2,1,0:T(8,128)(2,1)S(1)} %bitcast.31, bf16[1,128,512]{2,1,0:T(8,128)(2,1)} %bitcast.30), kind=kLoop, calls=%fused_computation.13 | loop fusion | flops 131072 | bytes 524288 | tf_op jit(solution)/shard_map/stack | solution.py:535
  20.4 6.4 %shard_map.110 = (bf16[2,128,256]{2,1,0:T(8,128)(2,1)}, f32[4,256,256]{2,1,0:T(8,128)}, f32[4,256,256]{2,1,0:T(8,128)}, f32[4,128,128]{2,1,0:T(8,128)}, f32[4,128,128]{2,1,0:T(8,128)}) custom-call(s32[2]{0:T(128)} %pad_add_fusion.refs_0_.place, bf16[128,512]{1,0:T(8,128)(2,1)} %q_ref.1, ...), custom_call_target="tpu_custom_call", output_to_operand_aliasing={{1}: (5, {}), {2}: (6, {}), {3}: (7, {}), {4}: (8, {})} | custom-call | flops 1048576 | bytes 65536 | tf_op jit(solution)/shard_map/pallas_call | solution.py:172
  28.0 1.7 %collective-permute-start.2 = (bf16[2,128,256]{2,1,0:T(8,128)(2,1)S(1)}, bf16[2,128,256]{2,1,0:T(8,128)(2,1)S(1)}, u32[]{:S(2)}, u32[]{:S(2)}) collective-permute-start(bf16[2,128,256]{2,1,0:T(8,128)(2,1)S(1)} %pad_maximum_fusion.1), channel_id=1, source_target_pairs={{0,16},{8,24},{16,0},{24,8},{32,48},{40,56},{48,32},{56,40},{64,80... | collective-permute-start | bytes 393224 | tf_op jit(solution)/shard_map/ppermute | solution.py:26
  30.8 4.2 %all-to-all-start = ((bf16[8,128,512]{2,1,0:T(8,128)(2,1)}), bf16[8,128,512]{2,1,0:T(8,128)(2,1)S(1)}, u32[]{:S(2)}, u32[]{:S(2)}) async-start(bf16[8,128,512]{2,1,0:T(8,128)(2,1)} %broadcast_in_dim.21), calls=%async_computation | async-start | bytes 2097152 | tf_op jit(solution)/shard_map/all_to_all | solution.py:539
  35.4 3.1 %collective-permute-start.3 = (bf16[2,128,256]{2,1,0:T(8,128)(2,1)S(1)}, bf16[2,128,256]{2,1,0:T(8,128)(2,1)S(1)}, u32[]{:S(2)}, u32[]{:S(2)}) collective-permute-start(bf16[2,128,256]{2,1,0:T(8,128)(2,1)S(1)} %pad_maximum_fusion.2), channel_id=1, source_target_pairs={{0,32},{8,40},{16,48},{24,56},{32,0},{40,8},{48,16},{56,24},{64,96... | collective-permute-start | bytes 393224 | tf_op jit(solution)/shard_map/ppermute | solution.py:26
  38.5 9.6 %collective-permute-done.3 = bf16[2,128,256]{2,1,0:T(8,128)(2,1)S(1)} collective-permute-done((bf16[2,128,256]{2,1,0:T(8,128)(2,1)S(1)}, bf16[2,128,256]{2,1,0:T(8,128)(2,1)S(1)}, u32[]{:S(2)}, u32[]{:S(2)}) %collective-permute-start.3) | collective-permute-done | bytes 131104 | tf_op jit(solution)/shard_map/ppermute | solution.py:26
  48.1 2.2 %all-to-all-done.refs_0_.refs_1_ = bf16[8,128,512]{2,1,0:T(8,128)(2,1)S(1)} async-done(((bf16[8,128,512]{2,1,0:T(8,128)(2,1)}), bf16[8,128,512]{2,1,0:T(8,128)(2,1)S(1)}, u32[]{:S(2)}, u32[]{:S(2)}) %all-to-all-start) | async-done | bytes 1048608 | tf_op jit(solution)/shard_map/all_to_all | solution.py:539
  50.3 1.4 collective-permute-start.4
  52.0 6.1 %collective-permute-start.5 = (bf16[2,128,256]{2,1,0:T(8,128)(2,1)S(1)}, bf16[2,128,256]{2,1,0:T(8,128)(2,1)S(1)}, u32[]{:S(2)}, u32[]{:S(2)}) collective-permute-start(bf16[2,128,256]{2,1,0:T(8,128)(2,1)S(1)} %pad_maximum_fusion.3), channel_id=1, source_target_pairs={{0,64},{8,72},{16,80},{24,88},{32,96},{40,104},{48,112},{56,120},{... | collective-permute-start | bytes 393224 | tf_op jit(solution)/shard_map/ppermute | solution.py:26
  58.3 7.6 %collective-permute-done.5 = bf16[2,128,256]{2,1,0:T(8,128)(2,1)S(1)} collective-permute-done((bf16[2,128,256]{2,1,0:T(8,128)(2,1)S(1)}, bf16[2,128,256]{2,1,0:T(8,128)(2,1)S(1)}, u32[]{:S(2)}, u32[]{:S(2)}) %collective-permute-start.5) | collective-permute-done | bytes 131104 | tf_op jit(solution)/shard_map/ppermute | solution.py:26
  67.2 2.9 %all-gather.3.cloned.1.call-done = bf16[16,128,512]{2,1,0:T(8,128)(2,1)} async-done(((bf16[2,128,512]{2,1,0:T(8,128)(2,1)}), bf16[16,128,512]{2,1,0:T(8,128)(2,1)}) %all-gather.3.cloned.1.call-update) | async-done | bytes 2097168 | tf_op jit(solution)/shard_map/all_gather | solution.py:538
  70.8 4.1 %collective-permute-start.6 = (bf16[2,128,128]{2,1,0:T(8,128)(2,1)}, bf16[2,128,128]{2,1,0:T(8,128)(2,1)}, u32[]{:S(2)}, u32[]{:S(2)}) collective-permute-start(bf16[2,128,128]{2,1,0:T(8,128)(2,1)} %slice.142), channel_id=1, source_target_pairs={{0,128},{8,136},{16,144},{24,152},{32,160},{40,168},{48,176},{56,1... | collective-permute-start | bytes 196616 | tf_op jit(solution)/shard_map/ppermute | solution.py:21
  75.8 5.2 %shard_map.111 = (f32[128,512]{1,0:T(8,128)}, f32[128,512]{1,0:T(8,128)}) custom-call(s32[2]{0:T(128)} %pad_add_fusion.refs_0_.place, bf16[8,128,512]{2,1,0:T(8,128)(2,1)} %copy-done, bf16[8,128,512]{2,1,0:T(8,128)(2,1)} %copy-done, bf16[8,128,512]{2,1,0:T(8,128)(2,1)} %copy-done.1, bf16[8,128,512]{2,1,0:T(8,128)(2,1)} %copy-done.1, ...), custom_call_target="tpu_custom_call" | custom-call | flops 536870912 | bytes 5242880 | tf_op jit(solution)/shard_map/pallas_call | solution.py:344
  81.0 3.0 %collective-permute-start.8 = (f32[128,512]{1,0:T(8,128)}, f32[128,512]{1,0:T(8,128)S(1)}, u32[]{:S(2)}, u32[]{:S(2)}) collective-permute-start(f32[128,512]{1,0:T(8,128)} %get-tuple-element.70), channel_id=1, source_target_pairs={{0,8},{8,0},{16,24},{24,16},{32,40},{40,32},{48,56},{56,48},{64,72... | collective-permute-start | bytes 786440 | tf_op jit(solution)/shard_map/ppermute | solution.py:26
  84.0 1.3 fusion.9
  85.6 1.2 collective-permute-done.7
  88.2 3.4 %shard_map.112 = (bf16[128,512]{1,0:T(8,128)(2,1)}, f32[128,512]{1,0:T(8,128)}, bf16[2,128,128]{2,1,0:T(8,128)(2,1)}, bf16[2,128,128]{2,1,0:T(8,128)(2,1)}) custom-call(s32[2]{0:T(128)} %pad_add_fusion.refs_0_.place, f32[4,128,128]{2,1,0:T(8,128)} %get-tuple-element.57.qt_ref, f32[4,128,128]{2,1,0:T(8,128)} %get-tuple-element.58.local_ref, ...), custom_call_target="tpu_custom_call" | custom-call | flops 33554432 | bytes 2097152 | tf_op jit(solution)/shard_map/pallas_call | solution.py:261
  91.8 1.4 collective-permute-done.9.heads_other_ref.refs_5_
  93.8 5.3 %shard_map.114 = bf16[8,256,512]{2,1,0:T(8,128)(2,1)} custom-call(s32[2]{0:T(128)} %pad_add_fusion.refs_0_.place, bf16[8,128,512]{2,1,0:T(8,128)(2,1)} %copy-done, bf16[8,128,512]{2,1,0:T(8,128)(2,1)} %copy-done, bf16[8,128,512]{2,1,0:T(8,128)(2,1)} %copy-done.1, bf16[8,128,512]{2,1,0:T(8,128)(2,1)} %copy-done.1, ...), custom_call_target="tpu_custom_call" | custom-call | flops 536870912 | bytes 5242880 | tf_op jit(solution)/shard_map/pallas_call | solution.py:286
  102.9 5.0 %shard_map.113 = bf16[8,256,256]{2,1,0:T(8,128)(2,1)} custom-call(s32[2]{0:T(128)} %pad_add_fusion.refs_0_.place, bf16[128,512]{1,0:T(8,128)(2,1)} %get-tuple-element.71.heads_ref.refs_4_, bf16[128,512]{1,0:T(8,128)(2,1)} %copy-done.4, bf16[8,2,128,512]{3,2,1,0:T(8,128)(2,1)} %bitcast.27), custom_call_target="tpu_custom_call" | custom-call | flops 536870912 | bytes 3145728 | tf_op jit(solution)/shard_map/pallas_call | solution.py:311
  109.1 6.8 %collective-permute-done.12 = bf16[2,128,128]{2,1,0:T(8,128)(2,1)S(1)} collective-permute-done((bf16[2,128,128]{2,1,0:T(8,128)(2,1)S(1)}, bf16[2,128,128]{2,1,0:T(8,128)(2,1)S(1)}, u32[]{:S(2)}, u32[]{:S(2)}) %collective-permute-start.12) | collective-permute-done | bytes 65568 | tf_op jit(solution)/shard_map/ppermute | solution.py:26
  116.1 1.5 collective-permute-start.13
  117.7 4.0 %all-to-all-start.1 = ((bf16[8,256,256]{2,1,0:T(8,128)(2,1)}), bf16[8,256,256]{2,1,0:T(8,128)(2,1)S(1)}, u32[]{:S(2)}, u32[]{:S(2)}) async-start(bf16[8,256,256]{2,1,0:T(8,128)(2,1)} %shard_map.113), calls=%async_computation.1 | async-start | bytes 2097152 | tf_op jit(solution)/shard_map/all_to_all | solution.py:554
  121.7 4.3 %collective-permute-done.13 = bf16[2,128,128]{2,1,0:T(8,128)(2,1)S(1)} collective-permute-done((bf16[2,128,128]{2,1,0:T(8,128)(2,1)S(1)}, bf16[2,128,128]{2,1,0:T(8,128)(2,1)S(1)}, u32[]{:S(2)}, u32[]{:S(2)}) %collective-permute-start.13) | collective-permute-done | bytes 65568 | tf_op jit(solution)/shard_map/ppermute | solution.py:26
  126.2 1.3 collective-permute-start.14
  127.8 5.3 %collective-permute-done.14 = bf16[2,128,128]{2,1,0:T(8,128)(2,1)S(1)} collective-permute-done((bf16[2,128,128]{2,1,0:T(8,128)(2,1)S(1)}, bf16[2,128,128]{2,1,0:T(8,128)(2,1)S(1)}, u32[]{:S(2)}, u32[]{:S(2)}) %collective-permute-start.14) | collective-permute-done | bytes 65568 | tf_op jit(solution)/shard_map/ppermute | solution.py:21
  133.9 3.8 %reduce-scatter.2.cloned.1.call-done = bf16[1,256,512]{2,1,0:T(8,128)(2,1)} async-done(((bf16[8,256,512]{2,1,0:T(8,128)(2,1)}), bf16[1,256,512]{2,1,0:T(8,128)(2,1)}) %reduce-scatter.2.cloned.1.call-update) | async-done | bytes 262160 | tf_op jit(solution)/shard_map/reduce_scatter | solution.py:548
  137.7 3.8 %collective-permute-start.16 = (bf16[2,128,128]{2,1,0:T(8,128)(2,1)S(1)}, bf16[2,128,128]{2,1,0:T(8,128)(2,1)S(1)}, u32[]{:S(2)}, u32[]{:S(2)}) collective-permute-start(bf16[2,128,128]{2,1,0:T(8,128)(2,1)S(1)} %get-tuple-element.79), channel_id=1, source_target_pairs={{0,8},{8,0},{16,24},{24,16},{32,40},{40,32},{48,56},{56,48},{64,72... | collective-permute-start | bytes 196616 | tf_op jit(solution)/shard_map/ppermute | solution.py:26
  142.4 1.5 collective-permute-start.15
  144.6 6.3 %shard_map.115 = (bf16[128,512]{1,0:T(8,128)(2,1)}, bf16[128,1024]{1,0:T(8,128)(2,1)}, bf16[128,1024]{1,0:T(8,128)(2,1)}, f32[4,256]{1,0:T(4,128)}) custom-call(s32[2]{0:T(128)} %pad_add_fusion.refs_0_.place, bf16[128,512]{1,0:T(8,128)(2,1)} %q_ref.1, bf16[128,1024]{1,0:T(8,128)(2,1)} %k_ref.1, f32[4,256]{1,0:T(4,128)} %logit_ref.1, ...), custom_call_target="tpu_custom_call" | custom-call | flops 1879048192 | bytes 5242880 | tf_op jit(solution)/shard_map/pallas_call | solution.py:416
  (99 shorter events, 20.2 us)
Async XLA Ops:
  7.2 63.0 %all-gather.3.cloned.1.call-start = ((), (), s32[]{:S(2)}) async-start(), calls=%async_computation.4 | async-start | bytes 2359296 | tf_op jit(solution)/shard_map/all_gather | solution.py:538
  7.2 10.5 %collective-permute-start = (bf16[128,512]{1,0:T(8,128)(2,1)}, bf16[128,512]{1,0:T(8,128)(2,1)S(1)}, u32[]{:S(2)}, u32[]{:S(2)}) collective-permute-start(bf16[128,512]{1,0:T(8,128)(2,1)} %param.10), channel_id=1, source_target_pairs={{0,128},{8,136},{16,144},{24,152},{32,160},{40,168},{48,176},{56,1... | collective-permute-start | bytes 393224 | tf_op jit(solution)/shard_map/ppermute | solution.py:26
  17.8 9.1 %collective-permute-start.1 = (bf16[2,128,256]{2,1,0:T(8,128)(2,1)}, bf16[2,128,256]{2,1,0:T(8,128)(2,1)S(1)}, u32[]{:S(2)}, u32[]{:S(2)}) collective-permute-start(bf16[2,128,256]{2,1,0:T(8,128)(2,1)} %get-tuple-element.59), channel_id=1, source_target_pairs={{0,8},{8,0},{16,24},{24,16},{32,40},{40,32},{48,56},{56,48},{64,72... | collective-permute-start | bytes 393224 | tf_op jit(solution)/shard_map/ppermute | solution.py:26
  20.4 9.4 %copy-start.9 = (bf16[128,512]{1,0:T(8,128)(2,1)S(1)}, bf16[128,512]{1,0:T(8,128)(2,1)}, u32[]{:S(2)}) copy-start(bf16[128,512]{1,0:T(8,128)(2,1)} %param.11) | copy-start | bytes 393220
  27.7 3.0 %copy-start.2 = (bf16[2,128,256]{2,1,0:T(8,128)(2,1)}, bf16[2,128,256]{2,1,0:T(8,128)(2,1)S(1)}, u32[]{:S(2)}) copy-start(bf16[2,128,256]{2,1,0:T(8,128)(2,1)S(1)} %get-tuple-element.94) | copy-start | bytes 393220
  28.0 7.1 %collective-permute-start.2 = (bf16[2,128,256]{2,1,0:T(8,128)(2,1)S(1)}, bf16[2,128,256]{2,1,0:T(8,128)(2,1)S(1)}, u32[]{:S(2)}, u32[]{:S(2)}) collective-permute-start(bf16[2,128,256]{2,1,0:T(8,128)(2,1)S(1)} %pad_maximum_fusion.1), channel_id=1, source_target_pairs={{0,16},{8,24},{16,0},{24,8},{32,48},{40,56},{48,32},{56,40},{64,80... | collective-permute-start | bytes 393224 | tf_op jit(solution)/shard_map/ppermute | solution.py:26
  30.8 19.5 %all-to-all-start = ((bf16[8,128,512]{2,1,0:T(8,128)(2,1)}), bf16[8,128,512]{2,1,0:T(8,128)(2,1)S(1)}, u32[]{:S(2)}, u32[]{:S(2)}) async-start(bf16[8,128,512]{2,1,0:T(8,128)(2,1)} %broadcast_in_dim.21), calls=%async_computation | async-start | bytes 2097152 | tf_op jit(solution)/shard_map/all_to_all | solution.py:539
  35.0 102.7 %reduce-scatter.2.cloned.1.call-start = ((), (), s32[]{:S(2)}) async-start(), calls=%async_computation.3 | async-start | bytes 2359296 | tf_op jit(solution)/shard_map/reduce_scatter | solution.py:548
  35.4 12.7 %collective-permute-start.3 = (bf16[2,128,256]{2,1,0:T(8,128)(2,1)S(1)}, bf16[2,128,256]{2,1,0:T(8,128)(2,1)S(1)}, u32[]{:S(2)}, u32[]{:S(2)}) collective-permute-start(bf16[2,128,256]{2,1,0:T(8,128)(2,1)S(1)} %pad_maximum_fusion.2), channel_id=1, source_target_pairs={{0,32},{8,40},{16,48},{24,56},{32,0},{40,8},{48,16},{56,24},{64,96... | collective-permute-start | bytes 393224 | tf_op jit(solution)/shard_map/ppermute | solution.py:26
  50.3 25.5 %copy-start = (bf16[8,128,512]{2,1,0:T(8,128)(2,1)}, bf16[8,128,512]{2,1,0:T(8,128)(2,1)S(1)}, u32[]{:S(2)}) copy-start(bf16[8,128,512]{2,1,0:T(8,128)(2,1)S(1)} %all-to-all-done.refs_0_.refs_1_) | copy-start | bytes 3145732
  50.3 15.7 %collective-permute-start.4 = (bf16[8,128,512]{2,1,0:T(8,128)(2,1)S(1)}, bf16[8,128,512]{2,1,0:T(8,128)(2,1)S(1)}, u32[]{:S(2)}, u32[]{:S(2)}) collective-permute-start(bf16[8,128,512]{2,1,0:T(8,128)(2,1)S(1)} %all-to-all-done.refs_0_.refs_1_), channel_id=1, source_target_pairs={{0,8},{8,0},{16,24},{24,16},{32,40},{40,32},{48,56},{56,48},{64,72... | collective-permute-start | bytes 3145736 | tf_op jit(solution)/shard_map/ppermute | solution.py:26
  52.0 14.0 %collective-permute-start.5 = (bf16[2,128,256]{2,1,0:T(8,128)(2,1)S(1)}, bf16[2,128,256]{2,1,0:T(8,128)(2,1)S(1)}, u32[]{:S(2)}, u32[]{:S(2)}) collective-permute-start(bf16[2,128,256]{2,1,0:T(8,128)(2,1)S(1)} %pad_maximum_fusion.3), channel_id=1, source_target_pairs={{0,64},{8,72},{16,80},{24,88},{32,96},{40,104},{48,112},{56,120},{... | collective-permute-start | bytes 393224 | tf_op jit(solution)/shard_map/ppermute | solution.py:26
  58.2 7.7 %copy-start.5 = (f32[2,128,256]{2,1,0:T(8,128)}, f32[2,128,256]{2,1,0:T(8,128)S(1)}, u32[]{:S(2)}) copy-start(f32[2,128,256]{2,1,0:T(8,128)S(1)} %fusion.61) | copy-start | bytes 786436
  58.3 16.6 %copy-start.6 = (bf16[2,128,128]{2,1,0:T(8,128)(2,1)}, bf16[2,128,128]{2,1,0:T(8,128)(2,1)S(1)}, u32[]{:S(2)}) copy-start(bf16[2,128,128]{2,1,0:T(8,128)(2,1)S(1)} %fusion.14) | copy-start | bytes 196612
  70.8 10.2 %collective-permute-start.6 = (bf16[2,128,128]{2,1,0:T(8,128)(2,1)}, bf16[2,128,128]{2,1,0:T(8,128)(2,1)}, u32[]{:S(2)}, u32[]{:S(2)}) collective-permute-start(bf16[2,128,128]{2,1,0:T(8,128)(2,1)} %slice.142), channel_id=1, source_target_pairs={{0,128},{8,136},{16,144},{24,152},{32,160},{40,168},{48,176},{56,1... | collective-permute-start | bytes 196616 | tf_op jit(solution)/shard_map/ppermute | solution.py:21
  81.0 6.5 %collective-permute-start.8 = (f32[128,512]{1,0:T(8,128)}, f32[128,512]{1,0:T(8,128)S(1)}, u32[]{:S(2)}, u32[]{:S(2)}) collective-permute-start(f32[128,512]{1,0:T(8,128)} %get-tuple-element.70), channel_id=1, source_target_pairs={{0,8},{8,0},{16,24},{24,16},{32,40},{40,32},{48,56},{56,48},{64,72... | collective-permute-start | bytes 786440 | tf_op jit(solution)/shard_map/ppermute | solution.py:26
  85.5 1.3 collective-permute-start.7
  91.6 1.6 collective-permute-start.9
  99.1 2.1 %copy-start.10 = (bf16[2,128,128]{2,1,0:T(8,128)(2,1)S(1)}, bf16[2,128,128]{2,1,0:T(8,128)(2,1)}, u32[]{:S(2)}) copy-start(bf16[2,128,128]{2,1,0:T(8,128)(2,1)} %get-tuple-element.72) | copy-start | bytes 196612
  100.0 1.3 collective-permute-start.10
  101.9 6.0 %collective-permute-start.11 = (bf16[2,128,128]{2,1,0:T(8,128)(2,1)S(1)}, bf16[2,128,128]{2,1,0:T(8,128)(2,1)S(1)}, u32[]{:S(2)}, u32[]{:S(2)}) collective-permute-start(bf16[2,128,128]{2,1,0:T(8,128)(2,1)S(1)} %add_convert_fusion.4), channel_id=1, source_target_pairs={{0,16},{8,24},{16,0},{24,8},{32,48},{40,56},{48,32},{56,40},{64,80... | collective-permute-start | bytes 196616 | tf_op jit(solution)/shard_map/ppermute | solution.py:26
  108.0 25.6 %copy-start.3 = (bf16[2,128,256]{2,1,0:T(8,128)(2,1)S(1)}, bf16[2,128,256]{2,1,0:T(8,128)(2,1)}, u32[]{:S(2)}) copy-start(bf16[2,128,256]{2,1,0:T(8,128)(2,1)} %copy-done.2) | copy-start | bytes 393220
  108.0 25.6 %copy-start.11 = (bf16[2,128,128]{2,1,0:T(8,128)(2,1)S(1)}, bf16[2,128,128]{2,1,0:T(8,128)(2,1)}, u32[]{:S(2)}) copy-start(bf16[2,128,128]{2,1,0:T(8,128)(2,1)} %get-tuple-element.72) | copy-start | bytes 196612
  108.1 25.6 %copy-start.13 = (bf16[2,128,128]{2,1,0:T(8,128)(2,1)S(1)}, bf16[2,128,128]{2,1,0:T(8,128)(2,1)}, u32[]{:S(2)}) copy-start(bf16[2,128,128]{2,1,0:T(8,128)(2,1)} %copy-done.12) | copy-start | bytes 196612
  108.1 7.8 %collective-permute-start.12 = (bf16[2,128,128]{2,1,0:T(8,128)(2,1)S(1)}, bf16[2,128,128]{2,1,0:T(8,128)(2,1)S(1)}, u32[]{:S(2)}, u32[]{:S(2)}) collective-permute-start(bf16[2,128,128]{2,1,0:T(8,128)(2,1)S(1)} %add_convert_fusion.3), channel_id=1, source_target_pairs={{0,32},{8,40},{16,48},{24,56},{32,0},{40,8},{48,16},{56,24},{64,96... | collective-permute-start | bytes 196616 | tf_op jit(solution)/shard_map/ppermute | solution.py:26
  116.1 9.9 %collective-permute-start.13 = (bf16[2,128,128]{2,1,0:T(8,128)(2,1)S(1)}, bf16[2,128,128]{2,1,0:T(8,128)(2,1)S(1)}, u32[]{:S(2)}, u32[]{:S(2)}) collective-permute-start(bf16[2,128,128]{2,1,0:T(8,128)(2,1)S(1)} %add_convert_fusion.2), channel_id=1, source_target_pairs={{0,64},{8,72},{16,80},{24,88},{32,96},{40,104},{48,112},{56,120},{... | collective-permute-start | bytes 196616 | tf_op jit(solution)/shard_map/ppermute | solution.py:26
  117.7 33.2 %all-to-all-start.1 = ((bf16[8,256,256]{2,1,0:T(8,128)(2,1)}), bf16[8,256,256]{2,1,0:T(8,128)(2,1)S(1)}, u32[]{:S(2)}, u32[]{:S(2)}) async-start(bf16[8,256,256]{2,1,0:T(8,128)(2,1)} %shard_map.113), calls=%async_computation.1 | async-start | bytes 2097152 | tf_op jit(solution)/shard_map/all_to_all | solution.py:554
  126.2 6.8 %collective-permute-start.14 = (bf16[2,128,128]{2,1,0:T(8,128)(2,1)S(1)}, bf16[2,128,128]{2,1,0:T(8,128)(2,1)S(1)}, u32[]{:S(2)}, u32[]{:S(2)}) collective-permute-start(bf16[2,128,128]{2,1,0:T(8,128)(2,1)S(1)} %add_convert_fusion.1), channel_id=1, source_target_pairs={{128,0},{136,8},{144,16},{152,24},{160,32},{168,40},{176,48},{184,... | collective-permute-start | bytes 196616 | tf_op jit(solution)/shard_map/ppermute | solution.py:21
  137.7 6.2 %collective-permute-start.16 = (bf16[2,128,128]{2,1,0:T(8,128)(2,1)S(1)}, bf16[2,128,128]{2,1,0:T(8,128)(2,1)S(1)}, u32[]{:S(2)}, u32[]{:S(2)}) collective-permute-start(bf16[2,128,128]{2,1,0:T(8,128)(2,1)S(1)} %get-tuple-element.79), channel_id=1, source_target_pairs={{0,8},{8,0},{16,24},{24,16},{32,40},{40,32},{48,56},{56,48},{64,72... | collective-permute-start | bytes 196616 | tf_op jit(solution)/shard_map/ppermute | solution.py:26
  142.4 8.5 %collective-permute-start.15 = (bf16[128,512]{1,0:T(8,128)(2,1)S(1)}, bf16[128,512]{1,0:T(8,128)(2,1)S(1)}, u32[]{:S(2)}, u32[]{:S(2)}) collective-permute-start(bf16[128,512]{1,0:T(8,128)(2,1)S(1)} %slice_bitcast_fusion), channel_id=1, source_target_pairs={{0,128},{8,136},{16,144},{24,152},{32,160},{40,168},{48,176},{56,1... | collective-permute-start | bytes 393224 | tf_op jit(solution)/shard_map/ppermute | solution.py:26
  144.6 6.8 %copy-start.7 = (bf16[1,256,512]{2,1,0:T(8,128)(2,1)S(1)}, bf16[1,256,512]{2,1,0:T(8,128)(2,1)}, u32[]{:S(2)}) copy-start(bf16[1,256,512]{2,1,0:T(8,128)(2,1)} %reduce-scatter.2.cloned.1.call-done) | copy-start | bytes 786436
  151.1 1.3 collective-permute-start.17
  (5 other events, 3.8 us)
Sparse Core Ops, SparseCore 0:
  20.5 49.5 all-gather.2
  99.3 38.3 reduce-scatter.1

commit v14 on v13

--- a/solution.py
+++ b/solution.py
@@ -519,8 +519,9 @@
     first = (odd.astype(F32) + mul_t(odd_a, second)).astype(BF16)
     kept = jnp.where(core == 0, first, second)
     given = jnp.where(core == 0, second, first)
-    last, given = lax.optimization_barrier((last, given))
-    return gate, last, jnp.concatenate([kept, exchange(given, 1)], axis=0)
+    end = jnp.concatenate([kept, exchange(given, 1)], axis=0)
+    last, end = lax.optimization_barrier((last, end))
+    return gate, last, end
 
 
 def local(queries, keys, values, beta_logit, out_weight, out_grad):

time: 161 us -> 160 us (level)
  waiting for transfers between devices: 46.5 us -> 43.5 us
  starting transfers between devices: 43.3 us -> 45.6 us
    reduce_scatter x1, waiting for transfers between devices: 3.82 us -> 0.01 us  [local(): lax.psum_scatter(terms, 'ctx', scatter_dimension=0, axis_index_groups=rings)]
    ppermute x16, starting transfers between devices: 29.6 us -> 31.9 us  [exchange(): return lax.ppermute(block, 'ctx', route)]
where the time goes in v14:
time: 160 us; the launch traced here: 159 us
  starting transfers between devices  45.6 us (28%)
  waiting for transfers between devices  43.5 us (27%)
  Pallas kernels  37.9 us (24%)
  between operations  14.4 us (9%)
  other arithmetic  6.41 us (4%)
  local copies, waits for them, and re-layouts  6.28 us (4%)
  matrix products  5.19 us (3%)
    ppermute x16, waiting for transfers between devices, exchange(): return lax.ppermute(block, 'ctx', route)  33.1 us
    ppermute x16, starting transfers between devices, exchange(): return lax.ppermute(block, 'ctx', route)  31.9 us
    pallas_call x2, Pallas kernels, prepare(): pl.pallas_call(functools.partial(prepare_kernel, mine), grid_spec=pltpu.P...  12.7 us
    pallas_call x1, Pallas kernels, pull(): call(pull_kernel, 2, [by_columns(WIDTH), by_columns(PAIRS), whole(4, PAIR...  6.28 us
    ppermute x2, starting transfers between devices, send(): return lax.ppermute(block, 'ctx', route)  5.43 us
    pallas_call x1, Pallas kernels, weight_terms(): call(weight_terms_kernel, STEPS, grad_specs() + [whole(WIDTH, 512), whole...  5.29 us
    ppermute x2, waiting for transfers between devices, send(): return lax.ppermute(block, 'ctx', route)  5.29 us
    pallas_call x1, Pallas kernels, head_gradient(): call(head_grad_kernel, STEPS, grad_specs() + [weight_tile()], [whole(WIDT...  5.21 us
  transfers between devices with their start and end apart: 22, of which 12 were waited for; matrix products, arithmetic and copies ran while one was open for 8% of the time, Pallas kernels for 18%

profile of v14, /device:TPU:1, one launch (start us, length us, event | category | flops | bytes accessed | tf_op | source)
XLA Modules:
  0.0 159.3 jit_solution(15009145256675609781)
XLA Ops:
  7.2 3.7 %collective-permute-start = (bf16[128,512]{1,0:T(8,128)(2,1)}, bf16[128,512]{1,0:T(8,128)(2,1)S(1)}, u32[]{:S(2)}, u32[]{:S(2)}) collective-permute-start(bf16[128,512]{1,0:T(8,128)(2,1)} %param.10), channel_id=1, source_target_pairs={{0,128},{8,136},{16,144},{24,152},{32,160},{40,168},{48,176},{56,1... | collective-permute-start | bytes 393224 | tf_op jit(solution)/shard_map/ppermute | solution.py:26
  11.5 6.3 %shard_map.109 = (bf16[2,128,256]{2,1,0:T(8,128)(2,1)}, f32[4,256,256]{2,1,0:T(8,128)}, f32[4,256,256]{2,1,0:T(8,128)}, f32[4,128,128]{2,1,0:T(8,128)}, f32[4,128,128]{2,1,0:T(8,128)}) custom-call(s32[2]{0:T(128)} %pad_add_fusion.refs_0_.place, bf16[128,512]{1,0:T(8,128)(2,1)} %q_ref.1, bf16[128,1024]{1,0:T(8,128)(2,1)} %k_ref.1, bf16[128,1024]{1,0:T(8,128)(2,1)} %refs_3_.2, ...), custom_call_target="tpu_custom_call" | custom-call | flops 104857600 | bytes 16777216 | tf_op jit(solution)/shard_map/pallas_call | solution.py:172
  18.7 1.6 %pad_maximum_fusion = bf16[2,128,512]{2,1,0:T(8,128)(2,1)} fusion(bf16[1,128,512]{2,1,0:T(8,128)(2,1)S(1)} %bitcast.31, bf16[1,128,512]{2,1,0:T(8,128)(2,1)} %bitcast.30), kind=kLoop, calls=%fused_computation.13 | loop fusion | flops 131072 | bytes 524288 | tf_op jit(solution)/shard_map/stack | solution.py:536
  20.4 6.4 %shard_map.110 = (bf16[2,128,256]{2,1,0:T(8,128)(2,1)}, f32[4,256,256]{2,1,0:T(8,128)}, f32[4,256,256]{2,1,0:T(8,128)}, f32[4,128,128]{2,1,0:T(8,128)}, f32[4,128,128]{2,1,0:T(8,128)}) custom-call(s32[2]{0:T(128)} %pad_add_fusion.refs_0_.place, bf16[128,512]{1,0:T(8,128)(2,1)} %q_ref.1, ...), custom_call_target="tpu_custom_call", output_to_operand_aliasing={{1}: (5, {}), {2}: (6, {}), {3}: (7, {}), {4}: (8, {})} | custom-call | flops 1048576 | bytes 65536 | tf_op jit(solution)/shard_map/pallas_call | solution.py:172
  28.0 1.7 %collective-permute-start.2 = (bf16[2,128,256]{2,1,0:T(8,128)(2,1)S(1)}, bf16[2,128,256]{2,1,0:T(8,128)(2,1)S(1)}, u32[]{:S(2)}, u32[]{:S(2)}) collective-permute-start(bf16[2,128,256]{2,1,0:T(8,128)(2,1)S(1)} %pad_maximum_fusion.1), channel_id=1, source_target_pairs={{0,16},{8,24},{16,0},{24,8},{32,48},{40,56},{48,32},{56,40},{64,80... | collective-permute-start | bytes 393224 | tf_op jit(solution)/shard_map/ppermute | solution.py:26
  30.8 4.2 %all-to-all-start = ((bf16[8,128,512]{2,1,0:T(8,128)(2,1)}), bf16[8,128,512]{2,1,0:T(8,128)(2,1)S(1)}, u32[]{:S(2)}, u32[]{:S(2)}) async-start(bf16[8,128,512]{2,1,0:T(8,128)(2,1)} %broadcast_in_dim.21), calls=%async_computation | async-start | bytes 2097152 | tf_op jit(solution)/shard_map/all_to_all | solution.py:540
  35.4 3.1 %collective-permute-start.3 = (bf16[2,128,256]{2,1,0:T(8,128)(2,1)S(1)}, bf16[2,128,256]{2,1,0:T(8,128)(2,1)S(1)}, u32[]{:S(2)}, u32[]{:S(2)}) collective-permute-start(bf16[2,128,256]{2,1,0:T(8,128)(2,1)S(1)} %pad_maximum_fusion.2), channel_id=1, source_target_pairs={{0,32},{8,40},{16,48},{24,56},{32,0},{40,8},{48,16},{56,24},{64,96... | collective-permute-start | bytes 393224 | tf_op jit(solution)/shard_map/ppermute | solution.py:26
  38.5 9.6 %collective-permute-done.3 = bf16[2,128,256]{2,1,0:T(8,128)(2,1)S(1)} collective-permute-done((bf16[2,128,256]{2,1,0:T(8,128)(2,1)S(1)}, bf16[2,128,256]{2,1,0:T(8,128)(2,1)S(1)}, u32[]{:S(2)}, u32[]{:S(2)}) %collective-permute-start.3) | collective-permute-done | bytes 131104 | tf_op jit(solution)/shard_map/ppermute | solution.py:26
  48.1 2.2 %all-to-all-done.refs_0_.refs_1_ = bf16[8,128,512]{2,1,0:T(8,128)(2,1)S(1)} async-done(((bf16[8,128,512]{2,1,0:T(8,128)(2,1)}), bf16[8,128,512]{2,1,0:T(8,128)(2,1)S(1)}, u32[]{:S(2)}, u32[]{:S(2)}) %all-to-all-start) | async-done | bytes 1048608 | tf_op jit(solution)/shard_map/all_to_all | solution.py:540
  50.3 1.4 collective-permute-start.4
  52.0 6.1 %collective-permute-start.5 = (bf16[2,128,256]{2,1,0:T(8,128)(2,1)S(1)}, bf16[2,128,256]{2,1,0:T(8,128)(2,1)S(1)}, u32[]{:S(2)}, u32[]{:S(2)}) collective-permute-start(bf16[2,128,256]{2,1,0:T(8,128)(2,1)S(1)} %pad_maximum_fusion.3), channel_id=1, source_target_pairs={{0,64},{8,72},{16,80},{24,88},{32,96},{40,104},{48,112},{56,120},{... | collective-permute-start | bytes 393224 | tf_op jit(solution)/shard_map/ppermute | solution.py:26
  58.3 7.6 %collective-permute-done.5 = bf16[2,128,256]{2,1,0:T(8,128)(2,1)S(1)} collective-permute-done((bf16[2,128,256]{2,1,0:T(8,128)(2,1)S(1)}, bf16[2,128,256]{2,1,0:T(8,128)(2,1)S(1)}, u32[]{:S(2)}, u32[]{:S(2)}) %collective-permute-start.5) | collective-permute-done | bytes 131104 | tf_op jit(solution)/shard_map/ppermute | solution.py:26
  67.2 2.9 %all-gather.3.cloned.1.call-done = bf16[16,128,512]{2,1,0:T(8,128)(2,1)} async-done(((bf16[2,128,512]{2,1,0:T(8,128)(2,1)}), bf16[16,128,512]{2,1,0:T(8,128)(2,1)}) %all-gather.3.cloned.1.call-update) | async-done | bytes 2097168 | tf_op jit(solution)/shard_map/all_gather | solution.py:539
  70.8 4.1 %collective-permute-start.6 = (bf16[2,128,128]{2,1,0:T(8,128)(2,1)}, bf16[2,128,128]{2,1,0:T(8,128)(2,1)}, u32[]{:S(2)}, u32[]{:S(2)}) collective-permute-start(bf16[2,128,128]{2,1,0:T(8,128)(2,1)} %slice.142), channel_id=1, source_target_pairs={{0,128},{8,136},{16,144},{24,152},{32,160},{40,168},{48,176},{56,1... | collective-permute-start | bytes 196616 | tf_op jit(solution)/shard_map/ppermute | solution.py:21
  75.8 5.2 %shard_map.111 = (f32[128,512]{1,0:T(8,128)}, f32[128,512]{1,0:T(8,128)}) custom-call(s32[2]{0:T(128)} %pad_add_fusion.refs_0_.place, bf16[8,128,512]{2,1,0:T(8,128)(2,1)} %copy-done, bf16[8,128,512]{2,1,0:T(8,128)(2,1)} %copy-done, bf16[8,128,512]{2,1,0:T(8,128)(2,1)} %copy-done.1, bf16[8,128,512]{2,1,0:T(8,128)(2,1)} %copy-done.1, ...), custom_call_target="tpu_custom_call" | custom-call | flops 536870912 | bytes 5242880 | tf_op jit(solution)/shard_map/pallas_call | solution.py:344
  81.0 3.0 %collective-permute-start.8 = (f32[128,512]{1,0:T(8,128)}, f32[128,512]{1,0:T(8,128)S(1)}, u32[]{:S(2)}, u32[]{:S(2)}) collective-permute-start(f32[128,512]{1,0:T(8,128)} %get-tuple-element.70), channel_id=1, source_target_pairs={{0,8},{8,0},{16,24},{24,16},{32,40},{40,32},{48,56},{56,48},{64,72... | collective-permute-start | bytes 786440 | tf_op jit(solution)/shard_map/ppermute | solution.py:26
  84.0 1.3 fusion.9
  85.6 1.2 collective-permute-done.7
  88.2 3.4 %shard_map.112 = (bf16[128,512]{1,0:T(8,128)(2,1)}, f32[128,512]{1,0:T(8,128)}, bf16[2,128,128]{2,1,0:T(8,128)(2,1)}, bf16[2,128,128]{2,1,0:T(8,128)(2,1)}) custom-call(s32[2]{0:T(128)} %pad_add_fusion.refs_0_.place, f32[4,128,128]{2,1,0:T(8,128)} %get-tuple-element.57.qt_ref, f32[4,128,128]{2,1,0:T(8,128)} %get-tuple-element.58.local_ref, ...), custom_call_target="tpu_custom_call" | custom-call | flops 33554432 | bytes 2097152 | tf_op jit(solution)/shard_map/pallas_call | solution.py:261
  91.8 1.4 collective-permute-done.9.heads_other_ref.refs_5_
  93.8 5.3 %shard_map.114 = bf16[8,256,512]{2,1,0:T(8,128)(2,1)} custom-call(s32[2]{0:T(128)} %pad_add_fusion.refs_0_.place, bf16[8,128,512]{2,1,0:T(8,128)(2,1)} %copy-done, bf16[8,128,512]{2,1,0:T(8,128)(2,1)} %copy-done, bf16[8,128,512]{2,1,0:T(8,128)(2,1)} %copy-done.1, bf16[8,128,512]{2,1,0:T(8,128)(2,1)} %copy-done.1, ...), custom_call_target="tpu_custom_call" | custom-call | flops 536870912 | bytes 5242880 | tf_op jit(solution)/shard_map/pallas_call | solution.py:286
  100.1 1.1 collective-permute-done.10
  102.9 5.0 %shard_map.113 = bf16[8,256,256]{2,1,0:T(8,128)(2,1)} custom-call(s32[2]{0:T(128)} %pad_add_fusion.refs_0_.place, bf16[128,512]{1,0:T(8,128)(2,1)} %get-tuple-element.71.heads_ref.refs_4_, bf16[128,512]{1,0:T(8,128)(2,1)} %copy-done.4, bf16[8,2,128,512]{3,2,1,0:T(8,128)(2,1)} %bitcast.27), custom_call_target="tpu_custom_call" | custom-call | flops 536870912 | bytes 3145728 | tf_op jit(solution)/shard_map/pallas_call | solution.py:311
  109.1 6.8 %collective-permute-done.12 = bf16[2,128,128]{2,1,0:T(8,128)(2,1)S(1)} collective-permute-done((bf16[2,128,128]{2,1,0:T(8,128)(2,1)S(1)}, bf16[2,128,128]{2,1,0:T(8,128)(2,1)S(1)}, u32[]{:S(2)}, u32[]{:S(2)}) %collective-permute-start.12) | collective-permute-done | bytes 65568 | tf_op jit(solution)/shard_map/ppermute | solution.py:26
  116.1 1.5 collective-permute-start.13
  117.7 4.0 %all-to-all-start.1 = ((bf16[8,256,256]{2,1,0:T(8,128)(2,1)}), bf16[8,256,256]{2,1,0:T(8,128)(2,1)S(1)}, u32[]{:S(2)}, u32[]{:S(2)}) async-start(bf16[8,256,256]{2,1,0:T(8,128)(2,1)} %shard_map.113), calls=%async_computation.1 | async-start | bytes 2097152 | tf_op jit(solution)/shard_map/all_to_all | solution.py:555
  121.7 4.3 %collective-permute-done.13 = bf16[2,128,128]{2,1,0:T(8,128)(2,1)S(1)} collective-permute-done((bf16[2,128,128]{2,1,0:T(8,128)(2,1)S(1)}, bf16[2,128,128]{2,1,0:T(8,128)(2,1)S(1)}, u32[]{:S(2)}, u32[]{:S(2)}) %collective-permute-start.13) | collective-permute-done | bytes 65568 | tf_op jit(solution)/shard_map/ppermute | solution.py:26
  126.2 1.3 collective-permute-start.14
  127.8 5.3 %collective-permute-done.14 = bf16[2,128,128]{2,1,0:T(8,128)(2,1)S(1)} collective-permute-done((bf16[2,128,128]{2,1,0:T(8,128)(2,1)S(1)}, bf16[2,128,128]{2,1,0:T(8,128)(2,1)S(1)}, u32[]{:S(2)}, u32[]{:S(2)}) %collective-permute-start.14) | collective-permute-done | bytes 65568 | tf_op jit(solution)/shard_map/ppermute | solution.py:21
  133.9 2.6 %collective-permute-start.15 = (bf16[2,128,128]{2,1,0:T(8,128)(2,1)S(1)}, bf16[2,128,128]{2,1,0:T(8,128)(2,1)S(1)}, u32[]{:S(2)}, u32[]{:S(2)}) collective-permute-start(bf16[2,128,128]{2,1,0:T(8,128)(2,1)S(1)} %get-tuple-element.99), channel_id=1, source_target_pairs={{0,8},{8,0},{16,24},{24,16},{32,40},{40,32},{48,56},{56,48},{64,72... | collective-permute-start | bytes 196616 | tf_op jit(solution)/shard_map/ppermute | solution.py:26
  139.4 6.3 %shard_map.115 = (bf16[128,512]{1,0:T(8,128)(2,1)}, bf16[128,1024]{1,0:T(8,128)(2,1)}, bf16[128,1024]{1,0:T(8,128)(2,1)}, f32[4,256]{1,0:T(4,128)}) custom-call(s32[2]{0:T(128)} %pad_add_fusion.refs_0_.place, bf16[128,512]{1,0:T(8,128)(2,1)} %q_ref.1, bf16[128,1024]{1,0:T(8,128)(2,1)} %k_ref.1, f32[4,256]{1,0:T(4,128)} %logit_ref.1, ...), custom_call_target="tpu_custom_call" | custom-call | flops 1879048192 | bytes 5242880 | tf_op jit(solution)/shard_map/pallas_call | solution.py:416
  145.9 5.0 %collective-permute-start.17 = (bf16[128,256]{1,0:T(8,128)(2,1)S(1)}, bf16[128,256]{1,0:T(8,128)(2,1)S(1)}, u32[]{:S(2)}, u32[]{:S(2)}) collective-permute-start(bf16[128,256]{1,0:T(8,128)(2,1)S(1)} %slice.187), channel_id=1, source_target_pairs={{0,8},{8,0},{16,24},{24,16},{32,40},{40,32},{48,56},{56,48},{64,72... | collective-permute-start | bytes 196616 | tf_op jit(solution)/shard_map/ppermute | solution.py:26
  (99 shorter events, 19.9 us)
Async XLA Ops:
  7.2 63.0 %all-gather.3.cloned.1.call-start = ((), (), s32[]{:S(2)}) async-start(), calls=%async_computation.4 | async-start | bytes 2359296 | tf_op jit(solution)/shard_map/all_gather | solution.py:539
  7.2 10.5 %collective-permute-start = (bf16[128,512]{1,0:T(8,128)(2,1)}, bf16[128,512]{1,0:T(8,128)(2,1)S(1)}, u32[]{:S(2)}, u32[]{:S(2)}) collective-permute-start(bf16[128,512]{1,0:T(8,128)(2,1)} %param.10), channel_id=1, source_target_pairs={{0,128},{8,136},{16,144},{24,152},{32,160},{40,168},{48,176},{56,1... | collective-permute-start | bytes 393224 | tf_op jit(solution)/shard_map/ppermute | solution.py:26
  17.8 9.1 %collective-permute-start.1 = (bf16[2,128,256]{2,1,0:T(8,128)(2,1)}, bf16[2,128,256]{2,1,0:T(8,128)(2,1)S(1)}, u32[]{:S(2)}, u32[]{:S(2)}) collective-permute-start(bf16[2,128,256]{2,1,0:T(8,128)(2,1)} %get-tuple-element.59), channel_id=1, source_target_pairs={{0,8},{8,0},{16,24},{24,16},{32,40},{40,32},{48,56},{56,48},{64,72... | collective-permute-start | bytes 393224 | tf_op jit(solution)/shard_map/ppermute | solution.py:26
  20.4 9.4 %copy-start.9 = (bf16[128,512]{1,0:T(8,128)(2,1)S(1)}, bf16[128,512]{1,0:T(8,128)(2,1)}, u32[]{:S(2)}) copy-start(bf16[128,512]{1,0:T(8,128)(2,1)} %param.11) | copy-start | bytes 393220
  27.7 3.0 %copy-start.2 = (bf16[2,128,256]{2,1,0:T(8,128)(2,1)}, bf16[2,128,256]{2,1,0:T(8,128)(2,1)S(1)}, u32[]{:S(2)}) copy-start(bf16[2,128,256]{2,1,0:T(8,128)(2,1)S(1)} %get-tuple-element.94) | copy-start | bytes 393220
  28.0 7.1 %collective-permute-start.2 = (bf16[2,128,256]{2,1,0:T(8,128)(2,1)S(1)}, bf16[2,128,256]{2,1,0:T(8,128)(2,1)S(1)}, u32[]{:S(2)}, u32[]{:S(2)}) collective-permute-start(bf16[2,128,256]{2,1,0:T(8,128)(2,1)S(1)} %pad_maximum_fusion.1), channel_id=1, source_target_pairs={{0,16},{8,24},{16,0},{24,8},{32,48},{40,56},{48,32},{56,40},{64,80... | collective-permute-start | bytes 393224 | tf_op jit(solution)/shard_map/ppermute | solution.py:26
  30.8 19.5 %all-to-all-start = ((bf16[8,128,512]{2,1,0:T(8,128)(2,1)}), bf16[8,128,512]{2,1,0:T(8,128)(2,1)S(1)}, u32[]{:S(2)}, u32[]{:S(2)}) async-start(bf16[8,128,512]{2,1,0:T(8,128)(2,1)} %broadcast_in_dim.21), calls=%async_computation | async-start | bytes 2097152 | tf_op jit(solution)/shard_map/all_to_all | solution.py:540
  35.0 103.1 %reduce-scatter.2.cloned.1.call-start = ((), (), s32[]{:S(2)}) async-start(), calls=%async_computation.3 | async-start | bytes 2359296 | tf_op jit(solution)/shard_map/reduce_scatter | solution.py:549
  35.4 12.7 %collective-permute-start.3 = (bf16[2,128,256]{2,1,0:T(8,128)(2,1)S(1)}, bf16[2,128,256]{2,1,0:T(8,128)(2,1)S(1)}, u32[]{:S(2)}, u32[]{:S(2)}) collective-permute-start(bf16[2,128,256]{2,1,0:T(8,128)(2,1)S(1)} %pad_maximum_fusion.2), channel_id=1, source_target_pairs={{0,32},{8,40},{16,48},{24,56},{32,0},{40,8},{48,16},{56,24},{64,96... | collective-permute-start | bytes 393224 | tf_op jit(solution)/shard_map/ppermute | solution.py:26
  50.3 25.5 %copy-start = (bf16[8,128,512]{2,1,0:T(8,128)(2,1)}, bf16[8,128,512]{2,1,0:T(8,128)(2,1)S(1)}, u32[]{:S(2)}) copy-start(bf16[8,128,512]{2,1,0:T(8,128)(2,1)S(1)} %all-to-all-done.refs_0_.refs_1_) | copy-start | bytes 3145732
  50.3 15.7 %collective-permute-start.4 = (bf16[8,128,512]{2,1,0:T(8,128)(2,1)S(1)}, bf16[8,128,512]{2,1,0:T(8,128)(2,1)S(1)}, u32[]{:S(2)}, u32[]{:S(2)}) collective-permute-start(bf16[8,128,512]{2,1,0:T(8,128)(2,1)S(1)} %all-to-all-done.refs_0_.refs_1_), channel_id=1, source_target_pairs={{0,8},{8,0},{16,24},{24,16},{32,40},{40,32},{48,56},{56,48},{64,72... | collective-permute-start | bytes 3145736 | tf_op jit(solution)/shard_map/ppermute | solution.py:26
  52.0 14.0 %collective-permute-start.5 = (bf16[2,128,256]{2,1,0:T(8,128)(2,1)S(1)}, bf16[2,128,256]{2,1,0:T(8,128)(2,1)S(1)}, u32[]{:S(2)}, u32[]{:S(2)}) collective-permute-start(bf16[2,128,256]{2,1,0:T(8,128)(2,1)S(1)} %pad_maximum_fusion.3), channel_id=1, source_target_pairs={{0,64},{8,72},{16,80},{24,88},{32,96},{40,104},{48,112},{56,120},{... | collective-permute-start | bytes 393224 | tf_op jit(solution)/shard_map/ppermute | solution.py:26
  58.2 7.7 %copy-start.5 = (f32[2,128,256]{2,1,0:T(8,128)}, f32[2,128,256]{2,1,0:T(8,128)S(1)}, u32[]{:S(2)}) copy-start(f32[2,128,256]{2,1,0:T(8,128)S(1)} %fusion.61) | copy-start | bytes 786436
  58.3 16.6 %copy-start.6 = (bf16[2,128,128]{2,1,0:T(8,128)(2,1)}, bf16[2,128,128]{2,1,0:T(8,128)(2,1)S(1)}, u32[]{:S(2)}) copy-start(bf16[2,128,128]{2,1,0:T(8,128)(2,1)S(1)} %fusion.14) | copy-start | bytes 196612
  70.8 10.2 %collective-permute-start.6 = (bf16[2,128,128]{2,1,0:T(8,128)(2,1)}, bf16[2,128,128]{2,1,0:T(8,128)(2,1)}, u32[]{:S(2)}, u32[]{:S(2)}) collective-permute-start(bf16[2,128,128]{2,1,0:T(8,128)(2,1)} %slice.142), channel_id=1, source_target_pairs={{0,128},{8,136},{16,144},{24,152},{32,160},{40,168},{48,176},{56,1... | collective-permute-start | bytes 196616 | tf_op jit(solution)/shard_map/ppermute | solution.py:21
  81.0 6.5 %collective-permute-start.8 = (f32[128,512]{1,0:T(8,128)}, f32[128,512]{1,0:T(8,128)S(1)}, u32[]{:S(2)}, u32[]{:S(2)}) collective-permute-start(f32[128,512]{1,0:T(8,128)} %get-tuple-element.70), channel_id=1, source_target_pairs={{0,8},{8,0},{16,24},{24,16},{32,40},{40,32},{48,56},{56,48},{64,72... | collective-permute-start | bytes 786440 | tf_op jit(solution)/shard_map/ppermute | solution.py:26
  85.5 1.3 collective-permute-start.7
  91.6 1.6 collective-permute-start.9
  99.1 2.1 %copy-start.10 = (bf16[2,128,128]{2,1,0:T(8,128)(2,1)S(1)}, bf16[2,128,128]{2,1,0:T(8,128)(2,1)}, u32[]{:S(2)}) copy-start(bf16[2,128,128]{2,1,0:T(8,128)(2,1)} %get-tuple-element.72) | copy-start | bytes 196612
  100.0 1.3 collective-permute-start.10
  101.9 6.0 %collective-permute-start.11 = (bf16[2,128,128]{2,1,0:T(8,128)(2,1)S(1)}, bf16[2,128,128]{2,1,0:T(8,128)(2,1)S(1)}, u32[]{:S(2)}, u32[]{:S(2)}) collective-permute-start(bf16[2,128,128]{2,1,0:T(8,128)(2,1)S(1)} %add_convert_fusion.4), channel_id=1, source_target_pairs={{0,16},{8,24},{16,0},{24,8},{32,48},{40,56},{48,32},{56,40},{64,80... | collective-permute-start | bytes 196616 | tf_op jit(solution)/shard_map/ppermute | solution.py:26
  108.0 25.6 %copy-start.3 = (bf16[2,128,256]{2,1,0:T(8,128)(2,1)S(1)}, bf16[2,128,256]{2,1,0:T(8,128)(2,1)}, u32[]{:S(2)}) copy-start(bf16[2,128,256]{2,1,0:T(8,128)(2,1)} %copy-done.2) | copy-start | bytes 393220
  108.0 25.6 %copy-start.11 = (bf16[2,128,128]{2,1,0:T(8,128)(2,1)S(1)}, bf16[2,128,128]{2,1,0:T(8,128)(2,1)}, u32[]{:S(2)}) copy-start(bf16[2,128,128]{2,1,0:T(8,128)(2,1)} %get-tuple-element.72) | copy-start | bytes 196612
  108.1 25.6 %copy-start.13 = (bf16[2,128,128]{2,1,0:T(8,128)(2,1)S(1)}, bf16[2,128,128]{2,1,0:T(8,128)(2,1)}, u32[]{:S(2)}) copy-start(bf16[2,128,128]{2,1,0:T(8,128)(2,1)} %copy-done.12) | copy-start | bytes 196612
  108.1 7.8 %collective-permute-start.12 = (bf16[2,128,128]{2,1,0:T(8,128)(2,1)S(1)}, bf16[2,128,128]{2,1,0:T(8,128)(2,1)S(1)}, u32[]{:S(2)}, u32[]{:S(2)}) collective-permute-start(bf16[2,128,128]{2,1,0:T(8,128)(2,1)S(1)} %add_convert_fusion.3), channel_id=1, source_target_pairs={{0,32},{8,40},{16,48},{24,56},{32,0},{40,8},{48,16},{56,24},{64,96... | collective-permute-start | bytes 196616 | tf_op jit(solution)/shard_map/ppermute | solution.py:26
  116.1 9.9 %collective-permute-start.13 = (bf16[2,128,128]{2,1,0:T(8,128)(2,1)S(1)}, bf16[2,128,128]{2,1,0:T(8,128)(2,1)S(1)}, u32[]{:S(2)}, u32[]{:S(2)}) collective-permute-start(bf16[2,128,128]{2,1,0:T(8,128)(2,1)S(1)} %add_convert_fusion.2), channel_id=1, source_target_pairs={{0,64},{8,72},{16,80},{24,88},{32,96},{40,104},{48,112},{56,120},{... | collective-permute-start | bytes 196616 | tf_op jit(solution)/shard_map/ppermute | solution.py:26
  117.7 27.9 %all-to-all-start.1 = ((bf16[8,256,256]{2,1,0:T(8,128)(2,1)}), bf16[8,256,256]{2,1,0:T(8,128)(2,1)S(1)}, u32[]{:S(2)}, u32[]{:S(2)}) async-start(bf16[8,256,256]{2,1,0:T(8,128)(2,1)} %shard_map.113), calls=%async_computation.1 | async-start | bytes 2097152 | tf_op jit(solution)/shard_map/all_to_all | solution.py:555
  126.2 6.8 %collective-permute-start.14 = (bf16[2,128,128]{2,1,0:T(8,128)(2,1)S(1)}, bf16[2,128,128]{2,1,0:T(8,128)(2,1)S(1)}, u32[]{:S(2)}, u32[]{:S(2)}) collective-permute-start(bf16[2,128,128]{2,1,0:T(8,128)(2,1)S(1)} %add_convert_fusion.1), channel_id=1, source_target_pairs={{128,0},{136,8},{144,16},{152,24},{160,32},{168,40},{176,48},{184,... | collective-permute-start | bytes 196616 | tf_op jit(solution)/shard_map/ppermute | solution.py:21
  133.9 3.5 %collective-permute-start.15 = (bf16[2,128,128]{2,1,0:T(8,128)(2,1)S(1)}, bf16[2,128,128]{2,1,0:T(8,128)(2,1)S(1)}, u32[]{:S(2)}, u32[]{:S(2)}) collective-permute-start(bf16[2,128,128]{2,1,0:T(8,128)(2,1)S(1)} %get-tuple-element.99), channel_id=1, source_target_pairs={{0,8},{8,0},{16,24},{24,16},{32,40},{40,32},{48,56},{56,48},{64,72... | collective-permute-start | bytes 196616 | tf_op jit(solution)/shard_map/ppermute | solution.py:26
  139.0 6.7 %collective-permute-start.16 = (bf16[128,512]{1,0:T(8,128)(2,1)S(1)}, bf16[128,512]{1,0:T(8,128)(2,1)S(1)}, u32[]{:S(2)}, u32[]{:S(2)}) collective-permute-start(bf16[128,512]{1,0:T(8,128)(2,1)S(1)} %slice_bitcast_fusion), channel_id=1, source_target_pairs={{0,128},{8,136},{16,144},{24,152},{32,160},{40,168},{48,176},{56,1... | collective-permute-start | bytes 393224 | tf_op jit(solution)/shard_map/ppermute | solution.py:26
  139.4 11.4 %copy-start.7 = (bf16[1,256,512]{2,1,0:T(8,128)(2,1)S(1)}, bf16[1,256,512]{2,1,0:T(8,128)(2,1)}, u32[]{:S(2)}) copy-start(bf16[1,256,512]{2,1,0:T(8,128)(2,1)} %reduce-scatter.2.cloned.1.call-done) | copy-start | bytes 786436
  145.9 5.9 %collective-permute-start.17 = (bf16[128,256]{1,0:T(8,128)(2,1)S(1)}, bf16[128,256]{1,0:T(8,128)(2,1)S(1)}, u32[]{:S(2)}, u32[]{:S(2)}) collective-permute-start(bf16[128,256]{1,0:T(8,128)(2,1)S(1)} %slice.187), channel_id=1, source_target_pairs={{0,8},{8,0},{16,24},{24,16},{32,40},{40,32},{48,56},{56,48},{64,72... | collective-permute-start | bytes 196616 | tf_op jit(solution)/shard_map/ppermute | solution.py:26
  (5 other events, 3.8 us)
Sparse Core Ops, SparseCore 0:
  20.5 49.5 all-gather.2
  99.3 38.3 reduce-scatter.1
